TPU v7x, 32 devices: a whole 2x2x4 slice. The times are simulated.
32 devices in a mesh: tower: 2 (over x), dp: 16 (over z, y, core).
Axes of the slice: x: 2, y: 2, z: 4, core: 2. Of those that a mesh axis runs over, the one named last changes fastest.
Arguments:
- tokens: bfloat16 [2, 128, 77, 768], P('tower', 'dp'), as said below
- lengths: int32 [128], P('dp'), may hold values from 5 to 77, as said below
- ln1_gain: bfloat16 [2, 768], P('tower', 'dp'), as said below
- ln1_bias: bfloat16 [2, 768], P('tower', 'dp'), as said below
- qkv_weight: bfloat16 [2, 768, 3, 768], P('tower', 'dp'), as said below
- qv_bias: bfloat16 [2, 2, 768], P('tower', None, 'dp'), as said below
- out_weight: bfloat16 [2, 768, 768], P('tower', 'dp'), as said below
- out_bias: bfloat16 [2, 768], P('tower', 'dp'), as said below
- ln2_gain: bfloat16 [2, 768], P('tower', 'dp'), as said below
- ln2_bias: bfloat16 [2, 768], P('tower', 'dp'), as said below
- fc_weight: bfloat16 [2, 768, 3072], P('tower', 'dp'), as said below
- fc_bias: bfloat16 [2, 3072], P('tower', 'dp'), as said below
- down_weight: bfloat16 [2, 3072, 768], P('tower', 'dp'), as said below
- down_bias: bfloat16 [2, 768], P('tower', 'dp'), as said below
- final_gain: bfloat16 [2, 768], P('tower', 'dp'), as said below
- final_bias: bfloat16 [2, 768], P('tower', 'dp'), as said below
- embed_weight: bfloat16 [2, 768, 512], P('tower', 'dp'), as said below
- logit_scale: float32 [1], replicated, may hold values from 3.4 to 4.1
Outputs:
- block_out: bfloat16 [2, 128, 77, 768], P('tower', 'dp')
- tokens_grad: float32 [2, 128, 77, 768], P('tower', 'dp')
- loss: float32 [1], replicated
- ln1_gain_grad: float32 [2, 768], P('tower', 'dp')
- ln1_bias_grad: float32 [2, 768], P('tower', 'dp')
- qkv_weight_grad: float32 [2, 768, 3, 768], P('tower', 'dp')
- qv_bias_grad: float32 [2, 2, 768], P('tower', None, 'dp')
- out_weight_grad: float32 [2, 768, 768], P('tower', 'dp')
- out_bias_grad: float32 [2, 768], P('tower', 'dp')
- ln2_gain_grad: float32 [2, 768], P('tower', 'dp')
- ln2_bias_grad: float32 [2, 768], P('tower', 'dp')
- fc_weight_grad: float32 [2, 768, 3072], P('tower', 'dp')
- fc_bias_grad: float32 [2, 3072], P('tower', 'dp')
- down_weight_grad: float32 [2, 3072, 768], P('tower', 'dp')
- down_bias_grad: float32 [2, 768], P('tower', 'dp')
- final_gain_grad: float32 [2, 768], P('tower', 'dp')
- final_bias_grad: float32 [2, 768], P('tower', 'dp')
- embed_weight_grad: float32 [2, 768, 512], P('tower', 'dp')
- logit_scale_grad: float32 [1], replicated
Inputs may be any that keep to these rules, and one draw needn't show every extreme that they name: `tokens`: image slot zero from row 50 on; text slot zero from feature 512 on. `lengths`: device 0 of dp holds a caption of 77 slots and one of 5. `ln1_gain`: text slot zero from feature 512 on. `ln1_bias`: text slot zero from feature 512 on. `qkv_weight`: text slot zero outside its first 512 rows and first 512 columns of each third. `qv_bias`: text slot zero from feature 512 on. `out_weight`: text slot zero outside its leading 512 x 512 block. `out_bias`: text slot zero from feature 512 on. `ln2_gain`: text slot zero from feature 512 on. `ln2_bias`: text slot zero from feature 512 on. `fc_weight`: text slot zero outside its leading 512 x 2048 block. `fc_bias`: text slot zero from unit 2048 on. `down_weight`: text slot zero outside its leading 2048 x 512 block. `down_bias`: text slot zero from feature 512 on. `final_gain`: text slot zero from feature 512 on. `final_bias`: text slot zero from feature 512 on. `embed_weight`: text slot zero from row 512 on.
All inputs are finite; a program needn't handle non-finite values.
Results may differ from a plain program's by a relative error of at most 0.02.
The roundings to bfloat16 on the way count: a program that leaves them out, or rounds other values in their place, can miss the bound.
Values may be sent and summed in bfloat16 or wider, within the bound.
No kernel may reach another device: no remote copies, remote signals or barrier semaphores. Data moves between devices by JAX's collectives and lax.ppermute only.
A program may use at most 192 MiB of HBM per device.

v0:
```python
import jax
import jax.numpy as jnp
from jax import lax
from jax.sharding import PartitionSpec as P

DI = 768
DT = 512
HD = 64
IMG_ROWS = 50


EPS = 1e-05
NORM_EPS = 1e-06
GELU_K = 1.702
NEG_FILL = -1e30


def swapped(block, axis, stride):
    count = lax.axis_size(axis)
    route = []
    for low in range(count):
        high = low | 1 << stride
        if high != low and high < count:
            route += [(low, high), (high, low)]
    return lax.ppermute(block, axis, route)


def masked_norm(values, norm_gain, norm_bias, col_keep, width_real):
    row_mean = jnp.sum(values * col_keep, axis=-1, keepdims=True) / width_real
    centred = (values - row_mean) * col_keep
    row_var = jnp.sum(centred * centred, axis=-1, keepdims=True) / width_real
    inv_std = lax.rsqrt(row_var + EPS)
    normed = centred * inv_std
    return (normed * norm_gain + norm_bias, normed, inv_std)


def masked_norm_back(grad_out, norm_gain, normed, inv_std, col_keep, width_real):
    grad_normed = grad_out * norm_gain
    mean_grad = jnp.sum(grad_normed, axis=-1, keepdims=True) / width_real
    mean_cross = jnp.sum(grad_normed * normed, axis=-1, keepdims=True) / width_real
    grad_in = col_keep * inv_std * (grad_normed - mean_grad - normed * mean_cross)
    return (grad_in, jnp.sum(grad_out * normed, axis=0), jnp.sum(grad_out, axis=0))


def contract_rows(left_op, right_op):
    return lax.dot_general(
        left_op, right_op, (((0,), (0,)), ((), ())), preferred_element_type=jnp.float32
    )


def contract_cols(left_op, right_op):
    return lax.dot_general(
        left_op, right_op, (((1,), (1,)), ((), ())), preferred_element_type=jnp.float32
    )


def column_sum(values):
    return jnp.sum(values, axis=0, dtype=jnp.float32)


def body(
    tokens,
    lengths,
    ln1_gain,
    ln1_bias,
    qkv_weight,
    qv_bias,
    out_weight,
    out_bias,
    ln2_gain,
    ln2_bias,
    fc_weight,
    fc_bias,
    down_weight,
    down_bias,
    final_gain,
    final_bias,
    embed_weight,
    logit_scale,
):
    f32 = jnp.float32
    bf16 = jnp.bfloat16
    tower_index = lax.axis_index("tower")
    dp_index = lax.axis_index("dp")
    dp_count = lax.axis_size("dp")
    samples, seq_rows, width_all = (tokens.shape[1], tokens.shape[2], tokens.shape[3])
    head_count = width_all // HD
    sample_total = samples * dp_count
    flat_rows = samples * seq_rows
    is_text = tower_index == 1
    width_int = jnp.where(is_text, DT, DI)
    width_real = width_int.astype(f32)
    col_keep = (lax.broadcasted_iota(jnp.int32, (width_all,), 0) < width_int).astype(f32)
    seq_lens = jnp.where(is_text, lengths, IMG_ROWS)
    positions = lax.broadcasted_iota(jnp.int32, (samples, seq_rows), 1)
    row_keep = (positions < seq_lens[:, None]).astype(f32).reshape(flat_rows, 1)
    query_pos = lax.broadcasted_iota(jnp.int32, (seq_rows, seq_rows), 0)
    key_pos = lax.broadcasted_iota(jnp.int32, (seq_rows, seq_rows), 1)
    allowed = (key_pos[None] < seq_lens[:, None, None]) & (
        jnp.logical_not(is_text) | (key_pos <= query_pos)
    )[None]
    pool_pos = jnp.where(is_text, lengths - 1, 0)
    pool_hot = (positions == pool_pos[:, None]).astype(f32)
    score_mult = float(HD) ** (-0.5)
    gathered = (
        lax.all_gather(ln1_gain[0], "dp", axis=0, tiled=True),
        lax.all_gather(ln1_bias[0], "dp", axis=0, tiled=True),
        lax.all_gather(qkv_weight[0], "dp", axis=0, tiled=True),
        lax.all_gather(qv_bias[0], "dp", axis=1, tiled=True),
        lax.all_gather(out_weight[0], "dp", axis=0, tiled=True),
        lax.all_gather(out_bias[0], "dp", axis=0, tiled=True),
        lax.all_gather(ln2_gain[0], "dp", axis=0, tiled=True),
        lax.all_gather(ln2_bias[0], "dp", axis=0, tiled=True),
        lax.all_gather(fc_weight[0], "dp", axis=0, tiled=True),
        lax.all_gather(fc_bias[0], "dp", axis=0, tiled=True),
        lax.all_gather(down_weight[0], "dp", axis=0, tiled=True),
        lax.all_gather(down_bias[0], "dp", axis=0, tiled=True),
        lax.all_gather(final_gain[0], "dp", axis=0, tiled=True),
        lax.all_gather(final_bias[0], "dp", axis=0, tiled=True),
        lax.all_gather(embed_weight[0], "dp", axis=0, tiled=True),
    )
    (
        gain_one,
        bias_one,
        w_qkv,
        b_qv,
        w_out,
        b_out,
        gain_two,
        bias_two,
        w_fc,
        b_fc,
        w_down,
        b_down,
        gain_final,
        bias_final,
        w_embed,
    ) = gathered
    stream = tokens[0].astype(f32).reshape(flat_rows, width_all)
    normed_h1, norm_one, inv_one = masked_norm(
        stream, gain_one.astype(f32), bias_one.astype(f32), col_keep, width_real
    )
    normed_one = normed_h1.astype(bf16)
    qkv_bias = jnp.concatenate(
        [b_qv[0].astype(f32), jnp.zeros((width_all,), f32), b_qv[1].astype(f32)]
    )
    qkv_flat = (
        jnp.dot(normed_one, w_qkv.reshape(width_all, 3 * width_all), preferred_element_type=f32)
        + qkv_bias
    )
    qkv_low = qkv_flat.astype(bf16).reshape(samples, seq_rows, 3, head_count, HD)
    query_all = qkv_low[:, :, 0]
    key_all = qkv_low[:, :, 1]
    value_all = qkv_low[:, :, 2]

    def masked_scores():
        raw = (
            jnp.einsum("sqhd,skhd->shqk", query_all, key_all, preferred_element_type=f32)
            * score_mult
        )
        return jnp.where(allowed[:, None], raw, NEG_FILL)

    scores = masked_scores()
    row_top = jnp.max(scores, axis=-1, keepdims=True)
    exp_terms = jnp.exp(scores - row_top)
    exp_sum = jnp.sum(exp_terms, axis=-1, keepdims=True)
    log_total = row_top + jnp.log(exp_sum)
    attn_probs = (exp_terms / exp_sum).astype(bf16)
    head_mix = jnp.einsum("shqk,skhd->sqhd", attn_probs, value_all, preferred_element_type=f32)
    head_mix_low = head_mix.astype(bf16).reshape(flat_rows, width_all)
    attn_out = jnp.dot(head_mix_low, w_out, preferred_element_type=f32) + b_out.astype(f32)
    middle = stream + attn_out
    normed_h2, norm_two, inv_two = masked_norm(
        middle, gain_two.astype(f32), bias_two.astype(f32), col_keep, width_real
    )
    normed_two = normed_h2.astype(bf16)
    hidden_pre = jnp.dot(normed_two, w_fc, preferred_element_type=f32) + b_fc.astype(f32)
    gate_sig = jax.nn.sigmoid(GELU_K * hidden_pre)
    act_low = (hidden_pre * gate_sig).astype(bf16)
    branch = jnp.dot(act_low, w_down, preferred_element_type=f32) + b_down.astype(f32)
    block_rows = row_keep * (middle + branch)
    block_out = block_rows.astype(bf16).reshape(1, samples, seq_rows, width_all)
    block_three = block_rows.reshape(samples, seq_rows, width_all)
    pooled = jnp.take_along_axis(block_three, pool_pos[:, None, None], axis=1)[:, 0]
    normed_hf, norm_final, inv_final = masked_norm(
        pooled, gain_final.astype(f32), bias_final.astype(f32), col_keep, width_real
    )
    head_low = normed_hf.astype(bf16)
    projected = jnp.dot(head_low, w_embed, preferred_element_type=f32)
    inv_norm = lax.rsqrt(jnp.sum(projected * projected, axis=-1, keepdims=True) + NORM_EPS)
    embed_low = (projected * inv_norm).astype(bf16)
    own_all = lax.all_gather(embed_low, "dp", axis=0, tiled=True)
    others = swapped(own_all, "tower", 0)
    logit_mult = jnp.exp(logit_scale[0])
    similar = contract_cols(embed_low, others)
    logits = logit_mult * similar
    logit_top = jnp.max(logits, axis=-1, keepdims=True)
    logit_total = logit_top + jnp.log(jnp.sum(jnp.exp(logits - logit_top), axis=-1, keepdims=True))
    label_col = dp_index * samples + lax.broadcasted_iota(jnp.int32, (samples, 1), 0)
    label_hot = (lax.broadcasted_iota(jnp.int32, (samples, sample_total), 1) == label_col).astype(
        f32
    )
    diag_logit = jnp.sum(label_hot * logits, axis=-1, keepdims=True)
    loss_part = jnp.sum(logit_total - diag_logit) / (2.0 * sample_total)
    grad_logits = (jnp.exp(logits - logit_total) - label_hot) * 0.5
    scale_part = logit_mult * jnp.sum(grad_logits * similar)
    grad_sims = (logit_mult * grad_logits).astype(bf16)
    grad_own = jnp.dot(grad_sims, others, preferred_element_type=f32)
    grad_others = contract_rows(grad_sims, embed_low)
    sent_back = swapped(grad_others, "tower", 0)
    returned = lax.psum_scatter(sent_back, "dp", scatter_dimension=0, tiled=True)
    totals = lax.psum((loss_part, scale_part), ("tower", "dp"))
    grad_embed = grad_own + returned
    again = (
        lax.all_gather(ln1_gain[0], "dp", axis=0, tiled=True),
        lax.all_gather(qkv_weight[0], "dp", axis=0, tiled=True),
        lax.all_gather(out_weight[0], "dp", axis=0, tiled=True),
        lax.all_gather(ln2_gain[0], "dp", axis=0, tiled=True),
        lax.all_gather(fc_weight[0], "dp", axis=0, tiled=True),
        lax.all_gather(down_weight[0], "dp", axis=0, tiled=True),
        lax.all_gather(final_gain[0], "dp", axis=0, tiled=True),
        lax.all_gather(embed_weight[0], "dp", axis=0, tiled=True),
    )
    (
        back_gain_one,
        back_qkv,
        back_out,
        back_gain_two,
        back_fc,
        back_down,
        back_gain_final,
        back_embed,
    ) = again
    cross_term = jnp.sum(grad_embed * projected, axis=-1, keepdims=True)
    grad_proj = inv_norm * grad_embed - projected * inv_norm * inv_norm * inv_norm * cross_term
    grad_proj_low = grad_proj.astype(bf16)
    grad_head = contract_cols(grad_proj_low, back_embed)
    grad_pooled, d_gain_final, d_bias_final = masked_norm_back(
        grad_head, back_gain_final.astype(f32), norm_final, inv_final, col_keep, width_real
    )
    grad_rows = (pool_hot[:, :, None] * grad_pooled[:, None, :]).reshape(flat_rows, width_all)
    grad_branch_low = grad_rows.astype(bf16)
    d_down_b = column_sum(grad_branch_low)
    grad_act = contract_cols(grad_branch_low, back_down)
    grad_pre_low = (
        grad_act * (gate_sig + GELU_K * hidden_pre * gate_sig * (1.0 - gate_sig))
    ).astype(bf16)
    d_fc_b = column_sum(grad_pre_low)
    grad_norm_two = contract_cols(grad_pre_low, back_fc)
    grad_mid_norm, d_gain_two, d_bias_two = masked_norm_back(
        grad_norm_two, back_gain_two.astype(f32), norm_two, inv_two, col_keep, width_real
    )
    grad_middle = grad_rows + grad_mid_norm
    grad_attn_low = grad_middle.astype(bf16)
    d_out_b = column_sum(grad_attn_low)
    grad_mix_low = (
        contract_cols(grad_attn_low, back_out)
        .astype(bf16)
        .reshape(samples, seq_rows, head_count, HD)
    )
    probs_again = jnp.exp(masked_scores() - log_total)
    probs_low = probs_again.astype(bf16)
    grad_value = jnp.einsum("shqk,sqhd->skhd", probs_low, grad_mix_low, preferred_element_type=f32)
    grad_probs = jnp.einsum("sqhd,skhd->shqk", grad_mix_low, value_all, preferred_element_type=f32)
    grad_scores = probs_again * (
        grad_probs - jnp.sum(probs_again * grad_probs, axis=-1, keepdims=True)
    )
    grad_scores_low = grad_scores.astype(bf16)
    grad_query = (
        jnp.einsum("shqk,skhd->sqhd", grad_scores_low, key_all, preferred_element_type=f32)
        * score_mult
    )
    grad_key = (
        jnp.einsum("shqk,sqhd->skhd", grad_scores_low, query_all, preferred_element_type=f32)
        * score_mult
    )
    grad_qkv_low = (
        jnp.stack([grad_query, grad_key, grad_value], axis=2)
        .astype(bf16)
        .reshape(flat_rows, 3 * width_all)
    )
    d_qkv_w = contract_rows(normed_one, grad_qkv_low).reshape(width_all, 3, width_all)
    qkv_sums = column_sum(grad_qkv_low).reshape(3, width_all)
    d_qv_b = jnp.stack([qkv_sums[0], qkv_sums[2]])
    grad_norm_one = contract_cols(grad_qkv_low, back_qkv.reshape(width_all, 3 * width_all))
    grad_in_norm, d_gain_one, d_bias_one = masked_norm_back(
        grad_norm_one, back_gain_one.astype(f32), norm_one, inv_one, col_keep, width_real
    )
    tokens_grad = (grad_middle + grad_in_norm).reshape(1, samples, seq_rows, width_all)
    d_embed_w = contract_rows(head_low, grad_proj_low)
    d_down_w = contract_rows(act_low, grad_branch_low)
    d_fc_w = contract_rows(normed_two, grad_pre_low)
    d_out_w = contract_rows(head_mix_low, grad_attn_low)
    shares = (
        lax.psum_scatter(d_gain_one, "dp", scatter_dimension=0, tiled=True),
        lax.psum_scatter(d_bias_one, "dp", scatter_dimension=0, tiled=True),
        lax.psum_scatter(d_qkv_w, "dp", scatter_dimension=0, tiled=True),
        lax.psum_scatter(d_qv_b, "dp", scatter_dimension=1, tiled=True),
        lax.psum_scatter(d_out_w, "dp", scatter_dimension=0, tiled=True),
        lax.psum_scatter(d_out_b, "dp", scatter_dimension=0, tiled=True),
        lax.psum_scatter(d_gain_two, "dp", scatter_dimension=0, tiled=True),
        lax.psum_scatter(d_bias_two, "dp", scatter_dimension=0, tiled=True),
        lax.psum_scatter(d_fc_w, "dp", scatter_dimension=0, tiled=True),
        lax.psum_scatter(d_fc_b, "dp", scatter_dimension=0, tiled=True),
        lax.psum_scatter(d_down_w, "dp", scatter_dimension=0, tiled=True),
        lax.psum_scatter(d_down_b, "dp", scatter_dimension=0, tiled=True),
        lax.psum_scatter(d_gain_final, "dp", scatter_dimension=0, tiled=True),
        lax.psum_scatter(d_bias_final, "dp", scatter_dimension=0, tiled=True),
        lax.psum_scatter(d_embed_w, "dp", scatter_dimension=0, tiled=True),
    )
    results = list(shares)
    outputs = [item[None] for item in results]
    loss = totals[0].reshape(1)
    logit_scale_grad = totals[1].reshape(1)
    return (
        block_out,
        tokens_grad,
        loss,
        outputs[0],
        outputs[1],
        outputs[2],
        outputs[3],
        outputs[4],
        outputs[5],
        outputs[6],
        outputs[7],
        outputs[8],
        outputs[9],
        outputs[10],
        outputs[11],
        outputs[12],
        outputs[13],
        outputs[14],
        logit_scale_grad,
    )


def solution(mesh):
    return jax.shard_map(
        body,
        mesh=mesh,
        in_specs=(
            P("tower", "dp", None, None),
            P("dp"),
            P("tower", "dp"),
            P("tower", "dp"),
            P("tower", "dp", None, None),
            P("tower", None, "dp"),
            P("tower", "dp", None),
            P("tower", "dp"),
            P("tower", "dp"),
            P("tower", "dp"),
            P("tower", "dp", None),
            P("tower", "dp"),
            P("tower", "dp", None),
            P("tower", "dp"),
            P("tower", "dp"),
            P("tower", "dp"),
            P("tower", "dp", None),
            P(),
        ),
        out_specs=(
            P("tower", "dp", None, None),
            P("tower", "dp", None, None),
            P(),
            P("tower", "dp"),
            P("tower", "dp"),
            P("tower", "dp", None, None),
            P("tower", None, "dp"),
            P("tower", "dp", None),
            P("tower", "dp"),
            P("tower", "dp"),
            P("tower", "dp"),
            P("tower", "dp", None),
            P("tower", "dp"),
            P("tower", "dp", None),
            P("tower", "dp"),
            P("tower", "dp"),
            P("tower", "dp"),
            P("tower", "dp", None),
            P(),
        ),
        check_vma=False,
    )
```

profile of v0, /device:TPU:0, one launch (start us, length us, event | category | flops | bytes accessed | tf_op | source)
XLA Modules:
  0.0 893.1 jit_solution(10914504779432311410)
XLA Ops:
  17.1 63.5 %all-reduce.20 = (bf16[768]{0:T(1024)(128)(2,1)S(1)}, bf16[768]{0:T(1024)(128)(2,1)S(1)}, bf16[768]{0:T(1024)(128)(2,1)S(1)}, bf16[768]{0:T(1024)(128)(2,1)S(1)}...) all-reduce(bf16[768]{0:T(1024)(128)(2,1)S(1)} %dynamic-update-slice, ...), channel_id=3, replica_groups=mesh['tower'=2,'dp'=16] {'dp'}, use_global_device_ids=true, to_apply=%add.1 | all-reduce | flops 9216 | bytes 36864
  87.5 18.4 %all-gather.3 = bf16[1,2,768]{1,0,2:T(2,128)(2,1)S(1)} all-gather(bf16[1,2,48]{1,0,2:T(2,128)(2,1)S(1)} %copy.125), channel_id=5, replica_groups=mesh['tower'=2,'dp'=16] {'dp'}, dimensions={2}, use_global_device_ids=true | all-gather | bytes 3264 | tf_op jit(solution)/shard_map/all_gather | solution.py:109
  113.2 25.5 %all-gather.14 = bf16[1,768,512]{2,1,0:T(8,128)(2,1)} all-gather(bf16[1,48,512]{2,1,0:T(8,128)(2,1)S(1)} %copy-done.29), channel_id=16, replica_groups=mesh['tower'=2,'dp'=16] {'dp'}, dimensions={1}, use_global_device_ids=true | all-gather | bytes 835584 | tf_op jit(solution)/shard_map/all_gather | solution.py:120
  143.2 5.9 add_convert_fusion
  149.1 9.7 %reshape.511 = bf16[8,77,3,12,64]{4,3,2,1,0:T(8,128)(2,1)} reshape(bf16[616,2304]{1,0:T(8,128)(2,1)} %add_convert_fusion) | data formatting | bytes 5677056 | tf_op jit(solution)/shard_map/reshape | solution.py:151
  188.7 8.2 fusion.5
  197.0 13.9 %all-gather.26.cloned.1.call-done = bf16[1,3072,768]{2,1,0:T(8,128)(2,1)} async-done(((bf16[1,192,768]{2,1,0:T(8,128)(2,1)}), bf16[1,3072,768]{2,1,0:T(8,128)(2,1)}) %all-gather.26.cloned.1.call-update) | async-done | bytes 4718608 | tf_op jit(solution)/shard_map/all_gather | solution.py:116
  210.8 10.2 %fusion.60 = (bf16[616,768]{1,0:T(8,128)(2,1)}, f32[616,768]{1,0:T(8,128)}) fusion(f32[616,768]{1,0:T(8,128)S(1)} %get-tuple-element.166, f32[768]{0:T(1024)S(1)} %copy-done.56, bf16[1,3072,768]{2,1,0:T(8,128)(2,1)} %all-gather.26.cloned.1.call-done, f32[616,3072]{1,0:T(8,128)} %fusion.5, f32[3072]{0:T(1024)S(1)} %copy-done.48, f32[616]{0:T(1024)S(1)} %copy-done.57), kind=kOutput, calls=%fused_computation.149 | convolution fusion | flops 2921791488 | bytes 17036704 | tf_op jit(solution)/shard_map/dot_general | solution.py:180
  231.4 20.7 %all_gather.71 = bf16[128,512]{1,0:T(8,128)(2,1)} all-gather(bf16[8,512]{1,0:T(8,128)(2,1)S(1)} %multiply_convert_fusion.5), channel_id=1, replica_groups=mesh['tower'=2,'dp'=16] {'dp'}, dimensions={0}, use_global_device_ids=true | all-gather | bytes 139264 | tf_op jit(solution)/shard_map/all_gather | solution.py:192
  261.4 6.4 collective-permute-done.1
  270.8 49.7 %reduce-scatter.10.cloned.1.call-done = f32[8,512]{1,0:T(8,128)} async-done(((f32[128,512]{1,0:T(8,128)}), f32[8,512]{1,0:T(8,128)}) %reduce-scatter.10.cloned.1.call-update) | async-done | bytes 16400 | tf_op jit(solution)/shard_map/reduce_scatter | solution.py:211
  330.6 9.5 %convert_reduce_fusion.1 = (f32[3072]{0:T(1024)}, bf16[616,3072]{1,0:T(8,128)(2,1)S(1)}) fusion(f32[616,3072]{1,0:T(8,128)} %fusion.5, f32[3072]{0:T(1024)} %convert_element_type.252, bf16[1,3072,768]{2,1,0:T(8,128)(2,1)} %all-gather.26.cloned.1.call-done, f32[616,768]{1,0:T(8,128)} %mul.407, f32[616]{0:T(1024)} %reshape.394), kind=kOutput, calls=%fused_computation.3 | convolution fusion | flops 2932196352 | bytes 17992096 | tf_op jit(solution)/shard_map/dot_general | solution.py:52
  340.1 8.0 multiply_reduce_fusion.1
  382.4 13.8 %copy.139 = bf16[8,77,3,12,64]{1,0,4,3,2:T(8,128)(2,1)} copy(bf16[8,77,3,12,64]{1,4,3,0,2:T(8,128)(2,1)} %get-tuple-element.151) | data formatting | bytes 5677056 | tf_op jit(solution)/shard_map/convert_element_type | solution.py:279
  396.2 8.2 convert_element_type.224
  404.3 6.8 fusion.61
  411.3 10.5 %fusion.39 = f32[768,3072]{1,0:T(8,128)} fusion(bf16[616,3072]{1,0:T(8,128)(2,1)} %copy-done.14, f32[768]{0:T(1024)S(1)} %convert_element_type.251, f32[768]{0:T(1024)S(1)} %convert_element_type.250, f32[616,768]{1,0:T(8,128)} %copy-done.2, f32[616]{0:T(1024)S(1)} %add_rsqrt_fusion, f32[616]{0:T(1024)S(1)} %broadcast_divide_fusion.4, f32[768]{0:T(1024)S(1)} %fusion.43), kind=kOutput, calls=%fused_computation.76 | convolution fusion | flops 2909491200 | bytes 15128384 | tf_op jit(solution)/shard_map/dot_general | solution.py:46
  422.4 12.2 %fusion.53 = f32[3072,768]{1,0:T(8,128)} fusion(f32[616,768]{1,0:T(8,128)} %mul.407, f32[616]{0:T(1024)S(1)} %copy-done.44, f32[616,3072]{1,0:T(8,128)} %fusion.5, f32[3072]{0:T(1024)S(1)} %copy-done.49), kind=kOutput, calls=%fused_computation.144 | convolution fusion | flops 2920845312 | bytes 18913696 | tf_op jit(solution)/shard_map/dot_general | solution.py:46
  442.1 41.8 %all-reduce.18 = (f32[1]{0:T(128)}, f32[1]{0:T(128)}) all-reduce(f32[1]{0:T(128)} %bitcast.29, f32[1]{0:T(128)} %bitcast.47), channel_id=1, replica_groups=mesh['tower'=2,'dp'=16] {'tower','dp'}, use_global_device_ids=true, to_apply=%region_22.23 | all-reduce | flops 2 | bytes 16 | tf_op jit(solution)/shard_map/psum | solution.py:212
  483.9 6.6 multiply_reduce_fusion.2
  497.0 58.9 %all-reduce.19 = (f32[768]{0:T(1024)S(1)}, f32[768]{0:T(1024)S(1)}, f32[768]{0:T(1024)S(1)}, f32[768]{0:T(1024)S(1)}, f32[768]{0:T(1024)S(1)}, /*index=5*/f32[30...) all-reduce(f32[768]{0:T(1024)S(1)} %get-tuple-element.116, ...), channel_id=18, replica_groups=mesh['tower'=2,'dp'=16] {'dp'}, use_global_device_ids=true, to_apply=%region_24.25.clone | all-reduce | flops 9216 | bytes 73728
  560.3 94.1 %reduce-scatter.12.cloned.1.call-done = f32[48,3,768]{2,0,1:T(8,128)} async-done(((f32[768,3,768]{2,0,1:T(8,128)}), f32[48,3,768]{2,0,1:T(8,128)}) %reduce-scatter.12.cloned.1.call-update) | async-done | bytes 442384 | tf_op jit(solution)/shard_map/reduce_scatter | solution.py:297
  654.4 115.4 %reduce-scatter.16.cloned.1.call-done = f32[48,3072]{1,0:T(8,128)} async-done(((f32[768,3072]{1,0:T(8,128)}), f32[48,3072]{1,0:T(8,128)}) %reduce-scatter.16.cloned.1.call-update) | async-done | bytes 589840 | tf_op jit(solution)/shard_map/reduce_scatter | solution.py:303
  769.8 116.4 %reduce-scatter.18.cloned.1.call-done = f32[192,768]{1,0:T(8,128)} async-done(((f32[3072,768]{1,0:T(8,128)}), f32[192,768]{1,0:T(8,128)}) %reduce-scatter.18.cloned.1.call-update) | async-done | bytes 589840 | tf_op jit(solution)/shard_map/reduce_scatter | solution.py:305
  (323 shorter events, 138.9 us)
Async XLA Ops:
  7.2 131.5 %all-gather.20.cloned.1.call-start = ((), (), s32[]{:S(2)}) async-start(), calls=%async_computation.13 | async-start | bytes 3760128 | tf_op jit(solution)/shard_map/all_gather | solution.py:108
  7.9 177.0 %all-gather.22.cloned.1.call-start = ((), (), s32[]{:S(2)}) async-start(), calls=%async_computation.14 | async-start | bytes 1253376 | tf_op jit(solution)/shard_map/all_gather | solution.py:110
  8.7 180.1 %all-gather.24.cloned.1.call-start = ((), (), s32[]{:S(2)}) async-start(), calls=%async_computation.15 | async-start | bytes 5013504 | tf_op jit(solution)/shard_map/all_gather | solution.py:114
  9.4 201.4 %all-gather.26.cloned.1.call-start = ((), (), s32[]{:S(2)}) async-start(), calls=%async_computation.16 | async-start | bytes 5013504 | tf_op jit(solution)/shard_map/all_gather | solution.py:116
  10.0 310.5 %reduce-scatter.10.cloned.1.call-start = ((), (), s32[]{:S(2)}) async-start(), calls=%async_computation.7 | async-start | bytes 278528 | tf_op jit(solution)/shard_map/reduce_scatter | solution.py:211
  11.6 69.6 %copy-start.3 = (bf16[1,8,77,768]{3,1,2,0:T(8,128)(2,1)S(1)}, bf16[1,8,77,768]{3,1,2,0:T(8,128)(2,1)}, u32[]{:S(2)}) copy-start(bf16[1,8,77,768]{3,1,2,0:T(8,128)(2,1)} %param.18) | copy-start | bytes 2838532
  83.6 55.1 %copy-start.7 = (bf16[1,8,77,768]{3,2,1,0:T(8,128)(2,1)}, bf16[1,8,77,768]{3,2,1,0:T(8,128)(2,1)S(1)}, u32[]{:S(2)}) copy-start(bf16[1,8,77,768]{3,2,1,0:T(8,128)(2,1)S(1)} %copy.123) | copy-start | bytes 2838532
  83.6 29.6 %copy-start.29 = (bf16[1,48,512]{2,1,0:T(8,128)(2,1)S(1)}, bf16[1,48,512]{2,1,0:T(8,128)(2,1)}, u32[]{:S(2)}) copy-start(bf16[1,48,512]{2,1,0:T(8,128)(2,1)} %param.34) | copy-start | bytes 147460
  106.5 32.2 %copy-start.66 = (s32[8]{0:T(128)}, s32[8]{0:T(128)S(1)}, u32[]{:S(2)}) copy-start(s32[8]{0:T(128)S(1)} %get-tuple-element.155) | copy-start | bytes 100
  188.2 151.9 %copy-start.2 = (f32[616,768]{1,0:T(8,128)}, f32[616,768]{1,0:T(8,128)S(1)}, u32[]{:S(2)}) copy-start(f32[616,768]{1,0:T(8,128)S(1)} %get-tuple-element.166) | copy-start | bytes 5677060
  188.7 22.1 %copy-start.48 = (f32[3072]{0:T(1024)S(1)}, f32[3072]{0:T(1024)}, u32[]{:S(2)}) copy-start(f32[3072]{0:T(1024)} %convert_element_type.252) | copy-start | bytes 36868
  229.4 39.2 %copy-start.17 = (f32[8,768]{1,0:T(8,128)}, f32[8,768]{1,0:T(8,128)S(1)}, u32[]{:S(2)}) copy-start(f32[8,768]{1,0:T(8,128)S(1)} %gather_fusion) | copy-start | bytes 73732
  229.8 38.8 %copy-start.53 = (f32[8]{0:T(128)}, f32[8]{0:T(128)S(1)}, u32[]{:S(2)}) copy-start(f32[8]{0:T(128)S(1)} %add_rsqrt_fusion.3) | copy-start | bytes 100
  231.3 22.9 %copy-start.28 = (f32[8,512]{1,0:T(8,128)}, f32[8,512]{1,0:T(8,128)S(1)}, u32[]{:S(2)}) copy-start(f32[8,512]{1,0:T(8,128)S(1)} %get-tuple-element.170) | copy-start | bytes 49156
  231.3 37.3 %copy-start.60 = (f32[8]{0:T(128)}, f32[8]{0:T(128)S(1)}, u32[]{:S(2)}) copy-start(f32[8]{0:T(128)S(1)} %add_rsqrt_fusion.2) | copy-start | bytes 100
  252.1 6.1 collective-permute-start
  259.9 7.9 collective-permute-start.1
  267.8 291.1 %reduce-scatter.22.cloned.1.call-start = ((), (), s32[]{:S(2)}) async-start(), calls=%async_computation.17 | async-start | bytes 417792
  375.6 184.7 %reduce-scatter.20.cloned.1.call-start = ((), (), s32[]{:S(2)}) async-start(), calls=%async_computation.12 | async-start | bytes 1671168 | tf_op jit(solution)/shard_map/reduce_scatter | solution.py:309
  377.4 182.9 %reduce-scatter.14.cloned.1.call-start = ((), (), s32[]{:S(2)}) async-start(), calls=%async_computation.9 | async-start | bytes 2506752 | tf_op jit(solution)/shard_map/reduce_scatter | solution.py:299
  380.0 274.3 %reduce-scatter.12.cloned.1.call-start = ((), (), s32[]{:S(2)}) async-start(), calls=%async_computation.8 | async-start | bytes 7520256 | tf_op jit(solution)/shard_map/reduce_scatter | solution.py:297
  411.2 358.5 %reduce-scatter.16.cloned.1.call-start = ((), (), s32[]{:S(2)}) async-start(), calls=%async_computation.10 | async-start | bytes 10027008 | tf_op jit(solution)/shard_map/reduce_scatter | solution.py:303
  421.8 464.4 %reduce-scatter.18.cloned.1.call-start = ((), (), s32[]{:S(2)}) async-start(), calls=%async_computation.11 | async-start | bytes 10027008 | tf_op jit(solution)/shard_map/reduce_scatter | solution.py:305
  436.8 47.1 %copy-start.31 = (f32[768]{0:T(1024)S(1)}, f32[768]{0:T(1024)}, u32[]{:S(2)}) copy-start(f32[768]{0:T(1024)} %copy-done.30) | copy-start | bytes 9220
  (68 other events, 288.1 us)
Sparse Core Ops, SparseCore 0:
  10.3 50.0 all-gather.19
  62.7 38.0 all-gather.21
  103.1 53.8 all-gather.23
  159.1 51.6 all-gather.25
  267.9 52.4 reduce-scatter.9
  375.7 54.6 reduce-scatter.21
  435.1 58.5 reduce-scatter.19
  498.0 62.1 reduce-scatter.13
  565.3 89.0 reduce-scatter.11
  658.9 110.8 reduce-scatter.15
  775.0 111.0 reduce-scatter.17
where the time goes:
time: 902 us; the launch traced here: 893 us
  waiting for transfers between devices  402 us (45%)
  blocking collectives  229 us (25%)
  local copies, waits for them, and re-layouts  109 us (12%)
  matrix products  102 us (11%)
  other arithmetic  27 us (3%)
  between operations  20 us (2%)
    unnamed x2, blocking collectives  122 us
    reduce_scatter x1, waiting for transfers between devices, body(): lax.psum_scatter(d_down_w, 'dp', scatter_dimension=0, tiled=True)  116 us
    reduce_scatter x1, waiting for transfers between devices, body(): lax.psum_scatter(d_fc_w, 'dp', scatter_dimension=0, tiled=True)  115 us
    reduce_scatter x1, waiting for transfers between devices, body(): lax.psum_scatter(d_qkv_w, 'dp', scatter_dimension=0, tiled=True)  94.1 us
    reduce_scatter x1, waiting for transfers between devices, body(): lax.psum_scatter(sent_back, 'dp', scatter_dimension=0, tiled=True)  49.7 us
    psum x1, blocking collectives, body(): totals = lax.psum((loss_part, scale_part), ('tower', 'dp'))  41.8 us
    dot_general x6, matrix products, contract_rows(): lax.dot_general(left_op, right_op, (((0,), (0,)), ((), ())), preferred_el...  34 us
    dot_general x6, matrix products, contract_cols(): lax.dot_general(left_op, right_op, (((1,), (1,)), ((), ())), preferred_el...  29.3 us
  transfers between devices with their start and end apart: 13, of which 7 were waited for; matrix products, arithmetic and copies ran while one was open for 17% of the time, Pallas kernels for 0%

commit v1 on v0

--- a/solution.py
+++ b/solution.py
@@ -1,12 +1,15 @@
 import jax
 import jax.numpy as jnp
 from jax import lax
+from jax.experimental import pallas as pl
+from jax.experimental.pallas import tpu as pltpu
 from jax.sharding import PartitionSpec as P
 
 DI = 768
 DT = 512
 HD = 64
 IMG_ROWS = 50
+EMB = 512
 
 
 EPS = 1e-05
@@ -335,9 +338,909 @@
     )
 
 
+RING_Z = (0, 1, 2, 3, 3, 2, 1, 0)
+RING_Y = (0, 0, 0, 0, 1, 1, 1, 1)
+ITEMS = 16
+PAD_ROWS = 80
+F32 = jnp.float32
+BF16 = jnp.bfloat16
+ANY = pl.BlockSpec(memory_space=pl.ANY)
+VMEM = pl.BlockSpec(memory_space=pltpu.VMEM)
+SMEM = pl.BlockSpec(memory_space=pltpu.SMEM)
+META_LEN, META_POOL, META_TEXT, META_Z = 16, 24, 32, 36
+
+
+def call(kernel, name, ins, outs, scratch, flops=0, touched=0):
+    specs = [spec for spec, _ in ins]
+    return pl.pallas_call(
+        kernel,
+        name=name,
+        out_shape=[jax.ShapeDtypeStruct(shape, dtype) for shape, dtype in outs],
+        in_specs=specs,
+        out_specs=[VMEM for _ in outs],
+        scratch_shapes=scratch,
+        compiler_params=pltpu.CompilerParams(vmem_limit_bytes=60 * 1024 * 1024),
+        cost_estimate=pl.CostEstimate(flops=flops, bytes_accessed=touched, transcendentals=0),
+    )(*[item for _, item in ins])
+
+
+def dot(left, right, left_dim=1, right_dim=0):
+    return lax.dot_general(
+        left, right, (((left_dim,), (right_dim,)), ((), ())), preferred_element_type=F32
+    )
+
+
+def slots(refs):
+    own, other, h1, s1, h2, s2, h3, s3, h4, s4 = refs
+    views = [own, other]
+    for pair in (h1, s1, h2, s2, h3, s3):
+        views += [pair.at[0], pair.at[1]]
+    return views + [h4, s4]
+
+
+def fetch(meta, refs, row, rows, lane, lanes, dst, dst_lane, sem, per_owner=None):
+    step = rows if per_owner is None else per_owner
+    for slot, view in enumerate(slots(refs)):
+        at = pl.multiple_of(meta[slot] * step, 16)
+        pltpu.make_async_copy(
+            view.at[pl.ds(row, rows), pl.ds(lane, lanes)],
+            dst.at[pl.ds(at, rows), pl.ds(dst_lane, lanes)],
+            sem,
+        ).start()
+
+
+def drain(dst, sem):
+    pltpu.make_async_copy(dst, dst, sem).wait()
+
+
+def lane_keep(meta, width):
+    real = jnp.where(meta[META_TEXT] == 1, DT, DI)
+    lanes = lax.broadcasted_iota(jnp.int32, (1, width), 1)
+    return (lanes < real).astype(F32)
+
+
+def width_inv(meta):
+    return jnp.where(meta[META_TEXT] == 1, 1.0 / DT, 1.0 / DI).astype(F32)
+
+
+def normalize(values, keep, winv):
+    mean = jnp.sum(values, axis=-1, keepdims=True) * winv
+    centred = (values - mean) * keep
+    var = jnp.sum(centred * centred, axis=-1, keepdims=True) * winv
+    inv = lax.rsqrt(var + EPS)
+    return centred * inv, inv
+
+
+def normalize_back(grad_out, gain, normed, inv, keep, winv):
+    grad_normed = grad_out * gain
+    mean_grad = jnp.sum(grad_normed, axis=-1, keepdims=True) * winv
+    mean_cross = jnp.sum(grad_normed * normed, axis=-1, keepdims=True) * winv
+    return keep * inv * (grad_normed - mean_grad - normed * mean_cross)
+
+
+def row_sum(values):
+    return jnp.sum(values, axis=0, keepdims=True)
+
+
+def head_rows(rows):
+    heads = lax.broadcasted_iota(jnp.int32, rows.shape, 1) // HD
+    parts = [jnp.where(heads == head, rows, 0.0) for head in range(16)]
+    return jnp.concatenate(parts, axis=0).astype(BF16)
+
+
+def attend_kernel(meta, tok, *rest):
+    refs, (mixed, keys, values, norm_low, small_out, pooled), scratch = rest[:10], rest[10:16], rest[16:]
+    weights, small, normed, queries, pool_acc, wsem, ssem = scratch
+    for slot, view in enumerate(slots(refs)):
+        pltpu.make_async_copy(view.at[pl.ds(160, 16), :], small.at[slot], ssem).start()
+    for third in range(3):
+        fetch(meta, refs, third * 48, 48, 0, DI, weights, third * DI, wsem)
+    keep, winv = lane_keep(meta, DI), width_inv(meta)
+    drain(small, ssem)
+    vectors = jnp.sum(small[...].astype(F32), axis=0)
+    small_out[...] = vectors
+    samples, seq = tok.shape[0], tok.shape[1]
+
+    @pl.loop(0, samples)
+    def _(s):
+        norm, _ = normalize(tok[s].astype(F32), keep, winv)
+        norm_low[s, 64:80, :] = jnp.zeros((16, DI), BF16)
+        normed[s, 64:80, :] = jnp.zeros((16, DI), BF16)
+        norm_low[s, 0:seq, :] = norm.astype(BF16)
+        normed[s, 0:seq, :] = (norm * small_out[0:1, :] + small_out[1:2, :]).astype(BF16)
+
+    drain(weights, wsem)
+    rows = samples * PAD_ROWS
+
+    for third, dst, bias in ((0, queries, 2), (1, keys, None), (2, values, 3)):
+
+        @pl.loop(0, DI // 256)
+        def _(j, third=third, dst=dst, bias=bias):
+            lanes = pl.ds(pl.multiple_of(j * 256, 256), 256)
+            wide = pl.ds(pl.multiple_of(third * DI + j * 256, 256), 256)
+            prod = dot(normed[...].reshape(rows, DI), weights[:, wide])
+            if bias is not None:
+                prod = prod + small_out[bias : bias + 1, lanes]
+            dst[:, lanes] = prod.astype(BF16)
+
+    text = meta[META_TEXT] == 1
+    query_pos = lax.broadcasted_iota(jnp.int32, (PAD_ROWS, PAD_ROWS), 0)
+    key_pos = lax.broadcasted_iota(jnp.int32, (PAD_ROWS, PAD_ROWS), 1)
+    head_of = lax.broadcasted_iota(jnp.int32, (PAD_ROWS, 256), 1) // HD
+    head_masks = [(head_of == i).astype(F32) for i in range(4)]
+    low_masks = [m.astype(BF16) for m in head_masks]
+    row_pos = lax.broadcasted_iota(jnp.int32, (PAD_ROWS, 256), 0)
+    reach = jnp.where(text, query_pos, PAD_ROWS)
+
+    @pl.loop(0, samples)
+    def _(s):
+        at = pl.ds(pl.multiple_of(s * PAD_ROWS, 16), PAD_ROWS)
+        length, pool = meta[META_LEN + s], meta[META_POOL + s]
+        allowed = (key_pos < length) & (key_pos <= reach)
+        for group in range(3):
+            lanes = pl.ds(group * 256, 256)
+            query, key, value = queries[at, lanes], keys[at, lanes], values[at, lanes]
+            spread = jnp.concatenate([query * m for m in low_masks], axis=0)
+            raw = dot(spread, key, 1, 1) * (float(HD) ** -0.5)
+            raw = jnp.where(allowed[None], raw.reshape(4, PAD_ROWS, PAD_ROWS), NEG_FILL)
+            terms = jnp.exp(raw - jnp.max(raw, axis=-1, keepdims=True))
+            probs = terms / jnp.sum(terms, axis=-1, keepdims=True)
+            out = dot(probs.astype(BF16).reshape(4 * PAD_ROWS, PAD_ROWS), value)
+            total = out[0:PAD_ROWS] * head_masks[0]
+            for i in range(1, 4):
+                total = total + out[i * PAD_ROWS : (i + 1) * PAD_ROWS] * head_masks[i]
+            low = total.astype(BF16)
+            mixed[s, :, lanes] = low
+            pool_acc[pl.ds(s, 1), lanes] = row_sum(jnp.where(row_pos == pool, low.astype(F32), 0.0))
+
+    pooled[...] = pool_acc[...].astype(BF16)
+
+
+def attend(meta, tok, refs):
+    samples = tok.shape[0]
+    rows = samples * PAD_ROWS
+    return call(
+        attend_kernel,
+        "attend",
+        [(SMEM, meta), (VMEM, tok)] + [(ANY, r) for r in refs],
+        [
+            ((samples, PAD_ROWS, DI), BF16),
+            ((rows, DI), BF16),
+            ((rows, DI), BF16),
+            ((samples, PAD_ROWS, DI), BF16),
+            ((16, DI), F32),
+            ((samples, DI), BF16),
+        ],
+        [
+            pltpu.VMEM((DI, 3 * DI), BF16),
+            pltpu.VMEM((ITEMS, 16, DI), BF16),
+            pltpu.VMEM((samples, PAD_ROWS, DI), BF16),
+            pltpu.VMEM((rows, DI), BF16),
+            pltpu.VMEM((samples, DI), F32),
+            pltpu.SemaphoreType.DMA,
+            pltpu.SemaphoreType.DMA,
+        ],
+        flops=2 * rows * DI * 3 * DI,
+        touched=10_000_000,
+    )
+
+
+def hidden_kernel(meta, tok, mixed, vec, *rest):
+    refs, (middle, act), (w_out, w_fc, normed, osem, fsem) = rest[:10], rest[10:12], rest[12:]
+    fetch(meta, refs, 0, 48, 0, DI, w_out, 0, osem)
+    for block in range(4):
+        fetch(meta, refs, 48 + 48 * block, 48, 0, DI, w_fc, block * DI, fsem)
+    keep, winv = lane_keep(meta, DI), width_inv(meta)
+    samples, seq = tok.shape[0], tok.shape[1]
+    rows = samples * PAD_ROWS
+    drain(w_out, osem)
+
+    @pl.loop(0, DI // 256)
+    def _(j):
+        lanes = pl.ds(pl.multiple_of(j * 256, 256), 256)
+        prod = dot(mixed[...].reshape(rows, DI), w_out[:, lanes]) + vec[4:5, lanes]
+        middle[:, :, lanes] = prod.reshape(samples, PAD_ROWS, 256)
+
+    @pl.loop(0, samples)
+    def _(s):
+        total = middle[s, 0:seq, :] + tok[s].astype(F32)
+        middle[s, 0:seq, :] = total
+        norm, _ = normalize(total, keep, winv)
+        normed[s, 64:80, :] = jnp.zeros((16, DI), BF16)
+        normed[s, 0:seq, :] = (norm * vec[5:6, :] + vec[6:7, :]).astype(BF16)
+
+    drain(w_fc, fsem)
+    for block in range(4):
+
+        @pl.loop(0, DI // 256)
+        def _(j, block=block):
+            lanes = pl.ds(pl.multiple_of(j * 256, 256), 256)
+            wide = pl.ds(pl.multiple_of(block * DI + j * 256, 256), 256)
+            pre = dot(normed[...].reshape(rows, DI), w_fc[:, wide])
+            pre = pre + vec[10 + block : 11 + block, lanes]
+            act[:, wide] = (pre * jax.nn.sigmoid(GELU_K * pre)).astype(BF16)
+
+
+def hidden(meta, tok, mixed, vec, refs):
+    samples = tok.shape[0]
+    rows = samples * PAD_ROWS
+    return call(
+        hidden_kernel,
+        "hidden",
+        [(SMEM, meta), (VMEM, tok), (VMEM, mixed), (VMEM, vec)] + [(ANY, r) for r in refs],
+        [((samples, PAD_ROWS, DI), F32), ((rows, 4 * DI), BF16)],
+        [
+            pltpu.VMEM((DI, DI), BF16),
+            pltpu.VMEM((DI, 4 * DI), BF16),
+            pltpu.VMEM((samples, PAD_ROWS, DI), BF16),
+            pltpu.SemaphoreType.DMA,
+            pltpu.SemaphoreType.DMA,
+        ],
+        flops=2 * rows * DI * 5 * DI,
+        touched=14_000_000,
+    )
+
+
+def finish_kernel(meta, middle, act, vec, *rest):
+    refs, (block_out,), (w_down, acc, sem) = rest[:10], rest[10:11], rest[11:]
+    fetch(meta, refs, 0, 192, 0, DI, w_down, 0, sem)
+    samples, seq = block_out.shape[0], block_out.shape[1]
+    drain(w_down, sem)
+
+    @pl.loop(0, DI // 256)
+    def _(j):
+        lanes = pl.ds(pl.multiple_of(j * 256, 256), 256)
+        prod = dot(act[...], w_down[:, lanes]) + vec[7:8, lanes]
+        acc[:, :, lanes] = prod.reshape(samples, PAD_ROWS, 256)
+
+    row_pos = lax.broadcasted_iota(jnp.int32, (seq, DI), 0)
+
+    @pl.loop(0, samples)
+    def _(s):
+        total = acc[s, 0:seq, :] + middle[s, 0:seq, :]
+        block_out[s] = jnp.where(row_pos < meta[META_LEN + s], total, 0.0).astype(BF16)
+
+
+def finish(meta, middle, act, vec, refs, seq):
+    samples = middle.shape[0]
+    rows = samples * PAD_ROWS
+    return call(
+        finish_kernel,
+        "finish",
+        [(SMEM, meta), (VMEM, middle), (VMEM, act), (VMEM, vec)] + [(ANY, r) for r in refs],
+        [((samples, seq, DI), BF16)],
+        [
+            pltpu.VMEM((4 * DI, DI), BF16),
+            pltpu.VMEM((samples, PAD_ROWS, DI), F32),
+            pltpu.SemaphoreType.DMA,
+        ],
+        flops=2 * rows * DI * 4 * DI,
+        touched=13_000_000,
+    )[0]
+
+
+def fetch_embed(meta, refs, dst, sem):
+    for slot, view in enumerate(slots(refs)):
+        at = pl.multiple_of(meta[slot] * 48, 16)
+        for row, rows, lane, lanes, to_row, to_lane in (
+            (192, 32, 0, EMB, 0, 0),
+            (192, 16, EMB, 256, 32, 0),
+            (208, 16, EMB, 256, 32, 256),
+        ):
+            pltpu.make_async_copy(
+                view.at[pl.ds(row, rows), pl.ds(lane, lanes)],
+                dst.at[pl.ds(pl.multiple_of(at + to_row, 16), rows), pl.ds(to_lane, lanes)],
+                sem,
+            ).start()
+
+
+def pooled_kernel(meta, vec, *rest):
+    first, second, third, mixes = rest[:10], rest[10:20], rest[20:30], rest[30:34]
+    outs, scratch = rest[34:47], rest[47:]
+    (e_out, proj_out, head_out, normf_out, invf_out, n2_out, norm2_out, inv2_out, pre_out,
+     act_out, q_out, norm1_out, mix_out) = outs
+    w_q, w_out, w_fc, w_down, w_emb, xs, mix, sems = scratch
+    for slot, view in enumerate(slots(first)):
+        pltpu.make_async_copy(view.at[pl.ds(144, 16), :], xs.at[meta[slot]], sems.at[0]).start()
+    for i, ref in enumerate(mixes):
+        pltpu.make_async_copy(ref, mix.at[meta[META_Z + i]], sems.at[1]).start()
+    fetch(meta, second, 0, 48, 0, DI, w_out, 0, sems.at[2])
+    for block in range(4):
+        fetch(meta, second, 48 + 48 * block, 48, 0, DI, w_fc, block * DI, sems.at[3])
+    fetch(meta, third, 0, 192, 0, DI, w_down, 0, sems.at[4])
+    fetch_embed(meta, third, w_emb, sems.at[5])
+    fetch(meta, first, 0, 48, 0, DI, w_q, 0, sems.at[6])
+    keep, winv = lane_keep(meta, DI), width_inv(meta)
+    drain(xs, sems.at[0])
+    stream = xs[...].astype(F32)[:, :8, :].reshape(ITEMS * 8, DI)
+    drain(mix, sems.at[1])
+    mixed = mix[...].reshape(ITEMS * 8, DI)
+    mix_out[...] = mixed
+    drain(w_out, sems.at[2])
+    middle = stream + dot(mixed, w_out[...]) + vec[4:5, :]
+    norm2, inv2 = normalize(middle, keep, winv)
+    n2 = (norm2 * vec[5:6, :] + vec[6:7, :]).astype(BF16)
+    n2_out[...] = n2
+    norm2_out[...] = norm2
+    inv2_out[...] = jnp.broadcast_to(inv2, (ITEMS * 8, 128))
+    drain(w_fc, sems.at[3])
+    for block in range(4):
+
+        @pl.loop(0, DI // 256)
+        def _(j, block=block):
+            lanes = pl.ds(pl.multiple_of(j * 256, 256), 256)
+            wide = pl.ds(pl.multiple_of(block * DI + j * 256, 256), 256)
+            pre = dot(n2_out[...], w_fc[:, wide]) + vec[10 + block : 11 + block, lanes]
+            pre_out[:, wide] = pre
+            act_out[:, wide] = (pre * jax.nn.sigmoid(GELU_K * pre)).astype(BF16)
+
+    drain(w_down, sems.at[4])
+    last = middle + dot(act_out[...], w_down[...]) + vec[7:8, :]
+    normf, invf = normalize(last, keep, winv)
+    normf_out[...] = normf
+    invf_out[...] = jnp.broadcast_to(invf, (ITEMS * 8, 128))
+    head = (normf * vec[8:9, :] + vec[9:10, :]).astype(BF16)
+    head_out[...] = head
+    drain(w_emb, sems.at[5])
+    proj = dot(head, w_emb[...])
+    proj_out[...] = proj
+    scale = lax.rsqrt(jnp.sum(proj * proj, axis=-1, keepdims=True) + NORM_EPS)
+    e_out[...] = (proj * scale).astype(BF16)
+    norm1, _ = normalize(stream, keep, winv)
+    norm1_out[...] = norm1.astype(BF16)
+    drain(w_q, sems.at[6])
+    n1 = (norm1 * vec[0:1, :] + vec[1:2, :]).astype(BF16)
+    q_out[...] = (dot(n1, w_q[...]) + vec[2:3, :]).astype(BF16)
+
+
+def pooled_forward(meta, vec, first, second, third, mixes):
+    n = ITEMS * 8
+    return call(
+        pooled_kernel,
+        "pooled_forward",
+        [(SMEM, meta), (VMEM, vec)] + [(ANY, r) for r in (*first, *second, *third, *mixes)],
+        [
+            ((n, EMB), BF16),
+            ((n, EMB), F32),
+            ((n, DI), BF16),
+            ((n, DI), F32),
+            ((n, 128), F32),
+            ((n, DI), BF16),
+            ((n, DI), F32),
+            ((n, 128), F32),
+            ((n, 4 * DI), F32),
+            ((n, 4 * DI), BF16),
+            ((n, DI), BF16),
+            ((n, DI), BF16),
+            ((n, DI), BF16),
+        ],
+        [
+            pltpu.VMEM((DI, DI), BF16),
+            pltpu.VMEM((DI, DI), BF16),
+            pltpu.VMEM((DI, 4 * DI), BF16),
+            pltpu.VMEM((4 * DI, DI), BF16),
+            pltpu.VMEM((DI, EMB), BF16),
+            pltpu.VMEM((ITEMS, 16, DI), BF16),
+            pltpu.VMEM((4, 32, DI), BF16),
+            pltpu.SemaphoreType.DMA((7,)),
+        ],
+        flops=2 * n * DI * 11 * DI,
+        touched=16_000_000,
+    )
+
+
+def one_direction(left, right, mult):
+    sims = dot(left, right, 1, 1)
+    logits = mult * sims
+    top = jnp.max(logits, axis=-1, keepdims=True)
+    total = top + jnp.log(jnp.sum(jnp.exp(logits - top), axis=-1, keepdims=True))
+    count = sims.shape[0]
+    eye = lax.broadcasted_iota(jnp.int32, (count, count), 0) == lax.broadcasted_iota(
+        jnp.int32, (count, count), 1
+    )
+    hot = eye.astype(F32)
+    lost = jnp.sum(total - jnp.sum(hot * logits, axis=-1, keepdims=True), axis=0, keepdims=True)
+    grad = (jnp.exp(logits - total) - hot) * 0.5
+    scale = jnp.sum(jnp.sum(grad * sims, axis=-1, keepdims=True), axis=0, keepdims=True)
+    return lost, scale, mult * grad
+
+
+def chain_kernel(meta, mult_ref, e_own_ref, e_oth_ref, vec, proj_ref, normf_ref, invf_ref, norm2_ref,
+                 inv2_ref, pre_ref, head_sl, act_sl, n2_sl, mix_sl, *rest):
+    second, third = rest[:10], rest[10:20]
+    outs, scratch = rest[20:30], rest[30:]
+    (loss_out, d_emb, d_down, d_fc, d_out, vec_grads, fcb_grads, mid_out, gm_out, unused) = outs
+    w_out, w_fc, w_down, w_emb, gpre, sems = scratch
+    fetch_embed(meta, third, w_emb, sems.at[0])
+    fetch(meta, third, 0, 192, 0, DI, w_down, 0, sems.at[1])
+    for block in range(4):
+        fetch(meta, second, 48 + 48 * block, 48, 0, DI, w_fc, block * DI, sems.at[2])
+    fetch(meta, second, 0, 48, 0, DI, w_out, 0, sems.at[3])
+    keep, winv = lane_keep(meta, DI), width_inv(meta)
+    text = meta[META_TEXT].astype(F32)
+    mult = mult_ref[0]
+    own, oth = e_own_ref[...].astype(F32), e_oth_ref[...].astype(F32)
+    e_img = (own * (1.0 - text) + oth * text).astype(BF16)
+    e_txt = (oth * (1.0 - text) + own * text).astype(BF16)
+    lost_img, scale_img, grad_img = one_direction(e_img, e_txt, mult)
+    lost_txt, scale_txt, grad_txt = one_direction(e_txt, e_img, mult)
+    count = own.shape[0]
+    loss = (lost_img + lost_txt) / (2.0 * count)
+    scale = mult * (scale_img + scale_txt)
+    row_id = lax.broadcasted_iota(jnp.int32, (8, 128), 0)
+    loss_out[...] = jnp.where(
+        row_id == 0, jnp.broadcast_to(loss, (8, 128)), jnp.broadcast_to(scale, (8, 128))
+    )
+    grad_own = (grad_img * (1.0 - text) + grad_txt * text).astype(BF16)
+    grad_oth = (grad_txt * (1.0 - text) + grad_img * text).astype(BF16)
+    oth_low = e_oth_ref[...]
+    grad_e = dot(grad_own, oth_low) + dot(grad_oth, oth_low, 0, 0)
+    proj = proj_ref[...]
+    r = lax.rsqrt(jnp.sum(proj * proj, axis=-1, keepdims=True) + NORM_EPS)
+    cross = jnp.sum(grad_e * proj, axis=-1, keepdims=True)
+    grad_proj = (r * grad_e - proj * (r * r * r) * cross).astype(BF16)
+    d_emb[...] = dot(head_sl[...], grad_proj, 0, 0)
+    drain(w_emb, sems.at[0])
+    grad_head = dot(grad_proj, w_emb[...], 1, 1)
+    normf = normf_ref[...]
+    grad_y = normalize_back(grad_head, vec[8:9, :], normf, invf_ref[:, 0:1], keep, winv)
+    vec_grads[0:1, :] = row_sum(grad_head * normf)
+    vec_grads[1:2, :] = row_sum(grad_head)
+    branch = grad_y.astype(BF16)
+    vec_grads[2:3, :] = row_sum(branch.astype(F32))
+    d_down[...] = dot(act_sl[...], branch, 0, 0)
+    drain(w_down, sems.at[1])
+
+    for block in range(6):
+        lanes = pl.ds(block * 512, 512)
+        grad_act = dot(branch, w_down[lanes, :], 1, 1)
+        pre = pre_ref[:, lanes]
+        gate = jax.nn.sigmoid(GELU_K * pre)
+        low = (grad_act * (gate + GELU_K * pre * gate * (1.0 - gate))).astype(BF16)
+        gpre[:, lanes] = low
+        fcb_grads[:, lanes] = jnp.broadcast_to(row_sum(low.astype(F32)), (8, 512))
+
+    drain(w_fc, sems.at[2])
+    grad_n2 = dot(gpre[...], w_fc[...], 1, 1)
+
+    @pl.loop(0, 6)
+    def _(j):
+        lanes = pl.ds(pl.multiple_of(j * 512, 512), 512)
+        d_fc[:, lanes] = dot(n2_sl[...], gpre[:, lanes], 0, 0)
+
+    norm2 = norm2_ref[...]
+    vec_grads[3:4, :] = row_sum(grad_n2 * norm2)
+    vec_grads[4:5, :] = row_sum(grad_n2)
+    grad_mid = grad_y + normalize_back(grad_n2, vec[5:6, :], norm2, inv2_ref[:, 0:1], keep, winv)
+    mid_out[...] = grad_mid
+    attn = grad_mid.astype(BF16)
+    vec_grads[5:6, :] = row_sum(attn.astype(F32))
+    d_out[...] = dot(mix_sl[...], attn, 0, 0)
+    drain(w_out, sems.at[3])
+    gm_out[...] = dot(attn, w_out[...], 1, 1).astype(BF16)
+    vec_grads[6:8, :] = jnp.zeros((2, DI), F32)
+    unused[...] = jnp.zeros((8, 128), F32)
+
+
+def chain(meta, mult, e_own, e_oth, vec, saved, slices, second, third):
+    n = ITEMS * 8
+    plain = [e_own, e_oth, vec, *saved, *slices]
+    return call(
+        chain_kernel,
+        "chain",
+        [(SMEM, meta), (SMEM, mult)]
+        + [(VMEM, item) for item in plain]
+        + [(ANY, r) for r in (*second, *third)],
+        [
+            ((8, 128), F32),
+            ((48, EMB), F32),
+            ((192, DI), F32),
+            ((48, 4 * DI), F32),
+            ((48, DI), F32),
+            ((8, DI), F32),
+            ((8, 4 * DI), F32),
+            ((n, DI), F32),
+            ((n, DI), BF16),
+            ((8, 128), F32),
+        ],
+        [
+            pltpu.VMEM((DI, DI), BF16),
+            pltpu.VMEM((DI, 4 * DI), BF16),
+            pltpu.VMEM((4 * DI, DI), BF16),
+            pltpu.VMEM((DI, EMB), BF16),
+            pltpu.VMEM((n, 4 * DI), BF16),
+            pltpu.SemaphoreType.DMA((4,)),
+        ],
+        flops=2 * n * DI * 10 * DI,
+        touched=16_000_000,
+    )
+
+
+PAYLOAD = 160
+
+
+def scores_kernel(meta, keys, values, norm_low, q_own, gm_own, payload, gk_out, gv_out, gq_out):
+    rows = keys.shape[0]
+    samples = rows // PAD_ROWS
+    q_rows = head_rows(q_own[...].astype(F32))
+    m_rows = head_rows(gm_own[...].astype(F32))
+    raw = dot(keys[...], q_rows, 1, 1) * (float(HD) ** -0.5)
+    shape = (samples, PAD_ROWS, 128)
+    row_sample = lax.broadcasted_iota(jnp.int32, shape, 0)
+    row_key = lax.broadcasted_iota(jnp.int32, shape, 1)
+    lane = lax.broadcasted_iota(jnp.int32, shape, 2)
+    limit = jnp.zeros((samples, 1, 128), jnp.int32)
+    sample_id = lax.broadcasted_iota(jnp.int32, (samples, 1, 128), 0)
+    for s in range(samples):
+        limit = jnp.where(sample_id == s, meta[META_LEN + s], limit)
+    valid = (lane % 8 == row_sample) & (row_key < limit) & (lane < 96)
+    raw = jnp.where(valid, raw.reshape(shape), NEG_FILL)
+    top = jnp.max(jnp.max(raw, axis=0, keepdims=True), axis=1, keepdims=True)
+    terms = jnp.where(valid, jnp.exp(raw - top), 0.0)
+    total = jnp.sum(jnp.sum(terms, axis=0, keepdims=True), axis=1, keepdims=True)
+    probs = terms / jnp.maximum(total, 1e-30)
+    grad_probs = dot(values[...], m_rows, 1, 1).reshape(shape)
+    cross = jnp.sum(jnp.sum(probs * grad_probs, axis=0, keepdims=True), axis=1, keepdims=True)
+    gk = (probs * (grad_probs - cross)).reshape(rows, 128).astype(BF16)
+    gv = probs.reshape(rows, 128).astype(BF16)
+    gk_out[...] = gk
+    gv_out[...] = gv
+    back = dot(gk, keys[...], 0, 0) * (float(HD) ** -0.5)
+    heads = lax.broadcasted_iota(jnp.int32, (8, DI), 1) // HD
+    grad_q = jnp.zeros((8, DI), F32)
+    for head in range(DI // HD):
+        grad_q = grad_q + jnp.where(heads == head, back[head * 8 : head * 8 + 8], 0.0)
+    gq_low = grad_q.astype(BF16)
+    gq_out[...] = gq_low
+    norm = norm_low[...].reshape(rows, DI)
+    z_key = dot(norm, gk, 0, 0).astype(BF16)
+    z_value = dot(norm, gv, 0, 0).astype(BF16)
+    sum_key = row_sum(gk.astype(F32))
+    sum_value = row_sum(gv.astype(F32))
+    key_high = sum_key.astype(BF16).astype(F32)
+    value_high = sum_value.astype(BF16).astype(F32)
+    row_id = lax.broadcasted_iota(jnp.int32, (16, 128), 0)
+    sums = jnp.zeros((16, 128), F32)
+    for at, value in enumerate((key_high, sum_key - key_high, value_high, sum_value - value_high)):
+        sums = jnp.where(row_id == at, jnp.broadcast_to(value, (16, 128)), sums)
+    sums = sums.astype(BF16)
+    gq_wide = gq_low.astype(F32)
+    gq_tall = jnp.concatenate(
+        [gq_wide[:, i * 128 : (i + 1) * 128] for i in range(DI // 128)], axis=0
+    ).astype(BF16)
+    for owner in range(ITEMS):
+        base = owner * PAYLOAD
+        payload[base : base + 48, :] = z_key[owner * 48 : owner * 48 + 48]
+        payload[base + 48 : base + 64, :] = sums
+        payload[base + 64 : base + 112, :] = z_value[owner * 48 : owner * 48 + 48]
+        payload[base + 112 : base + 160, :] = gq_tall
+
+
+def scores(meta, keys, values, norm_low, q_own, gm_own):
+    rows = keys.shape[0]
+    return call(
+        scores_kernel,
+        "scores",
+        [(SMEM, meta)] + [(VMEM, item) for item in (keys, values, norm_low, q_own, gm_own)],
+        [
+            ((ITEMS * PAYLOAD, 128), BF16),
+            ((rows, 128), BF16),
+            ((rows, 128), BF16),
+            ((8, DI), BF16),
+        ],
+        [],
+        flops=2 * rows * DI * 700,
+        touched=5_000_000,
+    )
+
+
+def shard_kernel(got, q_all, gm_all, norm_sl, w_own, gain, bias, d_qkv, sums_out, gains_out, big, left):
+    scale = float(HD) ** -0.5
+
+    def build(source):
+        @pl.loop(0, ITEMS)
+        def _(j):
+            rows = source[pl.ds(pl.multiple_of(j * 8, 8), 8), :]
+            big[pl.ds(pl.multiple_of(j * 128, 128), 128), :] = head_rows(rows)
+
+    def spread(start):
+        for j in range(ITEMS):
+            left[:, j * 128 : (j + 1) * 128] = got[j, start : start + 64, :]
+
+    build(q_all)
+    spread(0)
+    by_key = dot(left[...], big[...]) * scale
+    m_key, s_key = by_key[0:48], by_key[48:49] + by_key[49:50]
+    build(gm_all)
+    spread(48)
+    by_value = dot(left[...], big[...])
+    m_value, s_value = by_value[16:64], by_value[2:3] + by_value[3:4]
+    tall = got[:, 112:160, :].astype(F32)
+    grad_q = jnp.concatenate(
+        [tall[:, i * 8 : i * 8 + 8, :].reshape(ITEMS * 8, 128) for i in range(DI // 128)], axis=1
+    )
+    s_query = row_sum(grad_q)
+    m_query = dot(norm_sl[...], grad_q.astype(BF16), 0, 0)
+    gain_col, bias_col = gain[:, 0:1], bias[:, 0:1]
+    d_gain = jnp.zeros((48, 1), F32)
+    d_bias = jnp.zeros((48, 1), F32)
+    for third, (moment, total) in enumerate(((m_query, s_query), (m_key, s_key), (m_value, s_value))):
+        d_qkv[third] = gain_col * moment + bias_col * total
+        weight = w_own[third].astype(F32)
+        d_gain = d_gain + jnp.sum(weight * moment, axis=-1, keepdims=True)
+        d_bias = d_bias + jnp.sum(weight * total, axis=-1, keepdims=True)
+    lane = lax.broadcasted_iota(jnp.int32, (48, 128), 1)
+    gains_out[...] = jnp.where(
+        lane == 0, jnp.broadcast_to(d_gain, (48, 128)), jnp.broadcast_to(d_bias, (48, 128))
+    )
+    row_id = lax.broadcasted_iota(jnp.int32, (8, DI), 0)
+    sums_out[...] = jnp.where(
+        row_id == 0, jnp.broadcast_to(s_query, (8, DI)), jnp.broadcast_to(s_value, (8, DI))
+    )
+
+
+def shard_grads(got, q_all, gm_all, norm_sl, w_own, gain, bias):
+    return call(
+        shard_kernel,
+        "shard_grads",
+        [(VMEM, item) for item in (got, q_all, gm_all, norm_sl, w_own, gain, bias)],
+        [((3, 48, DI), F32), ((8, DI), F32), ((48, 128), F32)],
+        [pltpu.VMEM((ITEMS * 128, DI), BF16), pltpu.VMEM((64, ITEMS * 128), BF16)],
+        flops=2 * 64 * 2048 * DI * 2,
+        touched=2_000_000,
+    )
+
+
+def stream_kernel(meta, tok, gk, gv, q_own, gm_own, gq, mid_own, vec, *rest):
+    refs, (out,), (weights, acc, sem) = rest[:10], rest[10:11], rest[11:]
+    for third in range(3):
+        fetch(meta, refs, third * 48, 48, 0, DI, weights, third * DI, sem)
+    keep, winv = lane_keep(meta, DI), width_inv(meta)
+    samples, seq = tok.shape[0], tok.shape[1]
+    q_rows = head_rows(q_own[...].astype(F32))
+    m_rows = head_rows(gm_own[...].astype(F32))
+    drain(weights, sem)
+    u_key = (dot(q_rows, weights[:, DI : 2 * DI], 1, 1) * (float(HD) ** -0.5)).astype(BF16)
+    u_value = dot(m_rows, weights[:, 2 * DI :], 1, 1).astype(BF16)
+    u_query = dot(gq[...], weights[:, :DI], 1, 1)
+    grad = dot(gk[...], u_key) + dot(gv[...], u_value)
+    acc[...] = grad.reshape(samples, PAD_ROWS, DI)
+    row_pos = lax.broadcasted_iota(jnp.int32, (seq, DI), 0)
+    for s in range(samples):
+        hit = row_pos == meta[META_POOL + s]
+        norm, inv = normalize(tok[s].astype(F32), keep, winv)
+        total = acc[s, 0:seq, :] + jnp.where(hit, u_query[s : s + 1, :], 0.0)
+        back = normalize_back(total, vec[0:1, :], norm, inv, keep, winv)
+        out[s] = back + jnp.where(hit, mid_own[s : s + 1, :], 0.0)
+
+
+def stream_grads(meta, tok, gk, gv, q_own, gm_own, gq, mid_own, vec, refs):
+    samples, seq = tok.shape[0], tok.shape[1]
+    rows = samples * PAD_ROWS
+    return call(
+        stream_kernel,
+        "stream_grads",
+        [(SMEM, meta)]
+        + [(VMEM, item) for item in (tok, gk, gv, q_own, gm_own, gq, mid_own, vec)]
+        + [(ANY, r) for r in refs],
+        [((samples, seq, DI), F32)],
+        [
+            pltpu.VMEM((DI, 3 * DI), BF16),
+            pltpu.VMEM((samples, PAD_ROWS, DI), F32),
+            pltpu.SemaphoreType.DMA,
+        ],
+        flops=2 * rows * DI * 600,
+        touched=7_000_000,
+    )[0]
+
+
+BOTH = ("tower", "dp")
+
+
+def device(tower, place, core):
+    return tower * 16 + (RING_Z[place] * 2 + RING_Y[place]) * 2 + core
+
+
+def routes(towers):
+    swap, turn = [], []
+    for tower in range(towers):
+        for place in range(8):
+            for core, step in ((0, 1), (1, -1)):
+                here = device(tower, place, core)
+                swap.append((here, device(tower, place, 1 - core)))
+                turn.append((here, device(tower, (place + step) % 8, core)))
+    return swap, turn
+
+
+def ring_gather(shard, swap, turn):
+    other = lax.ppermute(shard, BOTH, swap)
+    held = jnp.stack([shard, other])
+    items = [shard, other]
+    for _ in range(3):
+        held = lax.ppermute(held, BOTH, turn)
+        items += [held, lax.ppermute(held, BOTH, swap)]
+    held = lax.ppermute(held[0], BOTH, turn)
+    return items + [held, lax.ppermute(held, BOTH, swap)]
+
+
+def owner_table(dp_index):
+    core = dp_index % 2
+    row = dp_index // 2 % 2
+    depth = dp_index // 4
+    place = jnp.where(row == 0, depth, 7 - depth)
+
+    def owner(where, which):
+        where = where % 8
+        z = jnp.where(where < 4, where, 7 - where)
+        y = (where >= 4).astype(jnp.int32)
+        return (z * 2 + y) * 2 + which
+
+    sign = jnp.where(core == 0, -1, 1)
+    found = [owner(place, core), owner(place, 1 - core)]
+    for hop in range(1, 4):
+        ahead, behind = place + sign * hop, place - sign * hop
+        found += [owner(ahead, core), owner(ahead, 1 - core)]
+        found += [owner(behind, 1 - core), owner(behind, core)]
+    return found + [owner(place + 4, core), owner(place + 4, 1 - core)]
+
+
+def gather_rows(rows, dp_index, towers):
+    def pairs(move):
+        return [
+            (tower * 16 + (z * 2 + y) * 2 + c, tower * 16 + move(z, y, c))
+            for tower in range(towers)
+            for z in range(4)
+            for y in range(2)
+            for c in range(2)
+        ]
+
+    other = lax.ppermute(rows, BOTH, pairs(lambda z, y, c: (z * 2 + y) * 2 + 1 - c))
+    first = dp_index % 2 == 0
+    rows = jnp.concatenate([jnp.where(first, rows, other), jnp.where(first, other, rows)])
+    other = lax.ppermute(rows, BOTH, pairs(lambda z, y, c: (z * 2 + 1 - y) * 2 + c))
+    first = dp_index // 2 % 2 == 0
+    rows = jnp.concatenate([jnp.where(first, rows, other), jnp.where(first, other, rows)])
+    blocks = [rows]
+    for hop in range(1, 4):
+        blocks.append(
+            lax.ppermute(rows, BOTH, pairs(lambda z, y, c, hop=hop: ((z + hop) % 4 * 2 + y) * 2 + c))
+        )
+    return blocks
+
+
+def ring_body(
+    tokens,
+    lengths,
+    ln1_gain,
+    ln1_bias,
+    qkv_weight,
+    qv_bias,
+    out_weight,
+    out_bias,
+    ln2_gain,
+    ln2_bias,
+    fc_weight,
+    fc_bias,
+    down_weight,
+    down_bias,
+    final_gain,
+    final_bias,
+    embed_weight,
+    logit_scale,
+):
+    towers = lax.axis_size("tower")
+    tower_index = lax.axis_index("tower")
+    dp_index = lax.axis_index("dp")
+    swap, turn = routes(towers)
+    is_text = tower_index == 1
+    tok = tokens[0]
+    seq = tok.shape[1]
+    seq_lens = jnp.where(is_text, lengths, IMG_ROWS)
+    pool_pos = jnp.where(is_text, lengths - 1, 0)
+    depth = dp_index // 4
+    meta = jnp.stack(
+        owner_table(dp_index)
+        + [seq_lens[i] for i in range(8)]
+        + [pool_pos[i] for i in range(8)]
+        + [is_text.astype(jnp.int32), dp_index, dp_index * 0, dp_index * 0]
+        + [(depth - hop) % 4 for hop in range(4)]
+    ).astype(jnp.int32)
+
+    w_own = qkv_weight[0].transpose(1, 0, 2)
+    vectors = jnp.concatenate(
+        [ln1_gain, ln1_bias, qv_bias[0], out_bias, ln2_gain, ln2_bias, down_bias, final_gain, final_bias]
+    )
+    lane = lax.broadcasted_iota(jnp.int32, (1, DI), 1)
+    spread = jnp.where(lane // 48 == dp_index, jnp.tile(vectors, (1, ITEMS)), 0)
+    wide = lax.broadcasted_iota(jnp.int32, (1, 4 * DI), 1)
+    fc_spread = jnp.where(wide // 192 == dp_index, jnp.tile(fc_bias, (1, ITEMS)), 0).reshape(4, DI)
+    x_pooled = jnp.take_along_axis(tok, pool_pos[:, None, None], axis=1)[:, 0]
+    first_own = jnp.concatenate(
+        [
+            w_own.reshape(144, DI),
+            x_pooled,
+            jnp.zeros((8, DI), BF16),
+            spread,
+            fc_spread,
+            jnp.zeros((2, DI), BF16),
+        ]
+    )
+    second_own = jnp.concatenate(
+        [out_weight[0], fc_weight[0].reshape(48, 4, DI).transpose(1, 0, 2).reshape(192, DI)]
+    )
+    emb = embed_weight[0]
+    tail = emb[32:48]
+    emb_rows = jnp.concatenate(
+        [emb[:32], jnp.concatenate([tail[:, :256], tail[:, 256:]], axis=0)], axis=1
+    )
+    third_own = jnp.concatenate([down_weight[0], emb_rows])
+
+    first = ring_gather(first_own, swap, turn)
+    second = ring_gather(second_own, swap, turn)
+    third = ring_gather(third_own, swap, turn)
+
+    mixed, keys, values, norm_low, vec, mixed_pooled = attend(meta, tok, first)
+    mixes = gather_rows(mixed_pooled, dp_index, towers)
+    middle, act = hidden(meta, tok, mixed, vec, second)
+    (e_own, proj, head, normf, invf, n2, norm2, inv2, pre, act_p, q_all, norm1, mix_all) = pooled_forward(
+        meta, vec, first, second, third, mixes
+    )
+    across = [(t * 16 + d, (1 - t) * 16 + d) for t in range(2) for d in range(16)]
+    e_oth = lax.ppermute(e_own, BOTH, across)
+
+    def columns(array, size):
+        return lax.dynamic_slice_in_dim(array, dp_index * size, size, axis=1)
+
+    slices = (columns(head, 48), columns(act_p, 192), columns(n2, 48), columns(mix_all, 48))
+    norm_sl = columns(norm1, 48)
+    block_out = finish(meta, middle, act, vec, third, seq)
+    mult = jnp.exp(logit_scale)
+    loss_rows, d_emb, d_down, d_fc, d_out, vec_grads, fcb_grads, mid_all, gm_all, _ = chain(
+        meta, mult, e_own, e_oth, vec, (proj, normf, invf, norm2, inv2, pre), slices, second, third
+    )
+
+    def own_rows(array):
+        return lax.dynamic_slice_in_dim(array, dp_index * 8, 8, axis=0)
+
+    q_own, gm_own, mid_own = own_rows(q_all), own_rows(gm_all), own_rows(mid_all)
+    payload, gk, gv, gq = scores(meta, keys, values, norm_low, q_own, gm_own)
+    got = lax.all_to_all(payload, "dp", 0, 0, tiled=True).reshape(ITEMS, PAYLOAD, 128)
+    tokens_grad = stream_grads(meta, tok, gk, gv, q_own, gm_own, gq, mid_own, vec, first)
+    gain = jnp.broadcast_to(ln1_gain[0].astype(F32)[:, None], (48, 128))
+    bias = jnp.broadcast_to(ln1_bias[0].astype(F32)[:, None], (48, 128))
+    d_qkv, sums, gains = shard_grads(
+        got, q_all.astype(F32), gm_all.astype(F32), norm_sl, w_own, gain, bias
+    )
+    own_vec = columns(vec_grads, 48)
+    own_sums = columns(sums, 48)
+    d_fcb = columns(fcb_grads, 192)[0:1]
+    return (
+        block_out[None],
+        tokens_grad[None],
+        loss_rows[0, 0:1],
+        gains[:, 0][None],
+        gains[:, 1][None],
+        d_qkv.transpose(1, 0, 2)[None],
+        own_sums[0:2][None],
+        d_out[None],
+        own_vec[5:6],
+        own_vec[3:4],
+        own_vec[4:5],
+        d_fc[None],
+        d_fcb,
+        d_down[None],
+        own_vec[2:3],
+        own_vec[0:1],
+        own_vec[1:2],
+        d_emb[None],
+        loss_rows[1, 0:1],
+    )
+
+
 def solution(mesh):
+    aligned = mesh.shape["dp"] == ITEMS and mesh.shape["tower"] == 2
     return jax.shard_map(
-        body,
+        ring_body if aligned else body,
         mesh=mesh,
         in_specs=(
             P("tower", "dp", None, None),

time: 902 us -> 217 us (0.24)
  waiting for transfers between devices: 402 us -> 49.2 us
  blocking collectives: 229 us -> 0 us
  matrix products: 102 us -> 0 us
  Pallas kernels: 0 us -> 81.9 us
  local copies, waits for them, and re-layouts: 109 us -> 39.1 us
  starting transfers between devices: 3.78 us -> 39.7 us
  other arithmetic: 27 us -> 4.14 us
  between operations: 20 us -> 1.88 us
    reduce_scatter x6 -> x0, waiting for transfers between devices: 376 us -> none  [the longest x1 116 us: body(): lax.psum_scatter(d_down_w, 'dp', scatter_dimension=0, tiled=True)]
    unnamed x2 -> x0, blocking collectives: 122 us -> none
    dot_general x24 -> x0, matrix products: 102 us -> none  [the longest x6 34 us: contract_rows(): lax.dot_general(left_op, right_op, (((0,), (0,)), ((), ())), preferred_el...]
    pallas_call x0 -> x8, Pallas kernels: none -> 81.9 us  [call(): pl.pallas_call(kernel, name=name, out_shape=[jax.ShapeDtypeStruct(shape,...]
    all_gather x3 -> x0, blocking collectives: 64.7 us -> none  [the longest x1 25.5 us: body(): lax.all_gather(embed_weight[0], 'dp', axis=0, tiled=True)]
    psum x1 -> x0, blocking collectives: 41.8 us -> none  [body(): totals = lax.psum((loss_part, scale_part), ('tower', 'dp'))]
    ppermute x2 -> x33, waiting for transfers between devices: 10.3 us -> 49.2 us  [the longest x9 25.4 us: ring_gather(): held = lax.ppermute(held, BOTH, turn)]
    ppermute x2 -> x33, starting transfers between devices: 2.92 us -> 34.1 us  [the longest x9 18.3 us: ring_gather(): held = lax.ppermute(held, BOTH, turn)]
  transfers between devices with their start and end apart: 13 -> 34, of which waited for: 7 -> 13; matrix products, arithmetic and copies ran while one was open for 17% -> 13% of each run, Pallas kernels for 0% -> 24%
where the time goes in v1:
time: 217 us; the launch traced here: 216 us
  Pallas kernels  81.9 us (38%)
  waiting for transfers between devices  49.2 us (23%)
  starting transfers between devices  39.7 us (18%)
  local copies, waits for them, and re-layouts  39.1 us (18%)
  other arithmetic  4.14 us (2%)
    pallas_call x8, Pallas kernels, call(): pl.pallas_call(kernel, name=name, out_shape=[jax.ShapeDtypeStruct(shape,...  81.9 us
    ppermute x9, waiting for transfers between devices, ring_gather(): held = lax.ppermute(held, BOTH, turn)  25.4 us
    ppermute x9, starting transfers between devices, ring_gather(): held = lax.ppermute(held, BOTH, turn)  18.3 us
    unnamed x74, local copies, waits for them, and re-layouts  12.3 us
    ppermute x1, waiting for transfers between devices, gather_rows(): lax.ppermute(rows, BOTH, pairs(lambda z, y, c: (z * 2 + 1 - y) * 2 + c))  8.62 us
    ppermute x3, starting transfers between devices, gather_rows(): lax.ppermute(rows, BOTH, pairs(lambda z, y, c, hop=hop: ((z + hop) % 4 *...  8.13 us
    dynamic_slice x6, local copies, waits for them, and re-layouts, columns(): return lax.dynamic_slice_in_dim(array, dp_index * size, size, axis=1)  7.75 us
    ppermute x3, waiting for transfers between devices, ring_gather(): held = lax.ppermute(held[0], BOTH, turn)  7.27 us
  transfers between devices with their start and end apart: 34, of which 13 were waited for; matrix products, arithmetic and copies ran while one was open for 13% of the time, Pallas kernels for 24%

profile of v1, /device:TPU:0, one launch (start us, length us, event | category | flops | bytes accessed | tf_op | source)
XLA Modules:
  0.0 215.8 jit_solution(9057361647618619723)
XLA Ops:
  8.2 3.0 %collective-permute-start.1 = (bf16[2,176,768]{2,1,0:T(8,128)(2,1)S(1)}, bf16[2,176,768]{2,1,0:T(8,128)(2,1)S(1)}, u32[]{:S(2)}, u32[]{:S(2)}) collective-permute-start(bf16[2,176,768]{2,1,0:T(8,128)(2,1)S(1)} %pad_maximum_fusion.2), channel_id=1, source_target_pairs={{0,4},{1,3},{4,8},{5,1},{8,12},{9,5},{12,14},{13,9},{14,10},{15,13... | collective-permute-start | bytes 1622024 | tf_op jit(solution)/shard_map/ppermute | solution.py:1060
  11.4 7.1 %collective-permute-done.1.rest_2_ = bf16[2,176,768]{2,1,0:T(8,128)(2,1)S(1)} collective-permute-done((bf16[2,176,768]{2,1,0:T(8,128)(2,1)S(1)}, bf16[2,176,768]{2,1,0:T(8,128)(2,1)S(1)}, u32[]{:S(2)}, u32[]{:S(2)}) %collective-permute-start.1) | collective-permute-done | bytes 540704 | tf_op jit(solution)/shard_map/ppermute | solution.py:1060
  22.7 5.2 %collective-permute-done.3.rest_4_ = bf16[2,176,768]{2,1,0:T(8,128)(2,1)} collective-permute-done((bf16[2,176,768]{2,1,0:T(8,128)(2,1)S(1)}, bf16[2,176,768]{2,1,0:T(8,128)(2,1)}, u32[]{:S(2)}, u32[]{:S(2)}) %collective-permute-start.3) | collective-permute-done | bytes 540704 | tf_op jit(solution)/shard_map/ppermute | solution.py:1060
  31.7 3.5 %collective-permute-done.19.rest_2_.rest_22_.rest_12_ = bf16[2,224,768]{2,1,0:T(8,128)(2,1)S(1)} collective-permute-done((bf16[2,224,768]{2,1,0:T(8,128)(2,1)S(1)}, bf16[2,224,768]{2,1,0:T(8,128)(2,1)S(1)}, u32[]{:S(2)}, u32[]{:S(2)}) %collective-permute-start.19) | collective-permute-done | bytes 688160 | tf_op jit(solution)/shard_map/ppermute | solution.py:1060
  37.3 3.7 %collective-permute-done.5.rest_6_ = bf16[2,176,768]{2,1,0:T(8,128)(2,1)S(1)} collective-permute-done((bf16[2,176,768]{2,1,0:T(8,128)(2,1)}, bf16[2,176,768]{2,1,0:T(8,128)(2,1)S(1)}, u32[]{:S(2)}, u32[]{:S(2)}) %collective-permute-start.5) | collective-permute-done | bytes 540704 | tf_op jit(solution)/shard_map/ppermute | solution.py:1060
  41.0 2.1 collective-permute-start.7
  43.1 5.8 %collective-permute-done.10.rest_2_.rest_12_ = bf16[2,240,768]{2,1,0:T(8,128)(2,1)} collective-permute-done((bf16[2,240,768]{2,1,0:T(8,128)(2,1)S(1)}, bf16[2,240,768]{2,1,0:T(8,128)(2,1)}, u32[]{:S(2)}, u32[]{:S(2)}) %collective-permute-start.10) | collective-permute-done | bytes 737312 | tf_op jit(solution)/shard_map/ppermute | solution.py:1060
  51.9 7.3 %collective-permute-done.7.rest_8_ = bf16[176,768]{1,0:T(8,128)(2,1)S(1)} collective-permute-done((bf16[176,768]{1,0:T(8,128)(2,1)S(1)}, bf16[176,768]{1,0:T(8,128)(2,1)S(1)}, u32[]{:S(2)}, u32[]{:S(2)}) %collective-permute-start.7) | collective-permute-done | bytes 270368 | tf_op jit(solution)/shard_map/ppermute | solution.py:1062
  59.2 2.4 %copy.49 = bf16[1,8,77,768]{3,2,1,0:T(8,128)(2,1)} copy(bf16[1,8,77,768]{3,1,2,0:T(8,128)(2,1)} %param.18) | data formatting | bytes 1892352 | tf_op args[0]
  61.6 2.1 collective-permute-start.23
  65.2 19.1 %attend.1 = (bf16[8,80,768]{2,1,0:T(8,128)(2,1)}, bf16[640,768]{1,0:T(8,128)(2,1)}, bf16[640,768]{1,0:T(8,128)(2,1)}, bf16[8,80,768]{2,1,0:T(8,128)(2,1)}, f32[16,768]{1,0:T(8,128)}, /*index=5*/bf16[8,768]{1,0:T(8,128)(2,1)}) custom-call(s32[40]{0:T(128)} %stack.122.meta, bf16[8,77,768]{2,1,0:T(8,128)(2,1)} %bitcast.86, bf16[176,768]{1,0:T(8,128)(2,1)} %copy-done.8, ...), custom_call_target="tpu_custom_call" | custom-call | flops 2264924160 | bytes 10000000 | tf_op jit(solution)/shard_map/attend/pallas_call | solution.py:355
  89.4 8.6 %collective-permute-done.28 = bf16[16,768]{1,0:T(8,128)(2,1)S(1)} collective-permute-done((bf16[16,768]{1,0:T(8,128)(2,1)S(1)}, bf16[16,768]{1,0:T(8,128)(2,1)S(1)}, u32[]{:S(2)}, u32[]{:S(2)}) %collective-permute-start.28) | collective-permute-done | bytes 24608 | tf_op jit(solution)/shard_map/ppermute | solution.py:1100
  104.5 4.0 %collective-permute-done.29.rest_31_ = bf16[32,768]{1,0:T(8,128)(2,1)S(1)} collective-permute-done((bf16[32,768]{1,0:T(8,128)(2,1)S(1)}, bf16[32,768]{1,0:T(8,128)(2,1)S(1)}, u32[]{:S(2)}, u32[]{:S(2)}) %collective-permute-start.29) | collective-permute-done | bytes 49184 | tf_op jit(solution)/shard_map/ppermute | solution.py:1106
  108.5 4.6 %collective-permute-start.31 = (bf16[32,768]{1,0:T(8,128)(2,1)S(1)}, bf16[32,768]{1,0:T(8,128)(2,1)S(1)}, u32[]{:S(2)}, u32[]{:S(2)}) collective-permute-start(bf16[32,768]{1,0:T(8,128)(2,1)S(1)} %pad_maximum_fusion.4.rest_30_), channel_id=1, source_target_pairs={{0,12},{1,13},{2,14},{3,15},{4,0},{5,1},{6,2},{7,3},{8,4},{9,5},{1... | collective-permute-start | bytes 147464 | tf_op jit(solution)/shard_map/ppermute | solution.py:1106
  118.9 10.5 %pooled_forward.1 = (bf16[128,512]{1,0:T(8,128)(2,1)}, f32[128,512]{1,0:T(8,128)}, bf16[128,768]{1,0:T(8,128)(2,1)}, f32[128,768]{1,0:T(8,128)}, f32[128,128]{1,...) custom-call(s32[40]{0:T(128)} %stack.122.meta, ...), custom_call_target="tpu_custom_call" | custom-call | flops 1660944384 | bytes 16000000 | tf_op jit(solution)/shard_map/pooled_forward/pallas_call | solution.py:355
  137.6 11.5 %chain.1 = (f32[8,128]{1,0:T(8,128)}, f32[48,512]{1,0:T(8,128)}, f32[192,768]{1,0:T(8,128)}, f32[48,3072]{1,0:T(8,128)}, f32[48,768]{1,0:T(8,128)}, /*index=5*/f...) custom-call(s32[40]{0:T(128)} %stack.122.meta, ...), custom_call_target="tpu_custom_call" | custom-call | flops 1509949440 | bytes 16000000 | tf_op jit(solution)/shard_map/chain/pallas_call | solution.py:355
  150.5 4.4 %scores.1 = (bf16[2560,128]{1,0:T(8,128)(2,1)}, bf16[640,128]{1,0:T(8,128)(2,1)}, bf16[640,128]{1,0:T(8,128)(2,1)}, bf16[8,768]{1,0:T(8,128)(2,1)}) custom-call(s32[40]{0:T(128)} %stack.122.meta, bf16[640,768]{1,0:T(8,128)(2,1)} %get-tuple-element.60.keys, bf16[640,768]{1,0:T(8,128)(2,1)} %get-tuple-element.61.values, ...), custom_call_target="tpu_custom_call" | custom-call | flops 688128000 | bytes 5000000 | tf_op jit(solution)/shard_map/scores/pallas_call | solution.py:355
  154.9 5.5 %all-to-all-start = ((bf16[16,160,128]{2,1,0:T(8,128)(2,1)}), bf16[16,160,128]{2,1,0:T(8,128)(2,1)S(1)}, u32[]{:S(2)}, u32[]{:S(2)}) async-start(bf16[16,160,128]{2,1,0:T(8,128)(2,1)} %bitcast.96), calls=%async_computation | async-start | bytes 1310720 | tf_op jit(solution)/shard_map/all_to_all | solution.py:1207
  160.4 14.8 %hidden.1 = (f32[8,80,768]{2,1,0:T(8,128)}, bf16[640,3072]{1,0:T(8,128)(2,1)}) custom-call(s32[40]{0:T(128)} %stack.122.meta, bf16[8,77,768]{2,1,0:T(8,128)(2,1)} %bitcast.87, bf16[8,80,768]{2,1,0:T(8,128)(2,1)} %get-tuple-element.56.mixed, f32[16,768]{1,0:T(8,128)} %get-tuple-element.57.vec, bf16[240,768]{1,0:T(8,128)(2,1)} %copy-done.10, ...), custom_call_target="tpu_custom_call" | custom-call | flops 3774873600 | bytes 14000000 | tf_op jit(solution)/shard_map/hidden/pallas_call | solution.py:355
  176.1 9.8 %finish.1 = bf16[8,77,768]{2,1,0:T(8,128)(2,1)} custom-call(s32[40]{0:T(128)} %stack.122.meta, f32[8,80,768]{2,1,0:T(8,128)} %get-tuple-element.58.middle, bf16[640,3072]{1,0:T(8,128)(2,1)} %get-tuple-element.59.act, f32[16,768]{1,0:T(8,128)} %get-tuple-element.57.vec, bf16[224,768]{1,0:T(8,128)(2,1)} %copy-done.6, bf16[224,768]{1,0:T(8,128)(2,1)} %copy-done.7, ...), custom_call_target="tpu_custom_call" | custom-call | flops 3019898880 | bytes 13000000 | tf_op jit(solution)/shard_map/finish/pallas_call | solution.py:355
  185.9 2.5 %copy.45 = bf16[1,8,77,768]{3,1,2,0:T(8,128)(2,1)} copy(bf16[1,8,77,768]{3,2,1,0:T(8,128)(2,1)} %bitcast.89) | data formatting | bytes 1892352
  192.0 7.4 %stream_grads.1 = f32[8,77,768]{2,1,0:T(8,128)} custom-call(s32[40]{0:T(128)} %stack.122.meta, bf16[8,77,768]{2,1,0:T(8,128)(2,1)} %bitcast.88, bf16[640,128]{1,0:T(8,128)(2,1)} %get-tuple-element.77.gk, bf16[640,128]{1,0:T(8,128)(2,1)} %get-tuple-element.78.gv, bf16[8,768]{1,0:T(8,128)(2,1)} %constant_dynamic-slice_fusion.10.q_own, ...), custom_call_target="tpu_custom_call" | custom-call | flops 589824000 | bytes 7000000 | tf_op jit(solution)/shard_map/stream_grads/pallas_call | solution.py:355
  199.4 3.9 %copy.46 = f32[1,8,77,768]{3,1,2,0:T(8,128)} copy(f32[1,8,77,768]{3,2,1,0:T(8,128)} %bitcast.83) | data formatting | bytes 3784704
  208.6 4.3 %shard_grads.1 = (f32[3,48,768]{2,1,0:T(8,128)}, f32[8,768]{1,0:T(8,128)}, f32[48,128]{1,0:T(8,128)}) custom-call(bf16[16,160,128]{2,1,0:T(8,128)(2,1)} %copy-done.14, f32[128,768]{1,0:T(8,128)} %convert_element_type.71.q_all, f32[128,768]{1,0:T(8,128)} %convert_element_type.72.gm_all, bf16[128,48]{1,0:T(8,128)(2,1)} %constant_dynamic-slice_fusion.3.norm_sl, ...), custom_call_target="tpu_custom_call" | custom-call | flops 402653184 | bytes 2000000 | tf_op jit(solution)/shard_map/shard_grads/pallas_call | solution.py:355
  (184 shorter events, 60.8 us)
Async XLA Ops:
  8.2 10.3 %collective-permute-start.1 = (bf16[2,176,768]{2,1,0:T(8,128)(2,1)S(1)}, bf16[2,176,768]{2,1,0:T(8,128)(2,1)S(1)}, u32[]{:S(2)}, u32[]{:S(2)}) collective-permute-start(bf16[2,176,768]{2,1,0:T(8,128)(2,1)S(1)} %pad_maximum_fusion.2), channel_id=1, source_target_pairs={{0,4},{1,3},{4,8},{5,1},{8,12},{9,5},{12,14},{13,9},{14,10},{15,13... | collective-permute-start | bytes 1622024 | tf_op jit(solution)/shard_map/ppermute | solution.py:1060
  11.3 9.7 %collective-permute-start.18 = (bf16[224,768]{1,0:T(8,128)(2,1)S(1)}, bf16[224,768]{1,0:T(8,128)(2,1)S(1)}, u32[]{:S(2)}, u32[]{:S(2)}) collective-permute-start(bf16[224,768]{1,0:T(8,128)(2,1)S(1)} %get-tuple-element.138.rest_0_.rest_20_.rest_10_), channel_id=1, source_target_pairs={{0,1},{1,0},{4,5},{5,4},{8,9},{9,8},{12,13},{13,12},{14,15},{15,14... | collective-permute-start | bytes 1032200 | tf_op jit(solution)/shard_map/ppermute | solution.py:1056
  18.5 9.5 %collective-permute-start.3 = (bf16[2,176,768]{2,1,0:T(8,128)(2,1)S(1)}, bf16[2,176,768]{2,1,0:T(8,128)(2,1)}, u32[]{:S(2)}, u32[]{:S(2)}) collective-permute-start(bf16[2,176,768]{2,1,0:T(8,128)(2,1)S(1)} %collective-permute-done.1.rest_2_), channel_id=1, source_target_pairs={{0,4},{1,3},{4,8},{5,1},{8,12},{9,5},{12,14},{13,9},{14,10},{15,13... | collective-permute-start | bytes 1622024 | tf_op jit(solution)/shard_map/ppermute | solution.py:1060
  20.9 9.1 %collective-permute-start.9 = (bf16[240,768]{1,0:T(8,128)(2,1)S(1)}, bf16[240,768]{1,0:T(8,128)(2,1)S(1)}, u32[]{:S(2)}, u32[]{:S(2)}) collective-permute-start(bf16[240,768]{1,0:T(8,128)(2,1)S(1)} %get-tuple-element.136.rest_0_.rest_10_), channel_id=1, source_target_pairs={{0,1},{1,0},{4,5},{5,4},{8,9},{9,8},{12,13},{13,12},{14,15},{15,14... | collective-permute-start | bytes 1105928 | tf_op jit(solution)/shard_map/ppermute | solution.py:1056
  21.1 14.1 %collective-permute-start.19 = (bf16[2,224,768]{2,1,0:T(8,128)(2,1)S(1)}, bf16[2,224,768]{2,1,0:T(8,128)(2,1)S(1)}, u32[]{:S(2)}, u32[]{:S(2)}) collective-permute-start(bf16[2,224,768]{2,1,0:T(8,128)(2,1)S(1)} %pad_maximum_fusion.1), channel_id=1, source_target_pairs={{0,4},{1,3},{4,8},{5,1},{8,12},{9,5},{12,14},{13,9},{14,10},{15,13... | collective-permute-start | bytes 2064392 | tf_op jit(solution)/shard_map/ppermute | solution.py:1060
  27.9 13.1 %collective-permute-start.5 = (bf16[2,176,768]{2,1,0:T(8,128)(2,1)}, bf16[2,176,768]{2,1,0:T(8,128)(2,1)S(1)}, u32[]{:S(2)}, u32[]{:S(2)}) collective-permute-start(bf16[2,176,768]{2,1,0:T(8,128)(2,1)} %collective-permute-done.3.rest_4_), channel_id=1, source_target_pairs={{0,4},{1,3},{4,8},{5,1},{8,12},{9,5},{12,14},{13,9},{14,10},{15,13... | collective-permute-start | bytes 1622024 | tf_op jit(solution)/shard_map/ppermute | solution.py:1060
  30.1 18.9 %collective-permute-start.10 = (bf16[2,240,768]{2,1,0:T(8,128)(2,1)S(1)}, bf16[2,240,768]{2,1,0:T(8,128)(2,1)}, u32[]{:S(2)}, u32[]{:S(2)}) collective-permute-start(bf16[2,240,768]{2,1,0:T(8,128)(2,1)S(1)} %pad_maximum_fusion), channel_id=1, source_target_pairs={{0,4},{1,3},{4,8},{5,1},{8,12},{9,5},{12,14},{13,9},{14,10},{15,13... | collective-permute-start | bytes 2211848 | tf_op jit(solution)/shard_map/ppermute | solution.py:1060
  31.7 17.3 %collective-permute-start.2 = (bf16[2,176,768]{2,1,0:T(8,128)(2,1)S(1)}, bf16[2,176,768]{2,1,0:T(8,128)(2,1)S(1)}, u32[]{:S(2)}, u32[]{:S(2)}) collective-permute-start(bf16[2,176,768]{2,1,0:T(8,128)(2,1)S(1)} %collective-permute-done.1.rest_2_), channel_id=1, source_target_pairs={{0,1},{1,0},{4,5},{5,4},{8,9},{9,8},{12,13},{13,12},{14,15},{15,14... | collective-permute-start | bytes 1622024 | tf_op jit(solution)/shard_map/ppermute | solution.py:1061
  35.2 26.4 %collective-permute-start.21 = (bf16[2,224,768]{2,1,0:T(8,128)(2,1)S(1)}, bf16[2,224,768]{2,1,0:T(8,128)(2,1)S(1)}, u32[]{:S(2)}, u32[]{:S(2)}) collective-permute-start(bf16[2,224,768]{2,1,0:T(8,128)(2,1)S(1)} %collective-permute-done.19.rest_2_.rest_22_.rest_12_), channel_id=1, source_target_pairs={{0,4},{1,3},{4,8},{5,1},{8,12},{9,5},{12,14},{13,9},{14,10},{15,13... | collective-permute-start | bytes 2064392 | tf_op jit(solution)/shard_map/ppermute | solution.py:1060
  37.3 27.2 %collective-permute-start.4 = (bf16[2,176,768]{2,1,0:T(8,128)(2,1)}, bf16[2,176,768]{2,1,0:T(8,128)(2,1)}, u32[]{:S(2)}, u32[]{:S(2)}) collective-permute-start(bf16[2,176,768]{2,1,0:T(8,128)(2,1)} %collective-permute-done.3.rest_4_), channel_id=1, source_target_pairs={{0,1},{1,0},{4,5},{5,4},{8,9},{9,8},{12,13},{13,12},{14,15},{15,14... | collective-permute-start | bytes 1622024 | tf_op jit(solution)/shard_map/ppermute | solution.py:1061
  41.0 18.1 %collective-permute-start.7 = (bf16[176,768]{1,0:T(8,128)(2,1)S(1)}, bf16[176,768]{1,0:T(8,128)(2,1)S(1)}, u32[]{:S(2)}, u32[]{:S(2)}) collective-permute-start(bf16[176,768]{1,0:T(8,128)(2,1)S(1)} %slice_bitcast_fusion.2), channel_id=1, source_target_pairs={{0,4},{1,3},{4,8},{5,1},{8,12},{9,5},{12,14},{13,9},{14,10},{15,13... | collective-permute-start | bytes 811016 | tf_op jit(solution)/shard_map/ppermute | solution.py:1062
  49.0 15.4 %collective-permute-start.6 = (bf16[2,176,768]{2,1,0:T(8,128)(2,1)S(1)}, bf16[2,176,768]{2,1,0:T(8,128)(2,1)}, u32[]{:S(2)}, u32[]{:S(2)}) collective-permute-start(bf16[2,176,768]{2,1,0:T(8,128)(2,1)S(1)} %collective-permute-done.5.rest_6_), channel_id=1, source_target_pairs={{0,1},{1,0},{4,5},{5,4},{8,9},{9,8},{12,13},{13,12},{14,15},{15,14... | collective-permute-start | bytes 1622024 | tf_op jit(solution)/shard_map/ppermute | solution.py:1061
  49.8 35.2 %collective-permute-start.12 = (bf16[2,240,768]{2,1,0:T(8,128)(2,1)}, bf16[2,240,768]{2,1,0:T(8,128)(2,1)}, u32[]{:S(2)}, u32[]{:S(2)}) collective-permute-start(bf16[2,240,768]{2,1,0:T(8,128)(2,1)} %collective-permute-done.10.rest_2_.rest_12_), channel_id=1, source_target_pairs={{0,4},{1,3},{4,8},{5,1},{8,12},{9,5},{12,14},{13,9},{14,10},{15,13... | collective-permute-start | bytes 2211848 | tf_op jit(solution)/shard_map/ppermute | solution.py:1060
  61.6 26.5 %collective-permute-start.23 = (bf16[2,224,768]{2,1,0:T(8,128)(2,1)S(1)}, bf16[2,224,768]{2,1,0:T(8,128)(2,1)S(1)}, u32[]{:S(2)}, u32[]{:S(2)}) collective-permute-start(bf16[2,224,768]{2,1,0:T(8,128)(2,1)S(1)} %collective-permute-done.21.rest_4_.rest_24_.rest_14_), channel_id=1, source_target_pairs={{0,4},{1,3},{4,8},{5,1},{8,12},{9,5},{12,14},{13,9},{14,10},{15,13... | collective-permute-start | bytes 2064392 | tf_op jit(solution)/shard_map/ppermute | solution.py:1060
  84.5 16.4 %collective-permute-start.20 = (bf16[2,224,768]{2,1,0:T(8,128)(2,1)S(1)}, bf16[2,224,768]{2,1,0:T(8,128)(2,1)S(1)}, u32[]{:S(2)}, u32[]{:S(2)}) collective-permute-start(bf16[2,224,768]{2,1,0:T(8,128)(2,1)S(1)} %collective-permute-done.19.rest_2_.rest_22_.rest_12_), channel_id=1, source_target_pairs={{0,1},{1,0},{4,5},{5,4},{8,9},{9,8},{12,13},{13,12},{14,15},{15,14... | collective-permute-start | bytes 2064392 | tf_op jit(solution)/shard_map/ppermute | solution.py:1061
  84.9 17.6 %collective-permute-start.11 = (bf16[2,240,768]{2,1,0:T(8,128)(2,1)}, bf16[2,240,768]{2,1,0:T(8,128)(2,1)S(1)}, u32[]{:S(2)}, u32[]{:S(2)}) collective-permute-start(bf16[2,240,768]{2,1,0:T(8,128)(2,1)} %collective-permute-done.10.rest_2_.rest_12_), channel_id=1, source_target_pairs={{0,1},{1,0},{4,5},{5,4},{8,9},{9,8},{12,13},{13,12},{14,15},{15,14... | collective-permute-start | bytes 2211848 | tf_op jit(solution)/shard_map/ppermute | solution.py:1061
  85.0 19.5 %collective-permute-start.22 = (bf16[2,224,768]{2,1,0:T(8,128)(2,1)S(1)}, bf16[2,224,768]{2,1,0:T(8,128)(2,1)S(1)}, u32[]{:S(2)}, u32[]{:S(2)}) collective-permute-start(bf16[2,224,768]{2,1,0:T(8,128)(2,1)S(1)} %collective-permute-done.21.rest_4_.rest_24_.rest_14_), channel_id=1, source_target_pairs={{0,1},{1,0},{4,5},{5,4},{8,9},{9,8},{12,13},{13,12},{14,15},{15,14... | collective-permute-start | bytes 2064392 | tf_op jit(solution)/shard_map/ppermute | solution.py:1061
  85.8 12.2 %collective-permute-start.14 = (bf16[2,240,768]{2,1,0:T(8,128)(2,1)}, bf16[2,240,768]{2,1,0:T(8,128)(2,1)}, u32[]{:S(2)}, u32[]{:S(2)}) collective-permute-start(bf16[2,240,768]{2,1,0:T(8,128)(2,1)} %collective-permute-done.12.rest_4_.rest_14_), channel_id=1, source_target_pairs={{0,4},{1,3},{4,8},{5,1},{8,12},{9,5},{12,14},{13,9},{14,10},{15,13... | collective-permute-start | bytes 2211848 | tf_op jit(solution)/shard_map/ppermute | solution.py:1060
  88.1 9.9 %collective-permute-start.28 = (bf16[16,768]{1,0:T(8,128)(2,1)S(1)}, bf16[16,768]{1,0:T(8,128)(2,1)S(1)}, u32[]{:S(2)}, u32[]{:S(2)}) collective-permute-start(bf16[16,768]{1,0:T(8,128)(2,1)S(1)} %pad_maximum_fusion.5), channel_id=1, source_target_pairs={{0,2},{1,3},{2,0},{3,1},{4,6},{5,7},{6,4},{7,5},{8,10},{9,11},{10,... | collective-permute-start | bytes 73736 | tf_op jit(solution)/shard_map/ppermute | solution.py:1100
  98.0 17.5 %collective-permute-start.25 = (bf16[224,768]{1,0:T(8,128)(2,1)}, bf16[224,768]{1,0:T(8,128)(2,1)}, u32[]{:S(2)}, u32[]{:S(2)}) collective-permute-start(bf16[224,768]{1,0:T(8,128)(2,1)} %slice_bitcast_fusion.1), channel_id=1, source_target_pairs={{0,4},{1,3},{4,8},{5,1},{8,12},{9,5},{12,14},{13,9},{14,10},{15,13... | collective-permute-start | bytes 1032200 | tf_op jit(solution)/shard_map/ppermute | solution.py:1062
  99.8 16.3 %collective-permute-start.16 = (bf16[240,768]{1,0:T(8,128)(2,1)}, bf16[240,768]{1,0:T(8,128)(2,1)}, u32[]{:S(2)}, u32[]{:S(2)}) collective-permute-start(bf16[240,768]{1,0:T(8,128)(2,1)} %slice_bitcast_fusion), channel_id=1, source_target_pairs={{0,4},{1,3},{4,8},{5,1},{8,12},{9,5},{12,14},{13,9},{14,10},{15,13... | collective-permute-start | bytes 1105928 | tf_op jit(solution)/shard_map/ppermute | solution.py:1062
  102.5 10.5 %collective-permute-start.30 = (bf16[32,768]{1,0:T(8,128)(2,1)S(1)}, bf16[32,768]{1,0:T(8,128)(2,1)S(1)}, u32[]{:S(2)}, u32[]{:S(2)}) collective-permute-start(bf16[32,768]{1,0:T(8,128)(2,1)S(1)} %pad_maximum_fusion.4.rest_30_), channel_id=1, source_target_pairs={{0,8},{1,9},{2,10},{3,11},{4,12},{5,13},{6,14},{7,15},{8,0},{9,1},... | collective-permute-start | bytes 147464 | tf_op jit(solution)/shard_map/ppermute | solution.py:1106
  104.5 11.7 %collective-permute-start.13 = (bf16[2,240,768]{2,1,0:T(8,128)(2,1)}, bf16[2,240,768]{2,1,0:T(8,128)(2,1)}, u32[]{:S(2)}, u32[]{:S(2)}) collective-permute-start(bf16[2,240,768]{2,1,0:T(8,128)(2,1)} %collective-permute-done.12.rest_4_.rest_14_), channel_id=1, source_target_pairs={{0,1},{1,0},{4,5},{5,4},{8,9},{9,8},{12,13},{13,12},{14,15},{15,14... | collective-permute-start | bytes 2211848 | tf_op jit(solution)/shard_map/ppermute | solution.py:1061
  154.9 52.3 %all-to-all-start = ((bf16[16,160,128]{2,1,0:T(8,128)(2,1)}), bf16[16,160,128]{2,1,0:T(8,128)(2,1)S(1)}, u32[]{:S(2)}, u32[]{:S(2)}) async-start(bf16[16,160,128]{2,1,0:T(8,128)(2,1)} %bitcast.96), calls=%async_computation | async-start | bytes 1310720 | tf_op jit(solution)/shard_map/all_to_all | solution.py:1207
  (45 other events, 587.1 us)

commit v2 on v0

--- a/solution.py
+++ b/solution.py
@@ -1,12 +1,15 @@
 import jax
 import jax.numpy as jnp
 from jax import lax
+from jax.experimental import pallas as pl
+from jax.experimental.pallas import tpu as pltpu
 from jax.sharding import PartitionSpec as P
 
 DI = 768
 DT = 512
 HD = 64
 IMG_ROWS = 50
+EMB = 512
 
 
 EPS = 1e-05
@@ -335,9 +338,1056 @@
     )
 
 
+RING_Z = (0, 1, 2, 3, 3, 2, 1, 0)
+RING_Y = (0, 0, 0, 0, 1, 1, 1, 1)
+ITEMS = 16
+N = ITEMS * 8
+F32 = jnp.float32
+BF16 = jnp.bfloat16
+ANY = pl.BlockSpec(memory_space=pl.ANY)
+VMEM = pl.BlockSpec(memory_space=pltpu.VMEM)
+SMEM = pl.BlockSpec(memory_space=pltpu.SMEM)
+SCALE = float(HD) ** -0.5
+PAYLOAD = 160
+
+
+def call(kernel, name, ins, outs, scratch, flops=0, touched=0):
+    return pl.pallas_call(
+        kernel,
+        name=name,
+        out_shape=[jax.ShapeDtypeStruct(shape, dtype) for _, shape, dtype in outs],
+        in_specs=[spec for spec, _ in ins],
+        out_specs=[spec for spec, _, _ in outs],
+        scratch_shapes=scratch,
+        compiler_params=pltpu.CompilerParams(vmem_limit_bytes=60 * 1024 * 1024),
+        cost_estimate=pl.CostEstimate(flops=flops, bytes_accessed=touched, transcendentals=0),
+    )(*[item for _, item in ins])
+
+
+def dot(left, right, left_dim=1, right_dim=0):
+    return lax.dot_general(
+        left, right, (((left_dim,), (right_dim,)), ((), ())), preferred_element_type=F32
+    )
+
+
+def aligned(index, size):
+    return pl.multiple_of(index, size)
+
+
+def owner_table(dp_index):
+    core = dp_index % 2
+    row = dp_index // 2 % 2
+    depth = dp_index // 4
+    place = jnp.where(row == 0, depth, 7 - depth)
+
+    def chip(where):
+        where = (where + 8) % 8
+        z = jnp.where(where < 4, where, 7 - where)
+        y = jnp.where(where < 4, 0, 1)
+        return (z * 2 + y) * 2
+
+    sign = jnp.where(core == 0, -1, 1)
+    found = [chip(place)]
+    for hop in range(1, 4):
+        found += [chip(place + sign * hop), chip(place - sign * hop)]
+    return found + [chip(place + 4) + core, chip(place + 4) + 1 - core]
+
+
+class Place:
+    def __init__(self, lengths):
+        self.dp = lax.axis_index("dp")
+        self.text = lax.axis_index("tower") == 1
+        self.lengths = lengths
+        self.keep = (
+            lax.broadcasted_iota(jnp.int32, (1, DI), 1) < jnp.where(self.text, DT, DI)
+        ).astype(F32)
+        self.winv = jnp.where(self.text, 1.0 / DT, 1.0 / DI).astype(F32)
+
+    def length(self, s):
+        return jnp.where(self.text, self.lengths[s], IMG_ROWS)
+
+    def pool(self, s):
+        return jnp.where(self.text, self.lengths[s] - 1, 0)
+
+    def column(self, pick):
+        ids = lax.broadcasted_iota(jnp.int32, (1, 8, 1), 1)
+        column = jnp.zeros((1, 8, 1), jnp.int32)
+        for s in range(8):
+            column = jnp.where(ids == s, pick(s), column)
+        return column
+
+    def either(self, path, image):
+        @pl.when(self.text)
+        def _():
+            path(DT, 77)
+
+        @pl.when(jnp.logical_not(self.text))
+        def _():
+            path(DI, image)
+
+    def mine(self, visit):
+        for owner in range(ITEMS):
+
+            @pl.when(self.dp == owner)
+            def _(owner=owner):
+                visit(owner)
+
+
+def copy(src, dst, sem):
+    found = pltpu.make_async_copy(src, dst, sem)
+    found.start()
+    return found
+
+
+def drain(dst, sem):
+    pltpu.make_async_copy(dst, dst, sem).wait()
+
+
+def fetch(owners, refs, row, rows, dst, sem):
+    for owner, ref in zip(owners, refs):
+        if len(ref.shape) == 3:
+            copy(ref.at[:, pl.ds(row, rows), :], dst.at[pl.ds(owner, 2)], sem)
+        else:
+            copy(ref.at[pl.ds(row, rows), :], dst.at[owner], sem)
+
+
+def embed_matrix(packed):
+    tail = jnp.concatenate([packed[:, 0:16, EMB:DI], packed[:, 16:32, EMB:DI]], axis=2)
+    return jnp.concatenate([packed[:, :, 0:EMB], tail], axis=1).reshape(DI, EMB)
+
+
+def normalize(values, keep, winv):
+    mean = jnp.sum(values, axis=-1, keepdims=True) * winv
+    centred = (values - mean) * keep
+    var = jnp.sum(centred * centred, axis=-1, keepdims=True) * winv
+    inv = lax.rsqrt(var + EPS)
+    return centred * inv, inv
+
+
+def normalize_back(grad_out, gain, normed, inv, keep, winv):
+    grad_normed = grad_out * gain
+    mean_grad = jnp.sum(grad_normed, axis=-1, keepdims=True) * winv
+    mean_cross = jnp.sum(grad_normed * normed, axis=-1, keepdims=True) * winv
+    return keep * inv * (grad_normed - mean_grad - normed * mean_cross)
+
+
+def row_sum(values):
+    return jnp.sum(values, axis=0, keepdims=True)
+
+
+def head_rows(rows):
+    heads = lax.broadcasted_iota(jnp.int32, rows.shape, 1) // HD
+    parts = [jnp.where(heads == head, rows, 0.0) for head in range(16)]
+    return jnp.concatenate(parts, axis=0).astype(BF16)
+
+
+def chunks(count, visit):
+    @pl.loop(0, count // 14)
+    def _(i):
+        visit(i * 14, aligned(i * 112, 16), 14)
+
+    if count % 14:
+        at = count - count % 14
+        visit(at, at * 8, count % 14)
+
+
+def pack_first_kernel(lengths, qkv, tok, *rest):
+    here = Place(lengths)
+    vectors, (qv_bias, fc_bias, out) = rest[:8], rest[8:]
+    out[0:144, :] = qkv[...]
+    sub = lax.broadcasted_iota(jnp.int32, (8, DI), 0)
+    pooled = jnp.zeros((8, DI), F32)
+    for s in range(8):
+        pooled = jnp.where(sub == s, tok[here.pool(s)].astype(F32), pooled)
+    out[144:160, :] = jnp.concatenate([pooled, jnp.zeros((8, DI), F32)], axis=0).astype(BF16)
+    lane = lax.broadcasted_iota(jnp.int32, (1, DI), 1) // 48 == here.dp
+    short = [v[...].astype(F32) for v in vectors]
+    pair = qv_bias[...].astype(F32)
+    short[2:2] = [pair[0:1], pair[1:2]]
+    rows = [jnp.where(lane, jnp.concatenate([v] * ITEMS, axis=1), 0.0) for v in short]
+    wide = lax.broadcasted_iota(jnp.int32, (1, 4 * DI), 1) // 192 == here.dp
+    fc = jnp.where(wide, jnp.concatenate([fc_bias[...].astype(F32)] * ITEMS, axis=1), 0.0)
+    rows += [fc[:, i * DI : (i + 1) * DI] for i in range(4)]
+    row_id = lax.broadcasted_iota(jnp.int32, (16, DI), 0)
+    small = jnp.zeros((16, DI), F32)
+    for at, row in enumerate(rows):
+        small = jnp.where(row_id == at, jnp.broadcast_to(row, (16, DI)), small)
+    out[160:176, :] = small.astype(BF16)
+
+
+def pack_first(lengths, qkv, tok, vectors, qv_bias, fc_bias):
+    return call(
+        pack_first_kernel,
+        "pack_first",
+        [(SMEM, lengths)] + [(VMEM, item) for item in (qkv, tok, *vectors, qv_bias, fc_bias)],
+        [(VMEM, (176, DI), BF16)],
+        [],
+        touched=1_500_000,
+    )[0]
+
+
+def pack_rest_kernel(w_out, w_fc, w_emb, out):
+    out[0:48, :] = w_out[...]
+    out[48:80, 0:EMB] = w_emb[0:32, :]
+    out[48:64, EMB:DI] = w_emb[32:48, 0:256]
+    out[64:80, EMB:DI] = w_emb[32:48, 256:EMB]
+    for block in range(4):
+        out[80 + 48 * block : 128 + 48 * block, :] = w_fc[:, block * DI : (block + 1) * DI]
+
+
+def pack_rest(w_out, w_fc, w_emb):
+    return call(
+        pack_rest_kernel,
+        "pack_rest",
+        [(VMEM, item) for item in (w_out, w_fc, w_emb)],
+        [(VMEM, (272, DI), BF16)],
+        [],
+        touched=1_500_000,
+    )[0]
+
+
+def attend_kernel(lengths, tok, *rest):
+    first, (keys_hbm, values_hbm, norm_hbm, mixed, vec, pooled), scratch = rest[:9], rest[9:15], rest[15:]
+    weights, small, normed, keys, values, norm_low, qf, kf, vf, mf, sems, outs = scratch
+    here = Place(lengths)
+    owners = owner_table(here.dp)
+    fetch(owners, first, 160, 16, small, sems.at[0])
+    fetch(owners, first, 0, 144, weights, sems.at[1])
+    keep, winv = here.keep, here.winv
+    drain(small, sems.at[0])
+    vec[...] = jnp.sum(small[...].astype(F32), axis=0)
+
+    def norm_chunk(position, row, count):
+        x = tok[pl.ds(position, count)].astype(F32).reshape(count * 8, DI)
+        norm, _ = normalize(x, keep, winv)
+        norm_low[pl.ds(row, count * 8), :] = norm.astype(BF16)
+        normed[pl.ds(row, count * 8), :] = (norm * vec[0:1, :] + vec[1:2, :]).astype(BF16)
+
+    def path(width, count):
+        rows = count * 8
+        span = 80 if count == 77 else count
+        chunks(count, norm_chunk)
+        if span > count:
+            for dst in (qf, kf, vf):
+                dst[:, rows : span * 8, :] = jnp.zeros((6, span * 8 - rows, 128), F32)
+        drain(weights, sems.at[1])
+        for third, dst, low, bias in ((0, qf, None, 2), (1, kf, keys, None), (2, vf, values, 3)):
+
+            @pl.loop(0, width // 256)
+            def _(j, third=third, dst=dst, low=low, bias=bias):
+                lanes = pl.ds(aligned(j * 256, 256), 256)
+                weight = weights[:, third * 48 : third * 48 + 48, lanes].reshape(DI, 256)
+                prod = dot(normed[0:rows, 0:width], weight[0:width])
+                if bias is not None:
+                    prod = prod + vec[bias : bias + 1, lanes]
+                if third == 0:
+                    prod = prod.astype(BF16).astype(F32) * SCALE
+                dst[2 * j, 0:rows, :] = prod[:, 0:128]
+                dst[2 * j + 1, 0:rows, :] = prod[:, 128:256]
+                if low is not None:
+                    low[0:rows, lanes] = prod.astype(BF16)
+
+        saved = [
+            copy(keys, keys_hbm, outs.at[0]),
+            copy(values, values_hbm, outs.at[1]),
+            copy(norm_low, norm_hbm, outs.at[2]),
+        ]
+        key_pos = lax.broadcasted_iota(jnp.int32, (span, 2 * span), 0)
+        query_pos = lax.broadcasted_iota(jnp.int32, (span, 2 * span), 1) % span
+        low_half = lax.broadcasted_iota(jnp.int32, (span, 128), 1) < HD
+
+        @pl.loop(0, 8)
+        def _(s):
+            at = pl.ds(s, span, stride=8)
+            allowed = key_pos < here.length(s)
+            if width == DT:
+                allowed = allowed & (key_pos <= query_pos)
+            pairs = range(width // 128)
+            raws = []
+            for pair in pairs:
+                query, key = qf.at[pair][at, :], kf.at[pair][at, :].astype(BF16)
+                spread = [jnp.where(low_half, query, 0.0), jnp.where(low_half, 0.0, query)]
+                spread = jnp.concatenate(spread, axis=0).astype(BF16)
+                raws.append(dot(key, spread, 1, 1))
+            probs = []
+            for raw in raws:
+                raw = jnp.where(allowed, raw, NEG_FILL)
+                terms = jnp.exp(raw - jnp.max(raw, axis=0, keepdims=True))
+                probs.append((terms / jnp.sum(terms, axis=0, keepdims=True)).astype(BF16))
+            for pair in pairs:
+                out = dot(probs[pair], vf.at[pair][at, :].astype(BF16), 0, 0)
+                mf.at[pair][at, :] = jnp.where(low_half, out[0:span], out[span : 2 * span])
+
+        for i in range(width // 128):
+            mixed[0:rows, 128 * i : 128 * i + 128] = mf[i, 0:rows, :].astype(BF16)
+        for item in saved:
+            item.wait()
+
+    here.either(path, 56)
+    row_id = lax.broadcasted_iota(jnp.int32, (8, DI), 0)
+    picked = jnp.zeros((8, DI), F32)
+    for s in range(8):
+        at = pl.ds(aligned(here.pool(s) * 8, 8), 8)
+        block = jnp.concatenate([mf[i, at, :] for i in range(6)], axis=1)
+        picked = jnp.where(row_id == s, block, picked)
+    tall = jnp.concatenate([jnp.where(keep > 0.0, picked, 0.0), jnp.zeros((8, DI), F32)], axis=0)
+    for owner in range(ITEMS):
+        pooled[owner] = tall.astype(BF16)
+
+
+def attend(lengths, tok, first):
+    rows = tok.shape[0] * tok.shape[1]
+    high = (tok.shape[0] + 3) * tok.shape[1]
+    return call(
+        attend_kernel,
+        "attend",
+        [(SMEM, lengths), (VMEM, tok)] + [(ANY, r) for r in first],
+        [
+            (ANY, (rows, DI), BF16),
+            (ANY, (rows, DI), BF16),
+            (ANY, (rows, DI), BF16),
+            (VMEM, (rows, DI), BF16),
+            (VMEM, (16, DI), F32),
+            (VMEM, (ITEMS, 16, DI), BF16),
+        ],
+        [
+            pltpu.VMEM((ITEMS, 144, DI), BF16),
+            pltpu.VMEM((ITEMS, 16, DI), BF16),
+            pltpu.VMEM((rows, DI), BF16),
+            pltpu.VMEM((rows, DI), BF16),
+            pltpu.VMEM((rows, DI), BF16),
+            pltpu.VMEM((rows, DI), BF16),
+            pltpu.VMEM((6, high, 128), F32),
+            pltpu.VMEM((6, high, 128), F32),
+            pltpu.VMEM((6, high, 128), F32),
+            pltpu.VMEM((6, high, 128), F32),
+            pltpu.SemaphoreType.DMA((2,)),
+            pltpu.SemaphoreType.DMA((3,)),
+        ],
+        flops=12_000_000_000,
+        touched=14_000_000,
+    )
+
+
+def widen_kernel(lengths, tok, vec, mixed_hbm, *rest):
+    first, second, mixes = rest[:9], rest[9:18], rest[18]
+    outs, scratch = rest[19:31], rest[31:]
+    (act_hbm, middle_hbm, mid_out, norm2_out, inv2_out, slope_out, act_p, q_out, q_own, n2_sl, mix_sl,
+     norm_sl) = outs
+    w_q, w_out, w_fc, xs, ms, mix, n2_all, norm1_all, middle, act, sems = scratch
+    here = Place(lengths)
+    owners = owner_table(here.dp)
+    rows_all = mixed_hbm.shape[0]
+    fetch(owners, second, 0, 48, w_out, sems.at[2])
+    pooled_in = copy(mixes, ms, sems.at[1])
+    full = copy(mixed_hbm, mix.at[pl.ds(N, rows_all), :], sems.at[5])
+    fetch(owners, first, 144, 16, xs, sems.at[0])
+    fetch(owners, second, 80, 192, w_fc, sems.at[3])
+    fetch(owners, first, 0, 48, w_q, sems.at[4])
+    keep, winv = here.keep, here.winv
+    drain(w_out, sems.at[2])
+    pooled_in.wait()
+    mix[0:N, :] = ms[...].astype(F32)[:, :8, :].reshape(N, DI).astype(BF16)
+    full.wait()
+
+    def norm_chunk(position, row, count):
+        at = pl.ds(N + row, count * 8)
+        total = middle[at, :] + tok[pl.ds(position, count)].astype(F32).reshape(count * 8, DI)
+        middle[at, :] = total
+        norm, _ = normalize(total, keep, winv)
+        n2_all[at, :] = (norm * vec[5:6, :] + vec[6:7, :]).astype(BF16)
+
+    def path(width, count):
+        rows = N + count * 8
+        norm_rows = N + (count if width == DT else 56) * 8
+
+        @pl.loop(0, width // 256)
+        def _(j):
+            lanes = pl.ds(aligned(j * 256, 256), 256)
+            weight = w_out[:, :, lanes].reshape(DI, 256)[0:width]
+            middle[0:norm_rows, lanes] = dot(mix[0:norm_rows, 0:width], weight) + vec[4:5, lanes]
+
+        if width < DI:
+            middle[0:norm_rows, width:DI] = jnp.zeros((norm_rows, DI - width), F32)
+        chunks(count if width == DT else 56, norm_chunk)
+        saved = copy(middle.at[pl.ds(N, rows_all), :], middle_hbm, sems.at[7])
+        drain(xs, sems.at[0])
+        stream = xs[...].astype(F32)[:, :8, :].reshape(N, DI)
+        pooled = stream + middle[0:N, :]
+        mid_out[...] = pooled
+        norm2, inv2 = normalize(pooled, keep, winv)
+        n2_all[0:N, :] = (norm2 * vec[5:6, :] + vec[6:7, :]).astype(BF16)
+        norm2_out[...] = norm2
+        inv2_out[...] = jnp.broadcast_to(inv2, (N, 128))
+        norm1, _ = normalize(stream, keep, winv)
+        norm1_all[...] = norm1.astype(BF16)
+        drain(w_fc, sems.at[3])
+        for block in range(4):
+
+            @pl.loop(0, 3 if width == DI else (3, 3, 2, 0)[block])
+            def _(j, block=block):
+                lanes = pl.ds(aligned(j * 256, 256), 256)
+                wide = pl.ds(aligned(block * DI + j * 256, 256), 256)
+                weight = w_fc[:, block * 48 : block * 48 + 48, lanes].reshape(DI, 256)[0:width]
+                pre = dot(n2_all[0:rows, 0:width], weight) + vec[10 + block : 11 + block, lanes]
+                gate = jax.nn.sigmoid(GELU_K * pre)
+                low = (pre * gate).astype(BF16)
+                act_p[:, wide] = low[0:N]
+                act[0 : rows - N, wide] = low[N:rows]
+                pre, gate = pre[0:N], gate[0:N]
+                slope_out[:, wide] = gate + GELU_K * pre * gate * (1.0 - gate)
+                copy(act.at[pl.ds(0, rows - N), wide], act_hbm.at[pl.ds(0, rows - N), wide], sems.at[6])
+
+        if width < DI:
+            act_p[:, 4 * width : 4 * DI] = jnp.zeros((N, 4 * DI - 4 * width), BF16)
+            slope_out[:, 4 * width : 4 * DI] = jnp.zeros((N, 4 * DI - 4 * width), F32)
+        drain(w_q, sems.at[4])
+        n1 = (norm1 * vec[0:1, :] + vec[1:2, :]).astype(BF16)
+        q_out[...] = (dot(n1, w_q[...].reshape(DI, DI)) + vec[2:3, :]).astype(BF16).astype(F32)
+        q_own[...] = q_out[pl.ds(aligned(here.dp * 8, 8), 8), :]
+        drain(act.at[pl.ds(0, rows - N), pl.ds(0, 4 * width)], sems.at[6])
+        saved.wait()
+
+    here.either(path, 50)
+
+    def mine(owner):
+        lanes = slice(owner * 48, owner * 48 + 48)
+        n2_sl[...] = n2_all[0:N, lanes]
+        mix_sl[...] = mix[0:N, lanes]
+        norm_sl[...] = norm1_all[:, lanes]
+
+    here.mine(mine)
+
+
+def widen(lengths, tok, vec, mixed, first, second, mixes):
+    rows = mixed.shape[0]
+    return call(
+        widen_kernel,
+        "widen",
+        [(SMEM, lengths), (VMEM, tok), (VMEM, vec), (ANY, mixed)]
+        + [(ANY, r) for r in (*first, *second, mixes)],
+        [
+            (ANY, (rows, 4 * DI), BF16),
+            (ANY, (rows, DI), F32),
+            (VMEM, (N, DI), F32),
+            (VMEM, (N, DI), F32),
+            (VMEM, (N, 128), F32),
+            (VMEM, (N, 4 * DI), F32),
+            (VMEM, (N, 4 * DI), BF16),
+            (VMEM, (N, DI), F32),
+            (VMEM, (8, DI), F32),
+            (VMEM, (N, 48), BF16),
+            (VMEM, (N, 48), BF16),
+            (VMEM, (N, 48), BF16),
+        ],
+        [
+            pltpu.VMEM((ITEMS, 48, DI), BF16),
+            pltpu.VMEM((ITEMS, 48, DI), BF16),
+            pltpu.VMEM((ITEMS, 192, DI), BF16),
+            pltpu.VMEM((ITEMS, 16, DI), BF16),
+            pltpu.VMEM((ITEMS, 16, DI), BF16),
+            pltpu.VMEM((N + rows, DI), BF16),
+            pltpu.VMEM((N + rows, DI), BF16),
+            pltpu.VMEM((N, DI), BF16),
+            pltpu.VMEM((N + rows, DI), F32),
+            pltpu.VMEM((rows, 4 * DI), BF16),
+            pltpu.SemaphoreType.DMA((8,)),
+        ],
+        flops=13_000_000_000,
+        touched=14_000_000,
+    )
+
+
+def head_kernel(lengths, vec, middle_hbm, act_hbm, *rest):
+    second, down, outs, scratch = rest[:9], rest[9:18], rest[18:24], rest[24:]
+    e_out, proj_out, normf_out, invf_out, head_sl, act_sl = outs
+    w_down, w_emb, head_all, middle, act, sems = scratch
+    here = Place(lengths)
+    owners = owner_table(here.dp)
+    early = [copy(act_hbm, act, sems.at[5]), copy(middle_hbm, middle, sems.at[6])]
+    for owner, ref in zip(owners, down):
+        dst = w_down.at[pl.ds(owner, 2)] if len(ref.shape) == 3 else w_down.at[owner]
+        copy(ref, dst, sems.at[owner // 4])
+    fetch(owners, second, 48, 32, w_emb, sems.at[4])
+    keep, winv = here.keep, here.winv
+    for item in early:
+        item.wait()
+    last = middle[...] + vec[7:8, :]
+    for part in range(4):
+        drain(w_down.at[pl.ds(part * 4, 4)], sems.at[part])
+        last = last + dot(act[:, part * DI : part * DI + DI], w_down[part * 4 : part * 4 + 4].reshape(DI, DI))
+    normf, invf = normalize(last, keep, winv)
+    normf_out[...] = normf
+    invf_out[...] = jnp.broadcast_to(invf, (N, 128))
+    head_all[...] = (normf * vec[8:9, :] + vec[9:10, :]).astype(BF16)
+    drain(w_emb, sems.at[4])
+    proj = dot(head_all[...], embed_matrix(w_emb[...]))
+    proj_out[...] = proj
+    scale = lax.rsqrt(jnp.sum(proj * proj, axis=-1, keepdims=True) + NORM_EPS)
+    e_out[...] = (proj * scale).astype(BF16)
+
+    def mine(owner):
+        head_sl[...] = head_all[:, owner * 48 : owner * 48 + 48]
+        act_sl[...] = act[:, owner * 192 : owner * 192 + 192]
+
+    here.mine(mine)
+
+
+def pooled_head(lengths, vec, middle, act, second, down):
+    return call(
+        head_kernel,
+        "pooled_head",
+        [(SMEM, lengths), (VMEM, vec), (ANY, middle), (ANY, act)] + [(ANY, r) for r in (*second, *down)],
+        [
+            (VMEM, (N, EMB), BF16),
+            (VMEM, (N, EMB), F32),
+            (VMEM, (N, DI), F32),
+            (VMEM, (N, 128), F32),
+            (VMEM, (N, 48), BF16),
+            (VMEM, (N, 192), BF16),
+        ],
+        [
+            pltpu.VMEM((ITEMS, 192, DI), BF16),
+            pltpu.VMEM((ITEMS, 32, DI), BF16),
+            pltpu.VMEM((N, DI), BF16),
+            pltpu.VMEM((N, DI), F32),
+            pltpu.VMEM((N, 4 * DI), BF16),
+            pltpu.SemaphoreType.DMA((7,)),
+        ],
+        flops=6_000_000_000,
+        touched=8_000_000,
+    )
+
+
+def one_direction(left, right, mult):
+    sims = dot(left, right, 1, 1)
+    logits = mult * sims
+    top = jnp.max(logits, axis=-1, keepdims=True)
+    total = top + jnp.log(jnp.sum(jnp.exp(logits - top), axis=-1, keepdims=True))
+    count = sims.shape[0]
+    eye = lax.broadcasted_iota(jnp.int32, (count, count), 0) == lax.broadcasted_iota(
+        jnp.int32, (count, count), 1
+    )
+    hot = eye.astype(F32)
+    lost = jnp.sum(total - jnp.sum(hot * logits, axis=-1, keepdims=True), axis=0, keepdims=True)
+    grad = (jnp.exp(logits - total) - hot) * 0.5
+    scale = jnp.sum(jnp.sum(grad * sims, axis=-1, keepdims=True), axis=0, keepdims=True)
+    return lost, scale, mult * grad
+
+
+def chain_kernel(lengths, log_mult, e_own_ref, e_oth_ref, vec, q_own, head_sl, act_sl, n2_sl, mix_sl, *rest):
+    (proj_hbm, normf_hbm, invf_hbm, norm2_hbm, inv2_hbm, slope_hbm, keys_hbm, values_hbm, norm_hbm), rest = (
+        rest[:9], rest[9:]
+    )
+    second, down = rest[:9], rest[9:18]
+    outs, scratch = rest[18:38], rest[38:]
+    (loss_out, scale_out, d_emb_hbm, d_down_hbm, d_fc_hbm, d_out_hbm, g_final, b_final, b_down, g_two, b_two, b_out, b_fc,
+     mid_own, gm_out, gm_own, payload, gk_out, gv_out, gq_out) = outs
+    (w_out, w_fc, w_down, w_emb, gpre, mid_all, proj_v, normf_v, invf_v, norm2_v, inv2_v, slope, keys,
+     values, norm_low, vec_grads, fcb_grads, d_emb, d_down, d_fc, d_out, sems, ins, ends) = scratch
+    here = Place(lengths)
+    owners = owner_table(here.dp)
+    early = [
+        copy(src, dst, ins.at[i])
+        for i, (src, dst) in enumerate(
+            ((proj_hbm, proj_v), (normf_hbm, normf_v), (invf_hbm, invf_v))
+        )
+    ]
+    fetch(owners, second, 48, 32, w_emb, sems.at[0])
+    fetch(owners, down, 0, 192, w_down, sems.at[1])
+    slope_in = copy(slope_hbm, slope, ins.at[3])
+    fetch(owners, second, 80, 192, w_fc, sems.at[2])
+    later = [copy(norm2_hbm, norm2_v, ins.at[4]), copy(inv2_hbm, inv2_v, ins.at[5])]
+    fetch(owners, second, 0, 48, w_out, sems.at[3])
+    last = [
+        copy(src, dst, ins.at[6 + i])
+        for i, (src, dst) in enumerate(((keys_hbm, keys), (values_hbm, values), (norm_hbm, norm_low)))
+    ]
+    keep, winv = here.keep, here.winv
+    text = here.text.astype(F32)
+    mult = jnp.exp(jnp.full((1, 128), log_mult[0], F32))[:, 0:1]
+    own, oth = e_own_ref[...].astype(F32), e_oth_ref[...].astype(F32)
+    e_img = (own * (1.0 - text) + oth * text).astype(BF16)
+    e_txt = (oth * (1.0 - text) + own * text).astype(BF16)
+    lost_img, scale_img, grad_img = one_direction(e_img, e_txt, mult)
+    lost_txt, scale_txt, grad_txt = one_direction(e_txt, e_img, mult)
+    loss_out[...] = (lost_img + lost_txt) / (2.0 * N)
+    scale_out[...] = mult * (scale_img + scale_txt)
+    grad_own = (grad_img * (1.0 - text) + grad_txt * text).astype(BF16)
+    grad_oth = (grad_txt * (1.0 - text) + grad_img * text).astype(BF16)
+    oth_low = e_oth_ref[...]
+    grad_e = dot(grad_own, oth_low) + dot(grad_oth, oth_low, 0, 0)
+    for item in early:
+        item.wait()
+    proj = proj_v[...]
+    r = lax.rsqrt(jnp.sum(proj * proj, axis=-1, keepdims=True) + NORM_EPS)
+    cross = jnp.sum(grad_e * proj, axis=-1, keepdims=True)
+    grad_proj = (r * grad_e - proj * (r * r * r) * cross).astype(BF16)
+    drain(w_emb, sems.at[0])
+    grad_head = dot(grad_proj, embed_matrix(w_emb[...]), 1, 1)
+    normf = normf_v[...]
+    grad_y = normalize_back(grad_head, vec[8:9, :], normf, invf_v[:, 0:1], keep, winv)
+    branch = grad_y.astype(BF16)
+    d_emb[...] = dot(head_sl[...], grad_proj, 0, 0)
+    stored = [copy(d_emb, d_emb_hbm, ends.at[0])]
+    vec_grads[0:1, :] = row_sum(grad_head * normf)
+    vec_grads[1:2, :] = row_sum(grad_head)
+    vec_grads[2:3, :] = row_sum(branch.astype(F32))
+    d_down[...] = dot(act_sl[...], branch, 0, 0)
+    stored.append(copy(d_down, d_down_hbm, ends.at[1]))
+    drain(w_down, sems.at[1])
+    slope_in.wait()
+    for block in range(4):
+        lanes = pl.ds(block * DI, DI)
+        back = dot(branch, w_down[block * 4 : block * 4 + 4].reshape(DI, DI), 1, 1)
+        low = (back * slope[:, lanes]).astype(BF16)
+        gpre[:, lanes] = low
+        fcb_grads[:, lanes] = jnp.broadcast_to(row_sum(low.astype(F32)), (8, DI))
+
+    drain(w_fc, sems.at[2])
+    grad_n2 = jnp.zeros((N, DI), F32)
+    for block in range(4):
+        weight = w_fc[:, block * 48 : block * 48 + 48, :].reshape(DI, DI)
+        grad_n2 = grad_n2 + dot(gpre[:, block * DI : block * DI + DI], weight, 1, 1)
+    for item in later:
+        item.wait()
+    norm2 = norm2_v[...]
+    vec_grads[3:4, :] = row_sum(grad_n2 * norm2)
+    vec_grads[4:5, :] = row_sum(grad_n2)
+    grad_mid = grad_y + normalize_back(grad_n2, vec[5:6, :], norm2, inv2_v[:, 0:1], keep, winv)
+    mid_all[...] = grad_mid
+    own_rows = pl.ds(aligned(here.dp * 8, 8), 8)
+    mid_own[...] = mid_all[own_rows, :]
+    attn = grad_mid.astype(BF16)
+    vec_grads[5:6, :] = row_sum(attn.astype(F32))
+    drain(w_out, sems.at[3])
+    gm_out[...] = dot(attn, w_out[...].reshape(DI, DI), 1, 1).astype(BF16).astype(F32)
+    gm_own[...] = gm_out[own_rows, :]
+
+    @pl.loop(0, 6)
+    def _(j):
+        lanes = pl.ds(aligned(j * 512, 512), 512)
+        d_fc[:, lanes] = dot(n2_sl[...], gpre[:, lanes], 0, 0)
+
+    d_out[...] = dot(mix_sl[...], attn, 0, 0)
+    stored += [copy(d_fc, d_fc_hbm, ends.at[2]), copy(d_out, d_out_hbm, ends.at[3])]
+
+    def mine(owner):
+        lanes = slice(owner * 48, owner * 48 + 48)
+        for at, dst in enumerate((g_final, b_final, b_down, g_two, b_two, b_out)):
+            dst[...] = vec_grads[at : at + 1, lanes]
+        b_fc[...] = fcb_grads[0:1, owner * 192 : owner * 192 + 192]
+
+    here.mine(mine)
+    for item in last:
+        item.wait()
+    q_rows = head_rows(q_own[...])
+    m_rows = head_rows(gm_own[...])
+    lane_sample = lax.broadcasted_iota(jnp.int32, (1, 128), 1) % 8
+    limit = jnp.zeros((1, 128), jnp.int32)
+    for s in range(8):
+        limit = jnp.where(lane_sample == s, here.length(s), limit)
+
+    def path(width, count):
+        rows = count * 8
+        raw = dot(keys[0:rows, 0:width], q_rows[:, 0:width], 1, 1) * SCALE
+        row = lax.broadcasted_iota(jnp.int32, (rows, 128), 0)
+        lane = lax.broadcasted_iota(jnp.int32, (rows, 128), 1)
+        valid = (lane % 8 == row % 8) & (row // 8 < limit) & (lane < width // 8)
+        raw = jnp.where(valid, raw, NEG_FILL)
+        top = jnp.max(raw, axis=0, keepdims=True)
+        terms = jnp.where(valid, jnp.exp(raw - top), 0.0)
+        probs = terms / jnp.maximum(row_sum(terms), 1e-30)
+        grad_probs = dot(values[0:rows, 0:width], m_rows[:, 0:width], 1, 1)
+        crossed = row_sum(probs * grad_probs)
+        gk = (probs * (grad_probs - crossed)).astype(BF16)
+        gv = probs.astype(BF16)
+        gk_out[0:rows, :] = gk
+        gv_out[0:rows, :] = gv
+        back = dot(gk, keys[0:rows, 0:width], 0, 0) * SCALE
+        heads = lax.broadcasted_iota(jnp.int32, (8, width), 1) // HD
+        grad_q = jnp.zeros((8, width), F32)
+        for head in range(width // HD):
+            grad_q = grad_q + jnp.where(heads == head, back[head * 8 : head * 8 + 8], 0.0)
+        if width < DI:
+            grad_q = jnp.concatenate([grad_q, jnp.zeros((8, DI - width), F32)], axis=1)
+        gq_low = grad_q.astype(BF16)
+        gq_out[...] = gq_low
+        norm = norm_low[0:rows, :]
+        z_key = dot(norm, gk, 0, 0).astype(BF16)
+        z_value = dot(norm, gv, 0, 0).astype(BF16)
+        sum_key = row_sum(gk.astype(F32))
+        sum_value = row_sum(gv.astype(F32))
+        key_high = sum_key.astype(BF16).astype(F32)
+        value_high = sum_value.astype(BF16).astype(F32)
+        row_id = lax.broadcasted_iota(jnp.int32, (16, 128), 0)
+        sums = jnp.zeros((16, 128), F32)
+        for at, value in enumerate((key_high, sum_key - key_high, value_high, sum_value - value_high)):
+            sums = jnp.where(row_id == at, jnp.broadcast_to(value, (16, 128)), sums)
+        sums = sums.astype(BF16)
+        gq_wide = gq_low.astype(F32)
+        gq_tall = jnp.concatenate(
+            [gq_wide[:, i * 128 : (i + 1) * 128] for i in range(DI // 128)], axis=0
+        ).astype(BF16)
+        for owner in range(ITEMS):
+            base = owner * PAYLOAD
+            payload[base : base + 48, :] = z_key[owner * 48 : owner * 48 + 48]
+            payload[base + 48 : base + 64, :] = sums
+            payload[base + 64 : base + 112, :] = z_value[owner * 48 : owner * 48 + 48]
+            payload[base + 112 : base + 160, :] = gq_tall
+
+    here.either(path, 56)
+    for item in stored:
+        item.wait()
+
+
+def chain(lengths, log_mult, e_own, e_oth, vec, q_own, slices, saved, second, down):
+    rows = saved[-1].shape[0]
+    return call(
+        chain_kernel,
+        "chain",
+        [(SMEM, lengths), (SMEM, log_mult)]
+        + [(VMEM, item) for item in (e_own, e_oth, vec, q_own, *slices)]
+        + [(ANY, r) for r in (*saved, *second, *down)],
+        [
+            (VMEM, (1, 1), F32),
+            (VMEM, (1, 1), F32),
+            (ANY, (48, EMB), F32),
+            (ANY, (192, DI), F32),
+            (ANY, (48, 4 * DI), F32),
+            (ANY, (48, DI), F32),
+        ]
+        + [(VMEM, (1, 48), F32)] * 6
+        + [
+            (VMEM, (1, 192), F32),
+            (VMEM, (8, DI), F32),
+            (VMEM, (N, DI), F32),
+            (VMEM, (8, DI), F32),
+            (VMEM, (ITEMS * PAYLOAD, 128), BF16),
+            (VMEM, (rows, 128), BF16),
+            (VMEM, (rows, 128), BF16),
+            (VMEM, (8, DI), BF16),
+        ],
+        [
+            pltpu.VMEM((ITEMS, 48, DI), BF16),
+            pltpu.VMEM((ITEMS, 192, DI), BF16),
+            pltpu.VMEM((ITEMS, 192, DI), BF16),
+            pltpu.VMEM((ITEMS, 32, DI), BF16),
+            pltpu.VMEM((N, 4 * DI), BF16),
+            pltpu.VMEM((N, DI), F32),
+            pltpu.VMEM((N, EMB), F32),
+            pltpu.VMEM((N, DI), F32),
+            pltpu.VMEM((N, 128), F32),
+            pltpu.VMEM((N, DI), F32),
+            pltpu.VMEM((N, 128), F32),
+            pltpu.VMEM((N, 4 * DI), F32),
+            pltpu.VMEM((rows, DI), BF16),
+            pltpu.VMEM((rows, DI), BF16),
+            pltpu.VMEM((rows, DI), BF16),
+            pltpu.VMEM((8, DI), F32),
+            pltpu.VMEM((8, 4 * DI), F32),
+            pltpu.VMEM((48, EMB), F32),
+            pltpu.VMEM((192, DI), F32),
+            pltpu.VMEM((48, 4 * DI), F32),
+            pltpu.VMEM((48, DI), F32),
+            pltpu.SemaphoreType.DMA((4,)),
+            pltpu.SemaphoreType.DMA((9,)),
+            pltpu.SemaphoreType.DMA((4,)),
+        ],
+        flops=15_000_000_000,
+        touched=20_000_000,
+    )
+
+
+def close_kernel(lengths, tok, vec, gk, gv, q_own, gm_own, gq, mid_own, act_hbm, middle_hbm, *rest):
+    first, down, (block_out, out), scratch = rest[:9], rest[9:18], rest[18:20], rest[20:]
+    weights, w_down, act, middle, acc, sems = scratch
+    here = Place(lengths)
+    owners = owner_table(here.dp)
+    fetch(owners, first, 0, 144, weights, sems.at[0])
+    early = [copy(act_hbm, act, sems.at[1]), copy(middle_hbm, middle, sems.at[2])]
+    fetch(owners, down, 0, 192, w_down, sems.at[3])
+    keep, winv = here.keep, here.winv
+    q_rows = head_rows(q_own[...])
+    m_rows = head_rows(gm_own[...])
+    pool = here.column(here.pool)
+    length = here.column(here.length)
+    all_rows = out.shape[0]
+    drain(weights, sems.at[0])
+    u_key = (dot(q_rows, weights[:, 48:96, :].reshape(DI, DI), 1, 1) * SCALE).astype(BF16)
+    u_value = dot(m_rows, weights[:, 96:144, :].reshape(DI, DI), 1, 1).astype(BF16)
+    u_query = dot(gq[...], weights[:, 0:48, :].reshape(DI, DI), 1, 1)
+
+    def path(width, count):
+        rows = count * 8
+        acc[0:rows, :] = dot(gk[0:rows, :], u_key) + dot(gv[0:rows, :], u_value)
+
+        def back_chunk(position, row, count):
+            at = pl.ds(row, count * 8)
+            hit = lax.broadcasted_iota(jnp.int32, (count, 8, DI), 0) + position == pool
+            norm, inv = normalize(tok[pl.ds(position, count)].astype(F32).reshape(count * 8, DI), keep, winv)
+            total = acc[at, :] + jnp.where(hit, u_query[None], 0.0).reshape(count * 8, DI)
+            back = normalize_back(total, vec[0:1, :], norm, inv, keep, winv)
+            out[at, :] = back + jnp.where(hit, mid_own[...][None], 0.0).reshape(count * 8, DI)
+
+        chunks(count, back_chunk)
+        if rows < all_rows:
+            out[rows:all_rows, :] = jnp.zeros((all_rows - rows, DI), F32)
+        for item in early:
+            item.wait()
+        drain(w_down, sems.at[3])
+        short = count if width == DT else IMG_ROWS
+        rows = short * 8
+
+        @pl.loop(0, width // 256)
+        def _(j):
+            lanes = pl.ds(aligned(j * 256, 256), 256)
+            weight = w_down[:, :, lanes].reshape(4 * DI, 256)[0 : 4 * width]
+            total = dot(act[0:rows, 0 : 4 * width], weight)
+            total = (total + vec[7:8, lanes] + middle[0:rows, lanes]).reshape(short, 8, 256)
+            where = lax.broadcasted_iota(jnp.int32, (short, 8, 256), 0)
+            block_out[0:rows, lanes] = jnp.where(where < length, total, 0.0).reshape(rows, 256).astype(BF16)
+
+        if width < DI:
+            block_out[:, width:DI] = jnp.zeros((all_rows, DI - width), BF16)
+        if rows < all_rows:
+            block_out[rows:all_rows, :] = jnp.zeros((all_rows - rows, DI), BF16)
+
+    here.either(path, 56)
+
+
+def close(lengths, tok, vec, gk, gv, q_own, gm_own, gq, mid_own, act, middle, first, down):
+    rows = tok.shape[0] * tok.shape[1]
+    return call(
+        close_kernel,
+        "close",
+        [(SMEM, lengths)]
+        + [(VMEM, item) for item in (tok, vec, gk, gv, q_own, gm_own, gq, mid_own)]
+        + [(ANY, r) for r in (act, middle, *first, *down)],
+        [(VMEM, (rows, DI), BF16), (VMEM, (rows, DI), F32)],
+        [
+            pltpu.VMEM((ITEMS, 144, DI), BF16),
+            pltpu.VMEM((ITEMS, 192, DI), BF16),
+            pltpu.VMEM((rows, 4 * DI), BF16),
+            pltpu.VMEM((rows, DI), F32),
+            pltpu.VMEM((rows, DI), F32),
+            pltpu.SemaphoreType.DMA((4,)),
+        ],
+        flops=10_000_000_000,
+        touched=18_000_000,
+    )
+
+
+def shard_kernel(got, q_all, gm_all, norm_sl, w_own, gain, bias, d_qkv, g_one, b_one, qv_out, big, left):
+    dp = lax.axis_index("dp")
+
+    def build(source):
+        @pl.loop(0, ITEMS)
+        def _(j):
+            rows = source[pl.ds(aligned(j * 8, 8), 8), :]
+            big[pl.ds(aligned(j * 128, 128), 128), :] = head_rows(rows)
+
+    def spread(start):
+        for j in range(ITEMS):
+            left[:, j * 128 : (j + 1) * 128] = got[j, start : start + 64, :]
+
+    def column(row):
+        square = (48, 48)
+        same = lax.broadcasted_iota(jnp.int32, square, 0) == lax.broadcasted_iota(jnp.int32, square, 1)
+        return jnp.sum(jnp.where(same, row[...].astype(F32), 0.0), axis=1, keepdims=True)
+
+    build(q_all)
+    spread(0)
+    by_key = dot(left[...], big[...]) * SCALE
+    m_key, s_key = by_key[0:48], by_key[48:49] + by_key[49:50]
+    build(gm_all)
+    spread(48)
+    by_value = dot(left[...], big[...])
+    m_value, s_value = by_value[16:64], by_value[2:3] + by_value[3:4]
+    tall = got[:, 112:160, :].astype(F32)
+    grad_q = jnp.concatenate(
+        [tall[:, i * 8 : i * 8 + 8, :].reshape(N, 128) for i in range(DI // 128)], axis=1
+    )
+    s_query = row_sum(grad_q)
+    m_query = dot(norm_sl[...], grad_q.astype(BF16), 0, 0)
+    gain_col, bias_col = column(gain), column(bias)
+    by_gain = jnp.zeros((48, DI), F32)
+    by_bias = jnp.zeros((48, DI), F32)
+    for third, (moment, total) in enumerate(((m_query, s_query), (m_key, s_key), (m_value, s_value))):
+        d_qkv[third] = gain_col * moment + bias_col * total
+        weight = w_own[third].astype(F32)
+        by_gain = by_gain + weight * moment
+        by_bias = by_bias + weight * total
+    ones = jnp.ones((8, DI), F32)
+    line = (((1,), (1,)), ((), ()))
+    for dst, item in ((g_one, by_gain), (b_one, by_bias)):
+        dst[...] = lax.dot_general(
+            ones, item, line, precision=lax.Precision.HIGHEST, preferred_element_type=F32
+        )[0:1]
+    for owner in range(ITEMS):
+
+        @pl.when(dp == owner)
+        def _(owner=owner):
+            lanes = slice(owner * 48, owner * 48 + 48)
+            qv_out[0:1, :] = s_query[:, lanes]
+            qv_out[1:2, :] = s_value[:, lanes]
+
+
+def shard_grads(got, q_all, gm_all, norm_sl, w_own, gain, bias):
+    plain = (got, q_all, gm_all, norm_sl, w_own, gain, bias)
+    return call(
+        shard_kernel,
+        "shard_grads",
+        [(VMEM, item) for item in plain],
+        [
+            (VMEM, (3, 48, DI), F32),
+            (VMEM, (1, 48), F32),
+            (VMEM, (1, 48), F32),
+            (VMEM, (2, 48), F32),
+        ],
+        [pltpu.VMEM((ITEMS * 128, DI), BF16), pltpu.VMEM((64, ITEMS * 128), BF16)],
+        flops=5_000_000_000,
+        touched=2_000_000,
+    )
+
+
+BOTH = ("tower", "dp")
+
+
+def device(tower, place, core):
+    return tower * 16 + (RING_Z[place] * 2 + RING_Y[place]) * 2 + core
+
+
+def routes(towers):
+    swap, turn = [], []
+    for tower in range(towers):
+        for place in range(8):
+            for core, step in ((0, 1), (1, -1)):
+                here = device(tower, place, core)
+                swap.append((here, device(tower, place, 1 - core)))
+                turn.append((here, device(tower, (place + step) % 8, core)))
+    return swap, turn
+
+
+def after(item, *earlier):
+    return lax.optimization_barrier((item, *earlier))[0] if earlier else item
+
+
+class Ring:
+    def __init__(self, shard, swap, turn, first_core):
+        other = lax.ppermute(shard, BOTH, swap)
+        self.swap, self.turn, self.first_core = swap, turn, first_core
+        held = jnp.stack([jnp.where(first_core, shard, other), jnp.where(first_core, other, shard)])
+        self.items = [held]
+        self.last = held
+        self.hops = 0
+
+    def step(self, *earlier, swap_after=()):
+        held = self.last
+        if self.hops == 3:
+            held = jnp.where(self.first_core, held[0], held[1])
+        held = lax.ppermute(after(held, *earlier), BOTH, self.turn)
+        self.items += [held, lax.ppermute(after(held, *swap_after), BOTH, self.swap)]
+        self.last = held
+        self.hops += 1
+        return held
+
+
+def ring_body(
+    tokens,
+    lengths,
+    ln1_gain,
+    ln1_bias,
+    qkv_weight,
+    qv_bias,
+    out_weight,
+    out_bias,
+    ln2_gain,
+    ln2_bias,
+    fc_weight,
+    fc_bias,
+    down_weight,
+    down_bias,
+    final_gain,
+    final_bias,
+    embed_weight,
+    logit_scale,
+):
+    towers = lax.axis_size("tower")
+    dp_index = lax.axis_index("dp")
+    swap, turn = routes(towers)
+    tok = tokens[0].transpose(1, 0, 2)
+    w_own = qkv_weight[0].transpose(1, 0, 2)
+    vectors = (ln1_gain, ln1_bias, out_bias, ln2_gain, ln2_bias, down_bias, final_gain, final_bias)
+    first_own = pack_first(lengths, w_own.reshape(144, DI), tok, vectors, qv_bias[0], fc_bias)
+    second_own = pack_rest(out_weight[0], fc_weight[0], embed_weight[0])
+    first_core = dp_index % 2 == 0
+
+    qkv_ring = Ring(first_own, swap, turn, first_core)
+    wide_ring = Ring(second_own, swap, turn, first_core)
+    down_ring = Ring(down_weight[0], swap, turn, first_core)
+    q1 = qkv_ring.step()
+    wide_ring.step(q1)
+    qkv_ring.step()
+    q3 = qkv_ring.step()
+    qkv_ring.step()
+    first = qkv_ring.items
+    keys, values, norm_low, mixed, vec, pooled = attend(lengths, tok, first)
+    w2 = wide_ring.step(q3, swap_after=(vec,))
+    d1 = down_ring.step(q3, swap_after=(vec,))
+    mixes = lax.all_to_all(after(pooled, w2, d1), "dp", 0, 0, tiled=True)
+    w3 = wide_ring.step(vec)
+    d2 = down_ring.step(vec)
+    wide_ring.step()
+    d3 = down_ring.step(w3, swap_after=(mixes,))
+    second = wide_ring.items
+    mixed = after(mixed, d3)
+    act, middle, mid_p, norm2, inv2, slope, act_p, q_all, q_own, n2_sl, mix_sl, norm_sl = widen(
+        lengths, tok, vec, mixed, first, second, mixes
+    )
+    down_ring.step(mixes, swap_after=(q_own,))
+    down = down_ring.items
+    e_own, proj, normf, invf, head_sl, act_sl = pooled_head(lengths, vec, mid_p, act_p, second, down)
+    across = [(t * 16 + d, (1 - t) * 16 + d) for t in range(2) for d in range(16)]
+    e_oth = lax.ppermute(e_own, BOTH, across)
+    (loss, scale, d_emb, d_down, d_fc, d_out, g_final, b_final, b_down, g_two, b_two, b_out, b_fc,
+     mid_own, gm_all, gm_own, payload, gk, gv, gq) = chain(
+        lengths, logit_scale, e_own, e_oth, vec, q_own, (head_sl, act_sl, n2_sl, mix_sl),
+        (proj, normf, invf, norm2, inv2, slope, keys, values, norm_low), second, down,
+    )
+    got = lax.all_to_all(payload, "dp", 0, 0, tiled=True).reshape(ITEMS, PAYLOAD, 128)
+    block_out, tokens_grad = close(
+        lengths, tok, vec, gk, gv, q_own, gm_own, gq, mid_own, act, middle, first, down
+    )
+    d_qkv, g_one, b_one, qv_sums = shard_grads(got, q_all, gm_all, norm_sl, w_own, ln1_gain, ln1_bias)
+    seq = tok.shape[0]
+    return (
+        block_out.reshape(seq, 8, DI).transpose(1, 0, 2)[None],
+        tokens_grad.reshape(seq, 8, DI).transpose(1, 0, 2)[None],
+        loss.reshape(1),
+        g_one,
+        b_one,
+        d_qkv.transpose(1, 0, 2)[None],
+        qv_sums[None],
+        d_out[None],
+        b_out,
+        g_two,
+        b_two,
+        d_fc[None],
+        b_fc,
+        d_down[None],
+        b_down,
+        g_final,
+        b_final,
+        d_emb[None],
+        scale.reshape(1),
+    )
+
+
 def solution(mesh):
+    fits = mesh.shape["dp"] == ITEMS and mesh.shape["tower"] == 2
     return jax.shard_map(
-        body,
+        ring_body if fits else body,
         mesh=mesh,
         in_specs=(
             P("tower", "dp", None, None),

time: 902 us -> 177 us (0.20)
  waiting for transfers between devices: 402 us -> 63.8 us
  blocking collectives: 229 us -> 0 us
  local copies, waits for them, and re-layouts: 109 us -> 3.78 us
  matrix products: 102 us -> 0 us
  Pallas kernels: 0 us -> 65 us
  starting transfers between devices: 3.78 us -> 40.1 us
  other arithmetic: 27 us -> 2.4 us
  between operations: 20 us -> 1.61 us
    reduce_scatter x6 -> x0, waiting for transfers between devices: 376 us -> none  [the longest x1 116 us: body(): lax.psum_scatter(d_down_w, 'dp', scatter_dimension=0, tiled=True)]
    unnamed x2 -> x0, blocking collectives: 122 us -> none
    dot_general x24 -> x0, matrix products: 102 us -> none  [the longest x6 34 us: contract_rows(): lax.dot_general(left_op, right_op, (((0,), (0,)), ((), ())), preferred_el...]
    pallas_call x0 -> x8, Pallas kernels: none -> 65 us  [call(): pl.pallas_call(kernel, name=name, out_shape=[jax.ShapeDtypeStruct(shape,...]
    all_gather x3 -> x0, blocking collectives: 64.7 us -> none  [the longest x1 25.5 us: body(): lax.all_gather(embed_weight[0], 'dp', axis=0, tiled=True)]
    ppermute x2 -> x28, waiting for transfers between devices: 10.3 us -> 57.8 us  [the longest x12 49.5 us: step(): held = lax.ppermute(after(held, *earlier), BOTH, self.turn)]
    psum x1 -> x0, blocking collectives: 41.8 us -> none  [body(): totals = lax.psum((loss_part, scale_part), ('tower', 'dp'))]
    reshape x8 -> x0, local copies, waits for them, and re-layouts: 31 us -> none  [the longest x1 9.7 us: body(): qkv_flat.astype(bf16).reshape(samples, seq_rows, 3, head_count, HD)]
  transfers between devices with their start and end apart: 13 -> 30, of which waited for: 7 -> 13; matrix products, arithmetic and copies ran while one was open for 17% -> 1% of each run, Pallas kernels for 0% -> 21%
where the time goes in v2:
time: 177 us
  Pallas kernels  65 us (37%)
  waiting for transfers between devices  63.8 us (36%)
  starting transfers between devices  40.1 us (23%)
  local copies, waits for them, and re-layouts  3.78 us (2%)
  other arithmetic  2.4 us (1%)
    pallas_call x8, Pallas kernels, call(): pl.pallas_call(kernel, name=name, out_shape=[jax.ShapeDtypeStruct(shape,...  65 us
    ppermute x12, waiting for transfers between devices, step(): held = lax.ppermute(after(held, *earlier), BOTH, self.turn)  49.5 us
    ppermute x12, starting transfers between devices, step(): held = lax.ppermute(after(held, *earlier), BOTH, self.turn)  28.5 us
    all_to_all x1, waiting for transfers between devices, ring_body(): lax.all_to_all(payload, 'dp', 0, 0, tiled=True).reshape(ITEMS, PAYLOAD, 128)  5.94 us
    ppermute x1, waiting for transfers between devices, ring_body(): e_oth = lax.ppermute(e_own, BOTH, across)  5.5 us
    all_to_all x1, starting transfers between devices, ring_body(): lax.all_to_all(payload, 'dp', 0, 0, tiled=True).reshape(ITEMS, PAYLOAD, 128)  4.97 us
    all_to_all x1, starting transfers between devices, ring_body(): mixes = lax.all_to_all(after(pooled, w2, d1), 'dp', 0, 0, tiled=True)  3.91 us
    unnamed x36, local copies, waits for them, and re-layouts  3.78 us
  transfers between devices with their start and end apart: 30, of which 13 were waited for; matrix products, arithmetic and copies ran while one was open for 1% of the time, Pallas kernels for 21%

profile of v2, /device:TPU:0, one launch (start us, length us, event | category | flops | bytes accessed | tf_op | source)
XLA Modules:
  0.0 176.7 jit_solution(6532622410814797396)
XLA Ops:
  0.7 2.2 %pack_first.1 = bf16[176,768]{1,0:T(8,128)(2,1)} custom-call(s32[8]{0:T(128)} %lengths.11, bf16[144,768]{1,0:T(8,128)(2,1)} %bitcast.61, bf16[77,8,768]{2,1,0:T(8,128)(2,1)} %bitcast.54, bf16[1,48]{1,0:T(2,128)(2,1)} %gain.1, bf16[1,48]{1,0:T(2,128)(2,1)} %bias.1, bf16[1,48]{1,0:T(2,128)(2,1)} %rest_2_.1, bf16[1,48]{1,0:T(2,128)(2,1)} %rest_3_.1, ...), custom_call_target="tpu_custom_call" | custom-call | bytes 1500000 | tf_op jit(solution)/shard_map/pack_first/pallas_call | solution.py:355
  5.8 3.0 %collective-permute-start.1 = (bf16[2,176,768]{2,1,0:T(8,128)(2,1)S(1)}, bf16[2,176,768]{2,1,0:T(8,128)(2,1)S(1)}, u32[]{:S(2)}, u32[]{:S(2)}) collective-permute-start(bf16[2,176,768]{2,1,0:T(8,128)(2,1)S(1)} %pad_maximum_fusion.2.rest_0_), channel_id=1, source_target_pairs={{0,4},{1,3},{4,8},{5,1},{8,12},{9,5},{12,14},{13,9},{14,10},{15,13... | collective-permute-start | bytes 1622024 | tf_op jit(solution)/shard_map/ppermute | solution.py:1289
  8.8 7.3 %collective-permute-done.1.rest_1_ = bf16[2,176,768]{2,1,0:T(8,128)(2,1)S(1)} collective-permute-done((bf16[2,176,768]{2,1,0:T(8,128)(2,1)S(1)}, bf16[2,176,768]{2,1,0:T(8,128)(2,1)S(1)}, u32[]{:S(2)}, u32[]{:S(2)}) %collective-permute-start.1) | collective-permute-done | bytes 540704 | tf_op jit(solution)/shard_map/ppermute | solution.py:1289
  19.9 5.6 %collective-permute-done.3.rest_3_ = bf16[2,176,768]{2,1,0:T(8,128)(2,1)} collective-permute-done((bf16[2,176,768]{2,1,0:T(8,128)(2,1)S(1)}, bf16[2,176,768]{2,1,0:T(8,128)(2,1)}, u32[]{:S(2)}, u32[]{:S(2)}) %collective-permute-start.3) | collective-permute-done | bytes 540704 | tf_op jit(solution)/shard_map/ppermute | solution.py:1289
  30.4 4.7 %collective-permute-done.5.rest_5_ = bf16[2,176,768]{2,1,0:T(8,128)(2,1)S(1)} collective-permute-done((bf16[2,176,768]{2,1,0:T(8,128)(2,1)}, bf16[2,176,768]{2,1,0:T(8,128)(2,1)S(1)}, u32[]{:S(2)}, u32[]{:S(2)}) %collective-permute-start.5) | collective-permute-done | bytes 540704 | tf_op jit(solution)/shard_map/ppermute | solution.py:1289
  35.1 2.1 %collective-permute-start.7 = (bf16[176,768]{1,0:T(8,128)(2,1)S(1)}, bf16[176,768]{1,0:T(8,128)(2,1)S(1)}, u32[]{:S(2)}, u32[]{:S(2)}) collective-permute-start(bf16[176,768]{1,0:T(8,128)(2,1)S(1)} %fusion.2), channel_id=1, source_target_pairs={{0,4},{1,3},{4,8},{5,1},{8,12},{9,5},{12,14},{13,9},{14,10},{15,13... | collective-permute-start | bytes 811016 | tf_op jit(solution)/shard_map/ppermute | solution.py:1289
  37.8 9.2 %collective-permute-done.7.rest_7_ = bf16[176,768]{1,0:T(8,128)(2,1)S(1)} collective-permute-done((bf16[176,768]{1,0:T(8,128)(2,1)S(1)}, bf16[176,768]{1,0:T(8,128)(2,1)S(1)}, u32[]{:S(2)}, u32[]{:S(2)}) %collective-permute-start.7) | collective-permute-done | bytes 270368 | tf_op jit(solution)/shard_map/ppermute | solution.py:1289
  52.3 11.8 %attend.1 = (bf16[616,768]{1,0:T(8,128)(2,1)}, bf16[616,768]{1,0:T(8,128)(2,1)}, bf16[616,768]{1,0:T(8,128)(2,1)}, bf16[616,768]{1,0:T(8,128)(2,1)}, f32[16,768]{1,0:T(8,128)}, /*index=5*/bf16[16,16,768]{2,1,0:T(8,128)(2,1)}) custom-call(s32[8]{0:T(128)} %lengths.11, bf16[77,8,768]{2,1,0:T(8,128)(2,1)} %bitcast.55, bf16[2,176,768]{2,1,0:T(8,128)(2,1)} %copy-done.5, ...), custom_call_target="tpu_custom_call" | custom-call | flops 12000000000 | bytes 14000000 | tf_op jit(solution)/shard_map/attend/pallas_call | solution.py:355
  70.2 3.9 %all-to-all-start = ((bf16[16,16,768]{2,1,0:T(8,128)(2,1)}), bf16[16,16,768]{2,1,0:T(8,128)(2,1)S(1)}, u32[]{:S(2)}, u32[]{:S(2)}) async-start(bf16[16,16,768]{2,1,0:T(8,128)(2,1)} %get-tuple-element.90), calls=%async_computation | async-start | bytes 786432 | tf_op jit(solution)/shard_map/all_to_all | solution.py:1338
  74.1 7.0 %collective-permute-done.15.rest_14_.rest_5_ = bf16[2,272,768]{2,1,0:T(8,128)(2,1)S(1)} collective-permute-done((bf16[2,272,768]{2,1,0:T(8,128)(2,1)S(1)}, bf16[2,272,768]{2,1,0:T(8,128)(2,1)S(1)}, u32[]{:S(2)}, u32[]{:S(2)}) %collective-permute-start.15) | collective-permute-done | bytes 835616 | tf_op jit(solution)/shard_map/ppermute | solution.py:1289
  81.1 2.9 %collective-permute-start.20 = (bf16[272,768]{1,0:T(8,128)(2,1)S(1)}, bf16[272,768]{1,0:T(8,128)(2,1)}, u32[]{:S(2)}, u32[]{:S(2)}) collective-permute-start(bf16[272,768]{1,0:T(8,128)(2,1)S(1)} %fusion), channel_id=1, source_target_pairs={{0,4},{1,3},{4,8},{5,1},{8,12},{9,5},{12,14},{13,9},{14,10},{15,13... | collective-permute-start | bytes 1253384 | tf_op jit(solution)/shard_map/ppermute | solution.py:1289
  84.0 3.7 %collective-permute-done.11.rest_12_.rest_21_ = bf16[2,192,768]{2,1,0:T(8,128)(2,1)} collective-permute-done((bf16[2,192,768]{2,1,0:T(8,128)(2,1)}, bf16[2,192,768]{2,1,0:T(8,128)(2,1)}, u32[]{:S(2)}, u32[]{:S(2)}) %collective-permute-start.11) | collective-permute-done | bytes 589856 | tf_op jit(solution)/shard_map/ppermute | solution.py:1289
  87.7 3.7 %collective-permute-start.16 = (bf16[2,192,768]{2,1,0:T(8,128)(2,1)}, bf16[2,192,768]{2,1,0:T(8,128)(2,1)S(1)}, u32[]{:S(2)}, u32[]{:S(2)}) collective-permute-start(bf16[2,192,768]{2,1,0:T(8,128)(2,1)} %collective-permute-done.11.rest_12_.rest_21_), channel_id=1, source_target_pairs={{0,4},{1,3},{4,8},{5,1},{8,12},{9,5},{12,14},{13,9},{14,10},{15,13... | collective-permute-start | bytes 1769480 | tf_op jit(solution)/shard_map/ppermute | solution.py:1289
  91.4 3.9 %collective-permute-done.20.rest_16_.rest_7_ = bf16[272,768]{1,0:T(8,128)(2,1)} collective-permute-done((bf16[272,768]{1,0:T(8,128)(2,1)S(1)}, bf16[272,768]{1,0:T(8,128)(2,1)}, u32[]{:S(2)}, u32[]{:S(2)}) %collective-permute-start.20) | collective-permute-done | bytes 417824 | tf_op jit(solution)/shard_map/ppermute | solution.py:1289
  95.3 6.4 %collective-permute-done.16.rest_14_.rest_23_ = bf16[2,192,768]{2,1,0:T(8,128)(2,1)S(1)} collective-permute-done((bf16[2,192,768]{2,1,0:T(8,128)(2,1)}, bf16[2,192,768]{2,1,0:T(8,128)(2,1)S(1)}, u32[]{:S(2)}, u32[]{:S(2)}) %collective-permute-start.16) | collective-permute-done | bytes 589856 | tf_op jit(solution)/shard_map/ppermute | solution.py:1289
  102.4 3.6 %collective-permute-start.25 = (bf16[192,768]{1,0:T(8,128)(2,1)S(1)}, bf16[192,768]{1,0:T(8,128)(2,1)}, u32[]{:S(2)}, u32[]{:S(2)}) collective-permute-start(bf16[192,768]{1,0:T(8,128)(2,1)S(1)} %fusion.1), channel_id=1, source_target_pairs={{0,4},{1,3},{4,8},{5,1},{8,12},{9,5},{12,14},{13,9},{14,10},{15,13... | collective-permute-start | bytes 884744 | tf_op jit(solution)/shard_map/ppermute | solution.py:1289
  106.0 13.2 %widen.1 = (bf16[616,3072]{1,0:T(8,128)(2,1)}, f32[616,768]{1,0:T(8,128)}, f32[128,768]{1,0:T(8,128)}, f32[128,768]{1,0:T(8,128)}, f32[128,128]{1,0:T(8,128)}, /...) custom-call(s32[8]{0:T(128)} %lengths.11, ...), custom_call_target="tpu_custom_call" | custom-call | flops 12999999488 | bytes 14000000 | tf_op jit(solution)/shard_map/widen/pallas_call | solution.py:355
  122.0 5.6 %pooled_head.1 = (bf16[128,512]{1,0:T(8,128)(2,1)}, f32[128,512]{1,0:T(8,128)}, f32[128,768]{1,0:T(8,128)}, f32[128,128]{1,0:T(8,128)}, bf16[128,48]{1,0:T(8,128)(2,1)}, /*index=5*/bf16[128,192]{1,0:T(8,128)(2,1)}) custom-call(s32[8]{0:T(128)} %lengths.11, f32[16,768]{1,0:T(8,128)} %get-tuple-element.80.vec, f32[128,768]{1,0:T(8,128)} %get-tuple-element.91.middle_hbm, ...), custom_call_target="tpu_custom_call" | custom-call | flops 6000000000 | bytes 8000000 | tf_op jit(solution)/shard_map/pooled_head/pallas_call | solution.py:355
  128.4 5.5 %collective-permute-done.27.e_oth_ref = bf16[128,512]{1,0:T(8,128)(2,1)S(1)} collective-permute-done((bf16[128,512]{1,0:T(8,128)(2,1)}, bf16[128,512]{1,0:T(8,128)(2,1)S(1)}, u32[]{:S(2)}, u32[]{:S(2)}) %collective-permute-start.27) | collective-permute-done | bytes 131104 | tf_op jit(solution)/shard_map/ppermute | solution.py:1352
  134.5 15.1 %chain.1 = (f32[1,1]{1,0:T(1,128)}, f32[1,1]{1,0:T(1,128)}, f32[48,512]{1,0:T(8,128)}, f32[192,768]{1,0:T(8,128)}, f32[48,3072]{1,0:T(8,128)}, /*index=5*/f32[48...) custom-call(s32[8]{0:T(128)} %lengths.11, ...), custom_call_target="tpu_custom_call" | custom-call | flops 15000000512 | bytes 20000000 | tf_op jit(solution)/shard_map/chain/pallas_call | solution.py:355
  149.7 5.0 %all-to-all-start.1 = ((bf16[16,160,128]{2,1,0:T(8,128)(2,1)}), bf16[16,160,128]{2,1,0:T(8,128)(2,1)S(1)}, u32[]{:S(2)}, u32[]{:S(2)}) async-start(bf16[16,160,128]{2,1,0:T(8,128)(2,1)} %bitcast.58), calls=%async_computation.1 | async-start | bytes 1310720 | tf_op jit(solution)/shard_map/all_to_all | solution.py:1358
  154.6 10.7 %close.1 = (bf16[616,768]{1,0:T(8,128)(2,1)}, f32[616,768]{1,0:T(8,128)}) custom-call(s32[8]{0:T(128)} %lengths.11, bf16[77,8,768]{2,1,0:T(8,128)(2,1)} %bitcast.57, f32[16,768]{1,0:T(8,128)} %get-tuple-element.80.vec, bf16[616,128]{1,0:T(8,128)(2,1)} %get-tuple-element.111.gk, bf16[616,128]{1,0:T(8,128)(2,1)} %get-tuple-element.112.gv, ...), custom_call_target="tpu_custom_call" | custom-call | flops 10000000000 | bytes 18000000 | tf_op jit(solution)/shard_map/close/pallas_call | solution.py:355
  165.3 5.9 %all-to-all-done.1.got = bf16[16,160,128]{2,1,0:T(8,128)(2,1)S(1)} async-done(((bf16[16,160,128]{2,1,0:T(8,128)(2,1)}), bf16[16,160,128]{2,1,0:T(8,128)(2,1)S(1)}, u32[]{:S(2)}, u32[]{:S(2)}) %all-to-all-start.1) | async-done | bytes 655392 | tf_op jit(solution)/shard_map/all_to_all | solution.py:1358
  172.1 4.6 %shard_grads.1 = (f32[3,48,768]{2,1,0:T(8,128)}, f32[1,48]{1,0:T(1,128)}, f32[1,48]{1,0:T(1,128)}, f32[2,48]{1,0:T(2,128)}) custom-call(bf16[16,160,128]{2,1,0:T(8,128)(2,1)} %copy-done.2, f32[128,768]{1,0:T(8,128)} %get-tuple-element.122.q_all, f32[128,768]{1,0:T(8,128)} %get-tuple-element.123.gm_all, bf16[128,48]{1,0:T(8,128)(2,1)} %get-tuple-element.124.norm_sl, ...), custom_call_target="tpu_custom_call" | custom-call | flops 5000000000 | bytes 2000000 | tf_op jit(solution)/shard_map/shard_grads/pallas_call | solution.py:355
  (89 shorter events, 28.4 us)
Async XLA Ops:
  5.8 10.3 %collective-permute-start.1 = (bf16[2,176,768]{2,1,0:T(8,128)(2,1)S(1)}, bf16[2,176,768]{2,1,0:T(8,128)(2,1)S(1)}, u32[]{:S(2)}, u32[]{:S(2)}) collective-permute-start(bf16[2,176,768]{2,1,0:T(8,128)(2,1)S(1)} %pad_maximum_fusion.2.rest_0_), channel_id=1, source_target_pairs={{0,4},{1,3},{4,8},{5,1},{8,12},{9,5},{12,14},{13,9},{14,10},{15,13... | collective-permute-start | bytes 1622024 | tf_op jit(solution)/shard_map/ppermute | solution.py:1289
  25.5 9.6 %collective-permute-start.5 = (bf16[2,176,768]{2,1,0:T(8,128)(2,1)}, bf16[2,176,768]{2,1,0:T(8,128)(2,1)S(1)}, u32[]{:S(2)}, u32[]{:S(2)}) collective-permute-start(bf16[2,176,768]{2,1,0:T(8,128)(2,1)} %collective-permute-done.3.rest_3_), channel_id=1, source_target_pairs={{0,4},{1,3},{4,8},{5,1},{8,12},{9,5},{12,14},{13,9},{14,10},{15,13... | collective-permute-start | bytes 1622024 | tf_op jit(solution)/shard_map/ppermute | solution.py:1289
  27.6 10.2 %collective-permute-start.9 = (bf16[192,768]{1,0:T(8,128)(2,1)S(1)}, bf16[192,768]{1,0:T(8,128)(2,1)S(1)}, u32[]{:S(2)}, u32[]{:S(2)}) collective-permute-start(bf16[192,768]{1,0:T(8,128)(2,1)S(1)} %bitcast.60), channel_id=1, source_target_pairs={{0,1},{1,0},{4,5},{5,4},{8,9},{9,8},{12,13},{13,12},{14,15},{15,14... | collective-permute-start | bytes 884744 | tf_op jit(solution)/shard_map/ppermute | solution.py:1278
  28.8 18.3 %collective-permute-start.13 = (bf16[2,272,768]{2,1,0:T(8,128)(2,1)S(1)}, bf16[2,272,768]{2,1,0:T(8,128)(2,1)S(1)}, u32[]{:S(2)}, u32[]{:S(2)}) collective-permute-start(bf16[2,272,768]{2,1,0:T(8,128)(2,1)S(1)} %pad_maximum_fusion.rest_9_.rest_0_), channel_id=1, source_target_pairs={{0,4},{1,3},{4,8},{5,1},{8,12},{9,5},{12,14},{13,9},{14,10},{15,13... | collective-permute-start | bytes 2506760 | tf_op jit(solution)/shard_map/ppermute | solution.py:1289
  35.1 11.8 %collective-permute-start.7 = (bf16[176,768]{1,0:T(8,128)(2,1)S(1)}, bf16[176,768]{1,0:T(8,128)(2,1)S(1)}, u32[]{:S(2)}, u32[]{:S(2)}) collective-permute-start(bf16[176,768]{1,0:T(8,128)(2,1)S(1)} %fusion.2), channel_id=1, source_target_pairs={{0,4},{1,3},{4,8},{5,1},{8,12},{9,5},{12,14},{13,9},{14,10},{15,13... | collective-permute-start | bytes 811016 | tf_op jit(solution)/shard_map/ppermute | solution.py:1289
  37.3 12.0 %collective-permute-start.2 = (bf16[2,176,768]{2,1,0:T(8,128)(2,1)S(1)}, bf16[2,176,768]{2,1,0:T(8,128)(2,1)S(1)}, u32[]{:S(2)}, u32[]{:S(2)}) collective-permute-start(bf16[2,176,768]{2,1,0:T(8,128)(2,1)S(1)} %collective-permute-done.1.rest_1_), channel_id=1, source_target_pairs={{0,1},{1,0},{4,5},{5,4},{8,9},{9,8},{12,13},{13,12},{14,15},{15,14... | collective-permute-start | bytes 1622024 | tf_op jit(solution)/shard_map/ppermute | solution.py:1290
  37.3 14.4 %collective-permute-start.4 = (bf16[2,176,768]{2,1,0:T(8,128)(2,1)}, bf16[2,176,768]{2,1,0:T(8,128)(2,1)}, u32[]{:S(2)}, u32[]{:S(2)}) collective-permute-start(bf16[2,176,768]{2,1,0:T(8,128)(2,1)} %collective-permute-done.3.rest_3_), channel_id=1, source_target_pairs={{0,1},{1,0},{4,5},{5,4},{8,9},{9,8},{12,13},{13,12},{14,15},{15,14... | collective-permute-start | bytes 1622024 | tf_op jit(solution)/shard_map/ppermute | solution.py:1290
  37.8 14.5 %collective-permute-start.6 = (bf16[2,176,768]{2,1,0:T(8,128)(2,1)S(1)}, bf16[2,176,768]{2,1,0:T(8,128)(2,1)}, u32[]{:S(2)}, u32[]{:S(2)}) collective-permute-start(bf16[2,176,768]{2,1,0:T(8,128)(2,1)S(1)} %collective-permute-done.5.rest_5_), channel_id=1, source_target_pairs={{0,1},{1,0},{4,5},{5,4},{8,9},{9,8},{12,13},{13,12},{14,15},{15,14... | collective-permute-start | bytes 1622024 | tf_op jit(solution)/shard_map/ppermute | solution.py:1290
  47.1 21.0 %collective-permute-start.10 = (bf16[2,192,768]{2,1,0:T(8,128)(2,1)S(1)}, bf16[2,192,768]{2,1,0:T(8,128)(2,1)}, u32[]{:S(2)}, u32[]{:S(2)}) collective-permute-start(bf16[2,192,768]{2,1,0:T(8,128)(2,1)S(1)} %pad_maximum_fusion.1.rest_9_.rest_18_), channel_id=1, source_target_pairs={{0,4},{1,3},{4,8},{5,1},{8,12},{9,5},{12,14},{13,9},{14,10},{15,13... | collective-permute-start | bytes 1769480 | tf_op jit(solution)/shard_map/ppermute | solution.py:1289
  50.0 15.9 %collective-permute-start.14 = (bf16[2,272,768]{2,1,0:T(8,128)(2,1)S(1)}, bf16[2,272,768]{2,1,0:T(8,128)(2,1)S(1)}, u32[]{:S(2)}, u32[]{:S(2)}) collective-permute-start(bf16[2,272,768]{2,1,0:T(8,128)(2,1)S(1)} %collective-permute-done.13.rest_10_.rest_1_), channel_id=1, source_target_pairs={{0,4},{1,3},{4,8},{5,1},{8,12},{9,5},{12,14},{13,9},{14,10},{15,13... | collective-permute-start | bytes 2506760 | tf_op jit(solution)/shard_map/ppermute | solution.py:1289
  66.0 15.1 %collective-permute-start.15 = (bf16[2,272,768]{2,1,0:T(8,128)(2,1)S(1)}, bf16[2,272,768]{2,1,0:T(8,128)(2,1)S(1)}, u32[]{:S(2)}, u32[]{:S(2)}) collective-permute-start(bf16[2,272,768]{2,1,0:T(8,128)(2,1)S(1)} %collective-permute-done.14.rest_12_.rest_3_), channel_id=1, source_target_pairs={{0,4},{1,3},{4,8},{5,1},{8,12},{9,5},{12,14},{13,9},{14,10},{15,13... | collective-permute-start | bytes 2506760 | tf_op jit(solution)/shard_map/ppermute | solution.py:1289
  68.1 19.6 %collective-permute-start.11 = (bf16[2,192,768]{2,1,0:T(8,128)(2,1)}, bf16[2,192,768]{2,1,0:T(8,128)(2,1)}, u32[]{:S(2)}, u32[]{:S(2)}) collective-permute-start(bf16[2,192,768]{2,1,0:T(8,128)(2,1)} %collective-permute-done.10.rest_10_.rest_19_), channel_id=1, source_target_pairs={{0,4},{1,3},{4,8},{5,1},{8,12},{9,5},{12,14},{13,9},{14,10},{15,13... | collective-permute-start | bytes 1769480 | tf_op jit(solution)/shard_map/ppermute | solution.py:1289
  69.6 32.1 %collective-permute-start.17 = (bf16[2,272,768]{2,1,0:T(8,128)(2,1)S(1)}, bf16[2,272,768]{2,1,0:T(8,128)(2,1)}, u32[]{:S(2)}, u32[]{:S(2)}) collective-permute-start(bf16[2,272,768]{2,1,0:T(8,128)(2,1)S(1)} %collective-permute-done.13.rest_10_.rest_1_), channel_id=1, source_target_pairs={{0,1},{1,0},{4,5},{5,4},{8,9},{9,8},{12,13},{13,12},{14,15},{15,14... | collective-permute-start | bytes 2506760 | tf_op jit(solution)/shard_map/ppermute | solution.py:1290
  69.6 32.7 %collective-permute-start.18 = (bf16[2,272,768]{2,1,0:T(8,128)(2,1)S(1)}, bf16[2,272,768]{2,1,0:T(8,128)(2,1)}, u32[]{:S(2)}, u32[]{:S(2)}) collective-permute-start(bf16[2,272,768]{2,1,0:T(8,128)(2,1)S(1)} %collective-permute-done.14.rest_12_.rest_3_), channel_id=1, source_target_pairs={{0,1},{1,0},{4,5},{5,4},{8,9},{9,8},{12,13},{13,12},{14,15},{15,14... | collective-permute-start | bytes 2506760 | tf_op jit(solution)/shard_map/ppermute | solution.py:1290
  70.2 31.6 %all-to-all-start = ((bf16[16,16,768]{2,1,0:T(8,128)(2,1)}), bf16[16,16,768]{2,1,0:T(8,128)(2,1)S(1)}, u32[]{:S(2)}, u32[]{:S(2)}) async-start(bf16[16,16,768]{2,1,0:T(8,128)(2,1)} %get-tuple-element.90), calls=%async_computation | async-start | bytes 786432 | tf_op jit(solution)/shard_map/all_to_all | solution.py:1338
  81.1 14.2 %collective-permute-start.20 = (bf16[272,768]{1,0:T(8,128)(2,1)S(1)}, bf16[272,768]{1,0:T(8,128)(2,1)}, u32[]{:S(2)}, u32[]{:S(2)}) collective-permute-start(bf16[272,768]{1,0:T(8,128)(2,1)S(1)} %fusion), channel_id=1, source_target_pairs={{0,4},{1,3},{4,8},{5,1},{8,12},{9,5},{12,14},{13,9},{14,10},{15,13... | collective-permute-start | bytes 1253384 | tf_op jit(solution)/shard_map/ppermute | solution.py:1289
  84.0 22.0 %collective-permute-start.19 = (bf16[2,272,768]{2,1,0:T(8,128)(2,1)S(1)}, bf16[2,272,768]{2,1,0:T(8,128)(2,1)}, u32[]{:S(2)}, u32[]{:S(2)}) collective-permute-start(bf16[2,272,768]{2,1,0:T(8,128)(2,1)S(1)} %collective-permute-done.15.rest_14_.rest_5_), channel_id=1, source_target_pairs={{0,1},{1,0},{4,5},{5,4},{8,9},{9,8},{12,13},{13,12},{14,15},{15,14... | collective-permute-start | bytes 2506760 | tf_op jit(solution)/shard_map/ppermute | solution.py:1290
  87.7 14.0 %collective-permute-start.16 = (bf16[2,192,768]{2,1,0:T(8,128)(2,1)}, bf16[2,192,768]{2,1,0:T(8,128)(2,1)S(1)}, u32[]{:S(2)}, u32[]{:S(2)}) collective-permute-start(bf16[2,192,768]{2,1,0:T(8,128)(2,1)} %collective-permute-done.11.rest_12_.rest_21_), channel_id=1, source_target_pairs={{0,4},{1,3},{4,8},{5,1},{8,12},{9,5},{12,14},{13,9},{14,10},{15,13... | collective-permute-start | bytes 1769480 | tf_op jit(solution)/shard_map/ppermute | solution.py:1289
  95.3 10.7 %collective-permute-start.21 = (bf16[272,768]{1,0:T(8,128)(2,1)}, bf16[272,768]{1,0:T(8,128)(2,1)}, u32[]{:S(2)}, u32[]{:S(2)}) collective-permute-start(bf16[272,768]{1,0:T(8,128)(2,1)} %collective-permute-done.20.rest_16_.rest_7_), channel_id=1, source_target_pairs={{0,1},{1,0},{4,5},{5,4},{8,9},{9,8},{12,13},{13,12},{14,15},{15,14... | collective-permute-start | bytes 1253384 | tf_op jit(solution)/shard_map/ppermute | solution.py:1290
  101.7 18.2 %collective-permute-start.22 = (bf16[2,192,768]{2,1,0:T(8,128)(2,1)}, bf16[2,192,768]{2,1,0:T(8,128)(2,1)}, u32[]{:S(2)}, u32[]{:S(2)}) collective-permute-start(bf16[2,192,768]{2,1,0:T(8,128)(2,1)} %collective-permute-done.10.rest_10_.rest_19_), channel_id=1, source_target_pairs={{0,1},{1,0},{4,5},{5,4},{8,9},{9,8},{12,13},{13,12},{14,15},{15,14... | collective-permute-start | bytes 1769480 | tf_op jit(solution)/shard_map/ppermute | solution.py:1290
  101.8 18.1 %collective-permute-start.23 = (bf16[2,192,768]{2,1,0:T(8,128)(2,1)}, bf16[2,192,768]{2,1,0:T(8,128)(2,1)S(1)}, u32[]{:S(2)}, u32[]{:S(2)}) collective-permute-start(bf16[2,192,768]{2,1,0:T(8,128)(2,1)} %collective-permute-done.11.rest_12_.rest_21_), channel_id=1, source_target_pairs={{0,1},{1,0},{4,5},{5,4},{8,9},{9,8},{12,13},{13,12},{14,15},{15,14... | collective-permute-start | bytes 1769480 | tf_op jit(solution)/shard_map/ppermute | solution.py:1290
  102.4 16.9 %collective-permute-start.25 = (bf16[192,768]{1,0:T(8,128)(2,1)S(1)}, bf16[192,768]{1,0:T(8,128)(2,1)}, u32[]{:S(2)}, u32[]{:S(2)}) collective-permute-start(bf16[192,768]{1,0:T(8,128)(2,1)S(1)} %fusion.1), channel_id=1, source_target_pairs={{0,4},{1,3},{4,8},{5,1},{8,12},{9,5},{12,14},{13,9},{14,10},{15,13... | collective-permute-start | bytes 884744 | tf_op jit(solution)/shard_map/ppermute | solution.py:1289
  106.0 13.9 %collective-permute-start.24 = (bf16[2,192,768]{2,1,0:T(8,128)(2,1)S(1)}, bf16[2,192,768]{2,1,0:T(8,128)(2,1)}, u32[]{:S(2)}, u32[]{:S(2)}) collective-permute-start(bf16[2,192,768]{2,1,0:T(8,128)(2,1)S(1)} %collective-permute-done.16.rest_14_.rest_23_), channel_id=1, source_target_pairs={{0,1},{1,0},{4,5},{5,4},{8,9},{9,8},{12,13},{13,12},{14,15},{15,14... | collective-permute-start | bytes 1769480 | tf_op jit(solution)/shard_map/ppermute | solution.py:1290
  149.7 21.6 %all-to-all-start.1 = ((bf16[16,160,128]{2,1,0:T(8,128)(2,1)}), bf16[16,160,128]{2,1,0:T(8,128)(2,1)S(1)}, u32[]{:S(2)}, u32[]{:S(2)}) async-start(bf16[16,160,128]{2,1,0:T(8,128)(2,1)} %bitcast.58), calls=%async_computation.1 | async-start | bytes 1310720 | tf_op jit(solution)/shard_map/all_to_all | solution.py:1358
  (24 other events, 292.0 us)

commit v3 on v2

--- a/solution.py
+++ b/solution.py
@@ -359,7 +359,7 @@
         in_specs=[spec for spec, _ in ins],
         out_specs=[spec for spec, _, _ in outs],
         scratch_shapes=scratch,
-        compiler_params=pltpu.CompilerParams(vmem_limit_bytes=60 * 1024 * 1024),
+        compiler_params=pltpu.CompilerParams(vmem_limit_bytes=67043328),
         cost_estimate=pl.CostEstimate(flops=flops, bytes_accessed=touched, transcendentals=0),
     )(*[item for _, item in ins])
 
@@ -546,9 +546,39 @@
     )[0]
 
 
-def attend_kernel(lengths, tok, *rest):
-    first, (keys_hbm, values_hbm, norm_hbm, mixed, vec, pooled), scratch = rest[:9], rest[9:15], rest[15:]
-    weights, small, normed, keys, values, norm_low, qf, kf, vf, mf, sems, outs = scratch
+def sample_limits(here):
+    lane_sample = lax.broadcasted_iota(jnp.int32, (1, 128), 1) % 8
+    limit = jnp.zeros((1, 128), jnp.int32)
+    for s in range(8):
+        limit = jnp.where(lane_sample == s, here.length(s), limit)
+    return limit
+
+
+def own_heads(tall, width):
+    heads = lax.broadcasted_iota(jnp.int32, (8, width), 1) // HD
+    total = jnp.zeros((8, width), F32)
+    for head in range(width // HD):
+        total = total + jnp.where(heads == head, tall[head * 8 : head * 8 + 8], 0.0)
+    if width < DI:
+        total = jnp.concatenate([total, jnp.zeros((8, DI - width), F32)], axis=1)
+    return total
+
+
+def tall_rows(rows):
+    return jnp.concatenate([rows[:, i * 128 : (i + 1) * 128] for i in range(DI // 128)], axis=0)
+
+
+def wide_rows(tall):
+    tall = tall.astype(F32)
+    return jnp.concatenate(
+        [tall[:, i * 8 : i * 8 + 8, :].reshape(N, 128) for i in range(DI // 128)], axis=1
+    )
+
+
+def pooled_kernel(lengths, tok, *rest):
+    first, outs, scratch = rest[:9], rest[9:18], rest[18:]
+    keys_hbm, values_hbm, norm_hbm, normed_hbm, vec, pooled, q_own, probs_out, gv_out = outs
+    weights, small, normed, keys, values, norm_low, sems, ends = scratch
     here = Place(lengths)
     owners = owner_table(here.dp)
     fetch(owners, first, 160, 16, small, sems.at[0])
@@ -556,6 +586,13 @@
     keep, winv = here.keep, here.winv
     drain(small, sems.at[0])
     vec[...] = jnp.sum(small[...].astype(F32), axis=0)
+    limit = sample_limits(here)
+    sub = lax.broadcasted_iota(jnp.int32, (8, DI), 0)
+    picked = jnp.zeros((8, DI), F32)
+    for s in range(8):
+        picked = jnp.where(sub == s, tok[here.pool(s)].astype(F32), picked)
+    pooled_norm, _ = normalize(picked, keep, winv)
+    pooled_normed = (pooled_norm * vec[0:1, :] + vec[1:2, :]).astype(BF16)
 
     def norm_chunk(position, row, count):
         x = tok[pl.ds(position, count)].astype(F32).reshape(count * 8, DI)
@@ -565,33 +602,107 @@
 
     def path(width, count):
         rows = count * 8
-        span = 80 if count == 77 else count
         chunks(count, norm_chunk)
-        if span > count:
-            for dst in (qf, kf, vf):
-                dst[:, rows : span * 8, :] = jnp.zeros((6, span * 8 - rows, 128), F32)
+        saved = [copy(norm_low, norm_hbm, ends.at[0]), copy(normed, normed_hbm, ends.at[1])]
         drain(weights, sems.at[1])
-        for third, dst, low, bias in ((0, qf, None, 2), (1, kf, keys, None), (2, vf, values, 3)):
+        for third, low, bias in ((1, keys, None), (2, values, 3)):
 
             @pl.loop(0, width // 256)
-            def _(j, third=third, dst=dst, low=low, bias=bias):
+            def _(j, third=third, low=low, bias=bias):
                 lanes = pl.ds(aligned(j * 256, 256), 256)
                 weight = weights[:, third * 48 : third * 48 + 48, lanes].reshape(DI, 256)
                 prod = dot(normed[0:rows, 0:width], weight[0:width])
                 if bias is not None:
                     prod = prod + vec[bias : bias + 1, lanes]
-                if third == 0:
-                    prod = prod.astype(BF16).astype(F32) * SCALE
-                dst[2 * j, 0:rows, :] = prod[:, 0:128]
-                dst[2 * j + 1, 0:rows, :] = prod[:, 128:256]
-                if low is not None:
-                    low[0:rows, lanes] = prod.astype(BF16)
-
-        saved = [
-            copy(keys, keys_hbm, outs.at[0]),
-            copy(values, values_hbm, outs.at[1]),
-            copy(norm_low, norm_hbm, outs.at[2]),
-        ]
+                low[0:rows, lanes] = prod.astype(BF16)
+
+        saved += [copy(keys, keys_hbm, ends.at[2]), copy(values, values_hbm, ends.at[3])]
+        query = dot(pooled_normed, weights[:, 0:48, :].reshape(DI, DI)) + vec[2:3, :]
+        query = query.astype(BF16).astype(F32)
+        q_own[...] = query
+        q_rows = head_rows(query)
+        raw = dot(keys[0:rows, 0:width], q_rows[:, 0:width], 1, 1) * SCALE
+        row = lax.broadcasted_iota(jnp.int32, (rows, 128), 0)
+        lane = lax.broadcasted_iota(jnp.int32, (rows, 128), 1)
+        valid = (lane % 8 == row % 8) & (row // 8 < limit) & (lane < width // 8)
+        raw = jnp.where(valid, raw, NEG_FILL)
+        terms = jnp.where(valid, jnp.exp(raw - jnp.max(raw, axis=0, keepdims=True)), 0.0)
+        probs = terms / jnp.maximum(row_sum(terms), 1e-30)
+        low_probs = probs.astype(BF16)
+        probs_out[0:rows, :] = probs
+        gv_out[0:rows, :] = low_probs
+        mixed = own_heads(dot(low_probs, values[0:rows, 0:width], 0, 0), width)
+        tall = tall_rows(mixed).astype(BF16)
+        for owner in range(ITEMS):
+            pooled[owner] = tall
+        for item in saved:
+            item.wait()
+
+    here.either(path, 56)
+
+
+def attend_pooled(lengths, tok, first):
+    rows = tok.shape[0] * tok.shape[1]
+    return call(
+        pooled_kernel,
+        "attend_pooled",
+        [(SMEM, lengths), (VMEM, tok)] + [(ANY, r) for r in first],
+        [(ANY, (rows, DI), BF16)] * 4
+        + [
+            (VMEM, (16, DI), F32),
+            (VMEM, (ITEMS, 48, 128), BF16),
+            (VMEM, (8, DI), F32),
+            (VMEM, (rows, 128), F32),
+            (VMEM, (rows, 128), BF16),
+        ],
+        [
+            pltpu.VMEM((ITEMS, 144, DI), BF16),
+            pltpu.VMEM((ITEMS, 16, DI), BF16),
+            pltpu.VMEM((rows, DI), BF16),
+            pltpu.VMEM((rows, DI), BF16),
+            pltpu.VMEM((rows, DI), BF16),
+            pltpu.VMEM((rows, DI), BF16),
+            pltpu.SemaphoreType.DMA((2,)),
+            pltpu.SemaphoreType.DMA((4,)),
+        ],
+        flops=7_000_000_000,
+        touched=10_000_000,
+    )
+
+
+def attend_kernel(lengths, vec, gv, normed_hbm, keys_hbm, values_hbm, norm_hbm, *rest):
+    first, (mixed, z_value), scratch = rest[:9], rest[9:11], rest[11:]
+    weights, normed, keys, values, norm_low, qf, kf, vf, mf, sems = scratch
+    here = Place(lengths)
+    owners = owner_table(here.dp)
+    fetch(owners, first, 0, 48, weights, sems.at[0])
+    early = [
+        copy(src, dst, sems.at[1 + i])
+        for i, (src, dst) in enumerate(
+            ((normed_hbm, normed), (keys_hbm, keys), (values_hbm, values), (norm_hbm, norm_low))
+        )
+    ]
+    drain(weights, sems.at[0])
+    for item in early:
+        item.wait()
+
+    def path(width, count):
+        rows = count * 8
+        span = 80 if count == 77 else count
+        if span > count:
+            for dst in (qf, kf, vf):
+                dst[:, rows : span * 8, :] = jnp.zeros((6, span * 8 - rows, 128), F32)
+
+        @pl.loop(0, width // 256)
+        def _(j):
+            lanes = pl.ds(aligned(j * 256, 256), 256)
+            weight = weights[:, :, lanes].reshape(DI, 256)
+            prod = dot(normed[0:rows, 0:width], weight[0:width]) + vec[2:3, lanes]
+            prod = prod.astype(BF16).astype(F32) * SCALE
+            for dst, item in ((qf, prod), (kf, keys[0:rows, lanes].astype(F32)), (vf, values[0:rows, lanes].astype(F32))):
+                dst[2 * j, 0:rows, :] = item[:, 0:128]
+                dst[2 * j + 1, 0:rows, :] = item[:, 128:256]
+
         key_pos = lax.broadcasted_iota(jnp.int32, (span, 2 * span), 0)
         query_pos = lax.broadcasted_iota(jnp.int32, (span, 2 * span), 1) % span
         low_half = lax.broadcasted_iota(jnp.int32, (span, 128), 1) < HD
@@ -620,39 +731,22 @@
 
         for i in range(width // 128):
             mixed[0:rows, 128 * i : 128 * i + 128] = mf[i, 0:rows, :].astype(BF16)
-        for item in saved:
-            item.wait()
+        z_value[...] = dot(norm_low[0:rows, :], gv[0:rows, :], 0, 0).astype(BF16)
 
     here.either(path, 56)
-    row_id = lax.broadcasted_iota(jnp.int32, (8, DI), 0)
-    picked = jnp.zeros((8, DI), F32)
-    for s in range(8):
-        at = pl.ds(aligned(here.pool(s) * 8, 8), 8)
-        block = jnp.concatenate([mf[i, at, :] for i in range(6)], axis=1)
-        picked = jnp.where(row_id == s, block, picked)
-    tall = jnp.concatenate([jnp.where(keep > 0.0, picked, 0.0), jnp.zeros((8, DI), F32)], axis=0)
-    for owner in range(ITEMS):
-        pooled[owner] = tall.astype(BF16)
-
-
-def attend(lengths, tok, first):
-    rows = tok.shape[0] * tok.shape[1]
-    high = (tok.shape[0] + 3) * tok.shape[1]
+
+
+def attend(lengths, vec, gv, normed, keys, values, norm_low, first):
+    rows = keys.shape[0]
+    high = rows + 24
     return call(
         attend_kernel,
         "attend",
-        [(SMEM, lengths), (VMEM, tok)] + [(ANY, r) for r in first],
+        [(SMEM, lengths), (VMEM, vec), (VMEM, gv)]
+        + [(ANY, r) for r in (normed, keys, values, norm_low, *first)],
+        [(VMEM, (rows, DI), BF16), (VMEM, (DI, 128), BF16)],
         [
-            (ANY, (rows, DI), BF16),
-            (ANY, (rows, DI), BF16),
-            (ANY, (rows, DI), BF16),
-            (VMEM, (rows, DI), BF16),
-            (VMEM, (16, DI), F32),
-            (VMEM, (ITEMS, 16, DI), BF16),
-        ],
-        [
-            pltpu.VMEM((ITEMS, 144, DI), BF16),
-            pltpu.VMEM((ITEMS, 16, DI), BF16),
+            pltpu.VMEM((ITEMS, 48, DI), BF16),
             pltpu.VMEM((rows, DI), BF16),
             pltpu.VMEM((rows, DI), BF16),
             pltpu.VMEM((rows, DI), BF16),
@@ -661,161 +755,47 @@
             pltpu.VMEM((6, high, 128), F32),
             pltpu.VMEM((6, high, 128), F32),
             pltpu.VMEM((6, high, 128), F32),
-            pltpu.SemaphoreType.DMA((2,)),
-            pltpu.SemaphoreType.DMA((3,)),
+            pltpu.SemaphoreType.DMA((5,)),
         ],
-        flops=12_000_000_000,
-        touched=14_000_000,
-    )
-
-
-def widen_kernel(lengths, tok, vec, mixed_hbm, *rest):
-    first, second, mixes = rest[:9], rest[9:18], rest[18]
-    outs, scratch = rest[19:31], rest[31:]
-    (act_hbm, middle_hbm, mid_out, norm2_out, inv2_out, slope_out, act_p, q_out, q_own, n2_sl, mix_sl,
-     norm_sl) = outs
-    w_q, w_out, w_fc, xs, ms, mix, n2_all, norm1_all, middle, act, sems = scratch
+        flops=9_000_000_000,
+        touched=10_000_000,
+    )
+
+
+def forward_kernel(lengths, vec, mixes, *rest):
+    first, second, down = rest[:9], rest[9:18], rest[18:27]
+    outs, scratch = rest[27:38], rest[38:]
+    (e_out, proj_out, normf_out, invf_out, norm2_out, inv2_out, slope_out, n2_sl, mix_sl, head_sl,
+     act_sl) = outs
+    w_out, w_fc, w_down, w_emb, xs, mix, n2, act, head_all, sems = scratch
     here = Place(lengths)
     owners = owner_table(here.dp)
-    rows_all = mixed_hbm.shape[0]
-    fetch(owners, second, 0, 48, w_out, sems.at[2])
-    pooled_in = copy(mixes, ms, sems.at[1])
-    full = copy(mixed_hbm, mix.at[pl.ds(N, rows_all), :], sems.at[5])
+    fetch(owners, second, 0, 48, w_out, sems.at[1])
     fetch(owners, first, 144, 16, xs, sems.at[0])
-    fetch(owners, second, 80, 192, w_fc, sems.at[3])
-    fetch(owners, first, 0, 48, w_q, sems.at[4])
+    fetch(owners, second, 80, 192, w_fc, sems.at[2])
     keep, winv = here.keep, here.winv
-    drain(w_out, sems.at[2])
-    pooled_in.wait()
-    mix[0:N, :] = ms[...].astype(F32)[:, :8, :].reshape(N, DI).astype(BF16)
-    full.wait()
-
-    def norm_chunk(position, row, count):
-        at = pl.ds(N + row, count * 8)
-        total = middle[at, :] + tok[pl.ds(position, count)].astype(F32).reshape(count * 8, DI)
-        middle[at, :] = total
-        norm, _ = normalize(total, keep, winv)
-        n2_all[at, :] = (norm * vec[5:6, :] + vec[6:7, :]).astype(BF16)
-
-    def path(width, count):
-        rows = N + count * 8
-        norm_rows = N + (count if width == DT else 56) * 8
-
-        @pl.loop(0, width // 256)
-        def _(j):
-            lanes = pl.ds(aligned(j * 256, 256), 256)
-            weight = w_out[:, :, lanes].reshape(DI, 256)[0:width]
-            middle[0:norm_rows, lanes] = dot(mix[0:norm_rows, 0:width], weight) + vec[4:5, lanes]
-
-        if width < DI:
-            middle[0:norm_rows, width:DI] = jnp.zeros((norm_rows, DI - width), F32)
-        chunks(count if width == DT else 56, norm_chunk)
-        saved = copy(middle.at[pl.ds(N, rows_all), :], middle_hbm, sems.at[7])
-        drain(xs, sems.at[0])
-        stream = xs[...].astype(F32)[:, :8, :].reshape(N, DI)
-        pooled = stream + middle[0:N, :]
-        mid_out[...] = pooled
-        norm2, inv2 = normalize(pooled, keep, winv)
-        n2_all[0:N, :] = (norm2 * vec[5:6, :] + vec[6:7, :]).astype(BF16)
-        norm2_out[...] = norm2
-        inv2_out[...] = jnp.broadcast_to(inv2, (N, 128))
-        norm1, _ = normalize(stream, keep, winv)
-        norm1_all[...] = norm1.astype(BF16)
-        drain(w_fc, sems.at[3])
-        for block in range(4):
-
-            @pl.loop(0, 3 if width == DI else (3, 3, 2, 0)[block])
-            def _(j, block=block):
-                lanes = pl.ds(aligned(j * 256, 256), 256)
-                wide = pl.ds(aligned(block * DI + j * 256, 256), 256)
-                weight = w_fc[:, block * 48 : block * 48 + 48, lanes].reshape(DI, 256)[0:width]
-                pre = dot(n2_all[0:rows, 0:width], weight) + vec[10 + block : 11 + block, lanes]
-                gate = jax.nn.sigmoid(GELU_K * pre)
-                low = (pre * gate).astype(BF16)
-                act_p[:, wide] = low[0:N]
-                act[0 : rows - N, wide] = low[N:rows]
-                pre, gate = pre[0:N], gate[0:N]
-                slope_out[:, wide] = gate + GELU_K * pre * gate * (1.0 - gate)
-                copy(act.at[pl.ds(0, rows - N), wide], act_hbm.at[pl.ds(0, rows - N), wide], sems.at[6])
-
-        if width < DI:
-            act_p[:, 4 * width : 4 * DI] = jnp.zeros((N, 4 * DI - 4 * width), BF16)
-            slope_out[:, 4 * width : 4 * DI] = jnp.zeros((N, 4 * DI - 4 * width), F32)
-        drain(w_q, sems.at[4])
-        n1 = (norm1 * vec[0:1, :] + vec[1:2, :]).astype(BF16)
-        q_out[...] = (dot(n1, w_q[...].reshape(DI, DI)) + vec[2:3, :]).astype(BF16).astype(F32)
-        q_own[...] = q_out[pl.ds(aligned(here.dp * 8, 8), 8), :]
-        drain(act.at[pl.ds(0, rows - N), pl.ds(0, 4 * width)], sems.at[6])
-        saved.wait()
-
-    here.either(path, 50)
-
-    def mine(owner):
-        lanes = slice(owner * 48, owner * 48 + 48)
-        n2_sl[...] = n2_all[0:N, lanes]
-        mix_sl[...] = mix[0:N, lanes]
-        norm_sl[...] = norm1_all[:, lanes]
-
-    here.mine(mine)
-
-
-def widen(lengths, tok, vec, mixed, first, second, mixes):
-    rows = mixed.shape[0]
-    return call(
-        widen_kernel,
-        "widen",
-        [(SMEM, lengths), (VMEM, tok), (VMEM, vec), (ANY, mixed)]
-        + [(ANY, r) for r in (*first, *second, mixes)],
-        [
-            (ANY, (rows, 4 * DI), BF16),
-            (ANY, (rows, DI), F32),
-            (VMEM, (N, DI), F32),
-            (VMEM, (N, DI), F32),
-            (VMEM, (N, 128), F32),
-            (VMEM, (N, 4 * DI), F32),
-            (VMEM, (N, 4 * DI), BF16),
-            (VMEM, (N, DI), F32),
-            (VMEM, (8, DI), F32),
-            (VMEM, (N, 48), BF16),
-            (VMEM, (N, 48), BF16),
-            (VMEM, (N, 48), BF16),
-        ],
-        [
-            pltpu.VMEM((ITEMS, 48, DI), BF16),
-            pltpu.VMEM((ITEMS, 48, DI), BF16),
-            pltpu.VMEM((ITEMS, 192, DI), BF16),
-            pltpu.VMEM((ITEMS, 16, DI), BF16),
-            pltpu.VMEM((ITEMS, 16, DI), BF16),
-            pltpu.VMEM((N + rows, DI), BF16),
-            pltpu.VMEM((N + rows, DI), BF16),
-            pltpu.VMEM((N, DI), BF16),
-            pltpu.VMEM((N + rows, DI), F32),
-            pltpu.VMEM((rows, 4 * DI), BF16),
-            pltpu.SemaphoreType.DMA((8,)),
-        ],
-        flops=13_000_000_000,
-        touched=14_000_000,
-    )
-
-
-def head_kernel(lengths, vec, middle_hbm, act_hbm, *rest):
-    second, down, outs, scratch = rest[:9], rest[9:18], rest[18:24], rest[24:]
-    e_out, proj_out, normf_out, invf_out, head_sl, act_sl = outs
-    w_down, w_emb, head_all, middle, act, sems = scratch
-    here = Place(lengths)
-    owners = owner_table(here.dp)
-    early = [copy(act_hbm, act, sems.at[5]), copy(middle_hbm, middle, sems.at[6])]
-    for owner, ref in zip(owners, down):
-        dst = w_down.at[pl.ds(owner, 2)] if len(ref.shape) == 3 else w_down.at[owner]
-        copy(ref, dst, sems.at[owner // 4])
+    mix[...] = wide_rows(mixes[...]).astype(BF16)
+    drain(w_out, sems.at[1])
+    drain(xs, sems.at[0])
+    fetch(owners, down, 0, 192, w_down, sems.at[3])
     fetch(owners, second, 48, 32, w_emb, sems.at[4])
-    keep, winv = here.keep, here.winv
-    for item in early:
-        item.wait()
-    last = middle[...] + vec[7:8, :]
-    for part in range(4):
-        drain(w_down.at[pl.ds(part * 4, 4)], sems.at[part])
-        last = last + dot(act[:, part * DI : part * DI + DI], w_down[part * 4 : part * 4 + 4].reshape(DI, DI))
+    stream = xs[...].astype(F32)[:, :8, :].reshape(N, DI)
+    middle = stream + dot(mix[...], w_out[...].reshape(DI, DI)) + vec[4:5, :]
+    norm2, inv2 = normalize(middle, keep, winv)
+    n2[...] = (norm2 * vec[5:6, :] + vec[6:7, :]).astype(BF16)
+    norm2_out[...] = norm2
+    inv2_out[...] = jnp.broadcast_to(inv2, (N, 128))
+    drain(w_fc, sems.at[2])
+    for block in range(4):
+        lanes = pl.ds(block * DI, DI)
+        weight = w_fc[:, block * 48 : block * 48 + 48, :].reshape(DI, DI)
+        pre = dot(n2[...], weight) + vec[10 + block : 11 + block, :]
+        gate = jax.nn.sigmoid(GELU_K * pre)
+        act[:, lanes] = (pre * gate).astype(BF16)
+        slope_out[:, lanes] = gate + GELU_K * pre * gate * (1.0 - gate)
+
+    drain(w_down, sems.at[3])
+    last = middle + dot(act[...], w_down[...].reshape(4 * DI, DI)) + vec[7:8, :]
     normf, invf = normalize(last, keep, winv)
     normf_out[...] = normf
     invf_out[...] = jnp.broadcast_to(invf, (N, 128))
@@ -827,34 +807,107 @@
     e_out[...] = (proj * scale).astype(BF16)
 
     def mine(owner):
-        head_sl[...] = head_all[:, owner * 48 : owner * 48 + 48]
+        lanes = slice(owner * 48, owner * 48 + 48)
+        n2_sl[...] = n2[:, lanes]
+        mix_sl[...] = mix[:, lanes]
+        head_sl[...] = head_all[:, lanes]
         act_sl[...] = act[:, owner * 192 : owner * 192 + 192]
 
     here.mine(mine)
 
 
-def pooled_head(lengths, vec, middle, act, second, down):
+def pooled_forward(lengths, vec, mixes, first, second, down):
     return call(
-        head_kernel,
-        "pooled_head",
-        [(SMEM, lengths), (VMEM, vec), (ANY, middle), (ANY, act)] + [(ANY, r) for r in (*second, *down)],
+        forward_kernel,
+        "pooled_forward",
+        [(SMEM, lengths), (VMEM, vec), (VMEM, mixes)] + [(ANY, r) for r in (*first, *second, *down)],
         [
             (VMEM, (N, EMB), BF16),
             (VMEM, (N, EMB), F32),
             (VMEM, (N, DI), F32),
             (VMEM, (N, 128), F32),
+            (VMEM, (N, DI), F32),
+            (VMEM, (N, 128), F32),
+            (VMEM, (N, 4 * DI), F32),
+            (VMEM, (N, 48), BF16),
+            (VMEM, (N, 48), BF16),
             (VMEM, (N, 48), BF16),
             (VMEM, (N, 192), BF16),
         ],
         [
+            pltpu.VMEM((ITEMS, 48, DI), BF16),
+            pltpu.VMEM((ITEMS, 192, DI), BF16),
             pltpu.VMEM((ITEMS, 192, DI), BF16),
             pltpu.VMEM((ITEMS, 32, DI), BF16),
+            pltpu.VMEM((ITEMS, 16, DI), BF16),
             pltpu.VMEM((N, DI), BF16),
-            pltpu.VMEM((N, DI), F32),
+            pltpu.VMEM((N, DI), BF16),
             pltpu.VMEM((N, 4 * DI), BF16),
-            pltpu.SemaphoreType.DMA((7,)),
+            pltpu.VMEM((N, DI), BF16),
+            pltpu.SemaphoreType.DMA((5,)),
         ],
-        flops=6_000_000_000,
+        flops=11_000_000_000,
+        touched=16_000_000,
+    )
+
+
+def middle_kernel(lengths, tok_hbm, vec, mixed_hbm, *rest):
+    second = rest[:9]
+    (n2_hbm, middle_hbm), scratch = rest[9:11], rest[11:]
+    w_out, middle, tok, mixed, n2, sems = scratch
+    here = Place(lengths)
+    owners = owner_table(here.dp)
+    rows_in = copy(mixed_hbm, mixed, sems.at[1])
+    fetch(owners, second, 0, 48, w_out, sems.at[0])
+    tok_in = copy(tok_hbm, tok, sems.at[2])
+    keep, winv = here.keep, here.winv
+    rows_in.wait()
+    drain(w_out, sems.at[0])
+
+    def norm_chunk(position, row, count):
+        at = pl.ds(row, count * 8)
+        total = middle[at, :] + tok[pl.ds(position, count)].astype(F32).reshape(count * 8, DI)
+        middle[at, :] = total
+        norm, _ = normalize(total, keep, winv)
+        n2[at, :] = (norm * vec[5:6, :] + vec[6:7, :]).astype(BF16)
+        copy(middle.at[at, :], middle_hbm.at[at, :], sems.at[3])
+        copy(n2.at[at, :], n2_hbm.at[at, :], sems.at[4])
+
+    def path(width, count):
+        rows = count * 8
+
+        @pl.loop(0, width // 256)
+        def _(j):
+            lanes = pl.ds(aligned(j * 256, 256), 256)
+            weight = w_out[:, :, lanes].reshape(DI, 256)[0:width]
+            middle[0:rows, lanes] = dot(mixed[0:rows, 0:width], weight) + vec[4:5, lanes]
+
+        if width < DI:
+            middle[0:rows, width:DI] = jnp.zeros((rows, DI - width), F32)
+        tok_in.wait()
+        chunks(count, norm_chunk)
+        drain(middle.at[pl.ds(0, rows), :], sems.at[3])
+        drain(n2.at[pl.ds(0, rows), :], sems.at[4])
+
+    here.either(path, 56)
+
+
+def middle_part(lengths, tok, vec, mixed, second):
+    rows = mixed.shape[0]
+    return call(
+        middle_kernel,
+        "middle_part",
+        [(SMEM, lengths), (ANY, tok), (VMEM, vec), (ANY, mixed)] + [(ANY, r) for r in second],
+        [(ANY, (rows, DI), BF16), (ANY, (rows, DI), F32)],
+        [
+            pltpu.VMEM((ITEMS, 48, DI), BF16),
+            pltpu.VMEM((rows, DI), F32),
+            pltpu.VMEM(tok.shape, BF16),
+            pltpu.VMEM((rows, DI), BF16),
+            pltpu.VMEM((rows, DI), BF16),
+            pltpu.SemaphoreType.DMA((5,)),
+        ],
+        flops=5_000_000_000,
         touched=8_000_000,
     )
 
@@ -875,16 +928,15 @@
     return lost, scale, mult * grad
 
 
-def chain_kernel(lengths, log_mult, e_own_ref, e_oth_ref, vec, q_own, head_sl, act_sl, n2_sl, mix_sl, *rest):
-    (proj_hbm, normf_hbm, invf_hbm, norm2_hbm, inv2_hbm, slope_hbm, keys_hbm, values_hbm, norm_hbm), rest = (
-        rest[:9], rest[9:]
-    )
+def chain_kernel(lengths, log_mult, e_own_ref, e_oth_ref, vec, head_sl, act_sl, n2_sl, mix_sl, *rest):
+    (proj_hbm, normf_hbm, invf_hbm, norm2_hbm, inv2_hbm, slope_hbm, keys_hbm, values_hbm, norm_hbm, probs_hbm,
+     gv_hbm, z_hbm), rest = rest[:12], rest[12:]
     second, down = rest[:9], rest[9:18]
-    outs, scratch = rest[18:38], rest[38:]
+    outs, scratch = rest[18:37], rest[37:]
     (loss_out, scale_out, d_emb_hbm, d_down_hbm, d_fc_hbm, d_out_hbm, g_final, b_final, b_down, g_two, b_two, b_out, b_fc,
-     mid_own, gm_out, gm_own, payload, gk_out, gv_out, gq_out) = outs
+     mid_own, gm_out, gm_own, payload, gk_out, gq_out) = outs
     (w_out, w_fc, w_down, w_emb, gpre, mid_all, proj_v, normf_v, invf_v, norm2_v, inv2_v, slope, keys,
-     values, norm_low, vec_grads, fcb_grads, d_emb, d_down, d_fc, d_out, sems, ins, ends) = scratch
+     values, norm_low, probs_v, gv_v, z_v, vec_grads, fcb_grads, d_emb, d_down, d_fc, d_out, sems, ins, ends) = scratch
     here = Place(lengths)
     owners = owner_table(here.dp)
     early = [
@@ -901,7 +953,10 @@
     fetch(owners, second, 0, 48, w_out, sems.at[3])
     last = [
         copy(src, dst, ins.at[6 + i])
-        for i, (src, dst) in enumerate(((keys_hbm, keys), (values_hbm, values), (norm_hbm, norm_low)))
+        for i, (src, dst) in enumerate(
+            ((keys_hbm, keys), (values_hbm, values), (norm_hbm, norm_low), (probs_hbm, probs_v),
+             (gv_hbm, gv_v), (z_hbm, z_v))
+        )
     ]
     keep, winv = here.keep, here.winv
     text = here.text.astype(F32)
@@ -919,11 +974,11 @@
     grad_e = dot(grad_own, oth_low) + dot(grad_oth, oth_low, 0, 0)
     for item in early:
         item.wait()
+    drain(w_emb, sems.at[0])
     proj = proj_v[...]
     r = lax.rsqrt(jnp.sum(proj * proj, axis=-1, keepdims=True) + NORM_EPS)
     cross = jnp.sum(grad_e * proj, axis=-1, keepdims=True)
     grad_proj = (r * grad_e - proj * (r * r * r) * cross).astype(BF16)
-    drain(w_emb, sems.at[0])
     grad_head = dot(grad_proj, embed_matrix(w_emb[...]), 1, 1)
     normf = normf_v[...]
     grad_y = normalize_back(grad_head, vec[8:9, :], normf, invf_v[:, 0:1], keep, winv)
@@ -981,41 +1036,20 @@
     here.mine(mine)
     for item in last:
         item.wait()
-    q_rows = head_rows(q_own[...])
     m_rows = head_rows(gm_own[...])
-    lane_sample = lax.broadcasted_iota(jnp.int32, (1, 128), 1) % 8
-    limit = jnp.zeros((1, 128), jnp.int32)
-    for s in range(8):
-        limit = jnp.where(lane_sample == s, here.length(s), limit)
 
     def path(width, count):
         rows = count * 8
-        raw = dot(keys[0:rows, 0:width], q_rows[:, 0:width], 1, 1) * SCALE
-        row = lax.broadcasted_iota(jnp.int32, (rows, 128), 0)
-        lane = lax.broadcasted_iota(jnp.int32, (rows, 128), 1)
-        valid = (lane % 8 == row % 8) & (row // 8 < limit) & (lane < width // 8)
-        raw = jnp.where(valid, raw, NEG_FILL)
-        top = jnp.max(raw, axis=0, keepdims=True)
-        terms = jnp.where(valid, jnp.exp(raw - top), 0.0)
-        probs = terms / jnp.maximum(row_sum(terms), 1e-30)
+        probs = probs_v[0:rows, :]
         grad_probs = dot(values[0:rows, 0:width], m_rows[:, 0:width], 1, 1)
-        crossed = row_sum(probs * grad_probs)
-        gk = (probs * (grad_probs - crossed)).astype(BF16)
-        gv = probs.astype(BF16)
+        gk = (probs * (grad_probs - row_sum(probs * grad_probs))).astype(BF16)
+        gv = gv_v[0:rows, :]
         gk_out[0:rows, :] = gk
-        gv_out[0:rows, :] = gv
-        back = dot(gk, keys[0:rows, 0:width], 0, 0) * SCALE
-        heads = lax.broadcasted_iota(jnp.int32, (8, width), 1) // HD
-        grad_q = jnp.zeros((8, width), F32)
-        for head in range(width // HD):
-            grad_q = grad_q + jnp.where(heads == head, back[head * 8 : head * 8 + 8], 0.0)
-        if width < DI:
-            grad_q = jnp.concatenate([grad_q, jnp.zeros((8, DI - width), F32)], axis=1)
-        gq_low = grad_q.astype(BF16)
+        gq_low = own_heads(dot(gk, keys[0:rows, 0:width], 0, 0) * SCALE, width).astype(BF16)
         gq_out[...] = gq_low
         norm = norm_low[0:rows, :]
         z_key = dot(norm, gk, 0, 0).astype(BF16)
-        z_value = dot(norm, gv, 0, 0).astype(BF16)
+        z_value = z_v[...]
         sum_key = row_sum(gk.astype(F32))
         sum_value = row_sum(gv.astype(F32))
         key_high = sum_key.astype(BF16).astype(F32)
@@ -1025,10 +1059,7 @@
         for at, value in enumerate((key_high, sum_key - key_high, value_high, sum_value - value_high)):
             sums = jnp.where(row_id == at, jnp.broadcast_to(value, (16, 128)), sums)
         sums = sums.astype(BF16)
-        gq_wide = gq_low.astype(F32)
-        gq_tall = jnp.concatenate(
-            [gq_wide[:, i * 128 : (i + 1) * 128] for i in range(DI // 128)], axis=0
-        ).astype(BF16)
+        gq_tall = tall_rows(gq_low.astype(F32)).astype(BF16)
         for owner in range(ITEMS):
             base = owner * PAYLOAD
             payload[base : base + 48, :] = z_key[owner * 48 : owner * 48 + 48]
@@ -1041,13 +1072,13 @@
         item.wait()
 
 
-def chain(lengths, log_mult, e_own, e_oth, vec, q_own, slices, saved, second, down):
-    rows = saved[-1].shape[0]
+def chain(lengths, log_mult, e_own, e_oth, vec, slices, saved, second, down):
+    rows = saved[-2].shape[0]
     return call(
         chain_kernel,
         "chain",
         [(SMEM, lengths), (SMEM, log_mult)]
-        + [(VMEM, item) for item in (e_own, e_oth, vec, q_own, *slices)]
+        + [(VMEM, item) for item in (e_own, e_oth, vec, *slices)]
         + [(ANY, r) for r in (*saved, *second, *down)],
         [
             (VMEM, (1, 1), F32),
@@ -1064,7 +1095,6 @@
             (VMEM, (N, DI), F32),
             (VMEM, (8, DI), F32),
             (VMEM, (ITEMS * PAYLOAD, 128), BF16),
-            (VMEM, (rows, 128), BF16),
             (VMEM, (rows, 128), BF16),
             (VMEM, (8, DI), BF16),
         ],
@@ -1084,6 +1114,9 @@
             pltpu.VMEM((rows, DI), BF16),
             pltpu.VMEM((rows, DI), BF16),
             pltpu.VMEM((rows, DI), BF16),
+            pltpu.VMEM((rows, 128), F32),
+            pltpu.VMEM((rows, 128), BF16),
+            pltpu.VMEM((DI, 128), BF16),
             pltpu.VMEM((8, DI), F32),
             pltpu.VMEM((8, 4 * DI), F32),
             pltpu.VMEM((48, EMB), F32),
@@ -1091,7 +1124,7 @@
             pltpu.VMEM((48, 4 * DI), F32),
             pltpu.VMEM((48, DI), F32),
             pltpu.SemaphoreType.DMA((4,)),
-            pltpu.SemaphoreType.DMA((9,)),
+            pltpu.SemaphoreType.DMA((12,)),
             pltpu.SemaphoreType.DMA((4,)),
         ],
         flops=15_000_000_000,
@@ -1099,14 +1132,18 @@
     )
 
 
-def close_kernel(lengths, tok, vec, gk, gv, q_own, gm_own, gq, mid_own, act_hbm, middle_hbm, *rest):
-    first, down, (block_out, out), scratch = rest[:9], rest[9:18], rest[18:20], rest[20:]
-    weights, w_down, act, middle, acc, sems = scratch
+def close_kernel(lengths, tok, vec, gk, gv, q_own, gm_own, gq, mid_own, n2_hbm, middle_hbm, *rest):
+    first, second, down = rest[:9], rest[9:18], rest[18:27]
+    (block_out, out, q_out, norm_sl), scratch = rest[27:31], rest[31:]
+    weights, w_fc, w_down, n2, act, middle, acc, xs, norm1_all, sems = scratch
     here = Place(lengths)
     owners = owner_table(here.dp)
     fetch(owners, first, 0, 144, weights, sems.at[0])
-    early = [copy(act_hbm, act, sems.at[1]), copy(middle_hbm, middle, sems.at[2])]
+    fetch(owners, first, 144, 16, xs, sems.at[5])
+    ready = copy(n2_hbm, n2, sems.at[1])
+    fetch(owners, second, 80, 192, w_fc, sems.at[4])
     fetch(owners, down, 0, 192, w_down, sems.at[3])
+    early = [copy(middle_hbm, middle, sems.at[2])]
     keep, winv = here.keep, here.winv
     q_rows = head_rows(q_own[...])
     m_rows = head_rows(gm_own[...])
@@ -1133,11 +1170,23 @@
         chunks(count, back_chunk)
         if rows < all_rows:
             out[rows:all_rows, :] = jnp.zeros((all_rows - rows, DI), F32)
+        short = count if width == DT else IMG_ROWS
+        rows = short * 8
+        ready.wait()
+        drain(w_fc, sems.at[4])
+        for block in range(4):
+
+            @pl.loop(0, 3 if width == DI else (3, 3, 2, 0)[block])
+            def _(j, block=block):
+                lanes = pl.ds(aligned(j * 256, 256), 256)
+                wide = pl.ds(aligned(block * DI + j * 256, 256), 256)
+                weight = w_fc[:, block * 48 : block * 48 + 48, lanes].reshape(DI, 256)[0:width]
+                pre = dot(n2[0:rows, 0:width], weight) + vec[10 + block : 11 + block, lanes]
+                act[0:rows, wide] = (pre * jax.nn.sigmoid(GELU_K * pre)).astype(BF16)
+
         for item in early:
             item.wait()
         drain(w_down, sems.at[3])
-        short = count if width == DT else IMG_ROWS
-        rows = short * 8
 
         @pl.loop(0, width // 256)
         def _(j):
@@ -1154,60 +1203,73 @@
             block_out[rows:all_rows, :] = jnp.zeros((all_rows - rows, DI), BF16)
 
     here.either(path, 56)
-
-
-def close(lengths, tok, vec, gk, gv, q_own, gm_own, gq, mid_own, act, middle, first, down):
+    drain(xs, sems.at[5])
+    stream = xs[...].astype(F32)[:, :8, :].reshape(N, DI)
+    norm1, _ = normalize(stream, keep, winv)
+    norm1_all[...] = norm1.astype(BF16)
+    n1 = (norm1 * vec[0:1, :] + vec[1:2, :]).astype(BF16)
+    q_out[...] = (dot(n1, weights[:, 0:48, :].reshape(DI, DI)) + vec[2:3, :]).astype(BF16).astype(F32)
+
+    def mine(owner):
+        norm_sl[...] = norm1_all[:, owner * 48 : owner * 48 + 48]
+
+    here.mine(mine)
+
+
+def close(lengths, tok, vec, gk, gv, q_own, gm_own, gq, mid_own, n2, middle, first, second, down):
     rows = tok.shape[0] * tok.shape[1]
     return call(
         close_kernel,
         "close",
         [(SMEM, lengths)]
         + [(VMEM, item) for item in (tok, vec, gk, gv, q_own, gm_own, gq, mid_own)]
-        + [(ANY, r) for r in (act, middle, *first, *down)],
-        [(VMEM, (rows, DI), BF16), (VMEM, (rows, DI), F32)],
+        + [(ANY, r) for r in (n2, middle, *first, *second, *down)],
+        [(VMEM, (rows, DI), BF16), (VMEM, (rows, DI), F32), (VMEM, (N, DI), F32), (VMEM, (N, 48), BF16)],
         [
             pltpu.VMEM((ITEMS, 144, DI), BF16),
             pltpu.VMEM((ITEMS, 192, DI), BF16),
+            pltpu.VMEM((ITEMS, 192, DI), BF16),
+            pltpu.VMEM((rows, DI), BF16),
             pltpu.VMEM((rows, 4 * DI), BF16),
             pltpu.VMEM((rows, DI), F32),
             pltpu.VMEM((rows, DI), F32),
-            pltpu.SemaphoreType.DMA((4,)),
+            pltpu.VMEM((ITEMS, 16, DI), BF16),
+            pltpu.VMEM((N, DI), BF16),
+            pltpu.SemaphoreType.DMA((6,)),
         ],
-        flops=10_000_000_000,
+        flops=17_000_000_000,
         touched=18_000_000,
     )
 
 
-def shard_kernel(got, q_all, gm_all, norm_sl, w_own, gain, bias, d_qkv, g_one, b_one, qv_out, big, left):
+def shard_kernel(got, q_all, gm_all, norm_sl, w_own, gain, bias, d_qkv, g_one, b_one, qv_out, turned, product):
     dp = lax.axis_index("dp")
 
-    def build(source):
-        @pl.loop(0, ITEMS)
-        def _(j):
-            rows = source[pl.ds(aligned(j * 8, 8), 8), :]
-            big[pl.ds(aligned(j * 128, 128), 128), :] = head_rows(rows)
-
-    def spread(start):
+    low_half = lax.broadcasted_iota(jnp.int32, (N, 128), 1) < HD
+
+    def moments(start, source):
         for j in range(ITEMS):
-            left[:, j * 128 : (j + 1) * 128] = got[j, start : start + 64, :]
+            turned[j] = got[j, start : start + 64, :].astype(F32).T
+        for pair in range(DI // 128):
+            lanes = slice(pair * 128, pair * 128 + 128)
+            rows = source[:, lanes]
+            both = [jnp.where(low_half, rows, 0.0), jnp.where(low_half, 0.0, rows)]
+            both = [half.reshape(ITEMS, 8, 128) for half in both]
+            both = jnp.concatenate(both, axis=1).reshape(2 * N, 128).astype(BF16)
+            part = turned[:, pair * 16 : pair * 16 + 16, :].reshape(2 * N, 64).astype(BF16)
+            product[:, lanes] = dot(part, both, 0, 0)
+        return product[...]
 
     def column(row):
         square = (48, 48)
         same = lax.broadcasted_iota(jnp.int32, square, 0) == lax.broadcasted_iota(jnp.int32, square, 1)
         return jnp.sum(jnp.where(same, row[...].astype(F32), 0.0), axis=1, keepdims=True)
 
-    build(q_all)
-    spread(0)
-    by_key = dot(left[...], big[...]) * SCALE
+    by_key = moments(0, q_all) * SCALE
     m_key, s_key = by_key[0:48], by_key[48:49] + by_key[49:50]
-    build(gm_all)
-    spread(48)
-    by_value = dot(left[...], big[...])
+    by_value = moments(48, gm_all)
     m_value, s_value = by_value[16:64], by_value[2:3] + by_value[3:4]
-    tall = got[:, 112:160, :].astype(F32)
-    grad_q = jnp.concatenate(
-        [tall[:, i * 8 : i * 8 + 8, :].reshape(N, 128) for i in range(DI // 128)], axis=1
-    )
+    grad_q = wide_rows(got[:, 112:160, :])
     s_query = row_sum(grad_q)
     m_query = dot(norm_sl[...], grad_q.astype(BF16), 0, 0)
     gain_col, bias_col = column(gain), column(bias)
@@ -1245,7 +1307,7 @@
             (VMEM, (1, 48), F32),
             (VMEM, (2, 48), F32),
         ],
-        [pltpu.VMEM((ITEMS * 128, DI), BF16), pltpu.VMEM((64, ITEMS * 128), BF16)],
+        [pltpu.VMEM((ITEMS, 128, 64), F32), pltpu.VMEM((64, DI), F32)],
         flops=5_000_000_000,
         touched=2_000_000,
     )
@@ -1282,15 +1344,21 @@
         self.last = held
         self.hops = 0
 
-    def step(self, *earlier, swap_after=()):
+    def step(self, *earlier, swap_after=(), later=False):
         held = self.last
         if self.hops == 3:
             held = jnp.where(self.first_core, held[0], held[1])
         held = lax.ppermute(after(held, *earlier), BOTH, self.turn)
-        self.items += [held, lax.ppermute(after(held, *swap_after), BOTH, self.swap)]
+        self.items += [held, None if later else lax.ppermute(after(held, *swap_after), BOTH, self.swap)]
         self.last = held
         self.hops += 1
         return held
+
+    def finish(self, *earlier):
+        for i, item in enumerate(self.items):
+            if item is None:
+                self.items[i] = lax.ppermute(after(self.items[i - 1], *earlier), BOTH, self.swap)
+        return self.items
 
 
 def ring_body(
@@ -1326,38 +1394,38 @@
     qkv_ring = Ring(first_own, swap, turn, first_core)
     wide_ring = Ring(second_own, swap, turn, first_core)
     down_ring = Ring(down_weight[0], swap, turn, first_core)
-    q1 = qkv_ring.step()
-    wide_ring.step(q1)
     qkv_ring.step()
-    q3 = qkv_ring.step()
+    d1 = down_ring.step()
+    qkv_ring.step()
+    q3 = qkv_ring.step(d1)
+    wide_ring.step()
     qkv_ring.step()
     first = qkv_ring.items
-    keys, values, norm_low, mixed, vec, pooled = attend(lengths, tok, first)
-    w2 = wide_ring.step(q3, swap_after=(vec,))
-    d1 = down_ring.step(q3, swap_after=(vec,))
-    mixes = lax.all_to_all(after(pooled, w2, d1), "dp", 0, 0, tiled=True)
-    w3 = wide_ring.step(vec)
-    d2 = down_ring.step(vec)
-    wide_ring.step()
-    d3 = down_ring.step(w3, swap_after=(mixes,))
+    keys, values, norm_low, normed, vec, pooled, q_own, probs, gv = attend_pooled(lengths, tok, first)
+    w2 = wide_ring.step(q3, swap_after=(q_own,))
+    d2 = down_ring.step(q3, swap_after=(q_own,))
+    mixes = lax.all_to_all(pooled, "dp", 0, 0, tiled=True)
+    w3 = wide_ring.step(q_own)
+    mixed, z_value = attend(lengths, vec, gv, after(normed, w2), keys, values, norm_low, first)
+    wide_ring.step(z_value)
+    d3 = down_ring.step(z_value, mixes)
     second = wide_ring.items
-    mixed = after(mixed, d3)
-    act, middle, mid_p, norm2, inv2, slope, act_p, q_all, q_own, n2_sl, mix_sl, norm_sl = widen(
-        lengths, tok, vec, mixed, first, second, mixes
-    )
-    down_ring.step(mixes, swap_after=(q_own,))
+    down_ring.step()
     down = down_ring.items
-    e_own, proj, normf, invf, head_sl, act_sl = pooled_head(lengths, vec, mid_p, act_p, second, down)
+    e_own, proj, normf, invf, norm2, inv2, slope, n2_sl, mix_sl, head_sl, act_sl = pooled_forward(
+        lengths, vec, mixes, first, second, down
+    )
     across = [(t * 16 + d, (1 - t) * 16 + d) for t in range(2) for d in range(16)]
     e_oth = lax.ppermute(e_own, BOTH, across)
+    n2, middle = middle_part(lengths, tok, vec, after(mixed, e_own), second)
     (loss, scale, d_emb, d_down, d_fc, d_out, g_final, b_final, b_down, g_two, b_two, b_out, b_fc,
-     mid_own, gm_all, gm_own, payload, gk, gv, gq) = chain(
-        lengths, logit_scale, e_own, e_oth, vec, q_own, (head_sl, act_sl, n2_sl, mix_sl),
-        (proj, normf, invf, norm2, inv2, slope, keys, values, norm_low), second, down,
+     mid_own, gm_all, gm_own, payload, gk, gq) = chain(
+        lengths, logit_scale, after(e_own, n2), e_oth, vec, (head_sl, act_sl, n2_sl, mix_sl),
+        (proj, normf, invf, norm2, inv2, slope, keys, values, norm_low, probs, gv, z_value), second, down,
     )
     got = lax.all_to_all(payload, "dp", 0, 0, tiled=True).reshape(ITEMS, PAYLOAD, 128)
-    block_out, tokens_grad = close(
-        lengths, tok, vec, gk, gv, q_own, gm_own, gq, mid_own, act, middle, first, down
+    block_out, tokens_grad, q_all, norm_sl = close(
+        lengths, tok, vec, gk, gv, q_own, gm_own, gq, mid_own, n2, middle, first, second, down
     )
     d_qkv, g_one, b_one, qv_sums = shard_grads(got, q_all, gm_all, norm_sl, w_own, ln1_gain, ln1_bias)
     seq = tok.shape[0]

time: 177 us -> 155 us (0.88)
  waiting for transfers between devices: 63.8 us -> 38.6 us
  Pallas kernels: 65 us -> 69.1 us
  starting transfers between devices: 40.1 us -> 37 us
  other arithmetic: 2.4 us -> 4.34 us
    ppermute x12, waiting for transfers between devices: 49.5 us -> 35.8 us  [step(): held = lax.ppermute(after(held, *earlier), BOTH, self.turn)]
    ppermute x1, waiting for transfers between devices: 5.5 us -> 0.3 us  [ring_body(): e_oth = lax.ppermute(e_own, BOTH, across)]
    all_to_all x1, waiting for transfers between devices: 5.94 us -> 1.17 us  [ring_body(): lax.all_to_all(payload, 'dp', 0, 0, tiled=True).reshape(ITEMS, PAYLOAD, 128)]
    ppermute x12, starting transfers between devices: 28.5 us -> 24.3 us  [step(): held = lax.ppermute(after(held, *earlier), BOTH, self.turn)]
    pallas_call x8 -> x9, Pallas kernels: 65 us -> 69.1 us  [call(): pl.pallas_call(kernel, name=name, out_shape=[jax.ShapeDtypeStruct(shape,...]
    unnamed x36 -> x28, local copies, waits for them, and re-layouts: 3.78 us -> 4.22 us
  transfers between devices with their start and end apart: 30 -> 30, of which waited for: 13 -> 12; matrix products, arithmetic and copies ran while one was open for 1% -> 3% of each run, Pallas kernels for 21% -> 26%
where the time goes in v3:
time: 155 us
  Pallas kernels  69.1 us (45%)
  waiting for transfers between devices  38.6 us (25%)
  starting transfers between devices  37 us (24%)
  other arithmetic  4.34 us (3%)
  local copies, waits for them, and re-layouts  4.22 us (3%)
  between operations  1.57 us (1%)
    pallas_call x9, Pallas kernels, call(): pl.pallas_call(kernel, name=name, out_shape=[jax.ShapeDtypeStruct(shape,...  69.1 us
    ppermute x12, waiting for transfers between devices, step(): held = lax.ppermute(after(held, *earlier), BOTH, self.turn)  35.8 us
    ppermute x12, starting transfers between devices, step(): held = lax.ppermute(after(held, *earlier), BOTH, self.turn)  24.3 us
    all_to_all x1, starting transfers between devices, ring_body(): lax.all_to_all(payload, 'dp', 0, 0, tiled=True).reshape(ITEMS, PAYLOAD, 128)  4.8 us
    all_to_all x1, starting transfers between devices, ring_body(): mixes = lax.all_to_all(pooled, 'dp', 0, 0, tiled=True)  4.6 us
    unnamed x28, local copies, waits for them, and re-layouts  4.22 us
    another operation x6, other arithmetic, __init__(): jnp.stack([jnp.where(first_core, shard, other), jnp.where(first_core, oth...  3.11 us
  transfers between devices with their start and end apart: 30, of which 12 were waited for; matrix products, arithmetic and copies ran while one was open for 3% of the time, Pallas kernels for 26%

profile of v3, /device:TPU:0, one launch (start us, length us, event | category | flops | bytes accessed | tf_op | source)
XLA Modules:
  0.0 154.8 jit_solution(7406466485139121700)
XLA Ops:
  0.7 2.2 %pack_first.1 = bf16[176,768]{1,0:T(8,128)(2,1)} custom-call(s32[8]{0:T(128)} %lengths.13, bf16[144,768]{1,0:T(8,128)(2,1)} %bitcast.61, bf16[77,8,768]{2,1,0:T(8,128)(2,1)} %bitcast.54, bf16[1,48]{1,0:T(2,128)(2,1)} %gain.1, bf16[1,48]{1,0:T(2,128)(2,1)} %bias.1, bf16[1,48]{1,0:T(2,128)(2,1)} %rest_2_.1, bf16[1,48]{1,0:T(2,128)(2,1)} %rest_3_.1, ...), custom_call_target="tpu_custom_call" | custom-call | bytes 1500000 | tf_op jit(solution)/shard_map/pack_first/pallas_call | solution.py:355
  5.7 3.0 %collective-permute-start.1 = (bf16[2,176,768]{2,1,0:T(8,128)(2,1)S(1)}, bf16[2,176,768]{2,1,0:T(8,128)(2,1)}, u32[]{:S(2)}, u32[]{:S(2)}) collective-permute-start(bf16[2,176,768]{2,1,0:T(8,128)(2,1)S(1)} %pad_maximum_fusion.2.rest_0_), channel_id=1, source_target_pairs={{0,4},{1,3},{4,8},{5,1},{8,12},{9,5},{12,14},{13,9},{14,10},{15,13... | collective-permute-start | bytes 1622024 | tf_op jit(solution)/shard_map/ppermute | solution.py:1351
  11.2 4.9 %collective-permute-done.1.rest_1_ = bf16[2,176,768]{2,1,0:T(8,128)(2,1)} collective-permute-done((bf16[2,176,768]{2,1,0:T(8,128)(2,1)S(1)}, bf16[2,176,768]{2,1,0:T(8,128)(2,1)}, u32[]{:S(2)}, u32[]{:S(2)}) %collective-permute-start.1) | collective-permute-done | bytes 540704 | tf_op jit(solution)/shard_map/ppermute | solution.py:1351
  16.1 2.1 %collective-permute-start.3 = (bf16[2,176,768]{2,1,0:T(8,128)(2,1)}, bf16[2,176,768]{2,1,0:T(8,128)(2,1)}, u32[]{:S(2)}, u32[]{:S(2)}) collective-permute-start(bf16[2,176,768]{2,1,0:T(8,128)(2,1)} %collective-permute-done.1.rest_1_), channel_id=1, source_target_pairs={{0,4},{1,3},{4,8},{5,1},{8,12},{9,5},{12,14},{13,9},{14,10},{15,13... | collective-permute-start | bytes 1622024 | tf_op jit(solution)/shard_map/ppermute | solution.py:1351
  20.0 2.5 %collective-permute-done.6.rest_19_.rest_22_ = bf16[2,192,768]{2,1,0:T(8,128)(2,1)} collective-permute-done((bf16[2,192,768]{2,1,0:T(8,128)(2,1)}, bf16[2,192,768]{2,1,0:T(8,128)(2,1)}, u32[]{:S(2)}, u32[]{:S(2)}) %collective-permute-start.6) | collective-permute-done | bytes 589856 | tf_op jit(solution)/shard_map/ppermute | solution.py:1351
  22.4 5.8 %collective-permute-done.3.rest_3_ = bf16[2,176,768]{2,1,0:T(8,128)(2,1)} collective-permute-done((bf16[2,176,768]{2,1,0:T(8,128)(2,1)}, bf16[2,176,768]{2,1,0:T(8,128)(2,1)}, u32[]{:S(2)}, u32[]{:S(2)}) %collective-permute-start.3) | collective-permute-done | bytes 540704 | tf_op jit(solution)/shard_map/ppermute | solution.py:1351
  28.2 2.1 %collective-permute-start.7 = (bf16[2,176,768]{2,1,0:T(8,128)(2,1)}, bf16[2,176,768]{2,1,0:T(8,128)(2,1)S(1)}, u32[]{:S(2)}, u32[]{:S(2)}) collective-permute-start(bf16[2,176,768]{2,1,0:T(8,128)(2,1)} %collective-permute-done.3.rest_3_), channel_id=1, source_target_pairs={{0,4},{1,3},{4,8},{5,1},{8,12},{9,5},{12,14},{13,9},{14,10},{15,13... | collective-permute-start | bytes 1622024 | tf_op jit(solution)/shard_map/ppermute | solution.py:1351
  34.5 3.3 %collective-permute-done.7.rest_5_ = bf16[2,176,768]{2,1,0:T(8,128)(2,1)S(1)} collective-permute-done((bf16[2,176,768]{2,1,0:T(8,128)(2,1)}, bf16[2,176,768]{2,1,0:T(8,128)(2,1)S(1)}, u32[]{:S(2)}, u32[]{:S(2)}) %collective-permute-start.7) | collective-permute-done | bytes 540704 | tf_op jit(solution)/shard_map/ppermute | solution.py:1351
  37.8 2.1 %collective-permute-start.9 = (bf16[176,768]{1,0:T(8,128)(2,1)S(1)}, bf16[176,768]{1,0:T(8,128)(2,1)S(1)}, u32[]{:S(2)}, u32[]{:S(2)}) collective-permute-start(bf16[176,768]{1,0:T(8,128)(2,1)S(1)} %fusion.2), channel_id=1, source_target_pairs={{0,4},{1,3},{4,8},{5,1},{8,12},{9,5},{12,14},{13,9},{14,10},{15,13... | collective-permute-start | bytes 811016 | tf_op jit(solution)/shard_map/ppermute | solution.py:1351
  40.0 9.7 %collective-permute-done.9.rest_7_ = bf16[176,768]{1,0:T(8,128)(2,1)S(1)} collective-permute-done((bf16[176,768]{1,0:T(8,128)(2,1)S(1)}, bf16[176,768]{1,0:T(8,128)(2,1)S(1)}, u32[]{:S(2)}, u32[]{:S(2)}) %collective-permute-start.9) | collective-permute-done | bytes 270368 | tf_op jit(solution)/shard_map/ppermute | solution.py:1351
  49.7 2.1 %collective-permute-start.14 = (bf16[2,272,768]{2,1,0:T(8,128)(2,1)}, bf16[2,272,768]{2,1,0:T(8,128)(2,1)}, u32[]{:S(2)}, u32[]{:S(2)}) collective-permute-start(bf16[2,272,768]{2,1,0:T(8,128)(2,1)} %collective-permute-done.12.rest_10_.rest_1_.rest_13_), channel_id=1, source_target_pairs={{0,4},{1,3},{4,8},{5,1},{8,12},{9,5},{12,14},{13,9},{14,10},{15,13... | collective-permute-start | bytes 2506760 | tf_op jit(solution)/shard_map/ppermute | solution.py:1351
  54.6 7.6 %attend_pooled.1 = (bf16[616,768]{1,0:T(8,128)(2,1)}, bf16[616,768]{1,0:T(8,128)(2,1)}, bf16[616,768]{1,0:T(8,128)(2,1)}, bf16[616,768]{1,0:T(8,128)(2,1)}, f32[...) custom-call(s32[8]{0:T(128)} %lengths.13, ...), custom_call_target="tpu_custom_call" | custom-call | flops 7000000000 | bytes 10000000 | tf_op jit(solution)/shard_map/attend_pooled/pallas_call | solution.py:355
  62.2 4.6 %all-to-all-start = ((bf16[16,48,128]{2,1,0:T(8,128)(2,1)}), bf16[16,48,128]{2,1,0:T(8,128)(2,1)}, u32[]{:S(2)}, u32[]{:S(2)}) async-start(bf16[16,48,128]{2,1,0:T(8,128)(2,1)} %get-tuple-element.82), calls=%async_computation | async-start | bytes 393216 | tf_op jit(solution)/shard_map/all_to_all | solution.py:1407
  68.8 10.3 %attend.1 = (bf16[616,768]{1,0:T(8,128)(2,1)}, bf16[768,128]{1,0:T(8,128)(2,1)}) custom-call(s32[8]{0:T(128)} %lengths.13, f32[16,768]{1,0:T(8,128)} %get-tuple-element.81.vec, bf16[616,128]{1,0:T(8,128)(2,1)} %get-tuple-element.86.gv.rest_10_, bf16[616,768]{1,0:T(8,128)(2,1)} %get-tuple-element.88.normed_hbm, ...), custom_call_target="tpu_custom_call" | custom-call | flops 8999999488 | bytes 10000000 | tf_op jit(solution)/shard_map/attend/pallas_call | solution.py:355
  83.1 2.8 %collective-permute-start.18 = (bf16[272,768]{1,0:T(8,128)(2,1)S(1)}, bf16[272,768]{1,0:T(8,128)(2,1)S(1)}, u32[]{:S(2)}, u32[]{:S(2)}) collective-permute-start(bf16[272,768]{1,0:T(8,128)(2,1)S(1)} %fusion), channel_id=1, source_target_pairs={{0,4},{1,3},{4,8},{5,1},{8,12},{9,5},{12,14},{13,9},{14,10},{15,13... | collective-permute-start | bytes 1253384 | tf_op jit(solution)/shard_map/ppermute | solution.py:1351
  85.9 3.4 %collective-permute-done.23.rest_23_.rest_26_ = bf16[2,192,768]{2,1,0:T(8,128)(2,1)S(1)} collective-permute-done((bf16[2,192,768]{2,1,0:T(8,128)(2,1)}, bf16[2,192,768]{2,1,0:T(8,128)(2,1)S(1)}, u32[]{:S(2)}, u32[]{:S(2)}) %collective-permute-start.23) | collective-permute-done | bytes 589856 | tf_op jit(solution)/shard_map/ppermute | solution.py:1351
  91.3 2.4 %collective-permute-done.18.rest_16_.rest_7_.rest_19_ = bf16[272,768]{1,0:T(8,128)(2,1)S(1)} collective-permute-done((bf16[272,768]{1,0:T(8,128)(2,1)S(1)}, bf16[272,768]{1,0:T(8,128)(2,1)S(1)}, u32[]{:S(2)}, u32[]{:S(2)}) %collective-permute-start.18) | collective-permute-done | bytes 417824 | tf_op jit(solution)/shard_map/ppermute | solution.py:1351
  93.7 3.2 %collective-permute-done.25.rest_25_.rest_28_ = bf16[192,768]{1,0:T(8,128)(2,1)S(1)} collective-permute-done((bf16[192,768]{1,0:T(8,128)(2,1)S(1)}, bf16[192,768]{1,0:T(8,128)(2,1)S(1)}, u32[]{:S(2)}, u32[]{:S(2)}) %collective-permute-start.25) | collective-permute-done | bytes 294944 | tf_op jit(solution)/shard_map/ppermute | solution.py:1351
  100.2 8.8 %pooled_forward.1 = (bf16[128,512]{1,0:T(8,128)(2,1)}, f32[128,512]{1,0:T(8,128)}, f32[128,768]{1,0:T(8,128)}, f32[128,128]{1,0:T(8,128)}, f32[128,768]{1,0:T(8,...) custom-call(s32[8]{0:T(128)} %lengths.13, ...), custom_call_target="tpu_custom_call" | custom-call | flops 11000000512 | bytes 16000000 | tf_op jit(solution)/shard_map/pooled_forward/pallas_call | solution.py:355
  110.1 5.0 %middle_part.1 = (bf16[616,768]{1,0:T(8,128)(2,1)}, f32[616,768]{1,0:T(8,128)}) custom-call(s32[8]{0:T(128)} %lengths.13, bf16[77,8,768]{2,1,0:T(8,128)(2,1)} %bitcast.56, f32[16,768]{1,0:T(8,128)} %get-tuple-element.81.vec, bf16[616,768]{1,0:T(8,128)(2,1)} %get-tuple-element.99.mixed_hbm, bf16[2,272,768]{2,1,0:T(8,128)(2,1)} %copy-done, ...), custom_call_target="tpu_custom_call" | custom-call | flops 5000000000 | bytes 8000000 | tf_op jit(solution)/shard_map/middle_part/pallas_call | solution.py:355
  115.4 14.6 %chain.1 = (f32[1,1]{1,0:T(1,128)}, f32[1,1]{1,0:T(1,128)}, f32[48,512]{1,0:T(8,128)}, f32[192,768]{1,0:T(8,128)}, f32[48,3072]{1,0:T(8,128)}, /*index=5*/f32[48...) custom-call(s32[8]{0:T(128)} %lengths.13, ...), custom_call_target="tpu_custom_call" | custom-call | flops 15000000512 | bytes 20000000 | tf_op jit(solution)/shard_map/chain/pallas_call | solution.py:355
  130.0 4.8 %all-to-all-start.1 = ((bf16[16,160,128]{2,1,0:T(8,128)(2,1)}), bf16[16,160,128]{2,1,0:T(8,128)(2,1)}, u32[]{:S(2)}, u32[]{:S(2)}) async-start(bf16[16,160,128]{2,1,0:T(8,128)(2,1)} %bitcast.58), calls=%async_computation.1 | async-start | bytes 1310720 | tf_op jit(solution)/shard_map/all_to_all | solution.py:1426
  134.8 15.5 %close.1 = (bf16[616,768]{1,0:T(8,128)(2,1)}, f32[616,768]{1,0:T(8,128)}, f32[128,768]{1,0:T(8,128)}, bf16[128,48]{1,0:T(8,128)(2,1)}) custom-call(s32[8]{0:T(128)} %lengths.13, bf16[77,8,768]{2,1,0:T(8,128)(2,1)} %bitcast.57, f32[16,768]{1,0:T(8,128)} %get-tuple-element.81.vec, bf16[616,128]{1,0:T(8,128)(2,1)} %get-tuple-element.113.gk, ...), custom_call_target="tpu_custom_call" | custom-call | flops 16999999488 | bytes 18000000 | tf_op jit(solution)/shard_map/close/pallas_call | solution.py:355
  151.5 3.3 %shard_grads.1 = (f32[3,48,768]{2,1,0:T(8,128)}, f32[1,48]{1,0:T(1,128)}, f32[1,48]{1,0:T(1,128)}, f32[2,48]{1,0:T(2,128)}) custom-call(bf16[16,160,128]{2,1,0:T(8,128)(2,1)} %all-to-all-done.1.got, f32[128,768]{1,0:T(8,128)} %get-tuple-element.122.q_all, f32[128,768]{1,0:T(8,128)} %get-tuple-element.123.gm_all, bf16[128,48]{1,0:T(8,128)(2,1)} %get-tuple-element.124.norm_sl, ...), custom_call_target="tpu_custom_call" | custom-call | flops 5000000000 | bytes 2000000 | tf_op jit(solution)/shard_map/shard_grads/pallas_call | solution.py:355
  (82 shorter events, 27.3 us)
Async XLA Ops:
  5.7 10.4 %collective-permute-start.1 = (bf16[2,176,768]{2,1,0:T(8,128)(2,1)S(1)}, bf16[2,176,768]{2,1,0:T(8,128)(2,1)}, u32[]{:S(2)}, u32[]{:S(2)}) collective-permute-start(bf16[2,176,768]{2,1,0:T(8,128)(2,1)S(1)} %pad_maximum_fusion.2.rest_0_), channel_id=1, source_target_pairs={{0,4},{1,3},{4,8},{5,1},{8,12},{9,5},{12,14},{13,9},{14,10},{15,13... | collective-permute-start | bytes 1622024 | tf_op jit(solution)/shard_map/ppermute | solution.py:1351
  9.7 12.8 %collective-permute-start.6 = (bf16[2,192,768]{2,1,0:T(8,128)(2,1)}, bf16[2,192,768]{2,1,0:T(8,128)(2,1)}, u32[]{:S(2)}, u32[]{:S(2)}) collective-permute-start(bf16[2,192,768]{2,1,0:T(8,128)(2,1)} %pad_maximum_fusion.1.rest_18_.rest_21_), channel_id=1, source_target_pairs={{0,4},{1,3},{4,8},{5,1},{8,12},{9,5},{12,14},{13,9},{14,10},{15,13... | collective-permute-start | bytes 1769480 | tf_op jit(solution)/shard_map/ppermute | solution.py:1351
  16.1 12.1 %collective-permute-start.3 = (bf16[2,176,768]{2,1,0:T(8,128)(2,1)}, bf16[2,176,768]{2,1,0:T(8,128)(2,1)}, u32[]{:S(2)}, u32[]{:S(2)}) collective-permute-start(bf16[2,176,768]{2,1,0:T(8,128)(2,1)} %collective-permute-done.1.rest_1_), channel_id=1, source_target_pairs={{0,4},{1,3},{4,8},{5,1},{8,12},{9,5},{12,14},{13,9},{14,10},{15,13... | collective-permute-start | bytes 1622024 | tf_op jit(solution)/shard_map/ppermute | solution.py:1351
  20.0 10.4 %collective-permute-start.11 = (bf16[272,768]{1,0:T(8,128)(2,1)}, bf16[272,768]{1,0:T(8,128)(2,1)S(1)}, u32[]{:S(2)}, u32[]{:S(2)}) collective-permute-start(bf16[272,768]{1,0:T(8,128)(2,1)} %pack_rest.1), channel_id=1, source_target_pairs={{0,1},{1,0},{4,5},{5,4},{8,9},{9,8},{12,13},{13,12},{14,15},{15,14... | collective-permute-start | bytes 1253384 | tf_op jit(solution)/shard_map/ppermute | solution.py:1340
  28.2 9.6 %collective-permute-start.7 = (bf16[2,176,768]{2,1,0:T(8,128)(2,1)}, bf16[2,176,768]{2,1,0:T(8,128)(2,1)S(1)}, u32[]{:S(2)}, u32[]{:S(2)}) collective-permute-start(bf16[2,176,768]{2,1,0:T(8,128)(2,1)} %collective-permute-done.3.rest_3_), channel_id=1, source_target_pairs={{0,4},{1,3},{4,8},{5,1},{8,12},{9,5},{12,14},{13,9},{14,10},{15,13... | collective-permute-start | bytes 1622024 | tf_op jit(solution)/shard_map/ppermute | solution.py:1351
  32.4 17.3 %collective-permute-start.12 = (bf16[2,272,768]{2,1,0:T(8,128)(2,1)S(1)}, bf16[2,272,768]{2,1,0:T(8,128)(2,1)}, u32[]{:S(2)}, u32[]{:S(2)}) collective-permute-start(bf16[2,272,768]{2,1,0:T(8,128)(2,1)S(1)} %pad_maximum_fusion.rest_9_.rest_0_.rest_12_), channel_id=1, source_target_pairs={{0,4},{1,3},{4,8},{5,1},{8,12},{9,5},{12,14},{13,9},{14,10},{15,13... | collective-permute-start | bytes 2506760 | tf_op jit(solution)/shard_map/ppermute | solution.py:1351
  34.0 17.8 %collective-permute-start.2 = (bf16[2,176,768]{2,1,0:T(8,128)(2,1)}, bf16[2,176,768]{2,1,0:T(8,128)(2,1)}, u32[]{:S(2)}, u32[]{:S(2)}) collective-permute-start(bf16[2,176,768]{2,1,0:T(8,128)(2,1)} %collective-permute-done.1.rest_1_), channel_id=1, source_target_pairs={{0,1},{1,0},{4,5},{5,4},{8,9},{9,8},{12,13},{13,12},{14,15},{15,14... | collective-permute-start | bytes 1622024 | tf_op jit(solution)/shard_map/ppermute | solution.py:1352
  34.0 17.9 %collective-permute-start.4 = (bf16[2,176,768]{2,1,0:T(8,128)(2,1)}, bf16[2,176,768]{2,1,0:T(8,128)(2,1)}, u32[]{:S(2)}, u32[]{:S(2)}) collective-permute-start(bf16[2,176,768]{2,1,0:T(8,128)(2,1)} %collective-permute-done.3.rest_3_), channel_id=1, source_target_pairs={{0,1},{1,0},{4,5},{5,4},{8,9},{9,8},{12,13},{13,12},{14,15},{15,14... | collective-permute-start | bytes 1622024 | tf_op jit(solution)/shard_map/ppermute | solution.py:1352
  37.8 11.8 %collective-permute-start.9 = (bf16[176,768]{1,0:T(8,128)(2,1)S(1)}, bf16[176,768]{1,0:T(8,128)(2,1)S(1)}, u32[]{:S(2)}, u32[]{:S(2)}) collective-permute-start(bf16[176,768]{1,0:T(8,128)(2,1)S(1)} %fusion.2), channel_id=1, source_target_pairs={{0,4},{1,3},{4,8},{5,1},{8,12},{9,5},{12,14},{13,9},{14,10},{15,13... | collective-permute-start | bytes 811016 | tf_op jit(solution)/shard_map/ppermute | solution.py:1351
  40.0 14.7 %collective-permute-start.8 = (bf16[2,176,768]{2,1,0:T(8,128)(2,1)S(1)}, bf16[2,176,768]{2,1,0:T(8,128)(2,1)}, u32[]{:S(2)}, u32[]{:S(2)}) collective-permute-start(bf16[2,176,768]{2,1,0:T(8,128)(2,1)S(1)} %collective-permute-done.7.rest_5_), channel_id=1, source_target_pairs={{0,1},{1,0},{4,5},{5,4},{8,9},{9,8},{12,13},{13,12},{14,15},{15,14... | collective-permute-start | bytes 1622024 | tf_op jit(solution)/shard_map/ppermute | solution.py:1352
  49.7 17.1 %collective-permute-start.14 = (bf16[2,272,768]{2,1,0:T(8,128)(2,1)}, bf16[2,272,768]{2,1,0:T(8,128)(2,1)}, u32[]{:S(2)}, u32[]{:S(2)}) collective-permute-start(bf16[2,272,768]{2,1,0:T(8,128)(2,1)} %collective-permute-done.12.rest_10_.rest_1_.rest_13_), channel_id=1, source_target_pairs={{0,4},{1,3},{4,8},{5,1},{8,12},{9,5},{12,14},{13,9},{14,10},{15,13... | collective-permute-start | bytes 2506760 | tf_op jit(solution)/shard_map/ppermute | solution.py:1351
  51.8 31.3 %collective-permute-start.20 = (bf16[2,192,768]{2,1,0:T(8,128)(2,1)}, bf16[2,192,768]{2,1,0:T(8,128)(2,1)}, u32[]{:S(2)}, u32[]{:S(2)}) collective-permute-start(bf16[2,192,768]{2,1,0:T(8,128)(2,1)} %collective-permute-done.6.rest_19_.rest_22_), channel_id=1, source_target_pairs={{0,1},{1,0},{4,5},{5,4},{8,9},{9,8},{12,13},{13,12},{14,15},{15,14... | collective-permute-start | bytes 1769480 | tf_op jit(solution)/shard_map/ppermute | solution.py:1352
  51.9 37.4 %collective-permute-start.13 = (bf16[2,272,768]{2,1,0:T(8,128)(2,1)}, bf16[2,272,768]{2,1,0:T(8,128)(2,1)}, u32[]{:S(2)}, u32[]{:S(2)}) collective-permute-start(bf16[2,272,768]{2,1,0:T(8,128)(2,1)} %collective-permute-done.12.rest_10_.rest_1_.rest_13_), channel_id=1, source_target_pairs={{0,1},{1,0},{4,5},{5,4},{8,9},{9,8},{12,13},{13,12},{14,15},{15,14... | collective-permute-start | bytes 2506760 | tf_op jit(solution)/shard_map/ppermute | solution.py:1352
  53.0 26.0 %collective-permute-start.21 = (bf16[2,192,768]{2,1,0:T(8,128)(2,1)}, bf16[2,192,768]{2,1,0:T(8,128)(2,1)}, u32[]{:S(2)}, u32[]{:S(2)}) collective-permute-start(bf16[2,192,768]{2,1,0:T(8,128)(2,1)} %collective-permute-done.6.rest_19_.rest_22_), channel_id=1, source_target_pairs={{0,4},{1,3},{4,8},{5,1},{8,12},{9,5},{12,14},{13,9},{14,10},{15,13... | collective-permute-start | bytes 1769480 | tf_op jit(solution)/shard_map/ppermute | solution.py:1351
  62.2 16.9 %all-to-all-start = ((bf16[16,48,128]{2,1,0:T(8,128)(2,1)}), bf16[16,48,128]{2,1,0:T(8,128)(2,1)}, u32[]{:S(2)}, u32[]{:S(2)}) async-start(bf16[16,48,128]{2,1,0:T(8,128)(2,1)} %get-tuple-element.82), calls=%async_computation | async-start | bytes 393216 | tf_op jit(solution)/shard_map/all_to_all | solution.py:1407
  66.8 14.5 %collective-permute-start.16 = (bf16[2,272,768]{2,1,0:T(8,128)(2,1)}, bf16[2,272,768]{2,1,0:T(8,128)(2,1)}, u32[]{:S(2)}, u32[]{:S(2)}) collective-permute-start(bf16[2,272,768]{2,1,0:T(8,128)(2,1)} %collective-permute-done.14.rest_12_.rest_3_.rest_15_), channel_id=1, source_target_pairs={{0,4},{1,3},{4,8},{5,1},{8,12},{9,5},{12,14},{13,9},{14,10},{15,13... | collective-permute-start | bytes 2506760 | tf_op jit(solution)/shard_map/ppermute | solution.py:1351
  79.1 10.1 %collective-permute-start.23 = (bf16[2,192,768]{2,1,0:T(8,128)(2,1)}, bf16[2,192,768]{2,1,0:T(8,128)(2,1)S(1)}, u32[]{:S(2)}, u32[]{:S(2)}) collective-permute-start(bf16[2,192,768]{2,1,0:T(8,128)(2,1)} %collective-permute-done.21.rest_21_.rest_24_), channel_id=1, source_target_pairs={{0,4},{1,3},{4,8},{5,1},{8,12},{9,5},{12,14},{13,9},{14,10},{15,13... | collective-permute-start | bytes 1769480 | tf_op jit(solution)/shard_map/ppermute | solution.py:1351
  80.6 10.6 %collective-permute-start.22 = (bf16[2,192,768]{2,1,0:T(8,128)(2,1)}, bf16[2,192,768]{2,1,0:T(8,128)(2,1)S(1)}, u32[]{:S(2)}, u32[]{:S(2)}) collective-permute-start(bf16[2,192,768]{2,1,0:T(8,128)(2,1)} %collective-permute-done.21.rest_21_.rest_24_), channel_id=1, source_target_pairs={{0,1},{1,0},{4,5},{5,4},{8,9},{9,8},{12,13},{13,12},{14,15},{15,14... | collective-permute-start | bytes 1769480 | tf_op jit(solution)/shard_map/ppermute | solution.py:1352
  81.3 16.2 %collective-permute-start.15 = (bf16[2,272,768]{2,1,0:T(8,128)(2,1)}, bf16[2,272,768]{2,1,0:T(8,128)(2,1)S(1)}, u32[]{:S(2)}, u32[]{:S(2)}) collective-permute-start(bf16[2,272,768]{2,1,0:T(8,128)(2,1)} %collective-permute-done.14.rest_12_.rest_3_.rest_15_), channel_id=1, source_target_pairs={{0,1},{1,0},{4,5},{5,4},{8,9},{9,8},{12,13},{13,12},{14,15},{15,14... | collective-permute-start | bytes 2506760 | tf_op jit(solution)/shard_map/ppermute | solution.py:1352
  83.1 10.6 %collective-permute-start.18 = (bf16[272,768]{1,0:T(8,128)(2,1)S(1)}, bf16[272,768]{1,0:T(8,128)(2,1)S(1)}, u32[]{:S(2)}, u32[]{:S(2)}) collective-permute-start(bf16[272,768]{1,0:T(8,128)(2,1)S(1)} %fusion), channel_id=1, source_target_pairs={{0,4},{1,3},{4,8},{5,1},{8,12},{9,5},{12,14},{13,9},{14,10},{15,13... | collective-permute-start | bytes 1253384 | tf_op jit(solution)/shard_map/ppermute | solution.py:1351
  89.2 10.9 %collective-permute-start.17 = (bf16[2,272,768]{2,1,0:T(8,128)(2,1)}, bf16[2,272,768]{2,1,0:T(8,128)(2,1)}, u32[]{:S(2)}, u32[]{:S(2)}) collective-permute-start(bf16[2,272,768]{2,1,0:T(8,128)(2,1)} %collective-permute-done.16.rest_14_.rest_5_.rest_17_), channel_id=1, source_target_pairs={{0,1},{1,0},{4,5},{5,4},{8,9},{9,8},{12,13},{13,12},{14,15},{15,14... | collective-permute-start | bytes 2506760 | tf_op jit(solution)/shard_map/ppermute | solution.py:1352
  89.3 7.6 %collective-permute-start.25 = (bf16[192,768]{1,0:T(8,128)(2,1)S(1)}, bf16[192,768]{1,0:T(8,128)(2,1)S(1)}, u32[]{:S(2)}, u32[]{:S(2)}) collective-permute-start(bf16[192,768]{1,0:T(8,128)(2,1)S(1)} %fusion.1), channel_id=1, source_target_pairs={{0,4},{1,3},{4,8},{5,1},{8,12},{9,5},{12,14},{13,9},{14,10},{15,13... | collective-permute-start | bytes 884744 | tf_op jit(solution)/shard_map/ppermute | solution.py:1351
  109.0 6.4 %collective-permute-start.27 = (bf16[128,512]{1,0:T(8,128)(2,1)}, bf16[128,512]{1,0:T(8,128)(2,1)}, u32[]{:S(2)}, u32[]{:S(2)}) collective-permute-start(bf16[128,512]{1,0:T(8,128)(2,1)} %get-tuple-element.101.e_own_ref), channel_id=1, source_target_pairs={{0,16},{1,17},{2,18},{3,19},{4,20},{5,21},{6,22},{7,23},{8,24},{9,... | collective-permute-start | bytes 393224 | tf_op jit(solution)/shard_map/ppermute | solution.py:1419
  130.0 21.5 %all-to-all-start.1 = ((bf16[16,160,128]{2,1,0:T(8,128)(2,1)}), bf16[16,160,128]{2,1,0:T(8,128)(2,1)}, u32[]{:S(2)}, u32[]{:S(2)}) async-start(bf16[16,160,128]{2,1,0:T(8,128)(2,1)} %bitcast.58), calls=%async_computation.1 | async-start | bytes 1310720 | tf_op jit(solution)/shard_map/all_to_all | solution.py:1426
  (20 other events, 67.2 us)

commit v4 on v3

--- a/solution.py
+++ b/solution.py
@@ -1,3 +1,5 @@
+import functools
+
 import jax
 import jax.numpy as jnp
 from jax import lax
@@ -499,7 +501,7 @@
     pooled = jnp.zeros((8, DI), F32)
     for s in range(8):
         pooled = jnp.where(sub == s, tok[here.pool(s)].astype(F32), pooled)
-    out[144:160, :] = jnp.concatenate([pooled, jnp.zeros((8, DI), F32)], axis=0).astype(BF16)
+    out[144:152, :] = pooled.astype(BF16)
     lane = lax.broadcasted_iota(jnp.int32, (1, DI), 1) // 48 == here.dp
     short = [v[...].astype(F32) for v in vectors]
     pair = qv_bias[...].astype(F32)
@@ -512,7 +514,7 @@
     small = jnp.zeros((16, DI), F32)
     for at, row in enumerate(rows):
         small = jnp.where(row_id == at, jnp.broadcast_to(row, (16, DI)), small)
-    out[160:176, :] = small.astype(BF16)
+    out[152:168, :] = small.astype(BF16)
 
 
 def pack_first(lengths, qkv, tok, vectors, qv_bias, fc_bias):
@@ -520,7 +522,7 @@
         pack_first_kernel,
         "pack_first",
         [(SMEM, lengths)] + [(VMEM, item) for item in (qkv, tok, *vectors, qv_bias, fc_bias)],
-        [(VMEM, (176, DI), BF16)],
+        [(VMEM, (168, DI), BF16)],
         [],
         touched=1_500_000,
     )[0]
@@ -581,7 +583,7 @@
     weights, small, normed, keys, values, norm_low, sems, ends = scratch
     here = Place(lengths)
     owners = owner_table(here.dp)
-    fetch(owners, first, 160, 16, small, sems.at[0])
+    fetch(owners, first, 152, 16, small, sems.at[0])
     fetch(owners, first, 0, 144, weights, sems.at[1])
     keep, winv = here.keep, here.winv
     drain(small, sems.at[0])
@@ -771,7 +773,7 @@
     here = Place(lengths)
     owners = owner_table(here.dp)
     fetch(owners, second, 0, 48, w_out, sems.at[1])
-    fetch(owners, first, 144, 16, xs, sems.at[0])
+    fetch(owners, first, 144, 8, xs, sems.at[0])
     fetch(owners, second, 80, 192, w_fc, sems.at[2])
     keep, winv = here.keep, here.winv
     mix[...] = wide_rows(mixes[...]).astype(BF16)
@@ -779,7 +781,7 @@
     drain(xs, sems.at[0])
     fetch(owners, down, 0, 192, w_down, sems.at[3])
     fetch(owners, second, 48, 32, w_emb, sems.at[4])
-    stream = xs[...].astype(F32)[:, :8, :].reshape(N, DI)
+    stream = xs[...].astype(F32).reshape(N, DI)
     middle = stream + dot(mix[...], w_out[...].reshape(DI, DI)) + vec[4:5, :]
     norm2, inv2 = normalize(middle, keep, winv)
     n2[...] = (norm2 * vec[5:6, :] + vec[6:7, :]).astype(BF16)
@@ -839,7 +841,7 @@
             pltpu.VMEM((ITEMS, 192, DI), BF16),
             pltpu.VMEM((ITEMS, 192, DI), BF16),
             pltpu.VMEM((ITEMS, 32, DI), BF16),
-            pltpu.VMEM((ITEMS, 16, DI), BF16),
+            pltpu.VMEM((ITEMS, 8, DI), BF16),
             pltpu.VMEM((N, DI), BF16),
             pltpu.VMEM((N, DI), BF16),
             pltpu.VMEM((N, 4 * DI), BF16),
@@ -1139,7 +1141,7 @@
     here = Place(lengths)
     owners = owner_table(here.dp)
     fetch(owners, first, 0, 144, weights, sems.at[0])
-    fetch(owners, first, 144, 16, xs, sems.at[5])
+    fetch(owners, first, 144, 8, xs, sems.at[5])
     ready = copy(n2_hbm, n2, sems.at[1])
     fetch(owners, second, 80, 192, w_fc, sems.at[4])
     fetch(owners, down, 0, 192, w_down, sems.at[3])
@@ -1204,7 +1206,7 @@
 
     here.either(path, 56)
     drain(xs, sems.at[5])
-    stream = xs[...].astype(F32)[:, :8, :].reshape(N, DI)
+    stream = xs[...].astype(F32).reshape(N, DI)
     norm1, _ = normalize(stream, keep, winv)
     norm1_all[...] = norm1.astype(BF16)
     n1 = (norm1 * vec[0:1, :] + vec[1:2, :]).astype(BF16)
@@ -1233,7 +1235,7 @@
             pltpu.VMEM((rows, 4 * DI), BF16),
             pltpu.VMEM((rows, DI), F32),
             pltpu.VMEM((rows, DI), F32),
-            pltpu.VMEM((ITEMS, 16, DI), BF16),
+            pltpu.VMEM((ITEMS, 8, DI), BF16),
             pltpu.VMEM((N, DI), BF16),
             pltpu.SemaphoreType.DMA((6,)),
         ],
@@ -1337,12 +1339,21 @@
 
 class Ring:
     def __init__(self, shard, swap, turn, first_core):
-        other = lax.ppermute(shard, BOTH, swap)
         self.swap, self.turn, self.first_core = swap, turn, first_core
-        held = jnp.stack([jnp.where(first_core, shard, other), jnp.where(first_core, other, shard)])
-        self.items = [held]
+        self.shard, self.other = shard, lax.ppermute(shard, BOTH, swap)
+        self.last = self.joined(shard, self.other)
+        self.items = [self.last]
+        self.hops = 0
+
+    def joined(self, own, other):
+        return jnp.stack([jnp.where(self.first_core, own, other), jnp.where(self.first_core, other, own)])
+
+    def first_step(self):
+        held = self.joined(*(lax.ppermute(item, BOTH, self.turn) for item in (self.shard, self.other)))
+        self.items += [held, lax.ppermute(held, BOTH, self.swap)]
         self.last = held
-        self.hops = 0
+        self.hops += 1
+        return held
 
     def step(self, *earlier, swap_after=(), later=False):
         held = self.last
@@ -1394,7 +1405,7 @@
     qkv_ring = Ring(first_own, swap, turn, first_core)
     wide_ring = Ring(second_own, swap, turn, first_core)
     down_ring = Ring(down_weight[0], swap, turn, first_core)
-    qkv_ring.step()
+    qkv_ring.first_step()
     d1 = down_ring.step()
     qkv_ring.step()
     q3 = qkv_ring.step(d1)

time: 155 us -> 154 us (level)
  waiting for transfers between devices: 38.6 us -> 32.2 us
  starting transfers between devices: 37 us -> 39.7 us
  other arithmetic: 4.34 us -> 6.11 us
    ppermute x12 -> x11, waiting for transfers between devices: 35.8 us -> 28.6 us  [step(): held = lax.ppermute(after(held, *earlier), BOTH, self.turn)]
    ppermute x3 -> x6, starting transfers between devices: 0.53 us -> 5.18 us  [the longest x2 4.6 us: first_step(): lax.ppermute(item, BOTH, self.turn)]
    ppermute x12 -> x11, starting transfers between devices: 24.3 us -> 21.5 us  [step(): held = lax.ppermute(after(held, *earlier), BOTH, self.turn)]
    another operation x6 -> x8, other arithmetic: 3.11 us -> 4.88 us  [joined(): jnp.stack([jnp.where(self.first_core, own, other), jnp.where(self.first_c...]
    unnamed x28 -> x34, local copies, waits for them, and re-layouts: 4.22 us -> 4.38 us
  transfers between devices with their start and end apart: 30 -> 31, of which waited for: 12 -> 12; matrix products, arithmetic and copies ran while one was open for 3% -> 4% of each run, Pallas kernels for 26% -> 28%
where the time goes in v4:
time: 154 us; the launch traced here: 153 us
  Pallas kernels  69 us (45%)
  starting transfers between devices  39.7 us (26%)
  waiting for transfers between devices  32.2 us (21%)
  other arithmetic  6.11 us (4%)
  local copies, waits for them, and re-layouts  4.38 us (3%)
  between operations  1.58 us (1%)
    pallas_call x9, Pallas kernels, call(): pl.pallas_call(kernel, name=name, out_shape=[jax.ShapeDtypeStruct(shape,...  69 us
    ppermute x11, waiting for transfers between devices, step(): held = lax.ppermute(after(held, *earlier), BOTH, self.turn)  28.6 us
    ppermute x11, starting transfers between devices, step(): held = lax.ppermute(after(held, *earlier), BOTH, self.turn)  21.5 us
    all_to_all x1, starting transfers between devices, ring_body(): mixes = lax.all_to_all(pooled, 'dp', 0, 0, tiled=True)  4.98 us
    another operation x8, other arithmetic, joined(): jnp.stack([jnp.where(self.first_core, own, other), jnp.where(self.first_c...  4.88 us
    all_to_all x1, starting transfers between devices, ring_body(): lax.all_to_all(payload, 'dp', 0, 0, tiled=True).reshape(ITEMS, PAYLOAD, 128)  4.77 us
    ppermute x2, starting transfers between devices, first_step(): lax.ppermute(item, BOTH, self.turn)  4.6 us
    unnamed x34, local copies, waits for them, and re-layouts  4.38 us
  transfers between devices with their start and end apart: 31, of which 12 were waited for; matrix products, arithmetic and copies ran while one was open for 4% of the time, Pallas kernels for 28%

profile of v4, /device:TPU:0, one launch (start us, length us, event | category | flops | bytes accessed | tf_op | source)
XLA Modules:
  0.0 152.9 jit_solution(8520969243487864124)
XLA Ops:
  1.2 2.2 %pack_first.1 = bf16[168,768]{1,0:T(8,128)(2,1)} custom-call(s32[8]{0:T(128)} %lengths.13, bf16[144,768]{1,0:T(8,128)(2,1)} %bitcast.65, bf16[77,8,768]{2,1,0:T(8,128)(2,1)} %bitcast.58, bf16[1,48]{1,0:T(2,128)(2,1)} %gain.1, bf16[1,48]{1,0:T(2,128)(2,1)} %bias.1, bf16[1,48]{1,0:T(2,128)(2,1)} %rest_2_.1, bf16[1,48]{1,0:T(2,128)(2,1)} %rest_3_.1, ...), custom_call_target="tpu_custom_call" | custom-call | bytes 1500000 | tf_op jit(solution)/shard_map/pack_first/pallas_call | solution.py:357
  3.4 3.0 %collective-permute-start.1 = (bf16[168,768]{1,0:T(8,128)(2,1)}, bf16[168,768]{1,0:T(8,128)(2,1)S(1)}, u32[]{:S(2)}, u32[]{:S(2)}) collective-permute-start(bf16[168,768]{1,0:T(8,128)(2,1)} %pack_first.1), channel_id=1, source_target_pairs={{0,4},{1,3},{4,8},{5,1},{8,12},{9,5},{12,14},{13,9},{14,10},{15,13... | collective-permute-start | bytes 774152 | tf_op jit(solution)/shard_map/ppermute | solution.py:1352
  11.5 2.1 %collective-permute-done.2 = bf16[168,768]{1,0:T(8,128)(2,1)S(1)} collective-permute-done((bf16[168,768]{1,0:T(8,128)(2,1)S(1)}, bf16[168,768]{1,0:T(8,128)(2,1)S(1)}, u32[]{:S(2)}, u32[]{:S(2)}) %collective-permute-start.2) | collective-permute-done | bytes 258080 | tf_op jit(solution)/shard_map/ppermute | solution.py:1352
  14.5 2.1 %collective-permute-start.4 = (bf16[2,168,768]{2,1,0:T(8,128)(2,1)}, bf16[2,168,768]{2,1,0:T(8,128)(2,1)}, u32[]{:S(2)}, u32[]{:S(2)}) collective-permute-start(bf16[2,168,768]{2,1,0:T(8,128)(2,1)} %pad_maximum_fusion.3.rest_1_), channel_id=1, source_target_pairs={{0,4},{1,3},{4,8},{5,1},{8,12},{9,5},{12,14},{13,9},{14,10},{15,13... | collective-permute-start | bytes 1548296 | tf_op jit(solution)/shard_map/ppermute | solution.py:1362
  20.2 5.5 %collective-permute-done.4.rest_3_ = bf16[2,168,768]{2,1,0:T(8,128)(2,1)} collective-permute-done((bf16[2,168,768]{2,1,0:T(8,128)(2,1)}, bf16[2,168,768]{2,1,0:T(8,128)(2,1)}, u32[]{:S(2)}, u32[]{:S(2)}) %collective-permute-start.4) | collective-permute-done | bytes 516128 | tf_op jit(solution)/shard_map/ppermute | solution.py:1362
  25.7 2.0 %collective-permute-start.8 = (bf16[2,168,768]{2,1,0:T(8,128)(2,1)}, bf16[2,168,768]{2,1,0:T(8,128)(2,1)S(1)}, u32[]{:S(2)}, u32[]{:S(2)}) collective-permute-start(bf16[2,168,768]{2,1,0:T(8,128)(2,1)} %collective-permute-done.4.rest_3_), channel_id=1, source_target_pairs={{0,4},{1,3},{4,8},{5,1},{8,12},{9,5},{12,14},{13,9},{14,10},{15,13... | collective-permute-start | bytes 1548296 | tf_op jit(solution)/shard_map/ppermute | solution.py:1362
  30.5 4.5 %collective-permute-done.8.rest_5_ = bf16[2,168,768]{2,1,0:T(8,128)(2,1)S(1)} collective-permute-done((bf16[2,168,768]{2,1,0:T(8,128)(2,1)}, bf16[2,168,768]{2,1,0:T(8,128)(2,1)S(1)}, u32[]{:S(2)}, u32[]{:S(2)}) %collective-permute-start.8) | collective-permute-done | bytes 516128 | tf_op jit(solution)/shard_map/ppermute | solution.py:1362
  35.0 2.0 %collective-permute-start.10 = (bf16[168,768]{1,0:T(8,128)(2,1)S(1)}, bf16[168,768]{1,0:T(8,128)(2,1)S(1)}, u32[]{:S(2)}, u32[]{:S(2)}) collective-permute-start(bf16[168,768]{1,0:T(8,128)(2,1)S(1)} %fusion.2), channel_id=1, source_target_pairs={{0,4},{1,3},{4,8},{5,1},{8,12},{9,5},{12,14},{13,9},{14,10},{15,13... | collective-permute-start | bytes 774152 | tf_op jit(solution)/shard_map/ppermute | solution.py:1362
  37.6 6.5 %collective-permute-done.13.rest_10_.rest_1_.rest_13_ = bf16[2,272,768]{2,1,0:T(8,128)(2,1)} collective-permute-done((bf16[2,272,768]{2,1,0:T(8,128)(2,1)S(1)}, bf16[2,272,768]{2,1,0:T(8,128)(2,1)}, u32[]{:S(2)}, u32[]{:S(2)}) %collective-permute-start.13) | collective-permute-done | bytes 835616 | tf_op jit(solution)/shard_map/ppermute | solution.py:1362
  44.1 2.0 %collective-permute-start.15 = (bf16[2,272,768]{2,1,0:T(8,128)(2,1)}, bf16[2,272,768]{2,1,0:T(8,128)(2,1)}, u32[]{:S(2)}, u32[]{:S(2)}) collective-permute-start(bf16[2,272,768]{2,1,0:T(8,128)(2,1)} %collective-permute-done.13.rest_10_.rest_1_.rest_13_), channel_id=1, source_target_pairs={{0,4},{1,3},{4,8},{5,1},{8,12},{9,5},{12,14},{13,9},{14,10},{15,13... | collective-permute-start | bytes 2506760 | tf_op jit(solution)/shard_map/ppermute | solution.py:1362
  52.5 7.6 %attend_pooled.1 = (bf16[616,768]{1,0:T(8,128)(2,1)}, bf16[616,768]{1,0:T(8,128)(2,1)}, bf16[616,768]{1,0:T(8,128)(2,1)}, bf16[616,768]{1,0:T(8,128)(2,1)}, f32[...) custom-call(s32[8]{0:T(128)} %lengths.13, ...), custom_call_target="tpu_custom_call" | custom-call | flops 7000000000 | bytes 10000000 | tf_op jit(solution)/shard_map/attend_pooled/pallas_call | solution.py:357
  60.1 5.0 %all-to-all-start = ((bf16[16,48,128]{2,1,0:T(8,128)(2,1)}), bf16[16,48,128]{2,1,0:T(8,128)(2,1)}, u32[]{:S(2)}, u32[]{:S(2)}) async-start(bf16[16,48,128]{2,1,0:T(8,128)(2,1)} %get-tuple-element.82), calls=%async_computation | async-start | bytes 393216 | tf_op jit(solution)/shard_map/all_to_all | solution.py:1418
  67.0 10.2 %attend.1 = (bf16[616,768]{1,0:T(8,128)(2,1)}, bf16[768,128]{1,0:T(8,128)(2,1)}) custom-call(s32[8]{0:T(128)} %lengths.13, f32[16,768]{1,0:T(8,128)} %get-tuple-element.81.vec, bf16[616,128]{1,0:T(8,128)(2,1)} %get-tuple-element.86.gv.rest_10_, bf16[616,768]{1,0:T(8,128)(2,1)} %get-tuple-element.88.normed_hbm, ...), custom_call_target="tpu_custom_call" | custom-call | flops 8999999488 | bytes 10000000 | tf_op jit(solution)/shard_map/attend/pallas_call | solution.py:357
  81.4 2.8 %collective-permute-start.19 = (bf16[272,768]{1,0:T(8,128)(2,1)S(1)}, bf16[272,768]{1,0:T(8,128)(2,1)S(1)}, u32[]{:S(2)}, u32[]{:S(2)}) collective-permute-start(bf16[272,768]{1,0:T(8,128)(2,1)S(1)} %fusion), channel_id=1, source_target_pairs={{0,4},{1,3},{4,8},{5,1},{8,12},{9,5},{12,14},{13,9},{14,10},{15,13... | collective-permute-start | bytes 1253384 | tf_op jit(solution)/shard_map/ppermute | solution.py:1362
  84.2 3.3 %collective-permute-done.24.rest_23_.rest_26_ = bf16[2,192,768]{2,1,0:T(8,128)(2,1)S(1)} collective-permute-done((bf16[2,192,768]{2,1,0:T(8,128)(2,1)}, bf16[2,192,768]{2,1,0:T(8,128)(2,1)S(1)}, u32[]{:S(2)}, u32[]{:S(2)}) %collective-permute-start.24) | collective-permute-done | bytes 589856 | tf_op jit(solution)/shard_map/ppermute | solution.py:1362
  87.5 2.0 %collective-permute-start.26 = (bf16[192,768]{1,0:T(8,128)(2,1)S(1)}, bf16[192,768]{1,0:T(8,128)(2,1)S(1)}, u32[]{:S(2)}, u32[]{:S(2)}) collective-permute-start(bf16[192,768]{1,0:T(8,128)(2,1)S(1)} %fusion.1), channel_id=1, source_target_pairs={{0,4},{1,3},{4,8},{5,1},{8,12},{9,5},{12,14},{13,9},{14,10},{15,13... | collective-permute-start | bytes 884744 | tf_op jit(solution)/shard_map/ppermute | solution.py:1362
  89.6 2.3 %collective-permute-done.19.rest_16_.rest_7_.rest_19_ = bf16[272,768]{1,0:T(8,128)(2,1)S(1)} collective-permute-done((bf16[272,768]{1,0:T(8,128)(2,1)S(1)}, bf16[272,768]{1,0:T(8,128)(2,1)S(1)}, u32[]{:S(2)}, u32[]{:S(2)}) %collective-permute-start.19) | collective-permute-done | bytes 417824 | tf_op jit(solution)/shard_map/ppermute | solution.py:1362
  91.9 3.2 %collective-permute-done.26.rest_25_.rest_28_ = bf16[192,768]{1,0:T(8,128)(2,1)S(1)} collective-permute-done((bf16[192,768]{1,0:T(8,128)(2,1)S(1)}, bf16[192,768]{1,0:T(8,128)(2,1)S(1)}, u32[]{:S(2)}, u32[]{:S(2)}) %collective-permute-start.26) | collective-permute-done | bytes 294944 | tf_op jit(solution)/shard_map/ppermute | solution.py:1362
  98.4 8.8 %pooled_forward.1 = (bf16[128,512]{1,0:T(8,128)(2,1)}, f32[128,512]{1,0:T(8,128)}, f32[128,768]{1,0:T(8,128)}, f32[128,128]{1,0:T(8,128)}, f32[128,768]{1,0:T(8,...) custom-call(s32[8]{0:T(128)} %lengths.13, ...), custom_call_target="tpu_custom_call" | custom-call | flops 11000000512 | bytes 16000000 | tf_op jit(solution)/shard_map/pooled_forward/pallas_call | solution.py:357
  108.2 5.0 %middle_part.1 = (bf16[616,768]{1,0:T(8,128)(2,1)}, f32[616,768]{1,0:T(8,128)}) custom-call(s32[8]{0:T(128)} %lengths.13, bf16[77,8,768]{2,1,0:T(8,128)(2,1)} %bitcast.60, f32[16,768]{1,0:T(8,128)} %get-tuple-element.81.vec, bf16[616,768]{1,0:T(8,128)(2,1)} %get-tuple-element.99.mixed_hbm, bf16[2,272,768]{2,1,0:T(8,128)(2,1)} %copy-done.1, ...), custom_call_target="tpu_custom_call" | custom-call | flops 5000000000 | bytes 8000000 | tf_op jit(solution)/shard_map/middle_part/pallas_call | solution.py:357
  113.5 14.7 %chain.1 = (f32[1,1]{1,0:T(1,128)}, f32[1,1]{1,0:T(1,128)}, f32[48,512]{1,0:T(8,128)}, f32[192,768]{1,0:T(8,128)}, f32[48,3072]{1,0:T(8,128)}, /*index=5*/f32[48...) custom-call(s32[8]{0:T(128)} %lengths.13, ...), custom_call_target="tpu_custom_call" | custom-call | flops 15000000512 | bytes 20000000 | tf_op jit(solution)/shard_map/chain/pallas_call | solution.py:357
  128.2 4.8 %all-to-all-start.1 = ((bf16[16,160,128]{2,1,0:T(8,128)(2,1)}), bf16[16,160,128]{2,1,0:T(8,128)(2,1)}, u32[]{:S(2)}, u32[]{:S(2)}) async-start(bf16[16,160,128]{2,1,0:T(8,128)(2,1)} %bitcast.62), calls=%async_computation.1 | async-start | bytes 1310720 | tf_op jit(solution)/shard_map/all_to_all | solution.py:1437
  133.0 15.5 %close.1 = (bf16[616,768]{1,0:T(8,128)(2,1)}, f32[616,768]{1,0:T(8,128)}, f32[128,768]{1,0:T(8,128)}, bf16[128,48]{1,0:T(8,128)(2,1)}) custom-call(s32[8]{0:T(128)} %lengths.13, bf16[77,8,768]{2,1,0:T(8,128)(2,1)} %bitcast.61, f32[16,768]{1,0:T(8,128)} %get-tuple-element.81.vec, bf16[616,128]{1,0:T(8,128)(2,1)} %get-tuple-element.113.gk, ...), custom_call_target="tpu_custom_call" | custom-call | flops 16999999488 | bytes 18000000 | tf_op jit(solution)/shard_map/close/pallas_call | solution.py:357
  149.6 3.3 %shard_grads.1 = (f32[3,48,768]{2,1,0:T(8,128)}, f32[1,48]{1,0:T(1,128)}, f32[1,48]{1,0:T(1,128)}, f32[2,48]{1,0:T(2,128)}) custom-call(bf16[16,160,128]{2,1,0:T(8,128)(2,1)} %all-to-all-done.1.got, f32[128,768]{1,0:T(8,128)} %get-tuple-element.122.q_all, f32[128,768]{1,0:T(8,128)} %get-tuple-element.123.gm_all, bf16[128,48]{1,0:T(8,128)(2,1)} %get-tuple-element.124.norm_sl, ...), custom_call_target="tpu_custom_call" | custom-call | flops 5000000000 | bytes 2000000 | tf_op jit(solution)/shard_map/shard_grads/pallas_call | solution.py:357
  (92 shorter events, 31.1 us)
Async XLA Ops:
  0.7 7.3 %collective-permute-start.6 = (bf16[192,768]{1,0:T(8,128)(2,1)}, bf16[192,768]{1,0:T(8,128)(2,1)}, u32[]{:S(2)}, u32[]{:S(2)}) collective-permute-start(bf16[192,768]{1,0:T(8,128)(2,1)} %bitcast.64), channel_id=1, source_target_pairs={{0,1},{1,0},{4,5},{5,4},{8,9},{9,8},{12,13},{13,12},{14,15},{15,14... | collective-permute-start | bytes 884744 | tf_op jit(solution)/shard_map/ppermute | solution.py:1343
  3.4 8.2 %collective-permute-start.1 = (bf16[168,768]{1,0:T(8,128)(2,1)}, bf16[168,768]{1,0:T(8,128)(2,1)S(1)}, u32[]{:S(2)}, u32[]{:S(2)}) collective-permute-start(bf16[168,768]{1,0:T(8,128)(2,1)} %pack_first.1), channel_id=1, source_target_pairs={{0,4},{1,3},{4,8},{5,1},{8,12},{9,5},{12,14},{13,9},{14,10},{15,13... | collective-permute-start | bytes 774152 | tf_op jit(solution)/shard_map/ppermute | solution.py:1352
  10.0 10.2 %collective-permute-start.7 = (bf16[2,192,768]{2,1,0:T(8,128)(2,1)}, bf16[2,192,768]{2,1,0:T(8,128)(2,1)}, u32[]{:S(2)}, u32[]{:S(2)}) collective-permute-start(bf16[2,192,768]{2,1,0:T(8,128)(2,1)} %pad_maximum_fusion.1.rest_18_.rest_21_), channel_id=1, source_target_pairs={{0,4},{1,3},{4,8},{5,1},{8,12},{9,5},{12,14},{13,9},{14,10},{15,13... | collective-permute-start | bytes 1769480 | tf_op jit(solution)/shard_map/ppermute | solution.py:1362
  14.5 11.2 %collective-permute-start.4 = (bf16[2,168,768]{2,1,0:T(8,128)(2,1)}, bf16[2,168,768]{2,1,0:T(8,128)(2,1)}, u32[]{:S(2)}, u32[]{:S(2)}) collective-permute-start(bf16[2,168,768]{2,1,0:T(8,128)(2,1)} %pad_maximum_fusion.3.rest_1_), channel_id=1, source_target_pairs={{0,4},{1,3},{4,8},{5,1},{8,12},{9,5},{12,14},{13,9},{14,10},{15,13... | collective-permute-start | bytes 1548296 | tf_op jit(solution)/shard_map/ppermute | solution.py:1362
  18.4 9.3 %collective-permute-start.12 = (bf16[272,768]{1,0:T(8,128)(2,1)}, bf16[272,768]{1,0:T(8,128)(2,1)S(1)}, u32[]{:S(2)}, u32[]{:S(2)}) collective-permute-start(bf16[272,768]{1,0:T(8,128)(2,1)} %pack_rest.1), channel_id=1, source_target_pairs={{0,1},{1,0},{4,5},{5,4},{8,9},{9,8},{12,13},{13,12},{14,15},{15,14... | collective-permute-start | bytes 1253384 | tf_op jit(solution)/shard_map/ppermute | solution.py:1343
  25.7 9.3 %collective-permute-start.8 = (bf16[2,168,768]{2,1,0:T(8,128)(2,1)}, bf16[2,168,768]{2,1,0:T(8,128)(2,1)S(1)}, u32[]{:S(2)}, u32[]{:S(2)}) collective-permute-start(bf16[2,168,768]{2,1,0:T(8,128)(2,1)} %collective-permute-done.4.rest_3_), channel_id=1, source_target_pairs={{0,4},{1,3},{4,8},{5,1},{8,12},{9,5},{12,14},{13,9},{14,10},{15,13... | collective-permute-start | bytes 1548296 | tf_op jit(solution)/shard_map/ppermute | solution.py:1362
  28.8 15.2 %collective-permute-start.13 = (bf16[2,272,768]{2,1,0:T(8,128)(2,1)S(1)}, bf16[2,272,768]{2,1,0:T(8,128)(2,1)}, u32[]{:S(2)}, u32[]{:S(2)}) collective-permute-start(bf16[2,272,768]{2,1,0:T(8,128)(2,1)S(1)} %pad_maximum_fusion.rest_9_.rest_0_.rest_12_), channel_id=1, source_target_pairs={{0,4},{1,3},{4,8},{5,1},{8,12},{9,5},{12,14},{13,9},{14,10},{15,13... | collective-permute-start | bytes 2506760 | tf_op jit(solution)/shard_map/ppermute | solution.py:1362
  35.0 11.7 %collective-permute-start.10 = (bf16[168,768]{1,0:T(8,128)(2,1)S(1)}, bf16[168,768]{1,0:T(8,128)(2,1)S(1)}, u32[]{:S(2)}, u32[]{:S(2)}) collective-permute-start(bf16[168,768]{1,0:T(8,128)(2,1)S(1)} %fusion.2), channel_id=1, source_target_pairs={{0,4},{1,3},{4,8},{5,1},{8,12},{9,5},{12,14},{13,9},{14,10},{15,13... | collective-permute-start | bytes 774152 | tf_op jit(solution)/shard_map/ppermute | solution.py:1362
  37.1 10.6 %collective-permute-start.3 = (bf16[2,168,768]{2,1,0:T(8,128)(2,1)}, bf16[2,168,768]{2,1,0:T(8,128)(2,1)S(1)}, u32[]{:S(2)}, u32[]{:S(2)}) collective-permute-start(bf16[2,168,768]{2,1,0:T(8,128)(2,1)} %pad_maximum_fusion.3.rest_1_), channel_id=1, source_target_pairs={{0,1},{1,0},{4,5},{5,4},{8,9},{9,8},{12,13},{13,12},{14,15},{15,14... | collective-permute-start | bytes 1548296 | tf_op jit(solution)/shard_map/ppermute | solution.py:1353
  37.1 11.4 %collective-permute-start.5 = (bf16[2,168,768]{2,1,0:T(8,128)(2,1)}, bf16[2,168,768]{2,1,0:T(8,128)(2,1)S(1)}, u32[]{:S(2)}, u32[]{:S(2)}) collective-permute-start(bf16[2,168,768]{2,1,0:T(8,128)(2,1)} %collective-permute-done.4.rest_3_), channel_id=1, source_target_pairs={{0,1},{1,0},{4,5},{5,4},{8,9},{9,8},{12,13},{13,12},{14,15},{15,14... | collective-permute-start | bytes 1548296 | tf_op jit(solution)/shard_map/ppermute | solution.py:1363
  37.6 14.9 %collective-permute-start.9 = (bf16[2,168,768]{2,1,0:T(8,128)(2,1)S(1)}, bf16[2,168,768]{2,1,0:T(8,128)(2,1)}, u32[]{:S(2)}, u32[]{:S(2)}) collective-permute-start(bf16[2,168,768]{2,1,0:T(8,128)(2,1)S(1)} %collective-permute-done.8.rest_5_), channel_id=1, source_target_pairs={{0,1},{1,0},{4,5},{5,4},{8,9},{9,8},{12,13},{13,12},{14,15},{15,14... | collective-permute-start | bytes 1548296 | tf_op jit(solution)/shard_map/ppermute | solution.py:1363
  44.1 21.0 %collective-permute-start.15 = (bf16[2,272,768]{2,1,0:T(8,128)(2,1)}, bf16[2,272,768]{2,1,0:T(8,128)(2,1)}, u32[]{:S(2)}, u32[]{:S(2)}) collective-permute-start(bf16[2,272,768]{2,1,0:T(8,128)(2,1)} %collective-permute-done.13.rest_10_.rest_1_.rest_13_), channel_id=1, source_target_pairs={{0,4},{1,3},{4,8},{5,1},{8,12},{9,5},{12,14},{13,9},{14,10},{15,13... | collective-permute-start | bytes 2506760 | tf_op jit(solution)/shard_map/ppermute | solution.py:1362
  47.6 33.7 %collective-permute-start.21 = (bf16[2,192,768]{2,1,0:T(8,128)(2,1)}, bf16[2,192,768]{2,1,0:T(8,128)(2,1)}, u32[]{:S(2)}, u32[]{:S(2)}) collective-permute-start(bf16[2,192,768]{2,1,0:T(8,128)(2,1)} %collective-permute-done.7.rest_19_.rest_22_), channel_id=1, source_target_pairs={{0,1},{1,0},{4,5},{5,4},{8,9},{9,8},{12,13},{13,12},{14,15},{15,14... | collective-permute-start | bytes 1769480 | tf_op jit(solution)/shard_map/ppermute | solution.py:1363
  49.3 38.2 %collective-permute-start.14 = (bf16[2,272,768]{2,1,0:T(8,128)(2,1)}, bf16[2,272,768]{2,1,0:T(8,128)(2,1)}, u32[]{:S(2)}, u32[]{:S(2)}) collective-permute-start(bf16[2,272,768]{2,1,0:T(8,128)(2,1)} %collective-permute-done.13.rest_10_.rest_1_.rest_13_), channel_id=1, source_target_pairs={{0,1},{1,0},{4,5},{5,4},{8,9},{9,8},{12,13},{13,12},{14,15},{15,14... | collective-permute-start | bytes 2506760 | tf_op jit(solution)/shard_map/ppermute | solution.py:1363
  50.5 26.8 %collective-permute-start.22 = (bf16[2,192,768]{2,1,0:T(8,128)(2,1)}, bf16[2,192,768]{2,1,0:T(8,128)(2,1)}, u32[]{:S(2)}, u32[]{:S(2)}) collective-permute-start(bf16[2,192,768]{2,1,0:T(8,128)(2,1)} %collective-permute-done.7.rest_19_.rest_22_), channel_id=1, source_target_pairs={{0,4},{1,3},{4,8},{5,1},{8,12},{9,5},{12,14},{13,9},{14,10},{15,13... | collective-permute-start | bytes 1769480 | tf_op jit(solution)/shard_map/ppermute | solution.py:1362
  60.1 17.2 %all-to-all-start = ((bf16[16,48,128]{2,1,0:T(8,128)(2,1)}), bf16[16,48,128]{2,1,0:T(8,128)(2,1)}, u32[]{:S(2)}, u32[]{:S(2)}) async-start(bf16[16,48,128]{2,1,0:T(8,128)(2,1)} %get-tuple-element.82), calls=%async_computation | async-start | bytes 393216 | tf_op jit(solution)/shard_map/all_to_all | solution.py:1418
  65.1 14.5 %collective-permute-start.17 = (bf16[2,272,768]{2,1,0:T(8,128)(2,1)}, bf16[2,272,768]{2,1,0:T(8,128)(2,1)}, u32[]{:S(2)}, u32[]{:S(2)}) collective-permute-start(bf16[2,272,768]{2,1,0:T(8,128)(2,1)} %collective-permute-done.15.rest_12_.rest_3_.rest_15_), channel_id=1, source_target_pairs={{0,4},{1,3},{4,8},{5,1},{8,12},{9,5},{12,14},{13,9},{14,10},{15,13... | collective-permute-start | bytes 2506760 | tf_op jit(solution)/shard_map/ppermute | solution.py:1362
  77.3 10.1 %collective-permute-start.24 = (bf16[2,192,768]{2,1,0:T(8,128)(2,1)}, bf16[2,192,768]{2,1,0:T(8,128)(2,1)S(1)}, u32[]{:S(2)}, u32[]{:S(2)}) collective-permute-start(bf16[2,192,768]{2,1,0:T(8,128)(2,1)} %collective-permute-done.22.rest_21_.rest_24_), channel_id=1, source_target_pairs={{0,4},{1,3},{4,8},{5,1},{8,12},{9,5},{12,14},{13,9},{14,10},{15,13... | collective-permute-start | bytes 1769480 | tf_op jit(solution)/shard_map/ppermute | solution.py:1362
  78.8 10.7 %collective-permute-start.23 = (bf16[2,192,768]{2,1,0:T(8,128)(2,1)}, bf16[2,192,768]{2,1,0:T(8,128)(2,1)S(1)}, u32[]{:S(2)}, u32[]{:S(2)}) collective-permute-start(bf16[2,192,768]{2,1,0:T(8,128)(2,1)} %collective-permute-done.22.rest_21_.rest_24_), channel_id=1, source_target_pairs={{0,1},{1,0},{4,5},{5,4},{8,9},{9,8},{12,13},{13,12},{14,15},{15,14... | collective-permute-start | bytes 1769480 | tf_op jit(solution)/shard_map/ppermute | solution.py:1363
  79.6 16.1 %collective-permute-start.16 = (bf16[2,272,768]{2,1,0:T(8,128)(2,1)}, bf16[2,272,768]{2,1,0:T(8,128)(2,1)S(1)}, u32[]{:S(2)}, u32[]{:S(2)}) collective-permute-start(bf16[2,272,768]{2,1,0:T(8,128)(2,1)} %collective-permute-done.15.rest_12_.rest_3_.rest_15_), channel_id=1, source_target_pairs={{0,1},{1,0},{4,5},{5,4},{8,9},{9,8},{12,13},{13,12},{14,15},{15,14... | collective-permute-start | bytes 2506760 | tf_op jit(solution)/shard_map/ppermute | solution.py:1363
  81.4 10.5 %collective-permute-start.19 = (bf16[272,768]{1,0:T(8,128)(2,1)S(1)}, bf16[272,768]{1,0:T(8,128)(2,1)S(1)}, u32[]{:S(2)}, u32[]{:S(2)}) collective-permute-start(bf16[272,768]{1,0:T(8,128)(2,1)S(1)} %fusion), channel_id=1, source_target_pairs={{0,4},{1,3},{4,8},{5,1},{8,12},{9,5},{12,14},{13,9},{14,10},{15,13... | collective-permute-start | bytes 1253384 | tf_op jit(solution)/shard_map/ppermute | solution.py:1362
  87.5 10.9 %collective-permute-start.18 = (bf16[2,272,768]{2,1,0:T(8,128)(2,1)}, bf16[2,272,768]{2,1,0:T(8,128)(2,1)}, u32[]{:S(2)}, u32[]{:S(2)}) collective-permute-start(bf16[2,272,768]{2,1,0:T(8,128)(2,1)} %collective-permute-done.17.rest_14_.rest_5_.rest_17_), channel_id=1, source_target_pairs={{0,1},{1,0},{4,5},{5,4},{8,9},{9,8},{12,13},{13,12},{14,15},{15,14... | collective-permute-start | bytes 2506760 | tf_op jit(solution)/shard_map/ppermute | solution.py:1363
  87.5 7.6 %collective-permute-start.26 = (bf16[192,768]{1,0:T(8,128)(2,1)S(1)}, bf16[192,768]{1,0:T(8,128)(2,1)S(1)}, u32[]{:S(2)}, u32[]{:S(2)}) collective-permute-start(bf16[192,768]{1,0:T(8,128)(2,1)S(1)} %fusion.1), channel_id=1, source_target_pairs={{0,4},{1,3},{4,8},{5,1},{8,12},{9,5},{12,14},{13,9},{14,10},{15,13... | collective-permute-start | bytes 884744 | tf_op jit(solution)/shard_map/ppermute | solution.py:1362
  128.2 21.4 %all-to-all-start.1 = ((bf16[16,160,128]{2,1,0:T(8,128)(2,1)}), bf16[16,160,128]{2,1,0:T(8,128)(2,1)}, u32[]{:S(2)}, u32[]{:S(2)}) async-start(bf16[16,160,128]{2,1,0:T(8,128)(2,1)} %bitcast.62), calls=%async_computation.1 | async-start | bytes 1310720 | tf_op jit(solution)/shard_map/all_to_all | solution.py:1437
  (24 other events, 153.1 us)

commit v5 on v4

--- a/solution.py
+++ b/solution.py
@@ -350,7 +350,7 @@
 VMEM = pl.BlockSpec(memory_space=pltpu.VMEM)
 SMEM = pl.BlockSpec(memory_space=pltpu.SMEM)
 SCALE = float(HD) ** -0.5
-PAYLOAD = 160
+PAYLOAD = 128
 
 
 def call(kernel, name, ins, outs, scratch, flops=0, touched=0):
@@ -577,18 +577,20 @@
     )
 
 
-def pooled_kernel(lengths, tok, *rest):
+def pooled_kernel(lengths, tok_hbm, *rest):
     first, outs, scratch = rest[:9], rest[9:18], rest[18:]
     keys_hbm, values_hbm, norm_hbm, normed_hbm, vec, pooled, q_own, probs_out, gv_out = outs
-    weights, small, normed, keys, values, norm_low, sems, ends = scratch
+    weights, small, tok, normed, keys, values, norm_low, sems, ends = scratch
     here = Place(lengths)
     owners = owner_table(here.dp)
+    tok_in = copy(tok_hbm, tok, sems.at[2])
     fetch(owners, first, 152, 16, small, sems.at[0])
     fetch(owners, first, 0, 144, weights, sems.at[1])
     keep, winv = here.keep, here.winv
     drain(small, sems.at[0])
     vec[...] = jnp.sum(small[...].astype(F32), axis=0)
     limit = sample_limits(here)
+    tok_in.wait()
     sub = lax.broadcasted_iota(jnp.int32, (8, DI), 0)
     picked = jnp.zeros((8, DI), F32)
     for s in range(8):
@@ -648,7 +650,7 @@
     return call(
         pooled_kernel,
         "attend_pooled",
-        [(SMEM, lengths), (VMEM, tok)] + [(ANY, r) for r in first],
+        [(SMEM, lengths), (ANY, tok)] + [(ANY, r) for r in first],
         [(ANY, (rows, DI), BF16)] * 4
         + [
             (VMEM, (16, DI), F32),
@@ -660,11 +662,12 @@
         [
             pltpu.VMEM((ITEMS, 144, DI), BF16),
             pltpu.VMEM((ITEMS, 16, DI), BF16),
+            pltpu.VMEM(tok.shape, BF16),
             pltpu.VMEM((rows, DI), BF16),
             pltpu.VMEM((rows, DI), BF16),
             pltpu.VMEM((rows, DI), BF16),
             pltpu.VMEM((rows, DI), BF16),
-            pltpu.SemaphoreType.DMA((2,)),
+            pltpu.SemaphoreType.DMA((3,)),
             pltpu.SemaphoreType.DMA((4,)),
         ],
         flops=7_000_000_000,
@@ -673,8 +676,8 @@
 
 
 def attend_kernel(lengths, vec, gv, normed_hbm, keys_hbm, values_hbm, norm_hbm, *rest):
-    first, (mixed, z_value), scratch = rest[:9], rest[9:11], rest[11:]
-    weights, normed, keys, values, norm_low, qf, kf, vf, mf, sems = scratch
+    first, (mixed_hbm, z_value), scratch = rest[:9], rest[9:11], rest[11:]
+    weights, normed, keys, values, norm_low, mixed, qf, kf, vf, mf, sems = scratch
     here = Place(lengths)
     owners = owner_table(here.dp)
     fetch(owners, first, 0, 48, weights, sems.at[0])
@@ -685,8 +688,9 @@
         )
     ]
     drain(weights, sems.at[0])
-    for item in early:
-        item.wait()
+    early[0].wait()
+    early[1].wait()
+    early[2].wait()
 
     def path(width, count):
         rows = count * 8
@@ -731,9 +735,15 @@
                 out = dot(probs[pair], vf.at[pair][at, :].astype(BF16), 0, 0)
                 mf.at[pair][at, :] = jnp.where(low_half, out[0:span], out[span : 2 * span])
 
+        stored = []
         for i in range(width // 128):
-            mixed[0:rows, 128 * i : 128 * i + 128] = mf[i, 0:rows, :].astype(BF16)
-        z_value[...] = dot(norm_low[0:rows, :], gv[0:rows, :], 0, 0).astype(BF16)
+            lanes = pl.ds(128 * i, 128)
+            mixed[0:rows, lanes] = mf[i, 0:rows, :].astype(BF16)
+            stored.append(copy(mixed.at[0:rows, lanes], mixed_hbm.at[0:rows, lanes], sems.at[5 + i]))
+        early[3].wait()
+        z_value[...] = pltpu.roll(dot(norm_low[0:rows, :], gv[0:rows, :], 0, 0), 96, 1).astype(BF16)
+        for item in stored:
+            item.wait()
 
     here.either(path, 56)
 
@@ -746,9 +756,10 @@
         "attend",
         [(SMEM, lengths), (VMEM, vec), (VMEM, gv)]
         + [(ANY, r) for r in (normed, keys, values, norm_low, *first)],
-        [(VMEM, (rows, DI), BF16), (VMEM, (DI, 128), BF16)],
+        [(ANY, (rows, DI), BF16), (VMEM, (DI, 128), BF16)],
         [
             pltpu.VMEM((ITEMS, 48, DI), BF16),
+            pltpu.VMEM((rows, DI), BF16),
             pltpu.VMEM((rows, DI), BF16),
             pltpu.VMEM((rows, DI), BF16),
             pltpu.VMEM((rows, DI), BF16),
@@ -757,7 +768,7 @@
             pltpu.VMEM((6, high, 128), F32),
             pltpu.VMEM((6, high, 128), F32),
             pltpu.VMEM((6, high, 128), F32),
-            pltpu.SemaphoreType.DMA((5,)),
+            pltpu.SemaphoreType.DMA((11,)),
         ],
         flops=9_000_000_000,
         touched=10_000_000,
@@ -928,6 +939,27 @@
     grad = (jnp.exp(logits - total) - hot) * 0.5
     scale = jnp.sum(jnp.sum(grad * sims, axis=-1, keepdims=True), axis=0, keepdims=True)
     return lost, scale, mult * grad
+
+
+def pack_payload(payload, z_key, z_value, sum_key, sum_value, grad_q):
+    lane = lax.broadcasted_iota(jnp.int32, (1, 128), 1)
+    upper = jnp.where(lane < 96, z_key, z_value).astype(BF16)
+    blocks = [grad_q[:, i * 128 : (i + 1) * 128] for i in range(6)]
+    beside = jnp.concatenate(
+        [half for block in blocks[:3] for half in (pltpu.roll(block, 64, 1), block)], axis=0
+    )
+    key_high = sum_key.astype(BF16).astype(F32)
+    value_high = sum_value.astype(BF16).astype(F32)
+    row_id = lax.broadcasted_iota(jnp.int32, (8, 128), 0)
+    sums = jnp.zeros((8, 128), F32)
+    for at, value in enumerate((key_high, sum_key - key_high, value_high, sum_value - value_high)):
+        sums = jnp.where(row_id == at, jnp.broadcast_to(value, (8, 128)), sums)
+    last = jnp.concatenate([*blocks[3:], sums], axis=0).astype(BF16)
+    for owner in range(ITEMS):
+        base, rows = owner * PAYLOAD, slice(owner * 48, owner * 48 + 48)
+        payload[base : base + 48, :] = upper[rows]
+        payload[base + 48 : base + 96, :] = jnp.where(lane < 64, z_value[rows], beside).astype(BF16)
+        payload[base + 96 : base + 128, :] = last
 
 
 def chain_kernel(lengths, log_mult, e_own_ref, e_oth_ref, vec, head_sl, act_sl, n2_sl, mix_sl, *rest):
@@ -1049,25 +1081,15 @@
         gk_out[0:rows, :] = gk
         gq_low = own_heads(dot(gk, keys[0:rows, 0:width], 0, 0) * SCALE, width).astype(BF16)
         gq_out[...] = gq_low
-        norm = norm_low[0:rows, :]
-        z_key = dot(norm, gk, 0, 0).astype(BF16)
-        z_value = z_v[...]
-        sum_key = row_sum(gk.astype(F32))
-        sum_value = row_sum(gv.astype(F32))
-        key_high = sum_key.astype(BF16).astype(F32)
-        value_high = sum_value.astype(BF16).astype(F32)
-        row_id = lax.broadcasted_iota(jnp.int32, (16, 128), 0)
-        sums = jnp.zeros((16, 128), F32)
-        for at, value in enumerate((key_high, sum_key - key_high, value_high, sum_value - value_high)):
-            sums = jnp.where(row_id == at, jnp.broadcast_to(value, (16, 128)), sums)
-        sums = sums.astype(BF16)
-        gq_tall = tall_rows(gq_low.astype(F32)).astype(BF16)
-        for owner in range(ITEMS):
-            base = owner * PAYLOAD
-            payload[base : base + 48, :] = z_key[owner * 48 : owner * 48 + 48]
-            payload[base + 48 : base + 64, :] = sums
-            payload[base + 64 : base + 112, :] = z_value[owner * 48 : owner * 48 + 48]
-            payload[base + 112 : base + 160, :] = gq_tall
+        z_key = dot(norm_low[0:rows, :], gk, 0, 0)
+        pack_payload(
+            payload,
+            z_key,
+            z_v[...].astype(F32),
+            row_sum(gk.astype(F32)),
+            pltpu.roll(jnp.broadcast_to(row_sum(gv.astype(F32)), (8, 128)), 96, 1)[0:1],
+            gq_low.astype(F32),
+        )
 
     here.either(path, 56)
     for item in stored:
@@ -1136,8 +1158,8 @@
 
 def close_kernel(lengths, tok, vec, gk, gv, q_own, gm_own, gq, mid_own, n2_hbm, middle_hbm, *rest):
     first, second, down = rest[:9], rest[9:18], rest[18:27]
-    (block_out, out, q_out, norm_sl), scratch = rest[27:31], rest[31:]
-    weights, w_fc, w_down, n2, act, middle, acc, xs, norm1_all, sems = scratch
+    (block_out, out_hbm, q_out, norm_sl), scratch = rest[27:31], rest[31:]
+    weights, w_fc, w_down, n2, act, middle, acc, xs, norm1_all, out, sems = scratch
     here = Place(lengths)
     owners = owner_table(here.dp)
     fetch(owners, first, 0, 144, weights, sems.at[0])
@@ -1169,9 +1191,10 @@
             back = normalize_back(total, vec[0:1, :], norm, inv, keep, winv)
             out[at, :] = back + jnp.where(hit, mid_own[...][None], 0.0).reshape(count * 8, DI)
 
-        chunks(count, back_chunk)
         if rows < all_rows:
             out[rows:all_rows, :] = jnp.zeros((all_rows - rows, DI), F32)
+        chunks(count, back_chunk)
+        stored = copy(out, out_hbm, sems.at[6])
         short = count if width == DT else IMG_ROWS
         rows = short * 8
         ready.wait()
@@ -1203,6 +1226,7 @@
             block_out[:, width:DI] = jnp.zeros((all_rows, DI - width), BF16)
         if rows < all_rows:
             block_out[rows:all_rows, :] = jnp.zeros((all_rows - rows, DI), BF16)
+        stored.wait()
 
     here.either(path, 56)
     drain(xs, sems.at[5])
@@ -1226,7 +1250,7 @@
         [(SMEM, lengths)]
         + [(VMEM, item) for item in (tok, vec, gk, gv, q_own, gm_own, gq, mid_own)]
         + [(ANY, r) for r in (n2, middle, *first, *second, *down)],
-        [(VMEM, (rows, DI), BF16), (VMEM, (rows, DI), F32), (VMEM, (N, DI), F32), (VMEM, (N, 48), BF16)],
+        [(VMEM, (rows, DI), BF16), (ANY, (rows, DI), F32), (VMEM, (N, DI), F32), (VMEM, (N, 48), BF16)],
         [
             pltpu.VMEM((ITEMS, 144, DI), BF16),
             pltpu.VMEM((ITEMS, 192, DI), BF16),
@@ -1237,28 +1261,35 @@
             pltpu.VMEM((rows, DI), F32),
             pltpu.VMEM((ITEMS, 8, DI), BF16),
             pltpu.VMEM((N, DI), BF16),
-            pltpu.SemaphoreType.DMA((6,)),
+            pltpu.VMEM((rows, DI), F32),
+            pltpu.SemaphoreType.DMA((7,)),
         ],
         flops=17_000_000_000,
         touched=18_000_000,
     )
 
 
-def shard_kernel(got, q_all, gm_all, norm_sl, w_own, gain, bias, d_qkv, g_one, b_one, qv_out, turned, product):
+def shard_kernel(got, q_all, gm_all, norm_sl, w_own, gain, bias, d_qkv, g_one, b_one, qv_out, by_keys, by_values, product):
     dp = lax.axis_index("dp")
 
     low_half = lax.broadcasted_iota(jnp.int32, (N, 128), 1) < HD
 
-    def moments(start, source):
-        for j in range(ITEMS):
-            turned[j] = got[j, start : start + 64, :].astype(F32).T
+    for j in range(ITEMS):
+        found = got[j].astype(F32)
+        upper = jnp.concatenate([found[0:48], found[120:128]], axis=0).T
+        lower = jnp.concatenate([found[48:96], found[120:128]], axis=0).T
+        by_keys[j] = upper[0:96]
+        by_values[j, 0:32, :] = upper[96:128]
+        by_values[j, 32:96, :] = lower[0:64]
+
+    def moments(turned, source):
         for pair in range(DI // 128):
             lanes = slice(pair * 128, pair * 128 + 128)
             rows = source[:, lanes]
             both = [jnp.where(low_half, rows, 0.0), jnp.where(low_half, 0.0, rows)]
             both = [half.reshape(ITEMS, 8, 128) for half in both]
             both = jnp.concatenate(both, axis=1).reshape(2 * N, 128).astype(BF16)
-            part = turned[:, pair * 16 : pair * 16 + 16, :].reshape(2 * N, 64).astype(BF16)
+            part = turned[:, pair * 16 : pair * 16 + 16, :].reshape(2 * N, 56).astype(BF16)
             product[:, lanes] = dot(part, both, 0, 0)
         return product[...]
 
@@ -1267,11 +1298,19 @@
         same = lax.broadcasted_iota(jnp.int32, square, 0) == lax.broadcasted_iota(jnp.int32, square, 1)
         return jnp.sum(jnp.where(same, row[...].astype(F32), 0.0), axis=1, keepdims=True)
 
-    by_key = moments(0, q_all) * SCALE
+    by_key = moments(by_keys, q_all) * SCALE
     m_key, s_key = by_key[0:48], by_key[48:49] + by_key[49:50]
-    by_value = moments(48, gm_all)
-    m_value, s_value = by_value[16:64], by_value[2:3] + by_value[3:4]
-    grad_q = wide_rows(got[:, 112:160, :])
+    by_value = moments(by_values, gm_all)
+    m_value, s_value = by_value[0:48], by_value[50:51] + by_value[51:52]
+    beside = got[:, 48:96, :].astype(F32)
+    last = got[:, 96:128, :].astype(F32)
+    lane = lax.broadcasted_iota(jnp.int32, (1, 1, 128), 2)
+    blocks = []
+    for i in range(3):
+        low = pltpu.roll(beside[:, 16 * i : 16 * i + 8, :], 64, 2)
+        blocks.append(jnp.where(lane < 64, low, beside[:, 16 * i + 8 : 16 * i + 16, :]).reshape(N, 128))
+    blocks += [last[:, 8 * i : 8 * i + 8, :].reshape(N, 128) for i in range(3)]
+    grad_q = jnp.concatenate(blocks, axis=1)
     s_query = row_sum(grad_q)
     m_query = dot(norm_sl[...], grad_q.astype(BF16), 0, 0)
     gain_col, bias_col = column(gain), column(bias)
@@ -1309,7 +1348,11 @@
             (VMEM, (1, 48), F32),
             (VMEM, (2, 48), F32),
         ],
-        [pltpu.VMEM((ITEMS, 128, 64), F32), pltpu.VMEM((64, DI), F32)],
+        [
+            pltpu.VMEM((ITEMS, 96, 56), F32),
+            pltpu.VMEM((ITEMS, 96, 56), F32),
+            pltpu.VMEM((56, DI), F32),
+        ],
         flops=5_000_000_000,
         touched=2_000_000,
     )

time: 154 us -> 151 us (0.981)
  transfers between devices with their start and end apart: 31 -> 31, of which waited for: 12 -> 11; matrix products, arithmetic and copies ran while one was open for 4% -> 4% of each run, Pallas kernels for 28% -> 27%
where the time goes in v5:
time: 151 us
  Pallas kernels  67.7 us (45%)
  starting transfers between devices  40 us (26%)
  waiting for transfers between devices  30.8 us (20%)
  other arithmetic  6.11 us (4%)
  local copies, waits for them, and re-layouts  4.38 us (3%)
  between operations  1.59 us (1%)
    pallas_call x9, Pallas kernels, call(): pl.pallas_call(kernel, name=name, out_shape=[jax.ShapeDtypeStruct(shape,...  67.7 us
    ppermute x11, waiting for transfers between devices, step(): held = lax.ppermute(after(held, *earlier), BOTH, self.turn)  28.4 us
    ppermute x11, starting transfers between devices, step(): held = lax.ppermute(after(held, *earlier), BOTH, self.turn)  21.6 us
    all_to_all x1, starting transfers between devices, ring_body(): mixes = lax.all_to_all(pooled, 'dp', 0, 0, tiled=True)  4.98 us
    another operation x8, other arithmetic, joined(): jnp.stack([jnp.where(self.first_core, own, other), jnp.where(self.first_c...  4.88 us
    all_to_all x1, starting transfers between devices, ring_body(): lax.all_to_all(payload, 'dp', 0, 0, tiled=True).reshape(ITEMS, PAYLOAD, 128)  4.79 us
    ppermute x2, starting transfers between devices, first_step(): lax.ppermute(item, BOTH, self.turn)  4.6 us
    unnamed x34, local copies, waits for them, and re-layouts  4.38 us
  transfers between devices with their start and end apart: 31, of which 11 were waited for; matrix products, arithmetic and copies ran while one was open for 4% of the time, Pallas kernels for 27%

profile of v5, /device:TPU:0, one launch (start us, length us, event | category | flops | bytes accessed | tf_op | source)
XLA Modules:
  0.0 150.5 jit_solution(229896445936411999)
XLA Ops:
  1.2 2.2 %pack_first.1 = bf16[168,768]{1,0:T(8,128)(2,1)} custom-call(s32[8]{0:T(128)} %lengths.13, bf16[144,768]{1,0:T(8,128)(2,1)} %bitcast.65, bf16[77,8,768]{2,1,0:T(8,128)(2,1)} %bitcast.58, bf16[1,48]{1,0:T(2,128)(2,1)} %gain.1, bf16[1,48]{1,0:T(2,128)(2,1)} %bias.1, bf16[1,48]{1,0:T(2,128)(2,1)} %rest_2_.1, bf16[1,48]{1,0:T(2,128)(2,1)} %rest_3_.1, ...), custom_call_target="tpu_custom_call" | custom-call | bytes 1500000 | tf_op jit(solution)/shard_map/pack_first/pallas_call | solution.py:357
  3.4 3.0 %collective-permute-start.1 = (bf16[168,768]{1,0:T(8,128)(2,1)}, bf16[168,768]{1,0:T(8,128)(2,1)S(1)}, u32[]{:S(2)}, u32[]{:S(2)}) collective-permute-start(bf16[168,768]{1,0:T(8,128)(2,1)} %pack_first.1), channel_id=1, source_target_pairs={{0,4},{1,3},{4,8},{5,1},{8,12},{9,5},{12,14},{13,9},{14,10},{15,13... | collective-permute-start | bytes 774152 | tf_op jit(solution)/shard_map/ppermute | solution.py:1395
  11.5 2.1 %collective-permute-done.2 = bf16[168,768]{1,0:T(8,128)(2,1)S(1)} collective-permute-done((bf16[168,768]{1,0:T(8,128)(2,1)S(1)}, bf16[168,768]{1,0:T(8,128)(2,1)S(1)}, u32[]{:S(2)}, u32[]{:S(2)}) %collective-permute-start.2) | collective-permute-done | bytes 258080 | tf_op jit(solution)/shard_map/ppermute | solution.py:1395
  14.5 2.1 %collective-permute-start.4 = (bf16[2,168,768]{2,1,0:T(8,128)(2,1)}, bf16[2,168,768]{2,1,0:T(8,128)(2,1)}, u32[]{:S(2)}, u32[]{:S(2)}) collective-permute-start(bf16[2,168,768]{2,1,0:T(8,128)(2,1)} %pad_maximum_fusion.3.rest_1_), channel_id=1, source_target_pairs={{0,4},{1,3},{4,8},{5,1},{8,12},{9,5},{12,14},{13,9},{14,10},{15,13... | collective-permute-start | bytes 1548296 | tf_op jit(solution)/shard_map/ppermute | solution.py:1405
  20.2 5.5 %collective-permute-done.4.rest_3_ = bf16[2,168,768]{2,1,0:T(8,128)(2,1)} collective-permute-done((bf16[2,168,768]{2,1,0:T(8,128)(2,1)}, bf16[2,168,768]{2,1,0:T(8,128)(2,1)}, u32[]{:S(2)}, u32[]{:S(2)}) %collective-permute-start.4) | collective-permute-done | bytes 516128 | tf_op jit(solution)/shard_map/ppermute | solution.py:1405
  25.7 2.0 %collective-permute-start.8 = (bf16[2,168,768]{2,1,0:T(8,128)(2,1)}, bf16[2,168,768]{2,1,0:T(8,128)(2,1)S(1)}, u32[]{:S(2)}, u32[]{:S(2)}) collective-permute-start(bf16[2,168,768]{2,1,0:T(8,128)(2,1)} %collective-permute-done.4.rest_3_), channel_id=1, source_target_pairs={{0,4},{1,3},{4,8},{5,1},{8,12},{9,5},{12,14},{13,9},{14,10},{15,13... | collective-permute-start | bytes 1548296 | tf_op jit(solution)/shard_map/ppermute | solution.py:1405
  30.5 4.5 %collective-permute-done.8.rest_5_ = bf16[2,168,768]{2,1,0:T(8,128)(2,1)S(1)} collective-permute-done((bf16[2,168,768]{2,1,0:T(8,128)(2,1)}, bf16[2,168,768]{2,1,0:T(8,128)(2,1)S(1)}, u32[]{:S(2)}, u32[]{:S(2)}) %collective-permute-start.8) | collective-permute-done | bytes 516128 | tf_op jit(solution)/shard_map/ppermute | solution.py:1405
  35.0 2.0 %collective-permute-start.10 = (bf16[168,768]{1,0:T(8,128)(2,1)S(1)}, bf16[168,768]{1,0:T(8,128)(2,1)S(1)}, u32[]{:S(2)}, u32[]{:S(2)}) collective-permute-start(bf16[168,768]{1,0:T(8,128)(2,1)S(1)} %fusion.2), channel_id=1, source_target_pairs={{0,4},{1,3},{4,8},{5,1},{8,12},{9,5},{12,14},{13,9},{14,10},{15,13... | collective-permute-start | bytes 774152 | tf_op jit(solution)/shard_map/ppermute | solution.py:1405
  37.6 6.5 %collective-permute-done.13.rest_10_.rest_1_.rest_13_ = bf16[2,272,768]{2,1,0:T(8,128)(2,1)} collective-permute-done((bf16[2,272,768]{2,1,0:T(8,128)(2,1)S(1)}, bf16[2,272,768]{2,1,0:T(8,128)(2,1)}, u32[]{:S(2)}, u32[]{:S(2)}) %collective-permute-start.13) | collective-permute-done | bytes 835616 | tf_op jit(solution)/shard_map/ppermute | solution.py:1405
  44.1 2.0 %collective-permute-start.15 = (bf16[2,272,768]{2,1,0:T(8,128)(2,1)}, bf16[2,272,768]{2,1,0:T(8,128)(2,1)}, u32[]{:S(2)}, u32[]{:S(2)}) collective-permute-start(bf16[2,272,768]{2,1,0:T(8,128)(2,1)} %collective-permute-done.13.rest_10_.rest_1_.rest_13_), channel_id=1, source_target_pairs={{0,4},{1,3},{4,8},{5,1},{8,12},{9,5},{12,14},{13,9},{14,10},{15,13... | collective-permute-start | bytes 2506760 | tf_op jit(solution)/shard_map/ppermute | solution.py:1405
  52.5 7.2 %attend_pooled.1 = (bf16[616,768]{1,0:T(8,128)(2,1)}, bf16[616,768]{1,0:T(8,128)(2,1)}, bf16[616,768]{1,0:T(8,128)(2,1)}, bf16[616,768]{1,0:T(8,128)(2,1)}, f32[...) custom-call(s32[8]{0:T(128)} %lengths.13, ...), custom_call_target="tpu_custom_call" | custom-call | flops 7000000000 | bytes 10000000 | tf_op jit(solution)/shard_map/attend_pooled/pallas_call | solution.py:357
  59.7 5.0 %all-to-all-start = ((bf16[16,48,128]{2,1,0:T(8,128)(2,1)}), bf16[16,48,128]{2,1,0:T(8,128)(2,1)}, u32[]{:S(2)}, u32[]{:S(2)}) async-start(bf16[16,48,128]{2,1,0:T(8,128)(2,1)} %get-tuple-element.82), calls=%async_computation | async-start | bytes 393216 | tf_op jit(solution)/shard_map/all_to_all | solution.py:1461
  66.7 10.1 %attend.1 = (bf16[616,768]{1,0:T(8,128)(2,1)}, bf16[768,128]{1,0:T(8,128)(2,1)}) custom-call(s32[8]{0:T(128)} %lengths.13, f32[16,768]{1,0:T(8,128)} %get-tuple-element.81.vec, bf16[616,128]{1,0:T(8,128)(2,1)} %get-tuple-element.86.gv.rest_10_, bf16[616,768]{1,0:T(8,128)(2,1)} %get-tuple-element.88.normed_hbm, ...), custom_call_target="tpu_custom_call" | custom-call | flops 8999999488 | bytes 10000000 | tf_op jit(solution)/shard_map/attend/pallas_call | solution.py:357
  81.0 2.8 %collective-permute-start.19 = (bf16[272,768]{1,0:T(8,128)(2,1)S(1)}, bf16[272,768]{1,0:T(8,128)(2,1)S(1)}, u32[]{:S(2)}, u32[]{:S(2)}) collective-permute-start(bf16[272,768]{1,0:T(8,128)(2,1)S(1)} %fusion), channel_id=1, source_target_pairs={{0,4},{1,3},{4,8},{5,1},{8,12},{9,5},{12,14},{13,9},{14,10},{15,13... | collective-permute-start | bytes 1253384 | tf_op jit(solution)/shard_map/ppermute | solution.py:1405
  83.8 3.1 %collective-permute-done.24.rest_23_.rest_26_ = bf16[2,192,768]{2,1,0:T(8,128)(2,1)S(1)} collective-permute-done((bf16[2,192,768]{2,1,0:T(8,128)(2,1)}, bf16[2,192,768]{2,1,0:T(8,128)(2,1)S(1)}, u32[]{:S(2)}, u32[]{:S(2)}) %collective-permute-start.24) | collective-permute-done | bytes 589856 | tf_op jit(solution)/shard_map/ppermute | solution.py:1405
  87.0 2.2 %collective-permute-start.26 = (bf16[192,768]{1,0:T(8,128)(2,1)S(1)}, bf16[192,768]{1,0:T(8,128)(2,1)S(1)}, u32[]{:S(2)}, u32[]{:S(2)}) collective-permute-start(bf16[192,768]{1,0:T(8,128)(2,1)S(1)} %fusion.1), channel_id=1, source_target_pairs={{0,4},{1,3},{4,8},{5,1},{8,12},{9,5},{12,14},{13,9},{14,10},{15,13... | collective-permute-start | bytes 884744 | tf_op jit(solution)/shard_map/ppermute | solution.py:1405
  89.2 2.2 %collective-permute-done.19.rest_16_.rest_7_.rest_19_ = bf16[272,768]{1,0:T(8,128)(2,1)S(1)} collective-permute-done((bf16[272,768]{1,0:T(8,128)(2,1)S(1)}, bf16[272,768]{1,0:T(8,128)(2,1)S(1)}, u32[]{:S(2)}, u32[]{:S(2)}) %collective-permute-start.19) | collective-permute-done | bytes 417824 | tf_op jit(solution)/shard_map/ppermute | solution.py:1405
  91.4 3.2 %collective-permute-done.26.rest_25_.rest_28_ = bf16[192,768]{1,0:T(8,128)(2,1)S(1)} collective-permute-done((bf16[192,768]{1,0:T(8,128)(2,1)S(1)}, bf16[192,768]{1,0:T(8,128)(2,1)S(1)}, u32[]{:S(2)}, u32[]{:S(2)}) %collective-permute-start.26) | collective-permute-done | bytes 294944 | tf_op jit(solution)/shard_map/ppermute | solution.py:1405
  97.8 8.8 %pooled_forward.1 = (bf16[128,512]{1,0:T(8,128)(2,1)}, f32[128,512]{1,0:T(8,128)}, f32[128,768]{1,0:T(8,128)}, f32[128,128]{1,0:T(8,128)}, f32[128,768]{1,0:T(8,...) custom-call(s32[8]{0:T(128)} %lengths.13, ...), custom_call_target="tpu_custom_call" | custom-call | flops 11000000512 | bytes 16000000 | tf_op jit(solution)/shard_map/pooled_forward/pallas_call | solution.py:357
  107.7 5.0 %middle_part.1 = (bf16[616,768]{1,0:T(8,128)(2,1)}, f32[616,768]{1,0:T(8,128)}) custom-call(s32[8]{0:T(128)} %lengths.13, bf16[77,8,768]{2,1,0:T(8,128)(2,1)} %bitcast.60, f32[16,768]{1,0:T(8,128)} %get-tuple-element.81.vec, bf16[616,768]{1,0:T(8,128)(2,1)} %get-tuple-element.99.mixed_hbm, bf16[2,272,768]{2,1,0:T(8,128)(2,1)} %copy-done.1, ...), custom_call_target="tpu_custom_call" | custom-call | flops 5000000000 | bytes 8000000 | tf_op jit(solution)/shard_map/middle_part/pallas_call | solution.py:357
  113.0 14.6 %chain.1 = (f32[1,1]{1,0:T(1,128)}, f32[1,1]{1,0:T(1,128)}, f32[48,512]{1,0:T(8,128)}, f32[192,768]{1,0:T(8,128)}, f32[48,3072]{1,0:T(8,128)}, /*index=5*/f32[48...) custom-call(s32[8]{0:T(128)} %lengths.13, ...), custom_call_target="tpu_custom_call" | custom-call | flops 15000000512 | bytes 20000000 | tf_op jit(solution)/shard_map/chain/pallas_call | solution.py:357
  127.6 4.8 %all-to-all-start.1 = ((bf16[16,128,128]{2,1,0:T(8,128)(2,1)}), bf16[16,128,128]{2,1,0:T(8,128)(2,1)}, u32[]{:S(2)}, u32[]{:S(2)}) async-start(bf16[16,128,128]{2,1,0:T(8,128)(2,1)} %bitcast.62), calls=%async_computation.1 | async-start | bytes 1048576 | tf_op jit(solution)/shard_map/all_to_all | solution.py:1480
  132.4 14.8 %close.1 = (bf16[616,768]{1,0:T(8,128)(2,1)}, f32[616,768]{1,0:T(8,128)}, f32[128,768]{1,0:T(8,128)}, bf16[128,48]{1,0:T(8,128)(2,1)}) custom-call(s32[8]{0:T(128)} %lengths.13, bf16[77,8,768]{2,1,0:T(8,128)(2,1)} %bitcast.61, f32[16,768]{1,0:T(8,128)} %get-tuple-element.81.vec, bf16[616,128]{1,0:T(8,128)(2,1)} %get-tuple-element.113.gk, ...), custom_call_target="tpu_custom_call" | custom-call | flops 16999999488 | bytes 18000000 | tf_op jit(solution)/shard_map/close/pallas_call | solution.py:357
  147.3 3.2 %shard_grads.1 = (f32[3,48,768]{2,1,0:T(8,128)}, f32[1,48]{1,0:T(1,128)}, f32[1,48]{1,0:T(1,128)}, f32[2,48]{1,0:T(2,128)}) custom-call(bf16[16,128,128]{2,1,0:T(8,128)(2,1)} %all-to-all-done.1.got, f32[128,768]{1,0:T(8,128)} %get-tuple-element.122.q_all, f32[128,768]{1,0:T(8,128)} %get-tuple-element.123.gm_all, bf16[128,48]{1,0:T(8,128)(2,1)} %get-tuple-element.124.norm_sl, ...), custom_call_target="tpu_custom_call" | custom-call | flops 5000000000 | bytes 2000000 | tf_op jit(solution)/shard_map/shard_grads/pallas_call | solution.py:357
  (92 shorter events, 30.1 us)
Async XLA Ops:
  0.7 7.3 %collective-permute-start.6 = (bf16[192,768]{1,0:T(8,128)(2,1)}, bf16[192,768]{1,0:T(8,128)(2,1)}, u32[]{:S(2)}, u32[]{:S(2)}) collective-permute-start(bf16[192,768]{1,0:T(8,128)(2,1)} %bitcast.64), channel_id=1, source_target_pairs={{0,1},{1,0},{4,5},{5,4},{8,9},{9,8},{12,13},{13,12},{14,15},{15,14... | collective-permute-start | bytes 884744 | tf_op jit(solution)/shard_map/ppermute | solution.py:1386
  3.4 8.2 %collective-permute-start.1 = (bf16[168,768]{1,0:T(8,128)(2,1)}, bf16[168,768]{1,0:T(8,128)(2,1)S(1)}, u32[]{:S(2)}, u32[]{:S(2)}) collective-permute-start(bf16[168,768]{1,0:T(8,128)(2,1)} %pack_first.1), channel_id=1, source_target_pairs={{0,4},{1,3},{4,8},{5,1},{8,12},{9,5},{12,14},{13,9},{14,10},{15,13... | collective-permute-start | bytes 774152 | tf_op jit(solution)/shard_map/ppermute | solution.py:1395
  10.0 10.2 %collective-permute-start.7 = (bf16[2,192,768]{2,1,0:T(8,128)(2,1)}, bf16[2,192,768]{2,1,0:T(8,128)(2,1)}, u32[]{:S(2)}, u32[]{:S(2)}) collective-permute-start(bf16[2,192,768]{2,1,0:T(8,128)(2,1)} %pad_maximum_fusion.1.rest_18_.rest_21_), channel_id=1, source_target_pairs={{0,4},{1,3},{4,8},{5,1},{8,12},{9,5},{12,14},{13,9},{14,10},{15,13... | collective-permute-start | bytes 1769480 | tf_op jit(solution)/shard_map/ppermute | solution.py:1405
  14.5 11.2 %collective-permute-start.4 = (bf16[2,168,768]{2,1,0:T(8,128)(2,1)}, bf16[2,168,768]{2,1,0:T(8,128)(2,1)}, u32[]{:S(2)}, u32[]{:S(2)}) collective-permute-start(bf16[2,168,768]{2,1,0:T(8,128)(2,1)} %pad_maximum_fusion.3.rest_1_), channel_id=1, source_target_pairs={{0,4},{1,3},{4,8},{5,1},{8,12},{9,5},{12,14},{13,9},{14,10},{15,13... | collective-permute-start | bytes 1548296 | tf_op jit(solution)/shard_map/ppermute | solution.py:1405
  18.4 9.3 %collective-permute-start.12 = (bf16[272,768]{1,0:T(8,128)(2,1)}, bf16[272,768]{1,0:T(8,128)(2,1)S(1)}, u32[]{:S(2)}, u32[]{:S(2)}) collective-permute-start(bf16[272,768]{1,0:T(8,128)(2,1)} %pack_rest.1), channel_id=1, source_target_pairs={{0,1},{1,0},{4,5},{5,4},{8,9},{9,8},{12,13},{13,12},{14,15},{15,14... | collective-permute-start | bytes 1253384 | tf_op jit(solution)/shard_map/ppermute | solution.py:1386
  25.7 9.3 %collective-permute-start.8 = (bf16[2,168,768]{2,1,0:T(8,128)(2,1)}, bf16[2,168,768]{2,1,0:T(8,128)(2,1)S(1)}, u32[]{:S(2)}, u32[]{:S(2)}) collective-permute-start(bf16[2,168,768]{2,1,0:T(8,128)(2,1)} %collective-permute-done.4.rest_3_), channel_id=1, source_target_pairs={{0,4},{1,3},{4,8},{5,1},{8,12},{9,5},{12,14},{13,9},{14,10},{15,13... | collective-permute-start | bytes 1548296 | tf_op jit(solution)/shard_map/ppermute | solution.py:1405
  28.8 15.2 %collective-permute-start.13 = (bf16[2,272,768]{2,1,0:T(8,128)(2,1)S(1)}, bf16[2,272,768]{2,1,0:T(8,128)(2,1)}, u32[]{:S(2)}, u32[]{:S(2)}) collective-permute-start(bf16[2,272,768]{2,1,0:T(8,128)(2,1)S(1)} %pad_maximum_fusion.rest_9_.rest_0_.rest_12_), channel_id=1, source_target_pairs={{0,4},{1,3},{4,8},{5,1},{8,12},{9,5},{12,14},{13,9},{14,10},{15,13... | collective-permute-start | bytes 2506760 | tf_op jit(solution)/shard_map/ppermute | solution.py:1405
  35.0 11.7 %collective-permute-start.10 = (bf16[168,768]{1,0:T(8,128)(2,1)S(1)}, bf16[168,768]{1,0:T(8,128)(2,1)S(1)}, u32[]{:S(2)}, u32[]{:S(2)}) collective-permute-start(bf16[168,768]{1,0:T(8,128)(2,1)S(1)} %fusion.2), channel_id=1, source_target_pairs={{0,4},{1,3},{4,8},{5,1},{8,12},{9,5},{12,14},{13,9},{14,10},{15,13... | collective-permute-start | bytes 774152 | tf_op jit(solution)/shard_map/ppermute | solution.py:1405
  37.1 10.6 %collective-permute-start.3 = (bf16[2,168,768]{2,1,0:T(8,128)(2,1)}, bf16[2,168,768]{2,1,0:T(8,128)(2,1)S(1)}, u32[]{:S(2)}, u32[]{:S(2)}) collective-permute-start(bf16[2,168,768]{2,1,0:T(8,128)(2,1)} %pad_maximum_fusion.3.rest_1_), channel_id=1, source_target_pairs={{0,1},{1,0},{4,5},{5,4},{8,9},{9,8},{12,13},{13,12},{14,15},{15,14... | collective-permute-start | bytes 1548296 | tf_op jit(solution)/shard_map/ppermute | solution.py:1396
  37.1 11.4 %collective-permute-start.5 = (bf16[2,168,768]{2,1,0:T(8,128)(2,1)}, bf16[2,168,768]{2,1,0:T(8,128)(2,1)S(1)}, u32[]{:S(2)}, u32[]{:S(2)}) collective-permute-start(bf16[2,168,768]{2,1,0:T(8,128)(2,1)} %collective-permute-done.4.rest_3_), channel_id=1, source_target_pairs={{0,1},{1,0},{4,5},{5,4},{8,9},{9,8},{12,13},{13,12},{14,15},{15,14... | collective-permute-start | bytes 1548296 | tf_op jit(solution)/shard_map/ppermute | solution.py:1406
  37.6 14.9 %collective-permute-start.9 = (bf16[2,168,768]{2,1,0:T(8,128)(2,1)S(1)}, bf16[2,168,768]{2,1,0:T(8,128)(2,1)}, u32[]{:S(2)}, u32[]{:S(2)}) collective-permute-start(bf16[2,168,768]{2,1,0:T(8,128)(2,1)S(1)} %collective-permute-done.8.rest_5_), channel_id=1, source_target_pairs={{0,1},{1,0},{4,5},{5,4},{8,9},{9,8},{12,13},{13,12},{14,15},{15,14... | collective-permute-start | bytes 1548296 | tf_op jit(solution)/shard_map/ppermute | solution.py:1406
  44.1 20.7 %collective-permute-start.15 = (bf16[2,272,768]{2,1,0:T(8,128)(2,1)}, bf16[2,272,768]{2,1,0:T(8,128)(2,1)}, u32[]{:S(2)}, u32[]{:S(2)}) collective-permute-start(bf16[2,272,768]{2,1,0:T(8,128)(2,1)} %collective-permute-done.13.rest_10_.rest_1_.rest_13_), channel_id=1, source_target_pairs={{0,4},{1,3},{4,8},{5,1},{8,12},{9,5},{12,14},{13,9},{14,10},{15,13... | collective-permute-start | bytes 2506760 | tf_op jit(solution)/shard_map/ppermute | solution.py:1405
  47.6 33.4 %collective-permute-start.21 = (bf16[2,192,768]{2,1,0:T(8,128)(2,1)}, bf16[2,192,768]{2,1,0:T(8,128)(2,1)}, u32[]{:S(2)}, u32[]{:S(2)}) collective-permute-start(bf16[2,192,768]{2,1,0:T(8,128)(2,1)} %collective-permute-done.7.rest_19_.rest_22_), channel_id=1, source_target_pairs={{0,1},{1,0},{4,5},{5,4},{8,9},{9,8},{12,13},{13,12},{14,15},{15,14... | collective-permute-start | bytes 1769480 | tf_op jit(solution)/shard_map/ppermute | solution.py:1406
  49.3 37.7 %collective-permute-start.14 = (bf16[2,272,768]{2,1,0:T(8,128)(2,1)}, bf16[2,272,768]{2,1,0:T(8,128)(2,1)}, u32[]{:S(2)}, u32[]{:S(2)}) collective-permute-start(bf16[2,272,768]{2,1,0:T(8,128)(2,1)} %collective-permute-done.13.rest_10_.rest_1_.rest_13_), channel_id=1, source_target_pairs={{0,1},{1,0},{4,5},{5,4},{8,9},{9,8},{12,13},{13,12},{14,15},{15,14... | collective-permute-start | bytes 2506760 | tf_op jit(solution)/shard_map/ppermute | solution.py:1406
  50.5 26.3 %collective-permute-start.22 = (bf16[2,192,768]{2,1,0:T(8,128)(2,1)}, bf16[2,192,768]{2,1,0:T(8,128)(2,1)}, u32[]{:S(2)}, u32[]{:S(2)}) collective-permute-start(bf16[2,192,768]{2,1,0:T(8,128)(2,1)} %collective-permute-done.7.rest_19_.rest_22_), channel_id=1, source_target_pairs={{0,4},{1,3},{4,8},{5,1},{8,12},{9,5},{12,14},{13,9},{14,10},{15,13... | collective-permute-start | bytes 1769480 | tf_op jit(solution)/shard_map/ppermute | solution.py:1405
  59.7 17.0 %all-to-all-start = ((bf16[16,48,128]{2,1,0:T(8,128)(2,1)}), bf16[16,48,128]{2,1,0:T(8,128)(2,1)}, u32[]{:S(2)}, u32[]{:S(2)}) async-start(bf16[16,48,128]{2,1,0:T(8,128)(2,1)} %get-tuple-element.82), calls=%async_computation | async-start | bytes 393216 | tf_op jit(solution)/shard_map/all_to_all | solution.py:1461
  64.7 14.5 %collective-permute-start.17 = (bf16[2,272,768]{2,1,0:T(8,128)(2,1)}, bf16[2,272,768]{2,1,0:T(8,128)(2,1)}, u32[]{:S(2)}, u32[]{:S(2)}) collective-permute-start(bf16[2,272,768]{2,1,0:T(8,128)(2,1)} %collective-permute-done.15.rest_12_.rest_3_.rest_15_), channel_id=1, source_target_pairs={{0,4},{1,3},{4,8},{5,1},{8,12},{9,5},{12,14},{13,9},{14,10},{15,13... | collective-permute-start | bytes 2506760 | tf_op jit(solution)/shard_map/ppermute | solution.py:1405
  76.8 10.1 %collective-permute-start.24 = (bf16[2,192,768]{2,1,0:T(8,128)(2,1)}, bf16[2,192,768]{2,1,0:T(8,128)(2,1)S(1)}, u32[]{:S(2)}, u32[]{:S(2)}) collective-permute-start(bf16[2,192,768]{2,1,0:T(8,128)(2,1)} %collective-permute-done.22.rest_21_.rest_24_), channel_id=1, source_target_pairs={{0,4},{1,3},{4,8},{5,1},{8,12},{9,5},{12,14},{13,9},{14,10},{15,13... | collective-permute-start | bytes 1769480 | tf_op jit(solution)/shard_map/ppermute | solution.py:1405
  78.3 10.9 %collective-permute-start.23 = (bf16[2,192,768]{2,1,0:T(8,128)(2,1)}, bf16[2,192,768]{2,1,0:T(8,128)(2,1)S(1)}, u32[]{:S(2)}, u32[]{:S(2)}) collective-permute-start(bf16[2,192,768]{2,1,0:T(8,128)(2,1)} %collective-permute-done.22.rest_21_.rest_24_), channel_id=1, source_target_pairs={{0,1},{1,0},{4,5},{5,4},{8,9},{9,8},{12,13},{13,12},{14,15},{15,14... | collective-permute-start | bytes 1769480 | tf_op jit(solution)/shard_map/ppermute | solution.py:1406
  79.3 16.0 %collective-permute-start.16 = (bf16[2,272,768]{2,1,0:T(8,128)(2,1)}, bf16[2,272,768]{2,1,0:T(8,128)(2,1)S(1)}, u32[]{:S(2)}, u32[]{:S(2)}) collective-permute-start(bf16[2,272,768]{2,1,0:T(8,128)(2,1)} %collective-permute-done.15.rest_12_.rest_3_.rest_15_), channel_id=1, source_target_pairs={{0,1},{1,0},{4,5},{5,4},{8,9},{9,8},{12,13},{13,12},{14,15},{15,14... | collective-permute-start | bytes 2506760 | tf_op jit(solution)/shard_map/ppermute | solution.py:1406
  81.0 10.4 %collective-permute-start.19 = (bf16[272,768]{1,0:T(8,128)(2,1)S(1)}, bf16[272,768]{1,0:T(8,128)(2,1)S(1)}, u32[]{:S(2)}, u32[]{:S(2)}) collective-permute-start(bf16[272,768]{1,0:T(8,128)(2,1)S(1)} %fusion), channel_id=1, source_target_pairs={{0,4},{1,3},{4,8},{5,1},{8,12},{9,5},{12,14},{13,9},{14,10},{15,13... | collective-permute-start | bytes 1253384 | tf_op jit(solution)/shard_map/ppermute | solution.py:1405
  86.9 10.9 %collective-permute-start.18 = (bf16[2,272,768]{2,1,0:T(8,128)(2,1)}, bf16[2,272,768]{2,1,0:T(8,128)(2,1)}, u32[]{:S(2)}, u32[]{:S(2)}) collective-permute-start(bf16[2,272,768]{2,1,0:T(8,128)(2,1)} %collective-permute-done.17.rest_14_.rest_5_.rest_17_), channel_id=1, source_target_pairs={{0,1},{1,0},{4,5},{5,4},{8,9},{9,8},{12,13},{13,12},{14,15},{15,14... | collective-permute-start | bytes 2506760 | tf_op jit(solution)/shard_map/ppermute | solution.py:1406
  87.0 7.6 %collective-permute-start.26 = (bf16[192,768]{1,0:T(8,128)(2,1)S(1)}, bf16[192,768]{1,0:T(8,128)(2,1)S(1)}, u32[]{:S(2)}, u32[]{:S(2)}) collective-permute-start(bf16[192,768]{1,0:T(8,128)(2,1)S(1)} %fusion.1), channel_id=1, source_target_pairs={{0,4},{1,3},{4,8},{5,1},{8,12},{9,5},{12,14},{13,9},{14,10},{15,13... | collective-permute-start | bytes 884744 | tf_op jit(solution)/shard_map/ppermute | solution.py:1405
  127.6 19.7 %all-to-all-start.1 = ((bf16[16,128,128]{2,1,0:T(8,128)(2,1)}), bf16[16,128,128]{2,1,0:T(8,128)(2,1)}, u32[]{:S(2)}, u32[]{:S(2)}) async-start(bf16[16,128,128]{2,1,0:T(8,128)(2,1)} %bitcast.62), calls=%async_computation.1 | async-start | bytes 1048576 | tf_op jit(solution)/shard_map/all_to_all | solution.py:1480
  (24 other events, 153.0 us)

commit v6 on v5

--- a/solution.py
+++ b/solution.py
@@ -611,14 +611,11 @@
         drain(weights, sems.at[1])
         for third, low, bias in ((1, keys, None), (2, values, 3)):
 
-            @pl.loop(0, width // 256)
-            def _(j, third=third, low=low, bias=bias):
-                lanes = pl.ds(aligned(j * 256, 256), 256)
-                weight = weights[:, third * 48 : third * 48 + 48, lanes].reshape(DI, 256)
-                prod = dot(normed[0:rows, 0:width], weight[0:width])
-                if bias is not None:
-                    prod = prod + vec[bias : bias + 1, lanes]
-                low[0:rows, lanes] = prod.astype(BF16)
+            weight = weights[:, third * 48 : third * 48 + 48, 0:width].reshape(DI, width)[0:width]
+            prod = dot(normed[0:rows, 0:width], weight)
+            if bias is not None:
+                prod = prod + vec[bias : bias + 1, 0:width]
+            low[0:rows, 0:width] = prod.astype(BF16)
 
         saved += [copy(keys, keys_hbm, ends.at[2]), copy(values, values_hbm, ends.at[3])]
         query = dot(pooled_normed, weights[:, 0:48, :].reshape(DI, DI)) + vec[2:3, :]
@@ -699,21 +696,20 @@
             for dst in (qf, kf, vf):
                 dst[:, rows : span * 8, :] = jnp.zeros((6, span * 8 - rows, 128), F32)
 
-        @pl.loop(0, width // 256)
-        def _(j):
-            lanes = pl.ds(aligned(j * 256, 256), 256)
-            weight = weights[:, :, lanes].reshape(DI, 256)
-            prod = dot(normed[0:rows, 0:width], weight[0:width]) + vec[2:3, lanes]
-            prod = prod.astype(BF16).astype(F32) * SCALE
-            for dst, item in ((qf, prod), (kf, keys[0:rows, lanes].astype(F32)), (vf, values[0:rows, lanes].astype(F32))):
-                dst[2 * j, 0:rows, :] = item[:, 0:128]
-                dst[2 * j + 1, 0:rows, :] = item[:, 128:256]
+        weight = weights[:, :, 0:width].reshape(DI, width)[0:width]
+        prod = dot(normed[0:rows, 0:width], weight) + vec[2:3, 0:width]
+        prod = prod.astype(BF16).astype(F32) * SCALE
+        for pair in range(width // 128):
+            lanes = pl.ds(pair * 128, 128)
+            qf[pair, 0:rows, :] = prod[:, pair * 128 : pair * 128 + 128]
+            kf[pair, 0:rows, :] = keys[0:rows, lanes].astype(F32)
+            vf[pair, 0:rows, :] = values[0:rows, lanes].astype(F32)
 
         key_pos = lax.broadcasted_iota(jnp.int32, (span, 2 * span), 0)
         query_pos = lax.broadcasted_iota(jnp.int32, (span, 2 * span), 1) % span
         low_half = lax.broadcasted_iota(jnp.int32, (span, 128), 1) < HD
 
-        @pl.loop(0, 8)
+        @pl.loop(0, 8, unroll=2)
         def _(s):
             at = pl.ds(s, span, stride=8)
             allowed = key_pos < here.length(s)
@@ -889,12 +885,8 @@
     def path(width, count):
         rows = count * 8
 
-        @pl.loop(0, width // 256)
-        def _(j):
-            lanes = pl.ds(aligned(j * 256, 256), 256)
-            weight = w_out[:, :, lanes].reshape(DI, 256)[0:width]
-            middle[0:rows, lanes] = dot(mixed[0:rows, 0:width], weight) + vec[4:5, lanes]
-
+        weight = w_out[:, :, 0:width].reshape(DI, width)[0:width]
+        middle[0:rows, 0:width] = dot(mixed[0:rows, 0:width], weight) + vec[4:5, 0:width]
         if width < DI:
             middle[0:rows, width:DI] = jnp.zeros((rows, DI - width), F32)
         tok_in.wait()
@@ -1200,27 +1192,22 @@
         ready.wait()
         drain(w_fc, sems.at[4])
         for block in range(4):
-
-            @pl.loop(0, 3 if width == DI else (3, 3, 2, 0)[block])
-            def _(j, block=block):
-                lanes = pl.ds(aligned(j * 256, 256), 256)
-                wide = pl.ds(aligned(block * DI + j * 256, 256), 256)
-                weight = w_fc[:, block * 48 : block * 48 + 48, lanes].reshape(DI, 256)[0:width]
-                pre = dot(n2[0:rows, 0:width], weight) + vec[10 + block : 11 + block, lanes]
-                act[0:rows, wide] = (pre * jax.nn.sigmoid(GELU_K * pre)).astype(BF16)
+            size = min(DI, 4 * width - block * DI)
+            if size > 0:
+                weight = w_fc[:, block * 48 : block * 48 + 48, 0:size].reshape(DI, size)[0:width]
+                pre = dot(n2[0:rows, 0:width], weight) + vec[10 + block : 11 + block, 0:size]
+                low = (pre * jax.nn.sigmoid(GELU_K * pre)).astype(BF16)
+                act[0:rows, block * DI : block * DI + size] = low
 
         for item in early:
             item.wait()
         drain(w_down, sems.at[3])
 
-        @pl.loop(0, width // 256)
-        def _(j):
-            lanes = pl.ds(aligned(j * 256, 256), 256)
-            weight = w_down[:, :, lanes].reshape(4 * DI, 256)[0 : 4 * width]
-            total = dot(act[0:rows, 0 : 4 * width], weight)
-            total = (total + vec[7:8, lanes] + middle[0:rows, lanes]).reshape(short, 8, 256)
-            where = lax.broadcasted_iota(jnp.int32, (short, 8, 256), 0)
-            block_out[0:rows, lanes] = jnp.where(where < length, total, 0.0).reshape(rows, 256).astype(BF16)
+        weight = w_down[:, :, 0:width].reshape(4 * DI, width)[0 : 4 * width]
+        total = dot(act[0:rows, 0 : 4 * width], weight)
+        total = (total + vec[7:8, 0:width] + middle[0:rows, 0:width]).reshape(short, 8, width)
+        where = lax.broadcasted_iota(jnp.int32, (short, 8, width), 0)
+        block_out[0:rows, 0:width] = jnp.where(where < length, total, 0.0).reshape(rows, width).astype(BF16)
 
         if width < DI:
             block_out[:, width:DI] = jnp.zeros((all_rows, DI - width), BF16)

time: 151 us -> 149 us (0.987)
  Pallas kernels: 67.7 us -> 64.3 us
  starting transfers between devices: 40 us -> 42.1 us
    pallas_call x9, Pallas kernels: 67.7 us -> 64.3 us  [call(): pl.pallas_call(kernel, name=name, out_shape=[jax.ShapeDtypeStruct(shape,...]
  transfers between devices with their start and end apart: 31 -> 31, of which waited for: 11 -> 11; matrix products, arithmetic and copies ran while one was open for 4% -> 4% of each run, Pallas kernels for 27% -> 25%
where the time goes in v6:
time: 149 us
  Pallas kernels  64.3 us (43%)
  starting transfers between devices  42.1 us (28%)
  waiting for transfers between devices  30.2 us (20%)
  other arithmetic  6.11 us (4%)
  local copies, waits for them, and re-layouts  4.38 us (3%)
  between operations  1.58 us (1%)
    pallas_call x9, Pallas kernels, call(): pl.pallas_call(kernel, name=name, out_shape=[jax.ShapeDtypeStruct(shape,...  64.3 us
    ppermute x11, waiting for transfers between devices, step(): held = lax.ppermute(after(held, *earlier), BOTH, self.turn)  27.2 us
    ppermute x11, starting transfers between devices, step(): held = lax.ppermute(after(held, *earlier), BOTH, self.turn)  22 us
    all_to_all x1, starting transfers between devices, ring_body(): lax.all_to_all(payload, 'dp', 0, 0, tiled=True).reshape(ITEMS, PAYLOAD, 128)  5.15 us
    all_to_all x1, starting transfers between devices, ring_body(): mixes = lax.all_to_all(pooled, 'dp', 0, 0, tiled=True)  4.98 us
    another operation x8, other arithmetic, joined(): jnp.stack([jnp.where(self.first_core, own, other), jnp.where(self.first_c...  4.88 us
    ppermute x2, starting transfers between devices, first_step(): lax.ppermute(item, BOTH, self.turn)  4.6 us
    unnamed x34, local copies, waits for them, and re-layouts  4.38 us
  transfers between devices with their start and end apart: 31, of which 11 were waited for; matrix products, arithmetic and copies ran while one was open for 4% of the time, Pallas kernels for 25%

profile of v6, /device:TPU:0, one launch (start us, length us, event | category | flops | bytes accessed | tf_op | source)
XLA Modules:
  0.0 148.7 jit_solution(15258673863306493545)
XLA Ops:
  1.2 2.2 %pack_first.1 = bf16[168,768]{1,0:T(8,128)(2,1)} custom-call(s32[8]{0:T(128)} %lengths.13, bf16[144,768]{1,0:T(8,128)(2,1)} %bitcast.65, bf16[77,8,768]{2,1,0:T(8,128)(2,1)} %bitcast.58, bf16[1,48]{1,0:T(2,128)(2,1)} %gain.1, bf16[1,48]{1,0:T(2,128)(2,1)} %bias.1, bf16[1,48]{1,0:T(2,128)(2,1)} %rest_2_.1, bf16[1,48]{1,0:T(2,128)(2,1)} %rest_3_.1, ...), custom_call_target="tpu_custom_call" | custom-call | bytes 1500000 | tf_op jit(solution)/shard_map/pack_first/pallas_call | solution.py:357
  3.4 3.0 %collective-permute-start.1 = (bf16[168,768]{1,0:T(8,128)(2,1)}, bf16[168,768]{1,0:T(8,128)(2,1)S(1)}, u32[]{:S(2)}, u32[]{:S(2)}) collective-permute-start(bf16[168,768]{1,0:T(8,128)(2,1)} %pack_first.1), channel_id=1, source_target_pairs={{0,4},{1,3},{4,8},{5,1},{8,12},{9,5},{12,14},{13,9},{14,10},{15,13... | collective-permute-start | bytes 774152 | tf_op jit(solution)/shard_map/ppermute | solution.py:1382
  11.5 2.1 %collective-permute-done.2 = bf16[168,768]{1,0:T(8,128)(2,1)S(1)} collective-permute-done((bf16[168,768]{1,0:T(8,128)(2,1)S(1)}, bf16[168,768]{1,0:T(8,128)(2,1)S(1)}, u32[]{:S(2)}, u32[]{:S(2)}) %collective-permute-start.2) | collective-permute-done | bytes 258080 | tf_op jit(solution)/shard_map/ppermute | solution.py:1382
  14.5 2.1 %collective-permute-start.4 = (bf16[2,168,768]{2,1,0:T(8,128)(2,1)}, bf16[2,168,768]{2,1,0:T(8,128)(2,1)}, u32[]{:S(2)}, u32[]{:S(2)}) collective-permute-start(bf16[2,168,768]{2,1,0:T(8,128)(2,1)} %pad_maximum_fusion.3.rest_1_), channel_id=1, source_target_pairs={{0,4},{1,3},{4,8},{5,1},{8,12},{9,5},{12,14},{13,9},{14,10},{15,13... | collective-permute-start | bytes 1548296 | tf_op jit(solution)/shard_map/ppermute | solution.py:1392
  20.2 5.5 %collective-permute-done.4.rest_3_ = bf16[2,168,768]{2,1,0:T(8,128)(2,1)} collective-permute-done((bf16[2,168,768]{2,1,0:T(8,128)(2,1)}, bf16[2,168,768]{2,1,0:T(8,128)(2,1)}, u32[]{:S(2)}, u32[]{:S(2)}) %collective-permute-start.4) | collective-permute-done | bytes 516128 | tf_op jit(solution)/shard_map/ppermute | solution.py:1392
  25.7 2.0 %collective-permute-start.8 = (bf16[2,168,768]{2,1,0:T(8,128)(2,1)}, bf16[2,168,768]{2,1,0:T(8,128)(2,1)S(1)}, u32[]{:S(2)}, u32[]{:S(2)}) collective-permute-start(bf16[2,168,768]{2,1,0:T(8,128)(2,1)} %collective-permute-done.4.rest_3_), channel_id=1, source_target_pairs={{0,4},{1,3},{4,8},{5,1},{8,12},{9,5},{12,14},{13,9},{14,10},{15,13... | collective-permute-start | bytes 1548296 | tf_op jit(solution)/shard_map/ppermute | solution.py:1392
  30.5 4.5 %collective-permute-done.8.rest_5_ = bf16[2,168,768]{2,1,0:T(8,128)(2,1)S(1)} collective-permute-done((bf16[2,168,768]{2,1,0:T(8,128)(2,1)}, bf16[2,168,768]{2,1,0:T(8,128)(2,1)S(1)}, u32[]{:S(2)}, u32[]{:S(2)}) %collective-permute-start.8) | collective-permute-done | bytes 516128 | tf_op jit(solution)/shard_map/ppermute | solution.py:1392
  35.0 2.0 %collective-permute-start.10 = (bf16[168,768]{1,0:T(8,128)(2,1)S(1)}, bf16[168,768]{1,0:T(8,128)(2,1)S(1)}, u32[]{:S(2)}, u32[]{:S(2)}) collective-permute-start(bf16[168,768]{1,0:T(8,128)(2,1)S(1)} %fusion.2), channel_id=1, source_target_pairs={{0,4},{1,3},{4,8},{5,1},{8,12},{9,5},{12,14},{13,9},{14,10},{15,13... | collective-permute-start | bytes 774152 | tf_op jit(solution)/shard_map/ppermute | solution.py:1392
  37.6 6.5 %collective-permute-done.13.rest_10_.rest_1_.rest_13_ = bf16[2,272,768]{2,1,0:T(8,128)(2,1)} collective-permute-done((bf16[2,272,768]{2,1,0:T(8,128)(2,1)S(1)}, bf16[2,272,768]{2,1,0:T(8,128)(2,1)}, u32[]{:S(2)}, u32[]{:S(2)}) %collective-permute-start.13) | collective-permute-done | bytes 835616 | tf_op jit(solution)/shard_map/ppermute | solution.py:1392
  44.1 2.0 %collective-permute-start.15 = (bf16[2,272,768]{2,1,0:T(8,128)(2,1)}, bf16[2,272,768]{2,1,0:T(8,128)(2,1)}, u32[]{:S(2)}, u32[]{:S(2)}) collective-permute-start(bf16[2,272,768]{2,1,0:T(8,128)(2,1)} %collective-permute-done.13.rest_10_.rest_1_.rest_13_), channel_id=1, source_target_pairs={{0,4},{1,3},{4,8},{5,1},{8,12},{9,5},{12,14},{13,9},{14,10},{15,13... | collective-permute-start | bytes 2506760 | tf_op jit(solution)/shard_map/ppermute | solution.py:1392
  50.5 2.0 %collective-permute-start.22 = (bf16[2,192,768]{2,1,0:T(8,128)(2,1)}, bf16[2,192,768]{2,1,0:T(8,128)(2,1)}, u32[]{:S(2)}, u32[]{:S(2)}) collective-permute-start(bf16[2,192,768]{2,1,0:T(8,128)(2,1)} %collective-permute-done.7.rest_19_.rest_22_), channel_id=1, source_target_pairs={{0,4},{1,3},{4,8},{5,1},{8,12},{9,5},{12,14},{13,9},{14,10},{15,13... | collective-permute-start | bytes 1769480 | tf_op jit(solution)/shard_map/ppermute | solution.py:1392
  52.5 6.2 %attend_pooled.1 = (bf16[616,768]{1,0:T(8,128)(2,1)}, bf16[616,768]{1,0:T(8,128)(2,1)}, bf16[616,768]{1,0:T(8,128)(2,1)}, bf16[616,768]{1,0:T(8,128)(2,1)}, f32[...) custom-call(s32[8]{0:T(128)} %lengths.13, ...), custom_call_target="tpu_custom_call" | custom-call | flops 7000000000 | bytes 10000000 | tf_op jit(solution)/shard_map/attend_pooled/pallas_call | solution.py:357
  58.7 5.0 %all-to-all-start = ((bf16[16,48,128]{2,1,0:T(8,128)(2,1)}), bf16[16,48,128]{2,1,0:T(8,128)(2,1)}, u32[]{:S(2)}, u32[]{:S(2)}) async-start(bf16[16,48,128]{2,1,0:T(8,128)(2,1)} %get-tuple-element.82), calls=%async_computation | async-start | bytes 393216 | tf_op jit(solution)/shard_map/all_to_all | solution.py:1448
  65.7 9.2 %attend.1 = (bf16[616,768]{1,0:T(8,128)(2,1)}, bf16[768,128]{1,0:T(8,128)(2,1)}) custom-call(s32[8]{0:T(128)} %lengths.13, f32[16,768]{1,0:T(8,128)} %get-tuple-element.81.vec, bf16[616,128]{1,0:T(8,128)(2,1)} %get-tuple-element.86.gv.rest_10_, bf16[616,768]{1,0:T(8,128)(2,1)} %get-tuple-element.88.normed_hbm, ...), custom_call_target="tpu_custom_call" | custom-call | flops 8999999488 | bytes 10000000 | tf_op jit(solution)/shard_map/attend/pallas_call | solution.py:357
  80.2 2.6 %collective-permute-start.19 = (bf16[272,768]{1,0:T(8,128)(2,1)S(1)}, bf16[272,768]{1,0:T(8,128)(2,1)S(1)}, u32[]{:S(2)}, u32[]{:S(2)}) collective-permute-start(bf16[272,768]{1,0:T(8,128)(2,1)S(1)} %fusion), channel_id=1, source_target_pairs={{0,4},{1,3},{4,8},{5,1},{8,12},{9,5},{12,14},{13,9},{14,10},{15,13... | collective-permute-start | bytes 1253384 | tf_op jit(solution)/shard_map/ppermute | solution.py:1392
  82.8 2.2 %collective-permute-done.24.rest_23_.rest_26_ = bf16[2,192,768]{2,1,0:T(8,128)(2,1)S(1)} collective-permute-done((bf16[2,192,768]{2,1,0:T(8,128)(2,1)}, bf16[2,192,768]{2,1,0:T(8,128)(2,1)S(1)}, u32[]{:S(2)}, u32[]{:S(2)}) %collective-permute-start.24) | collective-permute-done | bytes 589856 | tf_op jit(solution)/shard_map/ppermute | solution.py:1392
  85.4 2.8 %collective-permute-start.26 = (bf16[192,768]{1,0:T(8,128)(2,1)S(1)}, bf16[192,768]{1,0:T(8,128)(2,1)S(1)}, u32[]{:S(2)}, u32[]{:S(2)}) collective-permute-start(bf16[192,768]{1,0:T(8,128)(2,1)S(1)} %fusion.1), channel_id=1, source_target_pairs={{0,4},{1,3},{4,8},{5,1},{8,12},{9,5},{12,14},{13,9},{14,10},{15,13... | collective-permute-start | bytes 884744 | tf_op jit(solution)/shard_map/ppermute | solution.py:1392
  89.8 2.8 %collective-permute-done.26.rest_25_.rest_28_ = bf16[192,768]{1,0:T(8,128)(2,1)S(1)} collective-permute-done((bf16[192,768]{1,0:T(8,128)(2,1)S(1)}, bf16[192,768]{1,0:T(8,128)(2,1)S(1)}, u32[]{:S(2)}, u32[]{:S(2)}) %collective-permute-start.26) | collective-permute-done | bytes 294944 | tf_op jit(solution)/shard_map/ppermute | solution.py:1392
  96.0 8.8 %pooled_forward.1 = (bf16[128,512]{1,0:T(8,128)(2,1)}, f32[128,512]{1,0:T(8,128)}, f32[128,768]{1,0:T(8,128)}, f32[128,128]{1,0:T(8,128)}, f32[128,768]{1,0:T(8,...) custom-call(s32[8]{0:T(128)} %lengths.13, ...), custom_call_target="tpu_custom_call" | custom-call | flops 11000000512 | bytes 16000000 | tf_op jit(solution)/shard_map/pooled_forward/pallas_call | solution.py:357
  106.4 4.7 %middle_part.1 = (bf16[616,768]{1,0:T(8,128)(2,1)}, f32[616,768]{1,0:T(8,128)}) custom-call(s32[8]{0:T(128)} %lengths.13, bf16[77,8,768]{2,1,0:T(8,128)(2,1)} %bitcast.60, f32[16,768]{1,0:T(8,128)} %get-tuple-element.81.vec, bf16[616,768]{1,0:T(8,128)(2,1)} %get-tuple-element.99.mixed_hbm, bf16[2,272,768]{2,1,0:T(8,128)(2,1)} %copy-done.1, ...), custom_call_target="tpu_custom_call" | custom-call | flops 5000000000 | bytes 8000000 | tf_op jit(solution)/shard_map/middle_part/pallas_call | solution.py:357
  111.1 14.7 %chain.1 = (f32[1,1]{1,0:T(1,128)}, f32[1,1]{1,0:T(1,128)}, f32[48,512]{1,0:T(8,128)}, f32[192,768]{1,0:T(8,128)}, f32[48,3072]{1,0:T(8,128)}, /*index=5*/f32[48...) custom-call(s32[8]{0:T(128)} %lengths.13, ...), custom_call_target="tpu_custom_call" | custom-call | flops 15000000512 | bytes 20000000 | tf_op jit(solution)/shard_map/chain/pallas_call | solution.py:357
  125.8 5.1 %all-to-all-start.1 = ((bf16[16,128,128]{2,1,0:T(8,128)(2,1)}), bf16[16,128,128]{2,1,0:T(8,128)(2,1)}, u32[]{:S(2)}, u32[]{:S(2)}) async-start(bf16[16,128,128]{2,1,0:T(8,128)(2,1)} %bitcast.62), calls=%async_computation.1 | async-start | bytes 1048576 | tf_op jit(solution)/shard_map/all_to_all | solution.py:1467
  131.0 13.6 %close.1 = (bf16[616,768]{1,0:T(8,128)(2,1)}, f32[616,768]{1,0:T(8,128)}, f32[128,768]{1,0:T(8,128)}, bf16[128,48]{1,0:T(8,128)(2,1)}) custom-call(s32[8]{0:T(128)} %lengths.13, bf16[77,8,768]{2,1,0:T(8,128)(2,1)} %bitcast.61, f32[16,768]{1,0:T(8,128)} %get-tuple-element.81.vec, bf16[616,128]{1,0:T(8,128)(2,1)} %get-tuple-element.113.gk, ...), custom_call_target="tpu_custom_call" | custom-call | flops 16999999488 | bytes 18000000 | tf_op jit(solution)/shard_map/close/pallas_call | solution.py:357
  145.5 3.2 %shard_grads.1 = (f32[3,48,768]{2,1,0:T(8,128)}, f32[1,48]{1,0:T(1,128)}, f32[1,48]{1,0:T(1,128)}, f32[2,48]{1,0:T(2,128)}) custom-call(bf16[16,128,128]{2,1,0:T(8,128)(2,1)} %all-to-all-done.1.got, f32[128,768]{1,0:T(8,128)} %get-tuple-element.122.q_all, f32[128,768]{1,0:T(8,128)} %get-tuple-element.123.gm_all, bf16[128,48]{1,0:T(8,128)(2,1)} %get-tuple-element.124.norm_sl, ...), custom_call_target="tpu_custom_call" | custom-call | flops 5000000000 | bytes 2000000 | tf_op jit(solution)/shard_map/shard_grads/pallas_call | solution.py:357
  (92 shorter events, 32.4 us)
Async XLA Ops:
  0.7 7.3 %collective-permute-start.6 = (bf16[192,768]{1,0:T(8,128)(2,1)}, bf16[192,768]{1,0:T(8,128)(2,1)}, u32[]{:S(2)}, u32[]{:S(2)}) collective-permute-start(bf16[192,768]{1,0:T(8,128)(2,1)} %bitcast.64), channel_id=1, source_target_pairs={{0,1},{1,0},{4,5},{5,4},{8,9},{9,8},{12,13},{13,12},{14,15},{15,14... | collective-permute-start | bytes 884744 | tf_op jit(solution)/shard_map/ppermute | solution.py:1373
  3.4 8.2 %collective-permute-start.1 = (bf16[168,768]{1,0:T(8,128)(2,1)}, bf16[168,768]{1,0:T(8,128)(2,1)S(1)}, u32[]{:S(2)}, u32[]{:S(2)}) collective-permute-start(bf16[168,768]{1,0:T(8,128)(2,1)} %pack_first.1), channel_id=1, source_target_pairs={{0,4},{1,3},{4,8},{5,1},{8,12},{9,5},{12,14},{13,9},{14,10},{15,13... | collective-permute-start | bytes 774152 | tf_op jit(solution)/shard_map/ppermute | solution.py:1382
  10.0 10.2 %collective-permute-start.7 = (bf16[2,192,768]{2,1,0:T(8,128)(2,1)}, bf16[2,192,768]{2,1,0:T(8,128)(2,1)}, u32[]{:S(2)}, u32[]{:S(2)}) collective-permute-start(bf16[2,192,768]{2,1,0:T(8,128)(2,1)} %pad_maximum_fusion.1.rest_18_.rest_21_), channel_id=1, source_target_pairs={{0,4},{1,3},{4,8},{5,1},{8,12},{9,5},{12,14},{13,9},{14,10},{15,13... | collective-permute-start | bytes 1769480 | tf_op jit(solution)/shard_map/ppermute | solution.py:1392
  14.5 11.2 %collective-permute-start.4 = (bf16[2,168,768]{2,1,0:T(8,128)(2,1)}, bf16[2,168,768]{2,1,0:T(8,128)(2,1)}, u32[]{:S(2)}, u32[]{:S(2)}) collective-permute-start(bf16[2,168,768]{2,1,0:T(8,128)(2,1)} %pad_maximum_fusion.3.rest_1_), channel_id=1, source_target_pairs={{0,4},{1,3},{4,8},{5,1},{8,12},{9,5},{12,14},{13,9},{14,10},{15,13... | collective-permute-start | bytes 1548296 | tf_op jit(solution)/shard_map/ppermute | solution.py:1392
  18.4 9.3 %collective-permute-start.12 = (bf16[272,768]{1,0:T(8,128)(2,1)}, bf16[272,768]{1,0:T(8,128)(2,1)S(1)}, u32[]{:S(2)}, u32[]{:S(2)}) collective-permute-start(bf16[272,768]{1,0:T(8,128)(2,1)} %pack_rest.1), channel_id=1, source_target_pairs={{0,1},{1,0},{4,5},{5,4},{8,9},{9,8},{12,13},{13,12},{14,15},{15,14... | collective-permute-start | bytes 1253384 | tf_op jit(solution)/shard_map/ppermute | solution.py:1373
  25.7 9.3 %collective-permute-start.8 = (bf16[2,168,768]{2,1,0:T(8,128)(2,1)}, bf16[2,168,768]{2,1,0:T(8,128)(2,1)S(1)}, u32[]{:S(2)}, u32[]{:S(2)}) collective-permute-start(bf16[2,168,768]{2,1,0:T(8,128)(2,1)} %collective-permute-done.4.rest_3_), channel_id=1, source_target_pairs={{0,4},{1,3},{4,8},{5,1},{8,12},{9,5},{12,14},{13,9},{14,10},{15,13... | collective-permute-start | bytes 1548296 | tf_op jit(solution)/shard_map/ppermute | solution.py:1392
  28.8 15.2 %collective-permute-start.13 = (bf16[2,272,768]{2,1,0:T(8,128)(2,1)S(1)}, bf16[2,272,768]{2,1,0:T(8,128)(2,1)}, u32[]{:S(2)}, u32[]{:S(2)}) collective-permute-start(bf16[2,272,768]{2,1,0:T(8,128)(2,1)S(1)} %pad_maximum_fusion.rest_9_.rest_0_.rest_12_), channel_id=1, source_target_pairs={{0,4},{1,3},{4,8},{5,1},{8,12},{9,5},{12,14},{13,9},{14,10},{15,13... | collective-permute-start | bytes 2506760 | tf_op jit(solution)/shard_map/ppermute | solution.py:1392
  35.0 11.7 %collective-permute-start.10 = (bf16[168,768]{1,0:T(8,128)(2,1)S(1)}, bf16[168,768]{1,0:T(8,128)(2,1)S(1)}, u32[]{:S(2)}, u32[]{:S(2)}) collective-permute-start(bf16[168,768]{1,0:T(8,128)(2,1)S(1)} %fusion.2), channel_id=1, source_target_pairs={{0,4},{1,3},{4,8},{5,1},{8,12},{9,5},{12,14},{13,9},{14,10},{15,13... | collective-permute-start | bytes 774152 | tf_op jit(solution)/shard_map/ppermute | solution.py:1392
  37.1 10.6 %collective-permute-start.3 = (bf16[2,168,768]{2,1,0:T(8,128)(2,1)}, bf16[2,168,768]{2,1,0:T(8,128)(2,1)S(1)}, u32[]{:S(2)}, u32[]{:S(2)}) collective-permute-start(bf16[2,168,768]{2,1,0:T(8,128)(2,1)} %pad_maximum_fusion.3.rest_1_), channel_id=1, source_target_pairs={{0,1},{1,0},{4,5},{5,4},{8,9},{9,8},{12,13},{13,12},{14,15},{15,14... | collective-permute-start | bytes 1548296 | tf_op jit(solution)/shard_map/ppermute | solution.py:1383
  37.1 11.4 %collective-permute-start.5 = (bf16[2,168,768]{2,1,0:T(8,128)(2,1)}, bf16[2,168,768]{2,1,0:T(8,128)(2,1)S(1)}, u32[]{:S(2)}, u32[]{:S(2)}) collective-permute-start(bf16[2,168,768]{2,1,0:T(8,128)(2,1)} %collective-permute-done.4.rest_3_), channel_id=1, source_target_pairs={{0,1},{1,0},{4,5},{5,4},{8,9},{9,8},{12,13},{13,12},{14,15},{15,14... | collective-permute-start | bytes 1548296 | tf_op jit(solution)/shard_map/ppermute | solution.py:1393
  37.6 14.9 %collective-permute-start.9 = (bf16[2,168,768]{2,1,0:T(8,128)(2,1)S(1)}, bf16[2,168,768]{2,1,0:T(8,128)(2,1)}, u32[]{:S(2)}, u32[]{:S(2)}) collective-permute-start(bf16[2,168,768]{2,1,0:T(8,128)(2,1)S(1)} %collective-permute-done.8.rest_5_), channel_id=1, source_target_pairs={{0,1},{1,0},{4,5},{5,4},{8,9},{9,8},{12,13},{13,12},{14,15},{15,14... | collective-permute-start | bytes 1548296 | tf_op jit(solution)/shard_map/ppermute | solution.py:1393
  44.1 19.7 %collective-permute-start.15 = (bf16[2,272,768]{2,1,0:T(8,128)(2,1)}, bf16[2,272,768]{2,1,0:T(8,128)(2,1)}, u32[]{:S(2)}, u32[]{:S(2)}) collective-permute-start(bf16[2,272,768]{2,1,0:T(8,128)(2,1)} %collective-permute-done.13.rest_10_.rest_1_.rest_13_), channel_id=1, source_target_pairs={{0,4},{1,3},{4,8},{5,1},{8,12},{9,5},{12,14},{13,9},{14,10},{15,13... | collective-permute-start | bytes 2506760 | tf_op jit(solution)/shard_map/ppermute | solution.py:1392
  47.6 32.6 %collective-permute-start.21 = (bf16[2,192,768]{2,1,0:T(8,128)(2,1)}, bf16[2,192,768]{2,1,0:T(8,128)(2,1)}, u32[]{:S(2)}, u32[]{:S(2)}) collective-permute-start(bf16[2,192,768]{2,1,0:T(8,128)(2,1)} %collective-permute-done.7.rest_19_.rest_22_), channel_id=1, source_target_pairs={{0,1},{1,0},{4,5},{5,4},{8,9},{9,8},{12,13},{13,12},{14,15},{15,14... | collective-permute-start | bytes 1769480 | tf_op jit(solution)/shard_map/ppermute | solution.py:1393
  49.3 36.1 %collective-permute-start.14 = (bf16[2,272,768]{2,1,0:T(8,128)(2,1)}, bf16[2,272,768]{2,1,0:T(8,128)(2,1)}, u32[]{:S(2)}, u32[]{:S(2)}) collective-permute-start(bf16[2,272,768]{2,1,0:T(8,128)(2,1)} %collective-permute-done.13.rest_10_.rest_1_.rest_13_), channel_id=1, source_target_pairs={{0,1},{1,0},{4,5},{5,4},{8,9},{9,8},{12,13},{13,12},{14,15},{15,14... | collective-permute-start | bytes 2506760 | tf_op jit(solution)/shard_map/ppermute | solution.py:1393
  50.5 24.3 %collective-permute-start.22 = (bf16[2,192,768]{2,1,0:T(8,128)(2,1)}, bf16[2,192,768]{2,1,0:T(8,128)(2,1)}, u32[]{:S(2)}, u32[]{:S(2)}) collective-permute-start(bf16[2,192,768]{2,1,0:T(8,128)(2,1)} %collective-permute-done.7.rest_19_.rest_22_), channel_id=1, source_target_pairs={{0,4},{1,3},{4,8},{5,1},{8,12},{9,5},{12,14},{13,9},{14,10},{15,13... | collective-permute-start | bytes 1769480 | tf_op jit(solution)/shard_map/ppermute | solution.py:1392
  58.7 16.1 %all-to-all-start = ((bf16[16,48,128]{2,1,0:T(8,128)(2,1)}), bf16[16,48,128]{2,1,0:T(8,128)(2,1)}, u32[]{:S(2)}, u32[]{:S(2)}) async-start(bf16[16,48,128]{2,1,0:T(8,128)(2,1)} %get-tuple-element.82), calls=%async_computation | async-start | bytes 393216 | tf_op jit(solution)/shard_map/all_to_all | solution.py:1448
  63.7 14.5 %collective-permute-start.17 = (bf16[2,272,768]{2,1,0:T(8,128)(2,1)}, bf16[2,272,768]{2,1,0:T(8,128)(2,1)}, u32[]{:S(2)}, u32[]{:S(2)}) collective-permute-start(bf16[2,272,768]{2,1,0:T(8,128)(2,1)} %collective-permute-done.15.rest_12_.rest_3_.rest_15_), channel_id=1, source_target_pairs={{0,4},{1,3},{4,8},{5,1},{8,12},{9,5},{12,14},{13,9},{14,10},{15,13... | collective-permute-start | bytes 2506760 | tf_op jit(solution)/shard_map/ppermute | solution.py:1392
  74.9 10.1 %collective-permute-start.24 = (bf16[2,192,768]{2,1,0:T(8,128)(2,1)}, bf16[2,192,768]{2,1,0:T(8,128)(2,1)S(1)}, u32[]{:S(2)}, u32[]{:S(2)}) collective-permute-start(bf16[2,192,768]{2,1,0:T(8,128)(2,1)} %collective-permute-done.22.rest_21_.rest_24_), channel_id=1, source_target_pairs={{0,4},{1,3},{4,8},{5,1},{8,12},{9,5},{12,14},{13,9},{14,10},{15,13... | collective-permute-start | bytes 1769480 | tf_op jit(solution)/shard_map/ppermute | solution.py:1392
  76.4 11.8 %collective-permute-start.23 = (bf16[2,192,768]{2,1,0:T(8,128)(2,1)}, bf16[2,192,768]{2,1,0:T(8,128)(2,1)S(1)}, u32[]{:S(2)}, u32[]{:S(2)}) collective-permute-start(bf16[2,192,768]{2,1,0:T(8,128)(2,1)} %collective-permute-done.22.rest_21_.rest_24_), channel_id=1, source_target_pairs={{0,1},{1,0},{4,5},{5,4},{8,9},{9,8},{12,13},{13,12},{14,15},{15,14... | collective-permute-start | bytes 1769480 | tf_op jit(solution)/shard_map/ppermute | solution.py:1393
  78.3 15.2 %collective-permute-start.16 = (bf16[2,272,768]{2,1,0:T(8,128)(2,1)}, bf16[2,272,768]{2,1,0:T(8,128)(2,1)S(1)}, u32[]{:S(2)}, u32[]{:S(2)}) collective-permute-start(bf16[2,272,768]{2,1,0:T(8,128)(2,1)} %collective-permute-done.15.rest_12_.rest_3_.rest_15_), channel_id=1, source_target_pairs={{0,1},{1,0},{4,5},{5,4},{8,9},{9,8},{12,13},{13,12},{14,15},{15,14... | collective-permute-start | bytes 2506760 | tf_op jit(solution)/shard_map/ppermute | solution.py:1393
  80.2 9.3 %collective-permute-start.19 = (bf16[272,768]{1,0:T(8,128)(2,1)S(1)}, bf16[272,768]{1,0:T(8,128)(2,1)S(1)}, u32[]{:S(2)}, u32[]{:S(2)}) collective-permute-start(bf16[272,768]{1,0:T(8,128)(2,1)S(1)} %fusion), channel_id=1, source_target_pairs={{0,4},{1,3},{4,8},{5,1},{8,12},{9,5},{12,14},{13,9},{14,10},{15,13... | collective-permute-start | bytes 1253384 | tf_op jit(solution)/shard_map/ppermute | solution.py:1392
  85.0 11.0 %collective-permute-start.18 = (bf16[2,272,768]{2,1,0:T(8,128)(2,1)}, bf16[2,272,768]{2,1,0:T(8,128)(2,1)}, u32[]{:S(2)}, u32[]{:S(2)}) collective-permute-start(bf16[2,272,768]{2,1,0:T(8,128)(2,1)} %collective-permute-done.17.rest_14_.rest_5_.rest_17_), channel_id=1, source_target_pairs={{0,1},{1,0},{4,5},{5,4},{8,9},{9,8},{12,13},{13,12},{14,15},{15,14... | collective-permute-start | bytes 2506760 | tf_op jit(solution)/shard_map/ppermute | solution.py:1393
  85.4 7.2 %collective-permute-start.26 = (bf16[192,768]{1,0:T(8,128)(2,1)S(1)}, bf16[192,768]{1,0:T(8,128)(2,1)S(1)}, u32[]{:S(2)}, u32[]{:S(2)}) collective-permute-start(bf16[192,768]{1,0:T(8,128)(2,1)S(1)} %fusion.1), channel_id=1, source_target_pairs={{0,4},{1,3},{4,8},{5,1},{8,12},{9,5},{12,14},{13,9},{14,10},{15,13... | collective-permute-start | bytes 884744 | tf_op jit(solution)/shard_map/ppermute | solution.py:1392
  125.8 19.7 %all-to-all-start.1 = ((bf16[16,128,128]{2,1,0:T(8,128)(2,1)}), bf16[16,128,128]{2,1,0:T(8,128)(2,1)}, u32[]{:S(2)}, u32[]{:S(2)}) async-start(bf16[16,128,128]{2,1,0:T(8,128)(2,1)} %bitcast.62), calls=%async_computation.1 | async-start | bytes 1048576 | tf_op jit(solution)/shard_map/all_to_all | solution.py:1467
  (24 other events, 152.6 us)

commit v7 on v6

--- a/solution.py
+++ b/solution.py
@@ -353,7 +353,7 @@
 PAYLOAD = 128
 
 
-def call(kernel, name, ins, outs, scratch, flops=0, touched=0):
+def call(kernel, name, ins, outs, scratch, flops=0, touched=0, limit=67043328):
     return pl.pallas_call(
         kernel,
         name=name,
@@ -361,7 +361,7 @@
         in_specs=[spec for spec, _ in ins],
         out_specs=[spec for spec, _, _ in outs],
         scratch_shapes=scratch,
-        compiler_params=pltpu.CompilerParams(vmem_limit_bytes=67043328),
+        compiler_params=pltpu.CompilerParams(vmem_limit_bytes=limit),
         cost_estimate=pl.CostEstimate(flops=flops, bytes_accessed=touched, transcendentals=0),
     )(*[item for _, item in ins])
 
@@ -857,6 +857,7 @@
         ],
         flops=11_000_000_000,
         touched=16_000_000,
+        limit=50 * 1024 * 1024,
     )
 
 
@@ -914,6 +915,7 @@
         ],
         flops=5_000_000_000,
         touched=8_000_000,
+        limit=50 * 1024 * 1024,
     )
 
 
@@ -1145,6 +1147,7 @@
         ],
         flops=15_000_000_000,
         touched=20_000_000,
+        limit=50 * 1024 * 1024,
     )
 
 
@@ -1253,6 +1256,7 @@
         ],
         flops=17_000_000_000,
         touched=18_000_000,
+        limit=50 * 1024 * 1024,
     )
 
 
@@ -1342,6 +1346,7 @@
         ],
         flops=5_000_000_000,
         touched=2_000_000,
+        limit=50 * 1024 * 1024,
     )
 
 

time: 149 us -> 148 us (level)
  local copies, waits for them, and re-layouts: 4.38 us -> 8.72 us
  Pallas kernels: 64.3 us -> 60 us
    unnamed x34 -> x70, local copies, waits for them, and re-layouts: 4.38 us -> 8.72 us
    pallas_call x9, Pallas kernels: 64.3 us -> 60 us  [call(): pl.pallas_call(kernel, name=name, out_shape=[jax.ShapeDtypeStruct(shape,...]
where the time goes in v7:
time: 148 us; the launch traced here: 147 us
  Pallas kernels  60 us (41%)
  starting transfers between devices  41.3 us (28%)
  waiting for transfers between devices  29.4 us (20%)
  local copies, waits for them, and re-layouts  8.72 us (6%)
  other arithmetic  6.21 us (4%)
  between operations  1.74 us (1%)
    pallas_call x9, Pallas kernels, call(): pl.pallas_call(kernel, name=name, out_shape=[jax.ShapeDtypeStruct(shape,...  60 us
    ppermute x11, waiting for transfers between devices, step(): held = lax.ppermute(after(held, *earlier), BOTH, self.turn)  26.6 us
    ppermute x11, starting transfers between devices, step(): held = lax.ppermute(after(held, *earlier), BOTH, self.turn)  21.8 us
    unnamed x70, local copies, waits for them, and re-layouts  8.72 us
    all_to_all x1, starting transfers between devices, ring_body(): lax.all_to_all(payload, 'dp', 0, 0, tiled=True).reshape(ITEMS, PAYLOAD, 128)  5.05 us
    all_to_all x1, starting transfers between devices, ring_body(): mixes = lax.all_to_all(pooled, 'dp', 0, 0, tiled=True)  4.98 us
    another operation x8, other arithmetic, joined(): jnp.stack([jnp.where(self.first_core, own, other), jnp.where(self.first_c...  4.98 us
    ppermute x2, starting transfers between devices, first_step(): lax.ppermute(item, BOTH, self.turn)  4.6 us
  transfers between devices with their start and end apart: 31, of which 11 were waited for; matrix products, arithmetic and copies ran while one was open for 4% of the time, Pallas kernels for 25%

profile of v7, /device:TPU:0, one launch (start us, length us, event | category | flops | bytes accessed | tf_op | source)
XLA Modules:
  0.0 147.4 jit_solution(5557217382029778149)
XLA Ops:
  1.2 2.2 %pack_first.1 = bf16[168,768]{1,0:T(8,128)(2,1)} custom-call(s32[8]{0:T(128)} %lengths.13, bf16[144,768]{1,0:T(8,128)(2,1)} %bitcast.58, bf16[77,8,768]{2,1,0:T(8,128)(2,1)} %bitcast.60, bf16[1,48]{1,0:T(2,128)(2,1)} %gain.1, bf16[1,48]{1,0:T(2,128)(2,1)} %bias.1, bf16[1,48]{1,0:T(2,128)(2,1)} %rest_2_.1, bf16[1,48]{1,0:T(2,128)(2,1)} %rest_3_.1, ...), custom_call_target="tpu_custom_call" | custom-call | bytes 1500000 | tf_op jit(solution)/shard_map/pack_first/pallas_call | solution.py:357
  3.4 3.0 %collective-permute-start.1 = (bf16[168,768]{1,0:T(8,128)(2,1)}, bf16[168,768]{1,0:T(8,128)(2,1)S(1)}, u32[]{:S(2)}, u32[]{:S(2)}) collective-permute-start(bf16[168,768]{1,0:T(8,128)(2,1)} %pack_first.1), channel_id=1, source_target_pairs={{0,4},{1,3},{4,8},{5,1},{8,12},{9,5},{12,14},{13,9},{14,10},{15,13... | collective-permute-start | bytes 774152 | tf_op jit(solution)/shard_map/ppermute | solution.py:1387
  11.6 2.0 %collective-permute-done.2 = bf16[168,768]{1,0:T(8,128)(2,1)S(1)} collective-permute-done((bf16[168,768]{1,0:T(8,128)(2,1)S(1)}, bf16[168,768]{1,0:T(8,128)(2,1)S(1)}, u32[]{:S(2)}, u32[]{:S(2)}) %collective-permute-start.2) | collective-permute-done | bytes 258080 | tf_op jit(solution)/shard_map/ppermute | solution.py:1387
  14.6 2.1 %collective-permute-start.4 = (bf16[2,168,768]{2,1,0:T(8,128)(2,1)}, bf16[2,168,768]{2,1,0:T(8,128)(2,1)}, u32[]{:S(2)}, u32[]{:S(2)}) collective-permute-start(bf16[2,168,768]{2,1,0:T(8,128)(2,1)} %pad_maximum_fusion.3.rest_1_), channel_id=1, source_target_pairs={{0,4},{1,3},{4,8},{5,1},{8,12},{9,5},{12,14},{13,9},{14,10},{15,13... | collective-permute-start | bytes 1548296 | tf_op jit(solution)/shard_map/ppermute | solution.py:1397
  20.2 5.5 %collective-permute-done.4.rest_3_ = bf16[2,168,768]{2,1,0:T(8,128)(2,1)} collective-permute-done((bf16[2,168,768]{2,1,0:T(8,128)(2,1)}, bf16[2,168,768]{2,1,0:T(8,128)(2,1)}, u32[]{:S(2)}, u32[]{:S(2)}) %collective-permute-start.4) | collective-permute-done | bytes 516128 | tf_op jit(solution)/shard_map/ppermute | solution.py:1397
  25.7 1.9 %collective-permute-start.8 = (bf16[2,168,768]{2,1,0:T(8,128)(2,1)}, bf16[2,168,768]{2,1,0:T(8,128)(2,1)S(1)}, u32[]{:S(2)}, u32[]{:S(2)}) collective-permute-start(bf16[2,168,768]{2,1,0:T(8,128)(2,1)} %collective-permute-done.4.rest_3_), channel_id=1, source_target_pairs={{0,4},{1,3},{4,8},{5,1},{8,12},{9,5},{12,14},{13,9},{14,10},{15,13... | collective-permute-start | bytes 1548296 | tf_op jit(solution)/shard_map/ppermute | solution.py:1397
  31.3 3.8 %collective-permute-done.8.rest_5_ = bf16[2,168,768]{2,1,0:T(8,128)(2,1)S(1)} collective-permute-done((bf16[2,168,768]{2,1,0:T(8,128)(2,1)}, bf16[2,168,768]{2,1,0:T(8,128)(2,1)S(1)}, u32[]{:S(2)}, u32[]{:S(2)}) %collective-permute-start.8) | collective-permute-done | bytes 516128 | tf_op jit(solution)/shard_map/ppermute | solution.py:1397
  35.1 2.0 %collective-permute-start.10 = (bf16[168,768]{1,0:T(8,128)(2,1)S(1)}, bf16[168,768]{1,0:T(8,128)(2,1)S(1)}, u32[]{:S(2)}, u32[]{:S(2)}) collective-permute-start(bf16[168,768]{1,0:T(8,128)(2,1)S(1)} %fusion.2), channel_id=1, source_target_pairs={{0,4},{1,3},{4,8},{5,1},{8,12},{9,5},{12,14},{13,9},{14,10},{15,13... | collective-permute-start | bytes 774152 | tf_op jit(solution)/shard_map/ppermute | solution.py:1397
  37.6 6.5 %collective-permute-done.13.rest_10_.rest_1_.rest_13_ = bf16[2,272,768]{2,1,0:T(8,128)(2,1)} collective-permute-done((bf16[2,272,768]{2,1,0:T(8,128)(2,1)S(1)}, bf16[2,272,768]{2,1,0:T(8,128)(2,1)}, u32[]{:S(2)}, u32[]{:S(2)}) %collective-permute-start.13) | collective-permute-done | bytes 835616 | tf_op jit(solution)/shard_map/ppermute | solution.py:1397
  44.1 1.9 %collective-permute-start.15 = (bf16[2,272,768]{2,1,0:T(8,128)(2,1)}, bf16[2,272,768]{2,1,0:T(8,128)(2,1)}, u32[]{:S(2)}, u32[]{:S(2)}) collective-permute-start(bf16[2,272,768]{2,1,0:T(8,128)(2,1)} %collective-permute-done.13.rest_10_.rest_1_.rest_13_), channel_id=1, source_target_pairs={{0,4},{1,3},{4,8},{5,1},{8,12},{9,5},{12,14},{13,9},{14,10},{15,13... | collective-permute-start | bytes 2506760 | tf_op jit(solution)/shard_map/ppermute | solution.py:1397
  49.8 1.9 %collective-permute-start.22 = (bf16[2,192,768]{2,1,0:T(8,128)(2,1)}, bf16[2,192,768]{2,1,0:T(8,128)(2,1)}, u32[]{:S(2)}, u32[]{:S(2)}) collective-permute-start(bf16[2,192,768]{2,1,0:T(8,128)(2,1)} %collective-permute-done.7.rest_19_.rest_22_), channel_id=1, source_target_pairs={{0,4},{1,3},{4,8},{5,1},{8,12},{9,5},{12,14},{13,9},{14,10},{15,13... | collective-permute-start | bytes 1769480 | tf_op jit(solution)/shard_map/ppermute | solution.py:1397
  51.7 6.2 %attend_pooled.1 = (bf16[616,768]{1,0:T(8,128)(2,1)}, bf16[616,768]{1,0:T(8,128)(2,1)}, bf16[616,768]{1,0:T(8,128)(2,1)}, bf16[616,768]{1,0:T(8,128)(2,1)}, f32[...) custom-call(s32[8]{0:T(128)} %lengths.13, ...), custom_call_target="tpu_custom_call" | custom-call | flops 7000000000 | bytes 10000000 | tf_op jit(solution)/shard_map/attend_pooled/pallas_call | solution.py:357
  58.0 5.0 %all-to-all-start = ((bf16[16,48,128]{2,1,0:T(8,128)(2,1)}), bf16[16,48,128]{2,1,0:T(8,128)(2,1)}, u32[]{:S(2)}, u32[]{:S(2)}) async-start(bf16[16,48,128]{2,1,0:T(8,128)(2,1)} %get-tuple-element.82), calls=%async_computation | async-start | bytes 393216 | tf_op jit(solution)/shard_map/all_to_all | solution.py:1453
  63.0 1.9 %collective-permute-start.17 = (bf16[2,272,768]{2,1,0:T(8,128)(2,1)}, bf16[2,272,768]{2,1,0:T(8,128)(2,1)}, u32[]{:S(2)}, u32[]{:S(2)}) collective-permute-start(bf16[2,272,768]{2,1,0:T(8,128)(2,1)} %collective-permute-done.15.rest_12_.rest_3_.rest_15_), channel_id=1, source_target_pairs={{0,4},{1,3},{4,8},{5,1},{8,12},{9,5},{12,14},{13,9},{14,10},{15,13... | collective-permute-start | bytes 2506760 | tf_op jit(solution)/shard_map/ppermute | solution.py:1397
  64.9 9.1 %attend.1 = (bf16[616,768]{1,0:T(8,128)(2,1)}, bf16[768,128]{1,0:T(8,128)(2,1)}) custom-call(s32[8]{0:T(128)} %lengths.13, f32[16,768]{1,0:T(8,128)} %get-tuple-element.81.vec, bf16[616,128]{1,0:T(8,128)(2,1)} %get-tuple-element.86.gv.rest_10_, bf16[616,768]{1,0:T(8,128)(2,1)} %get-tuple-element.88.normed_hbm, ...), custom_call_target="tpu_custom_call" | custom-call | flops 8999999488 | bytes 10000000 | tf_op jit(solution)/shard_map/attend/pallas_call | solution.py:357
  79.5 2.6 %collective-permute-start.19 = (bf16[272,768]{1,0:T(8,128)(2,1)S(1)}, bf16[272,768]{1,0:T(8,128)(2,1)S(1)}, u32[]{:S(2)}, u32[]{:S(2)}) collective-permute-start(bf16[272,768]{1,0:T(8,128)(2,1)S(1)} %fusion), channel_id=1, source_target_pairs={{0,4},{1,3},{4,8},{5,1},{8,12},{9,5},{12,14},{13,9},{14,10},{15,13... | collective-permute-start | bytes 1253384 | tf_op jit(solution)/shard_map/ppermute | solution.py:1397
  82.0 2.2 %collective-permute-done.24.rest_23_.rest_26_ = bf16[2,192,768]{2,1,0:T(8,128)(2,1)S(1)} collective-permute-done((bf16[2,192,768]{2,1,0:T(8,128)(2,1)}, bf16[2,192,768]{2,1,0:T(8,128)(2,1)S(1)}, u32[]{:S(2)}, u32[]{:S(2)}) %collective-permute-start.24) | collective-permute-done | bytes 589856 | tf_op jit(solution)/shard_map/ppermute | solution.py:1397
  84.6 2.8 %collective-permute-start.26 = (bf16[192,768]{1,0:T(8,128)(2,1)S(1)}, bf16[192,768]{1,0:T(8,128)(2,1)S(1)}, u32[]{:S(2)}, u32[]{:S(2)}) collective-permute-start(bf16[192,768]{1,0:T(8,128)(2,1)S(1)} %fusion.1), channel_id=1, source_target_pairs={{0,4},{1,3},{4,8},{5,1},{8,12},{9,5},{12,14},{13,9},{14,10},{15,13... | collective-permute-start | bytes 884744 | tf_op jit(solution)/shard_map/ppermute | solution.py:1397
  89.1 2.8 %collective-permute-done.26.rest_25_.rest_28_ = bf16[192,768]{1,0:T(8,128)(2,1)S(1)} collective-permute-done((bf16[192,768]{1,0:T(8,128)(2,1)S(1)}, bf16[192,768]{1,0:T(8,128)(2,1)S(1)}, u32[]{:S(2)}, u32[]{:S(2)}) %collective-permute-start.26) | collective-permute-done | bytes 294944 | tf_op jit(solution)/shard_map/ppermute | solution.py:1397
  94.7 8.0 %pooled_forward.1 = (bf16[128,512]{1,0:T(8,128)(2,1)S(1)}, f32[128,512]{1,0:T(8,128)S(1)}, f32[128,768]{1,0:T(8,128)S(1)}, f32[128,128]{1,0:T(8,128)S(1)}, f32[1...) custom-call(s32[8]{0:T(128)S(1)} %copy-done.4, ...), custom_call_target="tpu_custom_call" | custom-call | flops 11000000512 | bytes 16000000 | tf_op jit(solution)/shard_map/pooled_forward/pallas_call | solution.py:357
  104.4 4.4 %middle_part.1 = (bf16[616,768]{1,0:T(8,128)(2,1)}, f32[616,768]{1,0:T(8,128)}) custom-call(s32[8]{0:T(128)S(1)} %copy-done.4, bf16[77,8,768]{2,1,0:T(8,128)(2,1)} %bitcast.62, f32[16,768]{1,0:T(8,128)S(1)} %copy-done.18, bf16[616,768]{1,0:T(8,128)(2,1)} %get-tuple-element.99.mixed_hbm, bf16[2,272,768]{2,1,0:T(8,128)(2,1)S(1)} %copy-done.1, ...), custom_call_target="tpu_custom_call" | custom-call | flops 5000000000 | bytes 8000000 | tf_op jit(solution)/shard_map/middle_part/pallas_call | solution.py:357
  108.8 13.2 %chain.1 = (f32[1,1]{1,0:T(1,128)}, f32[1,1]{1,0:T(1,128)}, f32[48,512]{1,0:T(8,128)}, f32[192,768]{1,0:T(8,128)}, f32[48,3072]{1,0:T(8,128)}, /*index=5*/f32[48...) custom-call(s32[8]{0:T(128)S(1)} %copy-done.4, ...), custom_call_target="tpu_custom_call" | custom-call | flops 15000000512 | bytes 20000000 | tf_op jit(solution)/shard_map/chain/pallas_call | solution.py:357
  123.5 5.1 %all-to-all-start.1 = ((bf16[16,128,128]{2,1,0:T(8,128)(2,1)}), bf16[16,128,128]{2,1,0:T(8,128)(2,1)S(1)}, u32[]{:S(2)}, u32[]{:S(2)}) async-start(bf16[16,128,128]{2,1,0:T(8,128)(2,1)} %bitcast.64), calls=%async_computation.1 | async-start | bytes 1048576 | tf_op jit(solution)/shard_map/all_to_all | solution.py:1472
  129.5 13.2 %close.1 = (bf16[616,768]{1,0:T(8,128)(2,1)}, f32[616,768]{1,0:T(8,128)}, f32[128,768]{1,0:T(8,128)S(1)}, bf16[128,48]{1,0:T(8,128)(2,1)S(1)}) custom-call(s32[8]{0:T(128)S(1)} %copy-done.4, bf16[77,8,768]{2,1,0:T(8,128)(2,1)} %bitcast.63, f32[16,768]{1,0:T(8,128)S(1)} %copy-done.18, bf16[616,128]{1,0:T(8,128)(2,1)S(1)} %copy-done.22, ...), custom_call_target="tpu_custom_call" | custom-call | flops 16999999488 | bytes 18000000 | tf_op jit(solution)/shard_map/close/pallas_call | solution.py:357
  (128 shorter events, 36.2 us)
Async XLA Ops:
  0.7 7.3 %collective-permute-start.6 = (bf16[192,768]{1,0:T(8,128)(2,1)}, bf16[192,768]{1,0:T(8,128)(2,1)}, u32[]{:S(2)}, u32[]{:S(2)}) collective-permute-start(bf16[192,768]{1,0:T(8,128)(2,1)} %bitcast.66), channel_id=1, source_target_pairs={{0,1},{1,0},{4,5},{5,4},{8,9},{9,8},{12,13},{13,12},{14,15},{15,14... | collective-permute-start | bytes 884744 | tf_op jit(solution)/shard_map/ppermute | solution.py:1378
  3.4 8.2 %collective-permute-start.1 = (bf16[168,768]{1,0:T(8,128)(2,1)}, bf16[168,768]{1,0:T(8,128)(2,1)S(1)}, u32[]{:S(2)}, u32[]{:S(2)}) collective-permute-start(bf16[168,768]{1,0:T(8,128)(2,1)} %pack_first.1), channel_id=1, source_target_pairs={{0,4},{1,3},{4,8},{5,1},{8,12},{9,5},{12,14},{13,9},{14,10},{15,13... | collective-permute-start | bytes 774152 | tf_op jit(solution)/shard_map/ppermute | solution.py:1387
  10.0 10.2 %collective-permute-start.7 = (bf16[2,192,768]{2,1,0:T(8,128)(2,1)}, bf16[2,192,768]{2,1,0:T(8,128)(2,1)}, u32[]{:S(2)}, u32[]{:S(2)}) collective-permute-start(bf16[2,192,768]{2,1,0:T(8,128)(2,1)} %pad_maximum_fusion.1.rest_18_.rest_21_), channel_id=1, source_target_pairs={{0,4},{1,3},{4,8},{5,1},{8,12},{9,5},{12,14},{13,9},{14,10},{15,13... | collective-permute-start | bytes 1769480 | tf_op jit(solution)/shard_map/ppermute | solution.py:1397
  14.6 11.2 %collective-permute-start.4 = (bf16[2,168,768]{2,1,0:T(8,128)(2,1)}, bf16[2,168,768]{2,1,0:T(8,128)(2,1)}, u32[]{:S(2)}, u32[]{:S(2)}) collective-permute-start(bf16[2,168,768]{2,1,0:T(8,128)(2,1)} %pad_maximum_fusion.3.rest_1_), channel_id=1, source_target_pairs={{0,4},{1,3},{4,8},{5,1},{8,12},{9,5},{12,14},{13,9},{14,10},{15,13... | collective-permute-start | bytes 1548296 | tf_op jit(solution)/shard_map/ppermute | solution.py:1397
  18.4 9.3 %collective-permute-start.12 = (bf16[272,768]{1,0:T(8,128)(2,1)}, bf16[272,768]{1,0:T(8,128)(2,1)S(1)}, u32[]{:S(2)}, u32[]{:S(2)}) collective-permute-start(bf16[272,768]{1,0:T(8,128)(2,1)} %pack_rest.1), channel_id=1, source_target_pairs={{0,1},{1,0},{4,5},{5,4},{8,9},{9,8},{12,13},{13,12},{14,15},{15,14... | collective-permute-start | bytes 1253384 | tf_op jit(solution)/shard_map/ppermute | solution.py:1378
  25.7 9.3 %collective-permute-start.8 = (bf16[2,168,768]{2,1,0:T(8,128)(2,1)}, bf16[2,168,768]{2,1,0:T(8,128)(2,1)S(1)}, u32[]{:S(2)}, u32[]{:S(2)}) collective-permute-start(bf16[2,168,768]{2,1,0:T(8,128)(2,1)} %collective-permute-done.4.rest_3_), channel_id=1, source_target_pairs={{0,4},{1,3},{4,8},{5,1},{8,12},{9,5},{12,14},{13,9},{14,10},{15,13... | collective-permute-start | bytes 1548296 | tf_op jit(solution)/shard_map/ppermute | solution.py:1397
  29.7 14.4 %collective-permute-start.13 = (bf16[2,272,768]{2,1,0:T(8,128)(2,1)S(1)}, bf16[2,272,768]{2,1,0:T(8,128)(2,1)}, u32[]{:S(2)}, u32[]{:S(2)}) collective-permute-start(bf16[2,272,768]{2,1,0:T(8,128)(2,1)S(1)} %pad_maximum_fusion.rest_9_.rest_0_.rest_12_), channel_id=1, source_target_pairs={{0,4},{1,3},{4,8},{5,1},{8,12},{9,5},{12,14},{13,9},{14,10},{15,13... | collective-permute-start | bytes 2506760 | tf_op jit(solution)/shard_map/ppermute | solution.py:1397
  35.1 11.7 %collective-permute-start.10 = (bf16[168,768]{1,0:T(8,128)(2,1)S(1)}, bf16[168,768]{1,0:T(8,128)(2,1)S(1)}, u32[]{:S(2)}, u32[]{:S(2)}) collective-permute-start(bf16[168,768]{1,0:T(8,128)(2,1)S(1)} %fusion.2), channel_id=1, source_target_pairs={{0,4},{1,3},{4,8},{5,1},{8,12},{9,5},{12,14},{13,9},{14,10},{15,13... | collective-permute-start | bytes 774152 | tf_op jit(solution)/shard_map/ppermute | solution.py:1397
  37.1 11.3 %collective-permute-start.3 = (bf16[2,168,768]{2,1,0:T(8,128)(2,1)}, bf16[2,168,768]{2,1,0:T(8,128)(2,1)S(1)}, u32[]{:S(2)}, u32[]{:S(2)}) collective-permute-start(bf16[2,168,768]{2,1,0:T(8,128)(2,1)} %pad_maximum_fusion.3.rest_1_), channel_id=1, source_target_pairs={{0,1},{1,0},{4,5},{5,4},{8,9},{9,8},{12,13},{13,12},{14,15},{15,14... | collective-permute-start | bytes 1548296 | tf_op jit(solution)/shard_map/ppermute | solution.py:1388
  37.1 11.8 %collective-permute-start.5 = (bf16[2,168,768]{2,1,0:T(8,128)(2,1)}, bf16[2,168,768]{2,1,0:T(8,128)(2,1)S(1)}, u32[]{:S(2)}, u32[]{:S(2)}) collective-permute-start(bf16[2,168,768]{2,1,0:T(8,128)(2,1)} %collective-permute-done.4.rest_3_), channel_id=1, source_target_pairs={{0,1},{1,0},{4,5},{5,4},{8,9},{9,8},{12,13},{13,12},{14,15},{15,14... | collective-permute-start | bytes 1548296 | tf_op jit(solution)/shard_map/ppermute | solution.py:1398
  37.6 14.1 %collective-permute-start.9 = (bf16[2,168,768]{2,1,0:T(8,128)(2,1)S(1)}, bf16[2,168,768]{2,1,0:T(8,128)(2,1)}, u32[]{:S(2)}, u32[]{:S(2)}) collective-permute-start(bf16[2,168,768]{2,1,0:T(8,128)(2,1)S(1)} %collective-permute-done.8.rest_5_), channel_id=1, source_target_pairs={{0,1},{1,0},{4,5},{5,4},{8,9},{9,8},{12,13},{13,12},{14,15},{15,14... | collective-permute-start | bytes 1548296 | tf_op jit(solution)/shard_map/ppermute | solution.py:1398
  44.1 18.8 %collective-permute-start.15 = (bf16[2,272,768]{2,1,0:T(8,128)(2,1)}, bf16[2,272,768]{2,1,0:T(8,128)(2,1)}, u32[]{:S(2)}, u32[]{:S(2)}) collective-permute-start(bf16[2,272,768]{2,1,0:T(8,128)(2,1)} %collective-permute-done.13.rest_10_.rest_1_.rest_13_), channel_id=1, source_target_pairs={{0,4},{1,3},{4,8},{5,1},{8,12},{9,5},{12,14},{13,9},{14,10},{15,13... | collective-permute-start | bytes 2506760 | tf_op jit(solution)/shard_map/ppermute | solution.py:1397
  48.4 31.0 %collective-permute-start.21 = (bf16[2,192,768]{2,1,0:T(8,128)(2,1)}, bf16[2,192,768]{2,1,0:T(8,128)(2,1)}, u32[]{:S(2)}, u32[]{:S(2)}) collective-permute-start(bf16[2,192,768]{2,1,0:T(8,128)(2,1)} %collective-permute-done.7.rest_19_.rest_22_), channel_id=1, source_target_pairs={{0,1},{1,0},{4,5},{5,4},{8,9},{9,8},{12,13},{13,12},{14,15},{15,14... | collective-permute-start | bytes 1769480 | tf_op jit(solution)/shard_map/ppermute | solution.py:1398
  48.9 35.7 %collective-permute-start.14 = (bf16[2,272,768]{2,1,0:T(8,128)(2,1)}, bf16[2,272,768]{2,1,0:T(8,128)(2,1)}, u32[]{:S(2)}, u32[]{:S(2)}) collective-permute-start(bf16[2,272,768]{2,1,0:T(8,128)(2,1)} %collective-permute-done.13.rest_10_.rest_1_.rest_13_), channel_id=1, source_target_pairs={{0,1},{1,0},{4,5},{5,4},{8,9},{9,8},{12,13},{13,12},{14,15},{15,14... | collective-permute-start | bytes 2506760 | tf_op jit(solution)/shard_map/ppermute | solution.py:1398
  49.8 24.3 %collective-permute-start.22 = (bf16[2,192,768]{2,1,0:T(8,128)(2,1)}, bf16[2,192,768]{2,1,0:T(8,128)(2,1)}, u32[]{:S(2)}, u32[]{:S(2)}) collective-permute-start(bf16[2,192,768]{2,1,0:T(8,128)(2,1)} %collective-permute-done.7.rest_19_.rest_22_), channel_id=1, source_target_pairs={{0,4},{1,3},{4,8},{5,1},{8,12},{9,5},{12,14},{13,9},{14,10},{15,13... | collective-permute-start | bytes 1769480 | tf_op jit(solution)/shard_map/ppermute | solution.py:1397
  58.0 16.1 %all-to-all-start = ((bf16[16,48,128]{2,1,0:T(8,128)(2,1)}), bf16[16,48,128]{2,1,0:T(8,128)(2,1)}, u32[]{:S(2)}, u32[]{:S(2)}) async-start(bf16[16,48,128]{2,1,0:T(8,128)(2,1)} %get-tuple-element.82), calls=%async_computation | async-start | bytes 393216 | tf_op jit(solution)/shard_map/all_to_all | solution.py:1453
  63.0 14.5 %collective-permute-start.17 = (bf16[2,272,768]{2,1,0:T(8,128)(2,1)}, bf16[2,272,768]{2,1,0:T(8,128)(2,1)}, u32[]{:S(2)}, u32[]{:S(2)}) collective-permute-start(bf16[2,272,768]{2,1,0:T(8,128)(2,1)} %collective-permute-done.15.rest_12_.rest_3_.rest_15_), channel_id=1, source_target_pairs={{0,4},{1,3},{4,8},{5,1},{8,12},{9,5},{12,14},{13,9},{14,10},{15,13... | collective-permute-start | bytes 2506760 | tf_op jit(solution)/shard_map/ppermute | solution.py:1397
  74.1 10.1 %collective-permute-start.24 = (bf16[2,192,768]{2,1,0:T(8,128)(2,1)}, bf16[2,192,768]{2,1,0:T(8,128)(2,1)S(1)}, u32[]{:S(2)}, u32[]{:S(2)}) collective-permute-start(bf16[2,192,768]{2,1,0:T(8,128)(2,1)} %collective-permute-done.22.rest_21_.rest_24_), channel_id=1, source_target_pairs={{0,4},{1,3},{4,8},{5,1},{8,12},{9,5},{12,14},{13,9},{14,10},{15,13... | collective-permute-start | bytes 1769480 | tf_op jit(solution)/shard_map/ppermute | solution.py:1397
  75.6 11.8 %collective-permute-start.23 = (bf16[2,192,768]{2,1,0:T(8,128)(2,1)}, bf16[2,192,768]{2,1,0:T(8,128)(2,1)S(1)}, u32[]{:S(2)}, u32[]{:S(2)}) collective-permute-start(bf16[2,192,768]{2,1,0:T(8,128)(2,1)} %collective-permute-done.22.rest_21_.rest_24_), channel_id=1, source_target_pairs={{0,1},{1,0},{4,5},{5,4},{8,9},{9,8},{12,13},{13,12},{14,15},{15,14... | collective-permute-start | bytes 1769480 | tf_op jit(solution)/shard_map/ppermute | solution.py:1398
  77.5 15.2 %collective-permute-start.16 = (bf16[2,272,768]{2,1,0:T(8,128)(2,1)}, bf16[2,272,768]{2,1,0:T(8,128)(2,1)S(1)}, u32[]{:S(2)}, u32[]{:S(2)}) collective-permute-start(bf16[2,272,768]{2,1,0:T(8,128)(2,1)} %collective-permute-done.15.rest_12_.rest_3_.rest_15_), channel_id=1, source_target_pairs={{0,1},{1,0},{4,5},{5,4},{8,9},{9,8},{12,13},{13,12},{14,15},{15,14... | collective-permute-start | bytes 2506760 | tf_op jit(solution)/shard_map/ppermute | solution.py:1398
  79.5 9.3 %collective-permute-start.19 = (bf16[272,768]{1,0:T(8,128)(2,1)S(1)}, bf16[272,768]{1,0:T(8,128)(2,1)S(1)}, u32[]{:S(2)}, u32[]{:S(2)}) collective-permute-start(bf16[272,768]{1,0:T(8,128)(2,1)S(1)} %fusion), channel_id=1, source_target_pairs={{0,4},{1,3},{4,8},{5,1},{8,12},{9,5},{12,14},{13,9},{14,10},{15,13... | collective-permute-start | bytes 1253384 | tf_op jit(solution)/shard_map/ppermute | solution.py:1397
  84.2 9.2 %collective-permute-start.18 = (bf16[2,272,768]{2,1,0:T(8,128)(2,1)}, bf16[2,272,768]{2,1,0:T(8,128)(2,1)S(1)}, u32[]{:S(2)}, u32[]{:S(2)}) collective-permute-start(bf16[2,272,768]{2,1,0:T(8,128)(2,1)} %collective-permute-done.17.rest_14_.rest_5_.rest_17_), channel_id=1, source_target_pairs={{0,1},{1,0},{4,5},{5,4},{8,9},{9,8},{12,13},{13,12},{14,15},{15,14... | collective-permute-start | bytes 2506760 | tf_op jit(solution)/shard_map/ppermute | solution.py:1398
  84.6 7.2 %collective-permute-start.26 = (bf16[192,768]{1,0:T(8,128)(2,1)S(1)}, bf16[192,768]{1,0:T(8,128)(2,1)S(1)}, u32[]{:S(2)}, u32[]{:S(2)}) collective-permute-start(bf16[192,768]{1,0:T(8,128)(2,1)S(1)} %fusion.1), channel_id=1, source_target_pairs={{0,4},{1,3},{4,8},{5,1},{8,12},{9,5},{12,14},{13,9},{14,10},{15,13... | collective-permute-start | bytes 884744 | tf_op jit(solution)/shard_map/ppermute | solution.py:1397
  123.5 20.0 %all-to-all-start.1 = ((bf16[16,128,128]{2,1,0:T(8,128)(2,1)}), bf16[16,128,128]{2,1,0:T(8,128)(2,1)S(1)}, u32[]{:S(2)}, u32[]{:S(2)}) async-start(bf16[16,128,128]{2,1,0:T(8,128)(2,1)} %bitcast.64), calls=%async_computation.1 | async-start | bytes 1048576 | tf_op jit(solution)/shard_map/all_to_all | solution.py:1472
  (42 other events, 364.1 us)

commit v8 on v7

--- a/solution.py
+++ b/solution.py
@@ -484,13 +484,13 @@
 
 
 def chunks(count, visit):
-    @pl.loop(0, count // 14)
+    @pl.loop(0, count // 28)
     def _(i):
-        visit(i * 14, aligned(i * 112, 16), 14)
-
-    if count % 14:
-        at = count - count % 14
-        visit(at, at * 8, count % 14)
+        visit(i * 28, aligned(i * 224, 16), 28)
+
+    if count % 28:
+        at = count - count % 28
+        visit(at, at * 8, count % 28)
 
 
 def pack_first_kernel(lengths, qkv, tok, *rest):

time: 148 us -> 148 us (level)
  transfers between devices with their start and end apart: 31 -> 31, of which waited for: 11 -> 12; matrix products, arithmetic and copies ran while one was open for 4% -> 4% of each run, Pallas kernels for 25% -> 25%
where the time goes in v8:
time: 148 us; the launch traced here: 147 us
  Pallas kernels  59.5 us (40%)
  starting transfers between devices  41 us (28%)
  waiting for transfers between devices  30 us (20%)
  local copies, waits for them, and re-layouts  8.72 us (6%)
  other arithmetic  6.21 us (4%)
  between operations  1.72 us (1%)
    pallas_call x9, Pallas kernels, call(): pl.pallas_call(kernel, name=name, out_shape=[jax.ShapeDtypeStruct(shape,...  59.5 us
    ppermute x11, waiting for transfers between devices, step(): held = lax.ppermute(after(held, *earlier), BOTH, self.turn)  26.6 us
    ppermute x11, starting transfers between devices, step(): held = lax.ppermute(after(held, *earlier), BOTH, self.turn)  21.8 us
    unnamed x70, local copies, waits for them, and re-layouts  8.72 us
    all_to_all x1, starting transfers between devices, ring_body(): lax.all_to_all(payload, 'dp', 0, 0, tiled=True).reshape(ITEMS, PAYLOAD, 128)  5.26 us
    all_to_all x1, starting transfers between devices, ring_body(): mixes = lax.all_to_all(pooled, 'dp', 0, 0, tiled=True)  4.98 us
    another operation x8, other arithmetic, joined(): jnp.stack([jnp.where(self.first_core, own, other), jnp.where(self.first_c...  4.98 us
    ppermute x2, starting transfers between devices, first_step(): lax.ppermute(item, BOTH, self.turn)  4.6 us
  transfers between devices with their start and end apart: 31, of which 12 were waited for; matrix products, arithmetic and copies ran while one was open for 4% of the time, Pallas kernels for 25%

profile of v8, /device:TPU:0, one launch (start us, length us, event | category | flops | bytes accessed | tf_op | source)
XLA Modules:
  0.0 147.2 jit_solution(17932780903038359995)
XLA Ops:
  1.2 2.2 %pack_first.1 = bf16[168,768]{1,0:T(8,128)(2,1)} custom-call(s32[8]{0:T(128)} %lengths.13, bf16[144,768]{1,0:T(8,128)(2,1)} %bitcast.58, bf16[77,8,768]{2,1,0:T(8,128)(2,1)} %bitcast.60, bf16[1,48]{1,0:T(2,128)(2,1)} %gain.1, bf16[1,48]{1,0:T(2,128)(2,1)} %bias.1, bf16[1,48]{1,0:T(2,128)(2,1)} %rest_2_.1, bf16[1,48]{1,0:T(2,128)(2,1)} %rest_3_.1, ...), custom_call_target="tpu_custom_call" | custom-call | bytes 1500000 | tf_op jit(solution)/shard_map/pack_first/pallas_call | solution.py:357
  3.4 3.0 %collective-permute-start.1 = (bf16[168,768]{1,0:T(8,128)(2,1)}, bf16[168,768]{1,0:T(8,128)(2,1)S(1)}, u32[]{:S(2)}, u32[]{:S(2)}) collective-permute-start(bf16[168,768]{1,0:T(8,128)(2,1)} %pack_first.1), channel_id=1, source_target_pairs={{0,4},{1,3},{4,8},{5,1},{8,12},{9,5},{12,14},{13,9},{14,10},{15,13... | collective-permute-start | bytes 774152 | tf_op jit(solution)/shard_map/ppermute | solution.py:1387
  11.6 2.0 %collective-permute-done.2 = bf16[168,768]{1,0:T(8,128)(2,1)S(1)} collective-permute-done((bf16[168,768]{1,0:T(8,128)(2,1)S(1)}, bf16[168,768]{1,0:T(8,128)(2,1)S(1)}, u32[]{:S(2)}, u32[]{:S(2)}) %collective-permute-start.2) | collective-permute-done | bytes 258080 | tf_op jit(solution)/shard_map/ppermute | solution.py:1387
  14.6 2.1 %collective-permute-start.4 = (bf16[2,168,768]{2,1,0:T(8,128)(2,1)}, bf16[2,168,768]{2,1,0:T(8,128)(2,1)}, u32[]{:S(2)}, u32[]{:S(2)}) collective-permute-start(bf16[2,168,768]{2,1,0:T(8,128)(2,1)} %pad_maximum_fusion.3.rest_1_), channel_id=1, source_target_pairs={{0,4},{1,3},{4,8},{5,1},{8,12},{9,5},{12,14},{13,9},{14,10},{15,13... | collective-permute-start | bytes 1548296 | tf_op jit(solution)/shard_map/ppermute | solution.py:1397
  20.2 5.5 %collective-permute-done.4.rest_3_ = bf16[2,168,768]{2,1,0:T(8,128)(2,1)} collective-permute-done((bf16[2,168,768]{2,1,0:T(8,128)(2,1)}, bf16[2,168,768]{2,1,0:T(8,128)(2,1)}, u32[]{:S(2)}, u32[]{:S(2)}) %collective-permute-start.4) | collective-permute-done | bytes 516128 | tf_op jit(solution)/shard_map/ppermute | solution.py:1397
  25.7 1.9 %collective-permute-start.8 = (bf16[2,168,768]{2,1,0:T(8,128)(2,1)}, bf16[2,168,768]{2,1,0:T(8,128)(2,1)S(1)}, u32[]{:S(2)}, u32[]{:S(2)}) collective-permute-start(bf16[2,168,768]{2,1,0:T(8,128)(2,1)} %collective-permute-done.4.rest_3_), channel_id=1, source_target_pairs={{0,4},{1,3},{4,8},{5,1},{8,12},{9,5},{12,14},{13,9},{14,10},{15,13... | collective-permute-start | bytes 1548296 | tf_op jit(solution)/shard_map/ppermute | solution.py:1397
  31.3 3.8 %collective-permute-done.8.rest_5_ = bf16[2,168,768]{2,1,0:T(8,128)(2,1)S(1)} collective-permute-done((bf16[2,168,768]{2,1,0:T(8,128)(2,1)}, bf16[2,168,768]{2,1,0:T(8,128)(2,1)S(1)}, u32[]{:S(2)}, u32[]{:S(2)}) %collective-permute-start.8) | collective-permute-done | bytes 516128 | tf_op jit(solution)/shard_map/ppermute | solution.py:1397
  35.1 2.0 %collective-permute-start.10 = (bf16[168,768]{1,0:T(8,128)(2,1)S(1)}, bf16[168,768]{1,0:T(8,128)(2,1)S(1)}, u32[]{:S(2)}, u32[]{:S(2)}) collective-permute-start(bf16[168,768]{1,0:T(8,128)(2,1)S(1)} %fusion.2), channel_id=1, source_target_pairs={{0,4},{1,3},{4,8},{5,1},{8,12},{9,5},{12,14},{13,9},{14,10},{15,13... | collective-permute-start | bytes 774152 | tf_op jit(solution)/shard_map/ppermute | solution.py:1397
  37.6 6.5 %collective-permute-done.13.rest_10_.rest_1_.rest_13_ = bf16[2,272,768]{2,1,0:T(8,128)(2,1)} collective-permute-done((bf16[2,272,768]{2,1,0:T(8,128)(2,1)S(1)}, bf16[2,272,768]{2,1,0:T(8,128)(2,1)}, u32[]{:S(2)}, u32[]{:S(2)}) %collective-permute-start.13) | collective-permute-done | bytes 835616 | tf_op jit(solution)/shard_map/ppermute | solution.py:1397
  44.1 1.9 %collective-permute-start.15 = (bf16[2,272,768]{2,1,0:T(8,128)(2,1)}, bf16[2,272,768]{2,1,0:T(8,128)(2,1)}, u32[]{:S(2)}, u32[]{:S(2)}) collective-permute-start(bf16[2,272,768]{2,1,0:T(8,128)(2,1)} %collective-permute-done.13.rest_10_.rest_1_.rest_13_), channel_id=1, source_target_pairs={{0,4},{1,3},{4,8},{5,1},{8,12},{9,5},{12,14},{13,9},{14,10},{15,13... | collective-permute-start | bytes 2506760 | tf_op jit(solution)/shard_map/ppermute | solution.py:1397
  49.8 1.9 %collective-permute-start.22 = (bf16[2,192,768]{2,1,0:T(8,128)(2,1)}, bf16[2,192,768]{2,1,0:T(8,128)(2,1)}, u32[]{:S(2)}, u32[]{:S(2)}) collective-permute-start(bf16[2,192,768]{2,1,0:T(8,128)(2,1)} %collective-permute-done.7.rest_19_.rest_22_), channel_id=1, source_target_pairs={{0,4},{1,3},{4,8},{5,1},{8,12},{9,5},{12,14},{13,9},{14,10},{15,13... | collective-permute-start | bytes 1769480 | tf_op jit(solution)/shard_map/ppermute | solution.py:1397
  51.7 6.2 %attend_pooled.1 = (bf16[616,768]{1,0:T(8,128)(2,1)}, bf16[616,768]{1,0:T(8,128)(2,1)}, bf16[616,768]{1,0:T(8,128)(2,1)}, bf16[616,768]{1,0:T(8,128)(2,1)}, f32[...) custom-call(s32[8]{0:T(128)} %lengths.13, ...), custom_call_target="tpu_custom_call" | custom-call | flops 7000000000 | bytes 10000000 | tf_op jit(solution)/shard_map/attend_pooled/pallas_call | solution.py:357
  57.9 5.0 %all-to-all-start = ((bf16[16,48,128]{2,1,0:T(8,128)(2,1)}), bf16[16,48,128]{2,1,0:T(8,128)(2,1)}, u32[]{:S(2)}, u32[]{:S(2)}) async-start(bf16[16,48,128]{2,1,0:T(8,128)(2,1)} %get-tuple-element.82), calls=%async_computation | async-start | bytes 393216 | tf_op jit(solution)/shard_map/all_to_all | solution.py:1453
  62.9 1.9 %collective-permute-start.17 = (bf16[2,272,768]{2,1,0:T(8,128)(2,1)}, bf16[2,272,768]{2,1,0:T(8,128)(2,1)}, u32[]{:S(2)}, u32[]{:S(2)}) collective-permute-start(bf16[2,272,768]{2,1,0:T(8,128)(2,1)} %collective-permute-done.15.rest_12_.rest_3_.rest_15_), channel_id=1, source_target_pairs={{0,4},{1,3},{4,8},{5,1},{8,12},{9,5},{12,14},{13,9},{14,10},{15,13... | collective-permute-start | bytes 2506760 | tf_op jit(solution)/shard_map/ppermute | solution.py:1397
  64.9 9.1 %attend.1 = (bf16[616,768]{1,0:T(8,128)(2,1)}, bf16[768,128]{1,0:T(8,128)(2,1)}) custom-call(s32[8]{0:T(128)} %lengths.13, f32[16,768]{1,0:T(8,128)} %get-tuple-element.81.vec, bf16[616,128]{1,0:T(8,128)(2,1)} %get-tuple-element.86.gv.rest_10_, bf16[616,768]{1,0:T(8,128)(2,1)} %get-tuple-element.88.normed_hbm, ...), custom_call_target="tpu_custom_call" | custom-call | flops 8999999488 | bytes 10000000 | tf_op jit(solution)/shard_map/attend/pallas_call | solution.py:357
  79.4 2.6 %collective-permute-start.19 = (bf16[272,768]{1,0:T(8,128)(2,1)S(1)}, bf16[272,768]{1,0:T(8,128)(2,1)S(1)}, u32[]{:S(2)}, u32[]{:S(2)}) collective-permute-start(bf16[272,768]{1,0:T(8,128)(2,1)S(1)} %fusion), channel_id=1, source_target_pairs={{0,4},{1,3},{4,8},{5,1},{8,12},{9,5},{12,14},{13,9},{14,10},{15,13... | collective-permute-start | bytes 1253384 | tf_op jit(solution)/shard_map/ppermute | solution.py:1397
  82.0 2.2 %collective-permute-done.24.rest_23_.rest_26_ = bf16[2,192,768]{2,1,0:T(8,128)(2,1)S(1)} collective-permute-done((bf16[2,192,768]{2,1,0:T(8,128)(2,1)}, bf16[2,192,768]{2,1,0:T(8,128)(2,1)S(1)}, u32[]{:S(2)}, u32[]{:S(2)}) %collective-permute-start.24) | collective-permute-done | bytes 589856 | tf_op jit(solution)/shard_map/ppermute | solution.py:1397
  84.6 2.8 %collective-permute-start.26 = (bf16[192,768]{1,0:T(8,128)(2,1)S(1)}, bf16[192,768]{1,0:T(8,128)(2,1)S(1)}, u32[]{:S(2)}, u32[]{:S(2)}) collective-permute-start(bf16[192,768]{1,0:T(8,128)(2,1)S(1)} %fusion.1), channel_id=1, source_target_pairs={{0,4},{1,3},{4,8},{5,1},{8,12},{9,5},{12,14},{13,9},{14,10},{15,13... | collective-permute-start | bytes 884744 | tf_op jit(solution)/shard_map/ppermute | solution.py:1397
  89.0 2.8 %collective-permute-done.26.rest_25_.rest_28_ = bf16[192,768]{1,0:T(8,128)(2,1)S(1)} collective-permute-done((bf16[192,768]{1,0:T(8,128)(2,1)S(1)}, bf16[192,768]{1,0:T(8,128)(2,1)S(1)}, u32[]{:S(2)}, u32[]{:S(2)}) %collective-permute-start.26) | collective-permute-done | bytes 294944 | tf_op jit(solution)/shard_map/ppermute | solution.py:1397
  94.7 8.0 %pooled_forward.1 = (bf16[128,512]{1,0:T(8,128)(2,1)S(1)}, f32[128,512]{1,0:T(8,128)S(1)}, f32[128,768]{1,0:T(8,128)S(1)}, f32[128,128]{1,0:T(8,128)S(1)}, f32[1...) custom-call(s32[8]{0:T(128)S(1)} %copy-done.4, ...), custom_call_target="tpu_custom_call" | custom-call | flops 11000000512 | bytes 16000000 | tf_op jit(solution)/shard_map/pooled_forward/pallas_call | solution.py:357
  103.9 4.2 %middle_part.1 = (bf16[616,768]{1,0:T(8,128)(2,1)}, f32[616,768]{1,0:T(8,128)}) custom-call(s32[8]{0:T(128)S(1)} %copy-done.4, bf16[77,8,768]{2,1,0:T(8,128)(2,1)} %bitcast.62, f32[16,768]{1,0:T(8,128)S(1)} %copy-done.18, bf16[616,768]{1,0:T(8,128)(2,1)} %get-tuple-element.99.mixed_hbm, bf16[2,272,768]{2,1,0:T(8,128)(2,1)S(1)} %copy-done.1, ...), custom_call_target="tpu_custom_call" | custom-call | flops 5000000000 | bytes 8000000 | tf_op jit(solution)/shard_map/middle_part/pallas_call | solution.py:357
  108.7 13.2 %chain.1 = (f32[1,1]{1,0:T(1,128)}, f32[1,1]{1,0:T(1,128)}, f32[48,512]{1,0:T(8,128)}, f32[192,768]{1,0:T(8,128)}, f32[48,3072]{1,0:T(8,128)}, /*index=5*/f32[48...) custom-call(s32[8]{0:T(128)S(1)} %copy-done.4, ...), custom_call_target="tpu_custom_call" | custom-call | flops 15000000512 | bytes 20000000 | tf_op jit(solution)/shard_map/chain/pallas_call | solution.py:357
  123.4 5.3 %all-to-all-start.1 = ((bf16[16,128,128]{2,1,0:T(8,128)(2,1)}), bf16[16,128,128]{2,1,0:T(8,128)(2,1)S(1)}, u32[]{:S(2)}, u32[]{:S(2)}) async-start(bf16[16,128,128]{2,1,0:T(8,128)(2,1)} %bitcast.64), calls=%async_computation.1 | async-start | bytes 1048576 | tf_op jit(solution)/shard_map/all_to_all | solution.py:1472
  129.6 12.9 %close.1 = (bf16[616,768]{1,0:T(8,128)(2,1)}, f32[616,768]{1,0:T(8,128)}, f32[128,768]{1,0:T(8,128)S(1)}, bf16[128,48]{1,0:T(8,128)(2,1)S(1)}) custom-call(s32[8]{0:T(128)S(1)} %copy-done.4, bf16[77,8,768]{2,1,0:T(8,128)(2,1)} %bitcast.63, f32[16,768]{1,0:T(8,128)S(1)} %copy-done.18, bf16[616,128]{1,0:T(8,128)(2,1)S(1)} %copy-done.22, ...), custom_call_target="tpu_custom_call" | custom-call | flops 16999999488 | bytes 18000000 | tf_op jit(solution)/shard_map/close/pallas_call | solution.py:357
  (128 shorter events, 36.3 us)
Async XLA Ops:
  0.7 7.3 %collective-permute-start.6 = (bf16[192,768]{1,0:T(8,128)(2,1)}, bf16[192,768]{1,0:T(8,128)(2,1)}, u32[]{:S(2)}, u32[]{:S(2)}) collective-permute-start(bf16[192,768]{1,0:T(8,128)(2,1)} %bitcast.66), channel_id=1, source_target_pairs={{0,1},{1,0},{4,5},{5,4},{8,9},{9,8},{12,13},{13,12},{14,15},{15,14... | collective-permute-start | bytes 884744 | tf_op jit(solution)/shard_map/ppermute | solution.py:1378
  3.4 8.2 %collective-permute-start.1 = (bf16[168,768]{1,0:T(8,128)(2,1)}, bf16[168,768]{1,0:T(8,128)(2,1)S(1)}, u32[]{:S(2)}, u32[]{:S(2)}) collective-permute-start(bf16[168,768]{1,0:T(8,128)(2,1)} %pack_first.1), channel_id=1, source_target_pairs={{0,4},{1,3},{4,8},{5,1},{8,12},{9,5},{12,14},{13,9},{14,10},{15,13... | collective-permute-start | bytes 774152 | tf_op jit(solution)/shard_map/ppermute | solution.py:1387
  10.0 10.2 %collective-permute-start.7 = (bf16[2,192,768]{2,1,0:T(8,128)(2,1)}, bf16[2,192,768]{2,1,0:T(8,128)(2,1)}, u32[]{:S(2)}, u32[]{:S(2)}) collective-permute-start(bf16[2,192,768]{2,1,0:T(8,128)(2,1)} %pad_maximum_fusion.1.rest_18_.rest_21_), channel_id=1, source_target_pairs={{0,4},{1,3},{4,8},{5,1},{8,12},{9,5},{12,14},{13,9},{14,10},{15,13... | collective-permute-start | bytes 1769480 | tf_op jit(solution)/shard_map/ppermute | solution.py:1397
  14.6 11.2 %collective-permute-start.4 = (bf16[2,168,768]{2,1,0:T(8,128)(2,1)}, bf16[2,168,768]{2,1,0:T(8,128)(2,1)}, u32[]{:S(2)}, u32[]{:S(2)}) collective-permute-start(bf16[2,168,768]{2,1,0:T(8,128)(2,1)} %pad_maximum_fusion.3.rest_1_), channel_id=1, source_target_pairs={{0,4},{1,3},{4,8},{5,1},{8,12},{9,5},{12,14},{13,9},{14,10},{15,13... | collective-permute-start | bytes 1548296 | tf_op jit(solution)/shard_map/ppermute | solution.py:1397
  18.4 9.3 %collective-permute-start.12 = (bf16[272,768]{1,0:T(8,128)(2,1)}, bf16[272,768]{1,0:T(8,128)(2,1)S(1)}, u32[]{:S(2)}, u32[]{:S(2)}) collective-permute-start(bf16[272,768]{1,0:T(8,128)(2,1)} %pack_rest.1), channel_id=1, source_target_pairs={{0,1},{1,0},{4,5},{5,4},{8,9},{9,8},{12,13},{13,12},{14,15},{15,14... | collective-permute-start | bytes 1253384 | tf_op jit(solution)/shard_map/ppermute | solution.py:1378
  25.7 9.3 %collective-permute-start.8 = (bf16[2,168,768]{2,1,0:T(8,128)(2,1)}, bf16[2,168,768]{2,1,0:T(8,128)(2,1)S(1)}, u32[]{:S(2)}, u32[]{:S(2)}) collective-permute-start(bf16[2,168,768]{2,1,0:T(8,128)(2,1)} %collective-permute-done.4.rest_3_), channel_id=1, source_target_pairs={{0,4},{1,3},{4,8},{5,1},{8,12},{9,5},{12,14},{13,9},{14,10},{15,13... | collective-permute-start | bytes 1548296 | tf_op jit(solution)/shard_map/ppermute | solution.py:1397
  29.7 14.4 %collective-permute-start.13 = (bf16[2,272,768]{2,1,0:T(8,128)(2,1)S(1)}, bf16[2,272,768]{2,1,0:T(8,128)(2,1)}, u32[]{:S(2)}, u32[]{:S(2)}) collective-permute-start(bf16[2,272,768]{2,1,0:T(8,128)(2,1)S(1)} %pad_maximum_fusion.rest_9_.rest_0_.rest_12_), channel_id=1, source_target_pairs={{0,4},{1,3},{4,8},{5,1},{8,12},{9,5},{12,14},{13,9},{14,10},{15,13... | collective-permute-start | bytes 2506760 | tf_op jit(solution)/shard_map/ppermute | solution.py:1397
  35.1 11.7 %collective-permute-start.10 = (bf16[168,768]{1,0:T(8,128)(2,1)S(1)}, bf16[168,768]{1,0:T(8,128)(2,1)S(1)}, u32[]{:S(2)}, u32[]{:S(2)}) collective-permute-start(bf16[168,768]{1,0:T(8,128)(2,1)S(1)} %fusion.2), channel_id=1, source_target_pairs={{0,4},{1,3},{4,8},{5,1},{8,12},{9,5},{12,14},{13,9},{14,10},{15,13... | collective-permute-start | bytes 774152 | tf_op jit(solution)/shard_map/ppermute | solution.py:1397
  37.1 11.3 %collective-permute-start.3 = (bf16[2,168,768]{2,1,0:T(8,128)(2,1)}, bf16[2,168,768]{2,1,0:T(8,128)(2,1)S(1)}, u32[]{:S(2)}, u32[]{:S(2)}) collective-permute-start(bf16[2,168,768]{2,1,0:T(8,128)(2,1)} %pad_maximum_fusion.3.rest_1_), channel_id=1, source_target_pairs={{0,1},{1,0},{4,5},{5,4},{8,9},{9,8},{12,13},{13,12},{14,15},{15,14... | collective-permute-start | bytes 1548296 | tf_op jit(solution)/shard_map/ppermute | solution.py:1388
  37.1 11.8 %collective-permute-start.5 = (bf16[2,168,768]{2,1,0:T(8,128)(2,1)}, bf16[2,168,768]{2,1,0:T(8,128)(2,1)S(1)}, u32[]{:S(2)}, u32[]{:S(2)}) collective-permute-start(bf16[2,168,768]{2,1,0:T(8,128)(2,1)} %collective-permute-done.4.rest_3_), channel_id=1, source_target_pairs={{0,1},{1,0},{4,5},{5,4},{8,9},{9,8},{12,13},{13,12},{14,15},{15,14... | collective-permute-start | bytes 1548296 | tf_op jit(solution)/shard_map/ppermute | solution.py:1398
  37.6 14.1 %collective-permute-start.9 = (bf16[2,168,768]{2,1,0:T(8,128)(2,1)S(1)}, bf16[2,168,768]{2,1,0:T(8,128)(2,1)}, u32[]{:S(2)}, u32[]{:S(2)}) collective-permute-start(bf16[2,168,768]{2,1,0:T(8,128)(2,1)S(1)} %collective-permute-done.8.rest_5_), channel_id=1, source_target_pairs={{0,1},{1,0},{4,5},{5,4},{8,9},{9,8},{12,13},{13,12},{14,15},{15,14... | collective-permute-start | bytes 1548296 | tf_op jit(solution)/shard_map/ppermute | solution.py:1398
  44.1 18.8 %collective-permute-start.15 = (bf16[2,272,768]{2,1,0:T(8,128)(2,1)}, bf16[2,272,768]{2,1,0:T(8,128)(2,1)}, u32[]{:S(2)}, u32[]{:S(2)}) collective-permute-start(bf16[2,272,768]{2,1,0:T(8,128)(2,1)} %collective-permute-done.13.rest_10_.rest_1_.rest_13_), channel_id=1, source_target_pairs={{0,4},{1,3},{4,8},{5,1},{8,12},{9,5},{12,14},{13,9},{14,10},{15,13... | collective-permute-start | bytes 2506760 | tf_op jit(solution)/shard_map/ppermute | solution.py:1397
  48.4 31.0 %collective-permute-start.21 = (bf16[2,192,768]{2,1,0:T(8,128)(2,1)}, bf16[2,192,768]{2,1,0:T(8,128)(2,1)}, u32[]{:S(2)}, u32[]{:S(2)}) collective-permute-start(bf16[2,192,768]{2,1,0:T(8,128)(2,1)} %collective-permute-done.7.rest_19_.rest_22_), channel_id=1, source_target_pairs={{0,1},{1,0},{4,5},{5,4},{8,9},{9,8},{12,13},{13,12},{14,15},{15,14... | collective-permute-start | bytes 1769480 | tf_op jit(solution)/shard_map/ppermute | solution.py:1398
  48.9 35.7 %collective-permute-start.14 = (bf16[2,272,768]{2,1,0:T(8,128)(2,1)}, bf16[2,272,768]{2,1,0:T(8,128)(2,1)}, u32[]{:S(2)}, u32[]{:S(2)}) collective-permute-start(bf16[2,272,768]{2,1,0:T(8,128)(2,1)} %collective-permute-done.13.rest_10_.rest_1_.rest_13_), channel_id=1, source_target_pairs={{0,1},{1,0},{4,5},{5,4},{8,9},{9,8},{12,13},{13,12},{14,15},{15,14... | collective-permute-start | bytes 2506760 | tf_op jit(solution)/shard_map/ppermute | solution.py:1398
  49.8 24.3 %collective-permute-start.22 = (bf16[2,192,768]{2,1,0:T(8,128)(2,1)}, bf16[2,192,768]{2,1,0:T(8,128)(2,1)}, u32[]{:S(2)}, u32[]{:S(2)}) collective-permute-start(bf16[2,192,768]{2,1,0:T(8,128)(2,1)} %collective-permute-done.7.rest_19_.rest_22_), channel_id=1, source_target_pairs={{0,4},{1,3},{4,8},{5,1},{8,12},{9,5},{12,14},{13,9},{14,10},{15,13... | collective-permute-start | bytes 1769480 | tf_op jit(solution)/shard_map/ppermute | solution.py:1397
  57.9 16.1 %all-to-all-start = ((bf16[16,48,128]{2,1,0:T(8,128)(2,1)}), bf16[16,48,128]{2,1,0:T(8,128)(2,1)}, u32[]{:S(2)}, u32[]{:S(2)}) async-start(bf16[16,48,128]{2,1,0:T(8,128)(2,1)} %get-tuple-element.82), calls=%async_computation | async-start | bytes 393216 | tf_op jit(solution)/shard_map/all_to_all | solution.py:1453
  62.9 14.5 %collective-permute-start.17 = (bf16[2,272,768]{2,1,0:T(8,128)(2,1)}, bf16[2,272,768]{2,1,0:T(8,128)(2,1)}, u32[]{:S(2)}, u32[]{:S(2)}) collective-permute-start(bf16[2,272,768]{2,1,0:T(8,128)(2,1)} %collective-permute-done.15.rest_12_.rest_3_.rest_15_), channel_id=1, source_target_pairs={{0,4},{1,3},{4,8},{5,1},{8,12},{9,5},{12,14},{13,9},{14,10},{15,13... | collective-permute-start | bytes 2506760 | tf_op jit(solution)/shard_map/ppermute | solution.py:1397
  74.1 10.1 %collective-permute-start.24 = (bf16[2,192,768]{2,1,0:T(8,128)(2,1)}, bf16[2,192,768]{2,1,0:T(8,128)(2,1)S(1)}, u32[]{:S(2)}, u32[]{:S(2)}) collective-permute-start(bf16[2,192,768]{2,1,0:T(8,128)(2,1)} %collective-permute-done.22.rest_21_.rest_24_), channel_id=1, source_target_pairs={{0,4},{1,3},{4,8},{5,1},{8,12},{9,5},{12,14},{13,9},{14,10},{15,13... | collective-permute-start | bytes 1769480 | tf_op jit(solution)/shard_map/ppermute | solution.py:1397
  75.6 11.8 %collective-permute-start.23 = (bf16[2,192,768]{2,1,0:T(8,128)(2,1)}, bf16[2,192,768]{2,1,0:T(8,128)(2,1)S(1)}, u32[]{:S(2)}, u32[]{:S(2)}) collective-permute-start(bf16[2,192,768]{2,1,0:T(8,128)(2,1)} %collective-permute-done.22.rest_21_.rest_24_), channel_id=1, source_target_pairs={{0,1},{1,0},{4,5},{5,4},{8,9},{9,8},{12,13},{13,12},{14,15},{15,14... | collective-permute-start | bytes 1769480 | tf_op jit(solution)/shard_map/ppermute | solution.py:1398
  77.5 15.2 %collective-permute-start.16 = (bf16[2,272,768]{2,1,0:T(8,128)(2,1)}, bf16[2,272,768]{2,1,0:T(8,128)(2,1)S(1)}, u32[]{:S(2)}, u32[]{:S(2)}) collective-permute-start(bf16[2,272,768]{2,1,0:T(8,128)(2,1)} %collective-permute-done.15.rest_12_.rest_3_.rest_15_), channel_id=1, source_target_pairs={{0,1},{1,0},{4,5},{5,4},{8,9},{9,8},{12,13},{13,12},{14,15},{15,14... | collective-permute-start | bytes 2506760 | tf_op jit(solution)/shard_map/ppermute | solution.py:1398
  79.4 9.3 %collective-permute-start.19 = (bf16[272,768]{1,0:T(8,128)(2,1)S(1)}, bf16[272,768]{1,0:T(8,128)(2,1)S(1)}, u32[]{:S(2)}, u32[]{:S(2)}) collective-permute-start(bf16[272,768]{1,0:T(8,128)(2,1)S(1)} %fusion), channel_id=1, source_target_pairs={{0,4},{1,3},{4,8},{5,1},{8,12},{9,5},{12,14},{13,9},{14,10},{15,13... | collective-permute-start | bytes 1253384 | tf_op jit(solution)/shard_map/ppermute | solution.py:1397
  84.2 9.2 %collective-permute-start.18 = (bf16[2,272,768]{2,1,0:T(8,128)(2,1)}, bf16[2,272,768]{2,1,0:T(8,128)(2,1)S(1)}, u32[]{:S(2)}, u32[]{:S(2)}) collective-permute-start(bf16[2,272,768]{2,1,0:T(8,128)(2,1)} %collective-permute-done.17.rest_14_.rest_5_.rest_17_), channel_id=1, source_target_pairs={{0,1},{1,0},{4,5},{5,4},{8,9},{9,8},{12,13},{13,12},{14,15},{15,14... | collective-permute-start | bytes 2506760 | tf_op jit(solution)/shard_map/ppermute | solution.py:1398
  84.6 7.2 %collective-permute-start.26 = (bf16[192,768]{1,0:T(8,128)(2,1)S(1)}, bf16[192,768]{1,0:T(8,128)(2,1)S(1)}, u32[]{:S(2)}, u32[]{:S(2)}) collective-permute-start(bf16[192,768]{1,0:T(8,128)(2,1)S(1)} %fusion.1), channel_id=1, source_target_pairs={{0,4},{1,3},{4,8},{5,1},{8,12},{9,5},{12,14},{13,9},{14,10},{15,13... | collective-permute-start | bytes 884744 | tf_op jit(solution)/shard_map/ppermute | solution.py:1397
  123.4 19.9 %all-to-all-start.1 = ((bf16[16,128,128]{2,1,0:T(8,128)(2,1)}), bf16[16,128,128]{2,1,0:T(8,128)(2,1)S(1)}, u32[]{:S(2)}, u32[]{:S(2)}) async-start(bf16[16,128,128]{2,1,0:T(8,128)(2,1)} %bitcast.64), calls=%async_computation.1 | async-start | bytes 1048576 | tf_op jit(solution)/shard_map/all_to_all | solution.py:1472
  (42 other events, 363.8 us)
